TPU v7x, 32 devices: a whole 2x2x4 slice. The times are simulated.
32 devices in a mesh: shard: 4 (over z), ctx: 4 (over x, core), tensor: 2 (over y).
Axes of the slice: x: 2, y: 2, z: 4, core: 2. Of those that a mesh axis runs over, the one named last changes fastest.
Arguments:
- tokens_in: bfloat16 [8192, 1024], P(('shard', 'ctx')), may hold values from -6 to 6
- cotangent: bfloat16 [8192, 1024], P(('shard', 'ctx')), may hold values from -6 to 6
- segment_ids: int32 [4, 2048], P('shard', 'ctx'), may hold values from 0 to 7, never falling along the last dimension, each value on 1 to 1024 neighbouring positions
- live_blocks: int32 [4, 4, 4], P('shard'), may hold values from 0 to 1, as said below
- routes: int32 [8192, 2], P(('shard', 'ctx')), may hold values from 0 to 3, all different within a row; in each aligned block of 512 rows (0 to 511, 512 to 1023, ...) at most 384 rows name the same one
- w_query: float32 [1024, 1024], P(('shard', 'ctx'), 'tensor'), may hold values from -0.1875 to 0.1875
- w_key: float32 [1024, 1024], P(('shard', 'ctx'), 'tensor'), may hold values from -0.1875 to 0.1875
- w_value: float32 [1024, 1024], P(('shard', 'ctx'), 'tensor'), may hold values from -0.1875 to 0.1875
- w_out: float32 [1024, 1024], P(('shard', 'ctx'), 'tensor'), may hold values from -0.75 to 0.75
- rel_bias: float32 [32, 16], P(None, 'tensor'), may hold values from -4 to 4
- attn_gain: float32 [1024], P(('shard', 'ctx')), may hold values from 0.5 to 1.5
- ffn_gain: float32 [1024], P(('shard', 'ctx')), may hold values from 0.5 to 1.5
- router: float32 [1024, 4], P(('shard', 'ctx')), may hold values from -0.125 to 0.125
- w_gate: float32 [4, 1024, 2816], P('shard', 'ctx', 'tensor'), may hold values from -0.1875 to 0.1875
- w_up: float32 [4, 1024, 2816], P('shard', 'ctx', 'tensor'), may hold values from -0.1875 to 0.1875
- w_down: float32 [4, 1024, 2816], P('shard', 'ctx', 'tensor'), may hold values from -0.109375 to 0.109375
Outputs:
- mixed: bfloat16 [8192, 1024], P(('shard', 'ctx'))
- grad_input: bfloat16 [8192, 1024], P(('shard', 'ctx'))
- grad_query: float32 [1024, 1024], P(('shard', 'ctx'), 'tensor')
- grad_key: float32 [1024, 1024], P(('shard', 'ctx'), 'tensor')
- grad_value: float32 [1024, 1024], P(('shard', 'ctx'), 'tensor')
- grad_out: float32 [1024, 1024], P(('shard', 'ctx'), 'tensor')
- grad_bias: float32 [32, 16], P(None, 'tensor')
- grad_attn_gain: float32 [1024], P(('shard', 'ctx'))
- grad_ffn_gain: float32 [1024], P(('shard', 'ctx'))
- grad_router: float32 [1024, 4], P(('shard', 'ctx'))
- grad_gate: float32 [4, 1024, 2816], P('shard', 'ctx', 'tensor')
- grad_up: float32 [4, 1024, 2816], P('shard', 'ctx', 'tensor')
- grad_down: float32 [4, 1024, 2816], P('shard', 'ctx', 'tensor')
Inputs may be any that keep to these rules, and one draw needn't show every extreme that they name: `segment_ids`: ids never fall along a sequence; each document has 1 to 1024 positions and one has exactly 1024. live_blocks[s, b, b] = 1 for every sequence s and block b. `routes`: the experts of a row differ; in the rows of one device (aligned blocks of 512 rows) no expert is named more than 384 times, and in some blocks one is named exactly 384 times.
All inputs are finite; a program needn't handle non-finite values.
Results may differ from a plain program's by a relative error of at most 0.025.
Values may be sent and summed in bfloat16 or wider, within the bound.
A program may use at most 192 MiB of HBM per device.

v0:
```python
from functools import partial

import jax
import jax.numpy as jnp
from jax import lax
from jax.sharding import PartitionSpec as P

HEAD = 64
NBUCK = 32
TOP = 2
ATT_BLK = 512


FAR_STEPS = (12, 16, 23, 32, 46, 64, 91)


def bucket_ids(relative):
    distance = jnp.abs(relative)
    far = jnp.full(distance.shape, 8, jnp.int32)
    for bound in FAR_STEPS:
        far = far + (distance >= bound).astype(jnp.int32)
    near = jnp.where(distance < 8, distance, far)
    return near + jnp.where(relative > 0, NBUCK // 2, 0)


def fold_blocks(part_fn, carry, pieces):
    count = pieces[0].shape[0]
    step_rows = ATT_BLK
    blocks = count // step_rows
    shaped = tuple((member.reshape((blocks, step_rows) + member.shape[1:]) for member in pieces))
    offsets = step_rows * jnp.arange(blocks, dtype=jnp.int32)

    def advance(state, element):
        return (part_fn(state, element[0], element[1]), None)

    carry, unused = lax.scan(advance, carry, (shaped, offsets))
    return carry


def contract_rows(left, right):
    return lax.dot_general(
        left, right, (((0,), (0,)), ((), ())), preferred_element_type=jnp.float32
    )


def contract_cols(left, right):
    return lax.dot_general(
        left, right, (((1,), (1,)), ((), ())), preferred_element_type=jnp.float32
    )


def local(
    tokens_in,
    cotangent,
    segment_ids,
    live_blocks,
    routes,
    w_query,
    w_key,
    w_value,
    w_out,
    rel_bias,
    attn_gain,
    ffn_gain,
    router,
    w_gate,
    w_up,
    w_down,
):
    width = tokens_in.shape[1]
    rows_here = tokens_in.shape[0]
    ctx_size = lax.axis_size("ctx")
    ctx_index = lax.axis_index("ctx")
    gathered = (
        lax.all_gather(w_query.astype(jnp.bfloat16), ("shard", "ctx"), axis=0, tiled=True),
        lax.all_gather(w_key.astype(jnp.bfloat16), ("shard", "ctx"), axis=0, tiled=True),
        lax.all_gather(w_value.astype(jnp.bfloat16), ("shard", "ctx"), axis=0, tiled=True),
        lax.all_gather(w_out.astype(jnp.bfloat16), ("shard", "ctx"), axis=0, tiled=True),
        lax.all_gather(attn_gain.astype(jnp.bfloat16), ("shard", "ctx"), axis=0, tiled=True),
        lax.all_gather(ffn_gain.astype(jnp.bfloat16), ("shard", "ctx"), axis=0, tiled=True),
        lax.all_gather(router.astype(jnp.bfloat16), ("shard", "ctx"), axis=0, tiled=True),
    )
    query_w, key_w, value_w, out_w, gain_one, gain_two, router_w = gathered
    inputs = tokens_in.astype(jnp.float32)
    scale_one = lax.rsqrt(jnp.mean(inputs * inputs, axis=1, keepdims=True) + 1e-06)
    normal_one = inputs * scale_one
    norm_one = (normal_one * gain_one.astype(jnp.float32)).astype(jnp.bfloat16)
    query = jnp.dot(norm_one, query_w, preferred_element_type=jnp.float32).astype(jnp.bfloat16)
    keys = jnp.dot(norm_one, key_w, preferred_element_type=jnp.float32).astype(jnp.bfloat16)
    values = jnp.dot(norm_one, value_w, preferred_element_type=jnp.float32).astype(jnp.bfloat16)
    head_cols = query.shape[1]
    local_heads = head_cols // HEAD
    buckets = rel_bias.shape[0]
    bucket_range = jnp.arange(buckets, dtype=jnp.int32)
    places = ctx_index * rows_here + jnp.arange(rows_here, dtype=jnp.int32)
    segments = segment_ids.reshape(-1)
    live_rows = jnp.take(live_blocks[0], places // ATT_BLK, axis=0)
    query_heads = query.reshape(rows_here, local_heads, HEAD)

    def block_scores(key_piece, segment_piece, start):
        count = key_piece.shape[0]
        key_places = start + jnp.arange(count, dtype=jnp.int32)
        key_heads = key_piece.reshape(count, local_heads, HEAD)
        scores = (
            jnp.einsum("qhd,khd->hqk", query_heads, key_heads, preferred_element_type=jnp.float32)
            * 0.125
        )
        index = bucket_ids(key_places[None, :] - places[:, None])
        onehot = (index[:, :, None] == bucket_range[None, None, :]).astype(jnp.float32)
        scores = scores + jnp.einsum(
            "qkb,bh->hqk", onehot, rel_bias, precision=lax.Precision.HIGHEST
        )
        allowed = (segments[:, None] == segment_piece[None, :]) & (
            jnp.take(live_rows, key_places // ATT_BLK, axis=1) == 1
        )
        return (scores, allowed, onehot, key_heads)

    def forward_part(carry, pieces, start):
        running_max, running_sum, weighted = carry
        key_piece, value_piece, segment_piece = pieces
        count = key_piece.shape[0]
        scores, allowed, onehot, key_heads = block_scores(key_piece, segment_piece, start)
        masked = jnp.where(allowed[None], scores, -1e30)
        new_max = jnp.maximum(running_max, jnp.max(masked, axis=2))
        weights = jnp.where(allowed[None], jnp.exp(masked - new_max[..., None]), 0.0)
        shrink = jnp.exp(running_max - new_max)
        running_sum = running_sum * shrink + jnp.sum(weights, axis=2)
        value_heads = value_piece.reshape(count, local_heads, HEAD)
        weighted = weighted * shrink[..., None] + jnp.einsum(
            "hqk,khd->hqd",
            weights.astype(jnp.bfloat16),
            value_heads,
            preferred_element_type=jnp.float32,
        )
        return (new_max, running_sum, weighted)

    start_state = (
        jnp.full((local_heads, rows_here), -1e30, jnp.float32),
        jnp.zeros((local_heads, rows_here), jnp.float32),
        jnp.zeros((local_heads, rows_here, HEAD), jnp.float32),
    )
    running_max, running_sum, weighted = fold_blocks(
        forward_part,
        start_state,
        (
            lax.all_gather(keys, "ctx", axis=0, tiled=True),
            lax.all_gather(values, "ctx", axis=0, tiled=True),
            lax.all_gather(segments, "ctx", axis=0, tiled=True),
        ),
    )
    attended = weighted / running_sum[..., None]
    log_total = running_max + jnp.log(running_sum)
    attended_low = (
        jnp.transpose(attended, (1, 0, 2)).reshape(rows_here, head_cols).astype(jnp.bfloat16)
    )
    branch = lax.psum(contract_cols(attended_low, out_w).astype(jnp.bfloat16), "tensor").astype(
        jnp.float32
    )
    hidden_one = inputs + branch
    scale_two = lax.rsqrt(jnp.mean(hidden_one * hidden_one, axis=1, keepdims=True) + 1e-06)
    normal_two = hidden_one * scale_two
    norm_two = (normal_two * gain_two.astype(jnp.float32)).astype(jnp.bfloat16)
    logits = jnp.dot(norm_two, router_w, preferred_element_type=jnp.float32)
    experts = router_w.shape[1]
    picks = routes[:, :, None] == jnp.arange(experts, dtype=jnp.int32)[None, None, :]
    chosen = jnp.sum(jnp.where(picks, logits[:, None, :], 0.0), axis=2)
    gates = jax.nn.softmax(chosen, axis=1)
    upstream = cotangent.astype(jnp.float32)
    flat_picks = picks.reshape(rows_here * TOP, experts).astype(jnp.int32)
    slot_of = jnp.sum(flat_picks * (jnp.cumsum(flat_picks, axis=0) - 1), axis=1)
    expert_of = routes.reshape(-1)
    capacity = max(2, 3 * rows_here // experts)
    shaped = (experts, capacity, width)
    send_rows = (
        jnp.zeros(shaped, jnp.bfloat16)
        .at[expert_of, slot_of]
        .set(jnp.repeat(norm_two, TOP, axis=0))
    )
    grad_rows = (
        (gates[:, :, None] * upstream[:, None, :])
        .reshape(rows_here * TOP, width)
        .astype(jnp.bfloat16)
    )
    send_grads = jnp.zeros(shaped, jnp.bfloat16).at[expert_of, slot_of].set(grad_rows)
    got_rows, got_grads = (
        lax.all_to_all(send_rows, "shard", split_axis=0, concat_axis=0, tiled=True),
        lax.all_to_all(send_grads, "shard", split_axis=0, concat_axis=0, tiled=True),
    )
    expert_gate, expert_up, expert_down = (
        lax.all_gather(w_gate.astype(jnp.bfloat16), "ctx", axis=1, tiled=True),
        lax.all_gather(w_up.astype(jnp.bfloat16), "ctx", axis=1, tiled=True),
        lax.all_gather(w_down.astype(jnp.bfloat16), "ctx", axis=1, tiled=True),
    )
    gate_mat = expert_gate[0]
    up_mat = expert_up[0]
    down_mat = expert_down[0]
    slot_rows = got_rows.reshape(-1, width)
    slot_grads = got_grads.reshape(-1, width)
    gate_pre = jnp.dot(slot_rows, gate_mat, preferred_element_type=jnp.float32)
    up_pre = jnp.dot(slot_rows, up_mat, preferred_element_type=jnp.float32)
    activated, gelu_back = jax.vjp(partial(jax.nn.gelu, approximate=True), gate_pre)
    inner = (activated * up_pre).astype(jnp.bfloat16)
    expert_out = contract_cols(inner, down_mat)
    inner_grad = jnp.dot(slot_grads, down_mat, preferred_element_type=jnp.float32)
    gate_grad = gelu_back(inner_grad * up_pre)[0].astype(jnp.bfloat16)
    up_grad = (inner_grad * activated).astype(jnp.bfloat16)
    rows_grad = contract_cols(gate_grad, gate_mat) + contract_cols(up_grad, up_mat)
    weight_grads = lax.psum_scatter(
        jnp.stack(
            [
                contract_rows(slot_rows, gate_grad),
                contract_rows(slot_rows, up_grad),
                contract_rows(slot_grads, inner),
            ],
            axis=1,
        ).astype(jnp.bfloat16),
        "ctx",
        scatter_dimension=0,
        tiled=True,
    ).astype(jnp.float32)
    expert_out, rows_grad = (
        lax.psum(expert_out.astype(jnp.bfloat16), "tensor").astype(jnp.float32),
        lax.psum(rows_grad.astype(jnp.bfloat16), "tensor").astype(jnp.float32),
    )
    back_out, back_grad = (
        lax.all_to_all(
            expert_out.reshape(shaped).astype(jnp.bfloat16),
            "shard",
            split_axis=0,
            concat_axis=0,
            tiled=True,
        ).astype(jnp.float32),
        lax.all_to_all(
            rows_grad.reshape(shaped).astype(jnp.bfloat16),
            "shard",
            split_axis=0,
            concat_axis=0,
            tiled=True,
        ).astype(jnp.float32),
    )
    per_choice = back_out[expert_of, slot_of].reshape(rows_here, TOP, width)
    mixture = jnp.sum(gates[:, :, None] * per_choice, axis=1)
    gate_dots = jnp.sum(per_choice * upstream[:, None, :], axis=2)
    norm_grad = jnp.sum(back_grad[expert_of, slot_of].reshape(rows_here, TOP, width), axis=1)
    mixed = (hidden_one + mixture).astype(jnp.bfloat16)
    gate_shift = gates * (gate_dots - jnp.sum(gates * gate_dots, axis=1, keepdims=True))
    logit_grad = jnp.sum(jnp.where(picks, gate_shift[:, :, None], 0.0), axis=1)
    router_f = router_w.astype(jnp.float32)
    norm_grad = norm_grad + jnp.dot(logit_grad, router_f.T, precision=lax.Precision.HIGHEST)
    spread_two = norm_grad * gain_two.astype(jnp.float32)
    hidden_grad = upstream + scale_two * (
        spread_two - normal_two * jnp.mean(spread_two * normal_two, axis=1, keepdims=True)
    )
    branch_grad = hidden_grad.astype(jnp.bfloat16)
    attended_grad = jnp.dot(branch_grad, out_w, preferred_element_type=jnp.float32).astype(
        jnp.bfloat16
    )
    grad_heads = attended_grad.reshape(rows_here, local_heads, HEAD)
    delta = jnp.sum(jnp.transpose(grad_heads.astype(jnp.float32), (1, 0, 2)) * attended, axis=2)

    def backward_part(carry, pieces, start):
        query_acc, pair_acc, bias_acc = carry
        key_piece, value_piece, segment_piece = pieces
        count = key_piece.shape[0]
        scores, allowed, onehot, key_heads = block_scores(key_piece, segment_piece, start)
        probs = jnp.where(allowed[None], jnp.exp(scores - log_total[..., None]), 0.0)
        value_heads = value_piece.reshape(count, local_heads, HEAD)
        prob_grad = jnp.einsum(
            "qhd,khd->hqk", grad_heads, value_heads, preferred_element_type=jnp.float32
        )
        score_grad = (probs * (prob_grad - delta[..., None])).astype(jnp.bfloat16)
        query_acc = (
            query_acc
            + jnp.einsum("hqk,khd->qhd", score_grad, key_heads, preferred_element_type=jnp.float32)
            * 0.125
        )
        key_part = (
            jnp.einsum("hqk,qhd->khd", score_grad, query_heads, preferred_element_type=jnp.float32)
            * 0.125
        )
        value_part = jnp.einsum(
            "hqk,qhd->khd",
            probs.astype(jnp.bfloat16),
            grad_heads,
            preferred_element_type=jnp.float32,
        )
        stacked_part = jnp.stack(
            [key_part.reshape(count, head_cols), value_part.reshape(count, head_cols)]
        )
        current = lax.dynamic_slice_in_dim(pair_acc, start, count, 1)
        pair_acc = lax.dynamic_update_slice_in_dim(pair_acc, current + stacked_part, start, 1)
        bias_acc = bias_acc + jnp.einsum(
            "hqk,qkb->bh", score_grad.astype(jnp.float32), onehot, precision=lax.Precision.HIGHEST
        )
        return (query_acc, pair_acc, bias_acc)

    back_state = (
        jnp.zeros((rows_here, local_heads, HEAD), jnp.float32),
        jnp.zeros((2, rows_here * ctx_size, head_cols), jnp.float32),
        jnp.zeros(rel_bias.shape, jnp.float32),
    )
    query_acc, pair_acc, bias_acc = fold_blocks(
        backward_part,
        back_state,
        (
            lax.all_gather(keys, "ctx", axis=0, tiled=True),
            lax.all_gather(values, "ctx", axis=0, tiled=True),
            lax.all_gather(segments, "ctx", axis=0, tiled=True),
        ),
    )
    pair_grads = lax.psum_scatter(
        pair_acc.astype(jnp.bfloat16), "ctx", scatter_dimension=1, tiled=True
    ).astype(jnp.float32)
    query_grad = query_acc.reshape(rows_here, head_cols).astype(jnp.bfloat16)
    key_grad = pair_grads[0].astype(jnp.bfloat16)
    value_grad = pair_grads[1].astype(jnp.bfloat16)
    norm_one_grad = lax.psum(
        (
            contract_cols(query_grad, query_w)
            + contract_cols(key_grad, key_w)
            + contract_cols(value_grad, value_w)
        ).astype(jnp.bfloat16),
        "tensor",
    ).astype(jnp.float32)
    spread_one = norm_one_grad * gain_one.astype(jnp.float32)
    input_grad = hidden_grad + scale_one * (
        spread_one - normal_one * jnp.mean(spread_one * normal_one, axis=1, keepdims=True)
    )
    gain_one_terms = norm_one_grad * normal_one
    gain_two_terms = norm_grad * normal_two
    cols_two = norm_two.astype(jnp.float32)
    first_gain = jnp.sum(gain_one_terms, axis=0)[:, None]
    second_gain = jnp.sum(gain_two_terms, axis=0)[:, None]
    router_part = jnp.dot(cols_two.T, logit_grad, precision=lax.Precision.HIGHEST)
    reduced = lax.psum_scatter(
        jnp.concatenate(
            [
                contract_rows(norm_one, query_grad),
                contract_rows(norm_one, key_grad),
                contract_rows(norm_one, value_grad),
                contract_rows(branch_grad, attended_low),
                first_gain,
                second_gain,
                router_part,
            ],
            axis=1,
        ),
        ("shard", "ctx"),
        scatter_dimension=0,
        tiled=True,
    )
    grad_bias = lax.psum(bias_acc, ("shard", "ctx"))
    return (
        mixed,
        input_grad.astype(jnp.bfloat16),
        reduced[:, :head_cols],
        reduced[:, head_cols : 2 * head_cols],
        reduced[:, 2 * head_cols : 3 * head_cols],
        reduced[:, 3 * head_cols : 4 * head_cols],
        grad_bias,
        reduced[:, 4 * head_cols],
        reduced[:, 4 * head_cols + 1],
        reduced[:, 4 * head_cols + 2 :],
        weight_grads[:, 0][None],
        weight_grads[:, 1][None],
        weight_grads[:, 2][None],
    )


def solution(mesh):
    placed = (
        P(("shard", "ctx"), None),
        P(("shard", "ctx"), None),
        P("shard", "ctx"),
        P("shard", None, None),
        P(("shard", "ctx"), None),
        P(("shard", "ctx"), "tensor"),
        P(("shard", "ctx"), "tensor"),
        P(("shard", "ctx"), "tensor"),
        P(("shard", "ctx"), "tensor"),
        P(None, "tensor"),
        P(("shard", "ctx")),
        P(("shard", "ctx")),
        P(("shard", "ctx"), None),
        P("shard", "ctx", "tensor"),
        P("shard", "ctx", "tensor"),
        P("shard", "ctx", "tensor"),
    )
    return jax.shard_map(
        local,
        mesh=mesh,
        in_specs=placed,
        out_specs=(
            P(("shard", "ctx"), None),
            P(("shard", "ctx"), None),
            P(("shard", "ctx"), "tensor"),
            P(("shard", "ctx"), "tensor"),
            P(("shard", "ctx"), "tensor"),
            P(("shard", "ctx"), "tensor"),
            P(None, "tensor"),
            P(("shard", "ctx")),
            P(("shard", "ctx")),
            P(("shard", "ctx"), None),
            P("shard", "ctx", "tensor"),
            P("shard", "ctx", "tensor"),
            P("shard", "ctx", "tensor"),
        ),
        check_vma=False,
    )
```

profile of v0, /device:TPU:0, one launch (start us, length us, event | category | flops | bytes accessed | tf_op | source)
XLA Modules:
  0.0 1539.8 jit_solution(14769240534803149191)
XLA Ops:
  15.9 35.1 %all-reduce.2 = (bf16[1024]{0:T(1024)(128)(2,1)S(1)}, bf16[1024]{0:T(1024)(128)(2,1)S(1)}) all-reduce(bf16[1024]{0:T(1024)(128)(2,1)S(1)} %dynamic-update-slice, bf16[1024]{0:T(1024)(128)(2,1)S(1)} %dynamic-update-slice.1), channel_id=1, replica_groups=mesh['shard'=4,'ctx'=4,'tensor'=2] {'shard','ctx'}, use_global_device_ids=true, to_apply=%add | all-reduce | flops 2048 | bytes 8192
  55.7 35.4 %all-gather.18.cloned.1.call-done = bf16[1024,512]{1,0:T(8,128)(2,1)} async-done(((bf16[64,512]{1,0:T(8,128)(2,1)}), bf16[1024,512]{1,0:T(8,128)(2,1)}) %all-gather.18.cloned.1.call-update) | async-done | bytes 1048592 | tf_op jit(solution)/shard_map/all_gather | solution.py:77
  102.5 28.3 %all-gather.16.cloned.1.call-done = bf16[1024,512]{1,0:T(8,128)(2,1)} async-done(((bf16[64,512]{1,0:T(8,128)(2,1)}), bf16[1024,512]{1,0:T(8,128)(2,1)}) %all-gather.16.cloned.1.call-update) | async-done | bytes 1048592 | tf_op jit(solution)/shard_map/all_gather | solution.py:75
  132.8 21.4 %all-gather.14.cloned.1.call-done = bf16[2048,512]{1,0:T(8,128)(2,1)} async-done(((bf16[512,512]{1,0:T(8,128)(2,1)}), bf16[2048,512]{1,0:T(8,128)(2,1)}) %all-gather.14.cloned.1.call-update) | async-done | bytes 2097168 | tf_op jit(solution)/shard_map/all_gather | solution.py:146
  158.4 20.4 %all-gather.20.cloned.1.call-done = bf16[2048,512]{1,0:T(8,128)(2,1)} async-done(((bf16[512,512]{1,0:T(8,128)(2,1)}), bf16[2048,512]{1,0:T(8,128)(2,1)}) %all-gather.20.cloned.1.call-update) | async-done | bytes 2097168 | tf_op jit(solution)/shard_map/all_gather | solution.py:147
  183.0 196.2 %while.34 = (s32[]{:T(128)}, f32[8,512]{1,0:T(8,128)S(1)}, f32[8,512]{1,0:T(8,128)S(1)}, f32[8,512,64]{1,2,0:T(8,128)}, s32[1,512]{1,0:T(1,128)S(1)}, /*index=5*...) while((s32[]{:T(128)}, f32[8,512]{1,0:T(8,128)S(1)}, ...), condition=%wide.region_4.6_spmd.clone, body=%wide.region_1.5_spmd.clone.sunk | while | flops 1380755456 | bytes 104624336 | solution.py:36
  188.4 12.3 fusion.215
  233.7 12.3 fusion.215
  388.9 35.3 %all-reduce.8.cloned.1.call-done = bf16[512,1024]{1,0:T(8,128)(2,1)} async-done(((bf16[512,1024]{1,0:T(8,128)(2,1)}), bf16[512,1024]{1,0:T(8,128)(2,1)}) %all-reduce.8.cloned.1.call-update) | async-done | bytes 1048592 | tf_op jit(solution)/shard_map/psum | solution.py:156
  449.6 64.3 %all-gather.1 = bf16[16,64,4]{1,2,0:T(4,128)(2,1)S(1)} all-gather(bf16[1,64,4]{1,2,0:T(4,128)(2,1)S(1)} %convert_bitcast_fusion), channel_id=1, replica_groups=mesh['shard'=4,'ctx'=4,'tensor'=2] {'shard','ctx'}, dimensions={0}, use_global_device_ids=true | all-gather | bytes 8704 | tf_op jit(solution)/shard_map/all_gather | solution.py:81
  533.8 17.2 %all-to-all-start.2 = ((bf16[4,384,1024]{2,1,0:T(8,128)(2,1)}), bf16[4,384,1024]{2,1,0:T(8,128)(2,1)}, u32[]{:S(2)}, u32[]{:S(2)}) async-start(bf16[4,384,1024]{2,1,0:T(8,128)(2,1)} %bitcast.264), calls=%async_computation.2 | async-start | bytes 6291456 | tf_op jit(solution)/shard_map/all_to_all | solution.py:187
  580.4 42.8 %all-to-all-done.2 = bf16[4,384,1024]{2,1,0:T(8,128)(2,1)} async-done(((bf16[4,384,1024]{2,1,0:T(8,128)(2,1)}), bf16[4,384,1024]{2,1,0:T(8,128)(2,1)}, u32[]{:S(2)}, u32[]{:S(2)}) %all-to-all-start.2) | async-done | bytes 3145760 | tf_op jit(solution)/shard_map/all_to_all | solution.py:187
  623.2 19.1 %multiply_convert_fusion = (bf16[1536,1408]{1,0:T(8,128)(2,1)S(1)}, bf16[1536,1408]{1,0:T(8,128)(2,1)}, bf16[1536,1408]{1,0:T(8,128)(2,1)}) fusion(f32[1536,1408]{1,0:T(8,128)} %fusion.90, f32[1536,1408]{1,0:T(8,128)} %fusion.86, bf16[1536,1024]{1,0:T(8,128)(2,1)} %bitcast.19, bf16[1,1024,1408]{2,1,0:T(8,128)(2,1)} %all-gather.28.cloned.1.call-done), kind=kOutput, calls=%fused_computation.121 | convolution fusion | flops 4485414912 | bytes 36306944 | tf_op jit(solution)/shard_map/dot_general | solution.py:204
  664.6 151.0 %all-reduce.12.cloned.1.call-done = (bf16[4,384,1024]{2,1,0:T(8,128)(2,1)}, bf16[4,384,1024]{2,1,0:T(8,128)(2,1)}) async-done(((bf16[4,384,1024]{2,1,0:T(8,128)(2,1)}, bf16[4,384,1024]{2,1,0:T(8,128)(2,1)}), (bf16[4,384,1024]{2,1,0:T(8,128)(2,1)}, bf16[4,384,1024]{2,1,0:T(8,128)(2,1)})) %all-reduce.12.cloned.1.call-update) | async-done | bytes 6291472 | tf_op jit(solution)/shard_map/psum | solution.py:222
  815.6 76.3 %all_to_all.20 = bf16[4,384,1024]{2,1,0:T(8,128)(2,1)} all-to-all(bf16[4,384,1024]{2,1,0:T(8,128)(2,1)} %get-tuple-element.787), channel_id=1, replica_groups=mesh['shard'=4,'ctx'=4,'tensor'=2] {'shard'}, dimensions={0} | all-to-all | bytes 6291456 | tf_op jit(solution)/shard_map/all_to_all | solution.py:226
  903.6 20.5 %gather_fusion.3 = f32[1024,1024]{1,0:T(8,128)} fusion(f32[4,384,1024]{2,1,0:T(8,128)} %convert_element_type.344, s32[1024]{0:T(1024)S(1)} %bitcast.251), kind=kCustom, calls=%fused_computation.3 | custom fusion | bytes 8396800 | tf_op jit(solution)/shard_map/gather | solution.py:241
  940.7 26.3 %all-to-all-done.3 = bf16[4,384,1024]{2,1,0:T(8,128)(2,1)} async-done(((bf16[4,384,1024]{2,1,0:T(8,128)(2,1)}), bf16[4,384,1024]{2,1,0:T(8,128)(2,1)}, u32[]{:S(2)}, u32[]{:S(2)}) %all-to-all-start.3) | async-done | bytes 3145760 | tf_op jit(solution)/shard_map/all_to_all | solution.py:233
  972.3 20.4 %gather_fusion.4 = f32[1024,1024]{1,0:T(8,128)} fusion(f32[4,384,1024]{2,1,0:T(8,128)} %convert_element_type.352, s32[1024]{0:T(1024)S(1)} %bitcast.252), kind=kCustom, calls=%fused_computation.4 | custom fusion | bytes 8396800 | tf_op jit(solution)/shard_map/gather | solution.py:244
  1020.1 226.4 %while.35 = (s32[]{:T(128)}, f32[512,8,64]{0,2,1:T(8,128)}, f32[2,2048,512]{1,2,0:T(8,128)}, f32[32,8]{0,1:T(8,128)S(1)}, bf16[4,512,512]{1,2,0:T(8,128)(2,1)}, ...) while((s32[]{:T(128)}, f32[512,8,64]{0,2,1:T(8,128)}, ...), condition=%wide.region_25.27_spmd.clone, body=%wide.region_24.26_spmd.clone.sunk | while | flops 2325764608 | bytes 130087360 | solution.py:36
  1273.9 21.5 %reduce-scatter.6.cloned.1.call-done = bf16[2,512,512]{1,2,0:T(8,128)(2,1)} async-done(((bf16[2,2048,512]{1,2,0:T(8,128)(2,1)}), bf16[2,512,512]{1,2,0:T(8,128)(2,1)}) %reduce-scatter.6.cloned.1.call-update) | async-done | bytes 1048592 | tf_op jit(solution)/shard_map/reduce_scatter | solution.py:311
  1323.9 15.4 %all-reduce.10.cloned.1.call-done = bf16[512,1024]{1,0:T(8,128)(2,1)} async-done(((bf16[512,1024]{1,0:T(8,128)(2,1)}), bf16[512,1024]{1,0:T(8,128)(2,1)}) %all-reduce.10.cloned.1.call-update) | async-done | bytes 1048592 | tf_op jit(solution)/shard_map/psum | solution.py:317
  1341.4 23.5 %concatenate.10 = f32[1024,2054]{0,1:T(8,128)} concatenate(f32[1024,512]{0,1:T(8,128)} %fusion.122, f32[1024,512]{0,1:T(8,128)} %fusion.110, f32[1024,512]{0,1:T(8,128)} %fusion.112, f32[1024,512]{0,1:T(8,128)} %fusion.107, f32[1024,1]{0,1:T(1,128)S(1)} %bitcast.277, f32[1024,1]{0,1:T(1,128)S(1)} %bitcast.279, f32[1024,4]{0,1:T(4,128)S(1)} %fusion.134), dimensions={1} | concatenate | bytes 16826368 | tf_op jit(solution)/shard_map/concatenate | solution.py:336
  1374.1 34.7 %psum.39 = f32[32,8]{0,1:T(8,128)} all-reduce(f32[32,8]{0,1:T(8,128)S(1)} %get-tuple-element.1144), channel_id=1, replica_groups=mesh['shard'=4,'ctx'=4,'tensor'=2] {'shard','ctx'}, use_global_device_ids=true, to_apply=%region_32.34 | all-reduce | flops 256 | bytes 2048 | tf_op jit(solution)/shard_map/psum | solution.py:352
  1421.5 106.1 %reduce-scatter.10.cloned.1.call-done = f32[64,2054]{1,0:T(8,128)} async-done(((f32[1024,2054]{1,0:T(8,128)}), f32[64,2054]{1,0:T(8,128)}) %reduce-scatter.10.cloned.1.call-update) | async-done | bytes 525840
  (470 shorter events, 664.4 us)
Async XLA Ops:
  7.2 87.6 %copy-start = (s32[1,4,4]{2,1,0:T(4,128)S(1)}, s32[1,4,4]{2,1,0:T(4,128)}, u32[]{:S(2)}) copy-start(s32[1,4,4]{2,1,0:T(4,128)} %param.25) | copy-start | bytes 196
  7.2 45.3 %all-gather.12.cloned.1.call-start = ((), (), s32[]{:S(2)}) async-start(), calls=%async_computation.7 | async-start | bytes 1114112 | tf_op jit(solution)/shard_map/all_gather | solution.py:76
  8.8 82.3 %copy-start.10 = (bf16[512,1024]{1,0:T(8,128)(2,1)S(1)}, bf16[512,1024]{1,0:T(8,128)(2,1)}, u32[]{:S(2)}) copy-start(bf16[512,1024]{1,0:T(8,128)(2,1)} %param.22) | copy-start | bytes 3145732
  8.8 82.3 %all-gather.18.cloned.1.call-start = ((), (), s32[]{:S(2)}) async-start(), calls=%async_computation.10 | async-start | bytes 1114112 | tf_op jit(solution)/shard_map/all_gather | solution.py:77
  10.5 120.2 %all-gather.16.cloned.1.call-start = ((), (), s32[]{:S(2)}) async-start(), calls=%async_computation.9 | async-start | bytes 1114112 | tf_op jit(solution)/shard_map/all_gather | solution.py:75
  12.1 142.1 %all-gather.14.cloned.1.call-start = ((), (), s32[]{:S(2)}) async-start(), calls=%async_computation.8 | async-start | bytes 2621440 | tf_op jit(solution)/shard_map/all_gather | solution.py:146
  50.9 79.8 %copy-start.39 = (f32[1024]{0:T(1024)}, f32[1024]{0:T(1024)S(1)}, u32[]{:S(2)}) copy-start(f32[1024]{0:T(1024)S(1)} %convert_element_type.319) | copy-start | bytes 12292
  52.4 78.3 %copy-start.43 = (f32[512]{0:T(512)}, f32[512]{0:T(512)S(1)}, u32[]{:S(2)}) copy-start(f32[512]{0:T(512)S(1)} %add_rsqrt_fusion.1) | copy-start | bytes 6148
  55.6 123.3 %all-gather.20.cloned.1.call-start = ((), (), s32[]{:S(2)}) async-start(), calls=%async_computation.11 | async-start | bytes 2621440 | tf_op jit(solution)/shard_map/all_gather | solution.py:147
  93.9 286.9 %all-gather.22.cloned.1.call-start = ((), (), s32[]{:S(2)}) async-start(), calls=%async_computation.12 | async-start | bytes 1114112 | tf_op jit(solution)/shard_map/all_gather | solution.py:78
  94.6 329.6 %all-reduce.8.cloned.1.call-start = ((), (), s32[]{:S(2)}) async-start(), calls=%async_computation.13 | async-start | bytes 2097152 | tf_op jit(solution)/shard_map/psum | solution.py:156
  384.0 168.1 %all-gather.26.cloned.1.call-start = ((), (), s32[]{:S(2)}) async-start(), calls=%async_computation.15 | async-start | bytes 3604480 | tf_op jit(solution)/shard_map/all_gather | solution.py:191
  427.5 96.8 %copy-start.17 = (bf16[512,1024]{1,0:T(8,128)(2,1)}, bf16[512,1024]{1,0:T(8,128)(2,1)S(1)}, u32[]{:S(2)}) copy-start(bf16[512,1024]{1,0:T(8,128)(2,1)S(1)} %multiply_convert_fusion.4) | copy-start | bytes 3145732
  442.3 91.5 %all-to-all-start = ((bf16[4,384,1024]{2,1,0:T(8,128)(2,1)}), bf16[4,384,1024]{2,1,0:T(8,128)(2,1)}, u32[]{:S(2)}, u32[]{:S(2)}) async-start(bf16[4,384,1024]{2,1,0:T(8,128)(2,1)} %bitcast.263), calls=%async_computation | async-start | bytes 6291456 | tf_op jit(solution)/shard_map/all_to_all | solution.py:186
  447.2 114.8 %all-gather.24.cloned.1.call-start = ((), (), s32[]{:S(2)}) async-start(), calls=%async_computation.14 | async-start | bytes 3604480 | tf_op jit(solution)/shard_map/all_gather | solution.py:190
  533.8 89.4 %all-to-all-start.2 = ((bf16[4,384,1024]{2,1,0:T(8,128)(2,1)}), bf16[4,384,1024]{2,1,0:T(8,128)(2,1)}, u32[]{:S(2)}, u32[]{:S(2)}) async-start(bf16[4,384,1024]{2,1,0:T(8,128)(2,1)} %bitcast.264), calls=%async_computation.2 | async-start | bytes 6291456 | tf_op jit(solution)/shard_map/all_to_all | solution.py:187
  551.0 29.4 %all-gather.28.cloned.1.call-start = ((), (), s32[]{:S(2)}) async-start(), calls=%async_computation.16 | async-start | bytes 3604480 | tf_op jit(solution)/shard_map/all_gather | solution.py:192
  552.0 263.6 %all-reduce.12.cloned.1.call-start = ((), (), s32[]{:S(2)}) async-start(), calls=%async_computation.21 | async-start | bytes 12582912 | tf_op jit(solution)/shard_map/psum | solution.py:222
  891.9 75.1 %all-to-all-start.3 = ((bf16[4,384,1024]{2,1,0:T(8,128)(2,1)}), bf16[4,384,1024]{2,1,0:T(8,128)(2,1)}, u32[]{:S(2)}, u32[]{:S(2)}) async-start(bf16[4,384,1024]{2,1,0:T(8,128)(2,1)} %get-tuple-element.788), calls=%async_computation.3 | async-start | bytes 6291456 | tf_op jit(solution)/shard_map/all_to_all | solution.py:233
  896.7 398.6 %reduce-scatter.6.cloned.1.call-start = ((), (), s32[]{:S(2)}) async-start(), calls=%async_computation.17 | async-start | bytes 5242880 | tf_op jit(solution)/shard_map/reduce_scatter | solution.py:311
  1252.5 86.8 %all-reduce.10.cloned.1.call-start = ((), (), s32[]{:S(2)}) async-start(), calls=%async_computation.18 | async-start | bytes 2097152 | tf_op jit(solution)/shard_map/psum | solution.py:317
  1299.1 116.7 %reduce-scatter.8.cloned.1.call-start = ((), (), s32[]{:S(2)}) async-start(), calls=%async_computation.19 | async-start | bytes 10813440 | tf_op jit(solution)/shard_map/reduce_scatter | solution.py:208
  1311.5 216.1 %reduce-scatter.10.cloned.1.call-start = ((), (), s32[]{:S(2)}) async-start(), calls=%async_computation.20 | async-start | bytes 9469952
  1419.8 113.2 %copy-start.1 = (s32[1,4,4]{2,1,0:T(4,128)S(1)}, s32[1,4,4]{2,1,0:T(4,128)}, u32[]{:S(2)}) copy-start(s32[1,4,4]{2,1,0:T(4,128)} %param.25) | copy-start | bytes 196
  (75 other events, 702.0 us)
Sparse Core Ops, SparseCore 0:
  10.8 40.6 all-gather.11
  54.2 36.8 all-gather.17
  93.9 36.8 all-gather.15
  132.7 21.4 all-gather.13
  156.2 22.5 all-gather.19
  181.5 37.9 all-gather.21
  384.1 40.1 all-reduce.7
  426.4 27.0 all-gather.25
  455.7 27.0 all-gather.23
  553.7 26.6 all-gather.27
  664.8 150.7 all-reduce.11
  1252.6 42.6 reduce-scatter.5
  1299.2 40.0 all-reduce.9
  1341.8 73.9 reduce-scatter.7
  1419.7 107.7 reduce-scatter.9
where the time goes:
time: 1550 us; the launch traced here: 1540 us
  waiting for transfers between devices  520 us (34%)
  matrix products  353 us (23%)
  local copies, waits for them, and re-layouts  253 us (16%)
  blocking collectives  215 us (14%)
  other arithmetic  134 us (9%)
  starting transfers between devices  27.6 us (2%)
  loops' own time  20.4 us (1%)
  between operations  15.5 us (1%)
    psum x1, waiting for transfers between devices, local(): lax.psum(expert_out.astype(jnp.bfloat16), 'tensor').astype(jnp.float32)  151 us
    unnamed x16, waiting for transfers between devices  106 us
    dot_general x8, matrix products, block_scores(): jnp.einsum('qkb,bh->hqk', onehot, rel_bias, precision=lax.Precision.HIGHEST)  91.3 us
    all_to_all x1, blocking collectives, local(): lax.all_to_all(expert_out.reshape(shaped).astype(jnp.bfloat16), 'shard',...  76.3 us
    all_gather x1, blocking collectives, local(): lax.all_gather(router.astype(jnp.bfloat16), ('shard', 'ctx'), axis=0, til...  64.3 us
    dot_general x8, matrix products, block_scores(): jnp.einsum('qhd,khd->hqk', query_heads, key_heads, preferred_element_type...  59.4 us
    all_to_all x1, waiting for transfers between devices, local(): lax.all_to_all(send_grads, 'shard', split_axis=0, concat_axis=0, tiled=True)  42.8 us
    dynamic_update_slice x4, local copies, waits for them, and re-layouts, backward_part(): lax.dynamic_update_slice_in_dim(pair_acc, current + stacked_part, start, 1)  41.2 us
  transfers between devices with their start and end apart: 18, of which 13 were waited for; matrix products, arithmetic and copies ran while one was open for 26% of the time, Pallas kernels for 0%

commit v1 on v0

v1 whole, which is shorter than its diff:
```python
from functools import partial

import jax
import jax.numpy as jnp
from jax import lax
from jax.experimental import pallas as pl
from jax.experimental.pallas import tpu as pltpu
from jax.sharding import PartitionSpec as P

HEAD = 64
NBUCK = 32
TOP = 2
ATT_BLK = 512


FAR_STEPS = (12, 16, 23, 32, 46, 64, 91)


def bucket_ids(relative):
    distance = jnp.abs(relative)
    far = jnp.full(distance.shape, 8, jnp.int32)
    for bound in FAR_STEPS:
        far = far + (distance >= bound).astype(jnp.int32)
    near = jnp.where(distance < 8, distance, far)
    return near + jnp.where(relative > 0, NBUCK // 2, 0)


TILE = 256
BIG = 2.0**100
SPAN = 4 * TILE


def place_mask(segment_row):
    rows = lax.broadcasted_iota(jnp.int32, (128, segment_row.shape[1]), 0).astype(jnp.float32)
    apart = jnp.where(rows == segment_row, 0.0, -BIG)
    return jnp.where(rows < 8.0, apart, jnp.where(rows < 11.0, 1.0, 0.0))


def seat_rows(segment_row, extra):
    rows = lax.broadcasted_iota(jnp.int32, (128, segment_row.shape[1]), 0).astype(jnp.float32)
    own = jnp.where((rows == segment_row) & (rows < 8.0), 1.0, 0.0)
    if extra is None:
        return own.astype(jnp.bfloat16)
    high = extra.astype(jnp.bfloat16).astype(jnp.float32)
    rest = extra - high
    middle = rest.astype(jnp.bfloat16).astype(jnp.float32)
    low = rest - middle
    own = jnp.where(rows == 8.0, high, own)
    own = jnp.where(rows == 9.0, middle, own)
    return jnp.where(rows == 10.0, low, own).astype(jnp.bfloat16)


def fill_bias(line_ref, bias_ref):
    for head in range(2):
        line = line_ref[head : head + 1, :]
        turned = pltpu.roll(
            jnp.broadcast_to(line, (TILE, SPAN)), 0, axis=1, stride=1, stride_axis=0
        )
        bias_ref[head, 1] = turned[:, TILE : 2 * TILE]
        bias_ref[head, 2] = turned[:, :TILE]
        bias_ref[head, 3] = turned[:, 3 * TILE :]
        bias_ref[head, 0] = jnp.broadcast_to(line[:, 511:512], (TILE, TILE))
        bias_ref[head, 4] = jnp.broadcast_to(line[:, 513:514], (TILE, TILE))


def tile_at(index):
    return pl.ds(pl.multiple_of(index * TILE, TILE), TILE)


def dot32(left, right):
    return jnp.dot(left, right, preferred_element_type=jnp.float32)


def attention_forward(
    alive, packed, segment, line, out, out_t, log_sum, key_side, query_side, value_t, bias, top, acc
):
    length = packed.shape[0]
    tiles = length // TILE
    fill_bias(line, bias)

    def prepare(index, unused):
        spot = tile_at(index)
        seg = segment[0:1, spot]
        block = packed[spot, :].astype(jnp.float32)
        key_side[spot, :128] = packed[spot, 128:256]
        key_side[spot, 128:] = jnp.transpose(place_mask(seg)).astype(jnp.bfloat16)
        query_t = jnp.transpose(block[:, :128]) * 0.125
        seats = seat_rows(seg, None)
        half = lax.broadcasted_iota(jnp.int32, (128, TILE), 0) // HEAD
        values = jnp.transpose(block[:, 256:]).astype(jnp.bfloat16)
        ones = jnp.where(lax.broadcasted_iota(jnp.int32, (16, TILE), 0) == 0, 1.0, 0.0)
        for head in range(2):
            query_side[head, :128, spot] = jnp.where(half == head, query_t, 0.0).astype(
                jnp.bfloat16
            )
            query_side[head, 128:, spot] = seats
            value_t[head, :HEAD, spot] = values[HEAD * head : HEAD * (head + 1)]
            value_t[head, HEAD:, spot] = ones.astype(jnp.bfloat16)
        return unused

    lax.fori_loop(0, tiles, prepare, 0)

    def query_tile(query_index, unused):
        query_spot = tile_at(query_index)
        top[...] = jnp.full(top.shape, -3e38, jnp.float32)
        acc[...] = jnp.zeros(acc.shape, jnp.float32)

        def key_tile(key_index, carried):
            @pl.when(alive[query_index * tiles + key_index] == 1)
            def _():
                key_spot = tile_at(key_index)
                slot = jnp.clip(key_index - query_index, -2, 2) + 2
                keys = key_side[key_spot, :]
                for head in range(2):
                    scores = dot32(keys, query_side[head, :, query_spot]) + bias[head, slot]
                    before = top[head : head + 1, :]
                    now = jnp.maximum(before, jnp.max(scores, axis=0, keepdims=True))
                    weights = jnp.exp(scores - now).astype(jnp.bfloat16)
                    top[head : head + 1, :] = now
                    acc[head] = acc[head] * jnp.exp(before - now) + dot32(
                        value_t[head, :, key_spot], weights
                    )

            return carried

        lax.fori_loop(0, tiles, key_tile, 0)
        parts = []
        for head in range(2):
            total = acc[head, HEAD : HEAD + 1, :]
            part = acc[head, :HEAD, :] / total
            out_t[HEAD * head : HEAD * (head + 1), query_spot] = part
            log_sum[head : head + 1, query_spot] = top[head : head + 1, :] + jnp.log(total)
            parts.append(part)
        out[query_spot, :] = jnp.transpose(jnp.concatenate(parts, axis=0)).astype(jnp.bfloat16)
        return unused

    lax.fori_loop(0, tiles, query_tile, 0)


def attention_backward(
    alive,
    packed,
    segment,
    line,
    grads,
    out_t,
    log_sum,
    packed_grad,
    bias_grad,
    key_side,
    value_side,
    query_side,
    grad_side,
    key_t,
    query_pair,
    grad_pair,
    bias,
    bias_acc,
    query_acc,
    key_acc,
    value_acc,
):
    length = packed.shape[0]
    tiles = length // TILE
    fill_bias(line, bias)
    bias_acc[...] = jnp.zeros(bias_acc.shape, jnp.float32)

    def prepare(index, unused):
        spot = tile_at(index)
        seg = segment[0:1, spot]
        block = packed[spot, :].astype(jnp.float32)
        grad = grads[spot, :].astype(jnp.float32)
        seats = jnp.transpose(place_mask(seg)).astype(jnp.bfloat16)
        key_side[spot, :128] = packed[spot, 128:256]
        key_side[spot, 128:] = seats
        value_side[spot, :128] = packed[spot, 256:]
        value_side[spot, 128:] = seats
        key_t[:, spot] = jnp.transpose(block[:, 128:256]).astype(jnp.bfloat16)
        query_t = jnp.transpose(block[:, :128]) * 0.125
        grad_t = jnp.transpose(grad)
        half = lax.broadcasted_iota(jnp.int32, (128, TILE), 0) // HEAD
        side = lax.broadcasted_iota(jnp.int32, (TILE, 128), 1) // HEAD
        products = grad_t * out_t[:, spot]
        query_acc[:, spot] = jnp.zeros((128, TILE), jnp.float32)
        for head in range(2):
            query_side[head, :128, spot] = jnp.where(half == head, query_t, 0.0).astype(
                jnp.bfloat16
            )
            query_side[head, 128:, spot] = seat_rows(seg, -log_sum[head : head + 1, spot])
            delta = jnp.sum(products[HEAD * head : HEAD * (head + 1)], axis=0, keepdims=True)
            grad_side[head, :128, spot] = jnp.where(half == head, grad_t, 0.0).astype(jnp.bfloat16)
            grad_side[head, 128:, spot] = seat_rows(jnp.full_like(seg, -1.0), -delta)
            query_pair[index, TILE * head : TILE * (head + 1), :] = jnp.where(
                side == head, block[:, :128] * 0.125, 0.0
            ).astype(jnp.bfloat16)
            grad_pair[index, TILE * head : TILE * (head + 1), :] = jnp.where(
                side == head, grad, 0.0
            ).astype(jnp.bfloat16)
        return unused

    lax.fori_loop(0, tiles, prepare, 0)

    def key_tile(key_index, unused):
        key_spot = tile_at(key_index)
        key_acc[...] = jnp.zeros(key_acc.shape, jnp.float32)
        value_acc[...] = jnp.zeros(value_acc.shape, jnp.float32)

        def query_tile(query_index, carried):
            @pl.when(alive[query_index * tiles + key_index] == 1)
            def _():
                query_spot = tile_at(query_index)
                slot = jnp.clip(key_index - query_index, -2, 2) + 2
                keys = key_side[key_spot, :]
                values = value_side[key_spot, :]
                probs, score_grads = [], []
                for head in range(2):
                    scores = dot32(keys, query_side[head, :, query_spot]) + bias[head, slot]
                    prob = jnp.exp(scores)
                    score_grad = prob * dot32(values, grad_side[head, :, query_spot])
                    bias_acc[head, slot] += score_grad
                    score_grad = score_grad.astype(jnp.bfloat16)
                    probs.append(prob.astype(jnp.bfloat16))
                    score_grads.append(score_grad)
                    rows = slice(HEAD * head, HEAD * (head + 1))
                    query_acc[rows, query_spot] += dot32(key_t[rows, key_spot], score_grad)
                value_acc[...] += dot32(jnp.concatenate(probs, axis=1), grad_pair[query_index])
                key_acc[...] += dot32(jnp.concatenate(score_grads, axis=1), query_pair[query_index])

            return carried

        lax.fori_loop(0, tiles, query_tile, 0)
        packed_grad[key_spot, 128:256] = key_acc[...].astype(jnp.bfloat16)
        packed_grad[key_spot, 256:] = value_acc[...].astype(jnp.bfloat16)
        return unused

    lax.fori_loop(0, tiles, key_tile, 0)

    def finish(index, unused):
        spot = tile_at(index)
        packed_grad[spot, :128] = (jnp.transpose(query_acc[:, spot]) * 0.125).astype(jnp.bfloat16)
        return unused

    lax.fori_loop(0, tiles, finish, 0)
    rows = lax.broadcasted_iota(jnp.int32, (TILE, TILE), 0)
    columns = lax.broadcasted_iota(jnp.int32, (TILE, TILE), 1)
    flip = jnp.where(rows + columns == TILE - 1, 1.0, 0.0)
    bias_grad[...] = jnp.zeros(bias_grad.shape, jnp.float32)
    for head in range(2):
        spread = jnp.concatenate(
            [
                bias_acc[head, 2],
                bias_acc[head, 1],
                jnp.zeros((TILE, TILE), jnp.float32),
                bias_acc[head, 3],
            ],
            axis=1,
        )
        flipped = jnp.dot(
            flip, spread, precision=lax.Precision.HIGHEST, preferred_element_type=jnp.float32
        )
        turned = pltpu.roll(flipped, SPAN - TILE + 1, axis=1, stride=1, stride_axis=0)
        bias_grad[head : head + 1, :] = jnp.sum(turned, axis=0, keepdims=True)
        bias_grad[2 + head : 3 + head, :TILE] = jnp.sum(bias_acc[head, 0], axis=0, keepdims=True)
        bias_grad[4 + head : 5 + head, :TILE] = jnp.sum(bias_acc[head, 4], axis=0, keepdims=True)


def in_vmem(count):
    return [pl.BlockSpec(memory_space=pltpu.VMEM)] * count


def run_forward(alive, packed, segment, line):
    length = packed.shape[0]
    return pl.pallas_call(
        attention_forward,
        out_shape=(
            jax.ShapeDtypeStruct((length, 128), jnp.bfloat16),
            jax.ShapeDtypeStruct((128, length), jnp.float32),
            jax.ShapeDtypeStruct((8, length), jnp.float32),
        ),
        in_specs=[pl.BlockSpec(memory_space=pltpu.SMEM)] + in_vmem(3),
        out_specs=tuple(in_vmem(3)),
        scratch_shapes=[
            pltpu.VMEM((length, 256), jnp.bfloat16),
            pltpu.VMEM((2, 256, length), jnp.bfloat16),
            pltpu.VMEM((2, HEAD + 16, length), jnp.bfloat16),
            pltpu.VMEM((2, 5, TILE, TILE), jnp.float32),
            pltpu.VMEM((8, TILE), jnp.float32),
            pltpu.VMEM((2, HEAD + 16, TILE), jnp.float32),
        ],
        compiler_params=pltpu.CompilerParams(vmem_limit_bytes=40 * 2**20),
        name="attention_forward",
    )(alive, packed, segment, line)


def run_backward(alive, packed, segment, line, grads, out_t, log_sum):
    length = packed.shape[0]
    tiles = length // TILE
    return pl.pallas_call(
        attention_backward,
        out_shape=(
            jax.ShapeDtypeStruct((length, 384), jnp.bfloat16),
            jax.ShapeDtypeStruct((8, SPAN), jnp.float32),
        ),
        in_specs=[pl.BlockSpec(memory_space=pltpu.SMEM)] + in_vmem(6),
        out_specs=tuple(in_vmem(2)),
        scratch_shapes=[
            pltpu.VMEM((length, 256), jnp.bfloat16),
            pltpu.VMEM((length, 256), jnp.bfloat16),
            pltpu.VMEM((2, 256, length), jnp.bfloat16),
            pltpu.VMEM((2, 256, length), jnp.bfloat16),
            pltpu.VMEM((128, length), jnp.bfloat16),
            pltpu.VMEM((tiles, 2 * TILE, 128), jnp.bfloat16),
            pltpu.VMEM((tiles, 2 * TILE, 128), jnp.bfloat16),
            pltpu.VMEM((2, 5, TILE, TILE), jnp.float32),
            pltpu.VMEM((2, 5, TILE, TILE), jnp.float32),
            pltpu.VMEM((128, length), jnp.float32),
            pltpu.VMEM((TILE, 128), jnp.float32),
            pltpu.VMEM((TILE, 128), jnp.float32),
        ],
        compiler_params=pltpu.CompilerParams(vmem_limit_bytes=48 * 2**20),
        name="attention_backward",
    )(alive, packed, segment, line, grads, out_t, log_sum)


def signed_span():
    places = jnp.arange(SPAN, dtype=jnp.int32)
    return jnp.where(places < SPAN // 2, -places, SPAN - places)


def span_buckets():
    return (bucket_ids(signed_span())[:, None] == jnp.arange(NBUCK)[None, :]).astype(jnp.float32)


def live_tiles(segments, live):
    tiles = segments.shape[0] // TILE
    grouped = segments.reshape(tiles, TILE)
    first, last = grouped[:, 0], grouped[:, -1]
    meets = (first[:, None] <= last[None, :]) & (first[None, :] <= last[:, None])
    spread = jnp.repeat(jnp.repeat(live, ATT_BLK // TILE, axis=0), ATT_BLK // TILE, axis=1)
    return (meets & (spread == 1)).astype(jnp.int32).reshape(-1)


def contract_rows(left, right):
    return lax.dot_general(
        left, right, (((0,), (0,)), ((), ())), preferred_element_type=jnp.float32
    )


def contract_cols(left, right):
    return lax.dot_general(
        left, right, (((1,), (1,)), ((), ())), preferred_element_type=jnp.float32
    )


def local(
    tokens_in,
    cotangent,
    segment_ids,
    live_blocks,
    routes,
    w_query,
    w_key,
    w_value,
    w_out,
    rel_bias,
    attn_gain,
    ffn_gain,
    router,
    w_gate,
    w_up,
    w_down,
):
    width = tokens_in.shape[1]
    rows_here = tokens_in.shape[0]
    ctx_size = lax.axis_size("ctx")
    ctx_index = lax.axis_index("ctx")
    heads_here = w_query.shape[1] // HEAD
    share = w_query.shape[1] // ctx_size

    def by_owner(member):
        return member.reshape(member.shape[0], ctx_size, share)

    packed_rows = jnp.stack([by_owner(w_query), by_owner(w_key), by_owner(w_value)], axis=2)
    experts = router.shape[1]
    gathered = lax.all_gather(
        jnp.concatenate(
            [
                packed_rows.reshape(w_query.shape[0], -1),
                w_out,
                attn_gain[:, None],
                ffn_gain[:, None],
                router,
            ],
            axis=1,
        ).astype(jnp.bfloat16),
        ("shard", "ctx"),
        axis=0,
        tiled=True,
    )
    head_cols = w_query.shape[1]
    packed_w = gathered[:, : 3 * head_cols]
    out_w = gathered[:, 3 * head_cols : 4 * head_cols]
    gain_one = gathered[:, 4 * head_cols]
    gain_two = gathered[:, 4 * head_cols + 1]
    router_w = gathered[:, 4 * head_cols + 2 :]
    inputs = tokens_in.astype(jnp.float32)
    scale_one = lax.rsqrt(jnp.mean(inputs * inputs, axis=1, keepdims=True) + 1e-06)
    normal_one = inputs * scale_one
    norm_one = (normal_one * gain_one.astype(jnp.float32)).astype(jnp.bfloat16)
    packed = jnp.dot(norm_one, packed_w, preferred_element_type=jnp.float32).astype(jnp.bfloat16)
    packed = jnp.transpose(packed.reshape(rows_here, ctx_size, 3 * share), (1, 0, 2))
    packed = lax.all_to_all(packed, "ctx", split_axis=0, concat_axis=0, tiled=True)
    packed = packed.reshape(ctx_size * rows_here, 3 * share)
    segments = lax.all_gather(segment_ids.reshape(-1), "ctx", axis=0, tiled=True)
    alive = live_tiles(segments, live_blocks[0])
    segment_row = segments.astype(jnp.float32)[None]
    pair_heads = share // HEAD
    own_bias = lax.dynamic_slice_in_dim(rel_bias, ctx_index * pair_heads, pair_heads, 1)
    buckets = span_buckets()
    line = jnp.dot(own_bias.T, buckets.T, precision=lax.Precision.HIGHEST)
    attended, attended_t, log_sum = run_forward(alive, packed, segment_row, line)
    attended_low = lax.all_to_all(
        attended.reshape(ctx_size, rows_here, share), "ctx", split_axis=0, concat_axis=0, tiled=True
    )
    attended_low = jnp.transpose(attended_low, (1, 0, 2)).reshape(rows_here, head_cols)
    branch = lax.psum(contract_cols(attended_low, out_w).astype(jnp.bfloat16), "tensor").astype(
        jnp.float32
    )
    hidden_one = inputs + branch
    scale_two = lax.rsqrt(jnp.mean(hidden_one * hidden_one, axis=1, keepdims=True) + 1e-06)
    normal_two = hidden_one * scale_two
    norm_two = (normal_two * gain_two.astype(jnp.float32)).astype(jnp.bfloat16)
    logits = jnp.dot(norm_two, router_w, preferred_element_type=jnp.float32)
    picks = routes[:, :, None] == jnp.arange(experts, dtype=jnp.int32)[None, None, :]
    chosen = jnp.sum(jnp.where(picks, logits[:, None, :], 0.0), axis=2)
    gates = jax.nn.softmax(chosen, axis=1)
    upstream = cotangent.astype(jnp.float32)
    flat_picks = picks.reshape(rows_here * TOP, experts).astype(jnp.int32)
    slot_of = jnp.sum(flat_picks * (jnp.cumsum(flat_picks, axis=0) - 1), axis=1)
    expert_of = routes.reshape(-1)
    capacity = max(2, 3 * rows_here // experts)
    shaped = (experts, capacity, width)
    send_rows = (
        jnp.zeros(shaped, jnp.bfloat16)
        .at[expert_of, slot_of]
        .set(jnp.repeat(norm_two, TOP, axis=0))
    )
    grad_rows = (
        (gates[:, :, None] * upstream[:, None, :])
        .reshape(rows_here * TOP, width)
        .astype(jnp.bfloat16)
    )
    send_grads = jnp.zeros(shaped, jnp.bfloat16).at[expert_of, slot_of].set(grad_rows)
    got_rows, got_grads = (
        lax.all_to_all(send_rows, "shard", split_axis=0, concat_axis=0, tiled=True),
        lax.all_to_all(send_grads, "shard", split_axis=0, concat_axis=0, tiled=True),
    )
    expert_gate, expert_up, expert_down = (
        lax.all_gather(w_gate.astype(jnp.bfloat16), "ctx", axis=1, tiled=True),
        lax.all_gather(w_up.astype(jnp.bfloat16), "ctx", axis=1, tiled=True),
        lax.all_gather(w_down.astype(jnp.bfloat16), "ctx", axis=1, tiled=True),
    )
    gate_mat = expert_gate[0]
    up_mat = expert_up[0]
    down_mat = expert_down[0]
    slot_rows = got_rows.reshape(-1, width)
    slot_grads = got_grads.reshape(-1, width)
    gate_pre = jnp.dot(slot_rows, gate_mat, preferred_element_type=jnp.float32)
    up_pre = jnp.dot(slot_rows, up_mat, preferred_element_type=jnp.float32)
    activated, gelu_back = jax.vjp(partial(jax.nn.gelu, approximate=True), gate_pre)
    inner = (activated * up_pre).astype(jnp.bfloat16)
    expert_out = contract_cols(inner, down_mat)
    inner_grad = jnp.dot(slot_grads, down_mat, preferred_element_type=jnp.float32)
    gate_grad = gelu_back(inner_grad * up_pre)[0].astype(jnp.bfloat16)
    up_grad = (inner_grad * activated).astype(jnp.bfloat16)
    rows_grad = contract_cols(gate_grad, gate_mat) + contract_cols(up_grad, up_mat)
    weight_grads = lax.psum_scatter(
        jnp.stack(
            [
                contract_rows(slot_rows, gate_grad),
                contract_rows(slot_rows, up_grad),
                contract_rows(slot_grads, inner),
            ],
            axis=1,
        ).astype(jnp.bfloat16),
        "ctx",
        scatter_dimension=0,
        tiled=True,
    ).astype(jnp.float32)
    expert_out, rows_grad = (
        lax.psum(expert_out.astype(jnp.bfloat16), "tensor").astype(jnp.float32),
        lax.psum(rows_grad.astype(jnp.bfloat16), "tensor").astype(jnp.float32),
    )
    back_out, back_grad = (
        lax.all_to_all(
            expert_out.reshape(shaped).astype(jnp.bfloat16),
            "shard",
            split_axis=0,
            concat_axis=0,
            tiled=True,
        ).astype(jnp.float32),
        lax.all_to_all(
            rows_grad.reshape(shaped).astype(jnp.bfloat16),
            "shard",
            split_axis=0,
            concat_axis=0,
            tiled=True,
        ).astype(jnp.float32),
    )
    per_choice = back_out[expert_of, slot_of].reshape(rows_here, TOP, width)
    mixture = jnp.sum(gates[:, :, None] * per_choice, axis=1)
    gate_dots = jnp.sum(per_choice * upstream[:, None, :], axis=2)
    norm_grad = jnp.sum(back_grad[expert_of, slot_of].reshape(rows_here, TOP, width), axis=1)
    mixed = (hidden_one + mixture).astype(jnp.bfloat16)
    gate_shift = gates * (gate_dots - jnp.sum(gates * gate_dots, axis=1, keepdims=True))
    logit_grad = jnp.sum(jnp.where(picks, gate_shift[:, :, None], 0.0), axis=1)
    router_f = router_w.astype(jnp.float32)
    norm_grad = norm_grad + jnp.dot(logit_grad, router_f.T, precision=lax.Precision.HIGHEST)
    spread_two = norm_grad * gain_two.astype(jnp.float32)
    hidden_grad = upstream + scale_two * (
        spread_two - normal_two * jnp.mean(spread_two * normal_two, axis=1, keepdims=True)
    )
    branch_grad = hidden_grad.astype(jnp.bfloat16)
    attended_grad = jnp.dot(branch_grad, out_w, preferred_element_type=jnp.float32).astype(
        jnp.bfloat16
    )
    grad_heads = jnp.transpose(attended_grad.reshape(rows_here, ctx_size, share), (1, 0, 2))
    grad_heads = lax.all_to_all(grad_heads, "ctx", split_axis=0, concat_axis=0, tiled=True)
    packed_grad, bias_line = run_backward(
        alive, packed, segment_row, line, grad_heads.reshape(-1, share), attended_t, log_sum
    )
    own_grad = jnp.dot(buckets.T, bias_line[:pair_heads].T, precision=lax.Precision.HIGHEST)
    far = jnp.sum(bias_line[pair_heads : 3 * pair_heads], axis=1)
    half = NBUCK // 2
    own_grad = own_grad.at[half - 1].add(far[:pair_heads]).at[NBUCK - 1].add(far[pair_heads:])
    bias_acc = lax.dynamic_update_slice_in_dim(
        jnp.zeros(rel_bias.shape, jnp.float32), own_grad, ctx_index * pair_heads, 1
    )
    packed_grad = lax.all_to_all(
        packed_grad.reshape(ctx_size, rows_here, 3 * share),
        "ctx",
        split_axis=0,
        concat_axis=0,
        tiled=True,
    )
    packed_grad = jnp.transpose(packed_grad, (1, 0, 2)).reshape(rows_here, 3 * head_cols)
    norm_one_grad = lax.psum(
        contract_cols(packed_grad, packed_w).astype(jnp.bfloat16), "tensor"
    ).astype(jnp.float32)
    spread_one = norm_one_grad * gain_one.astype(jnp.float32)
    input_grad = hidden_grad + scale_one * (
        spread_one - normal_one * jnp.mean(spread_one * normal_one, axis=1, keepdims=True)
    )
    gain_one_terms = norm_one_grad * normal_one
    gain_two_terms = norm_grad * normal_two
    cols_two = norm_two.astype(jnp.float32)
    first_gain = jnp.sum(gain_one_terms, axis=0)[:, None]
    second_gain = jnp.sum(gain_two_terms, axis=0)[:, None]
    router_part = jnp.dot(cols_two.T, logit_grad, precision=lax.Precision.HIGHEST)
    reduced = lax.psum_scatter(
        jnp.concatenate(
            [
                contract_rows(norm_one, packed_grad),
                contract_rows(branch_grad, attended_low),
                first_gain,
                second_gain,
                router_part,
            ],
            axis=1,
        ),
        ("shard", "ctx"),
        scatter_dimension=0,
        tiled=True,
    )
    grad_bias = lax.psum(bias_acc, ("shard", "ctx"))
    packed_rows = reduced[:, : 3 * head_cols].reshape(-1, ctx_size, 3, share)
    return (
        mixed,
        input_grad.astype(jnp.bfloat16),
        packed_rows[:, :, 0].reshape(-1, head_cols),
        packed_rows[:, :, 1].reshape(-1, head_cols),
        packed_rows[:, :, 2].reshape(-1, head_cols),
        reduced[:, 3 * head_cols : 4 * head_cols],
        grad_bias,
        reduced[:, 4 * head_cols],
        reduced[:, 4 * head_cols + 1],
        reduced[:, 4 * head_cols + 2 :],
        weight_grads[:, 0][None],
        weight_grads[:, 1][None],
        weight_grads[:, 2][None],
    )


def solution(mesh):
    placed = (
        P(("shard", "ctx"), None),
        P(("shard", "ctx"), None),
        P("shard", "ctx"),
        P("shard", None, None),
        P(("shard", "ctx"), None),
        P(("shard", "ctx"), "tensor"),
        P(("shard", "ctx"), "tensor"),
        P(("shard", "ctx"), "tensor"),
        P(("shard", "ctx"), "tensor"),
        P(None, "tensor"),
        P(("shard", "ctx")),
        P(("shard", "ctx")),
        P(("shard", "ctx"), None),
        P("shard", "ctx", "tensor"),
        P("shard", "ctx", "tensor"),
        P("shard", "ctx", "tensor"),
    )
    return jax.shard_map(
        local,
        mesh=mesh,
        in_specs=placed,
        out_specs=(
            P(("shard", "ctx"), None),
            P(("shard", "ctx"), None),
            P(("shard", "ctx"), "tensor"),
            P(("shard", "ctx"), "tensor"),
            P(("shard", "ctx"), "tensor"),
            P(("shard", "ctx"), "tensor"),
            P(None, "tensor"),
            P(("shard", "ctx")),
            P(("shard", "ctx")),
            P(("shard", "ctx"), None),
            P("shard", "ctx", "tensor"),
            P("shard", "ctx", "tensor"),
            P("shard", "ctx", "tensor"),
        ),
        check_vma=False,
    )
```

time: 1550 us -> 1030 us (0.66)
  matrix products: 353 us -> 119 us
  local copies, waits for them, and re-layouts: 253 us -> 112 us
  blocking collectives: 215 us -> 141 us
  other arithmetic: 134 us -> 74.1 us
  Pallas kernels: 0 us -> 48.7 us
  waiting for transfers between devices: 520 us -> 493 us
  loops' own time: 20.4 us -> 0 us
    dot_general x43 -> x3, matrix products: 241 us -> 4.61 us  [the longest x1 3.79 us: local(): jnp.dot(norm_one, packed_w, preferred_element_type=jnp.float32)]
    unnamed x16 -> x9, waiting for transfers between devices: 106 us -> 0.15 us
    reduce_scatter x1, waiting for transfers between devices: 21.5 us -> 103 us  [local(): lax.psum_scatter(jnp.concatenate([contract_rows(norm_one, packed_grad), c...]
    all_gather x2 -> x1, blocking collectives: 69.4 us -> 6.11 us  [local(): lax.all_gather(segment_ids.reshape(-1), 'ctx', axis=0, tiled=True)]
    all_gather x6 -> x1, waiting for transfers between devices: 106 us -> 47.2 us  [local(): lax.all_gather(jnp.concatenate([packed_rows.reshape(w_query.shape[0], -1)...]
    pallas_call x0 -> x2, Pallas kernels: none -> 48.7 us  [the longest x1 26.7 us: run_backward(): pl.pallas_call(attention_backward, out_shape=(jax.ShapeDtypeStruct((lengt...]
    all_to_all x1, waiting for transfers between devices: 0.01 us -> 47 us  [local(): lax.all_to_all(send_rows, 'shard', split_axis=0, concat_axis=0, tiled=True)]
    dynamic_update_slice x4 -> x1, local copies, waits for them, and re-layouts: 41.2 us -> 0.01 us  [local(): lax.dynamic_update_slice_in_dim(jnp.zeros(rel_bias.shape, jnp.float32), o...]
  transfers between devices with their start and end apart: 18 -> 14, of which waited for: 13 -> 11; matrix products, arithmetic and copies ran while one was open for 26% -> 17% of each run, Pallas kernels for 0% -> 0%
where the time goes in v1:
time: 1030 us
  waiting for transfers between devices  493 us (48%)
  blocking collectives  141 us (14%)
  matrix products  119 us (12%)
  local copies, waits for them, and re-layouts  112 us (11%)
  other arithmetic  74.1 us (7%)
  Pallas kernels  48.7 us (5%)
  starting transfers between devices  22.4 us (2%)
  between operations  16.6 us (2%)
    psum x1, waiting for transfers between devices, local(): lax.psum(expert_out.astype(jnp.bfloat16), 'tensor').astype(jnp.float32)  152 us
    reduce_scatter x1, waiting for transfers between devices, local(): lax.psum_scatter(jnp.concatenate([contract_rows(norm_one, packed_grad), c...  103 us
    all_to_all x1, blocking collectives, local(): lax.all_to_all(expert_out.reshape(shaped).astype(jnp.bfloat16), 'shard',...  76.3 us
    all_gather x1, waiting for transfers between devices, local(): lax.all_gather(jnp.concatenate([packed_rows.reshape(w_query.shape[0], -1)...  47.2 us
    all_to_all x1, waiting for transfers between devices, local(): lax.all_to_all(send_rows, 'shard', split_axis=0, concat_axis=0, tiled=True)  47 us
    all_to_all x1, waiting for transfers between devices, local(): lax.all_to_all(send_grads, 'shard', split_axis=0, concat_axis=0, tiled=True)  40.2 us
    dot_general x5, matrix products, contract_rows(): lax.dot_general(left, right, (((0,), (0,)), ((), ())), preferred_element_...  36.6 us
    psum x1, waiting for transfers between devices, local(): lax.psum(contract_cols(attended_low, out_w).astype(jnp.bfloat16), 'tensor')  34.6 us
  transfers between devices with their start and end apart: 14, of which 11 were waited for; matrix products, arithmetic and copies ran while one was open for 17% of the time, Pallas kernels for 0%

profile of v1, /device:TPU:0, one launch (start us, length us, event | category | flops | bytes accessed | tf_op | source)
XLA Modules:
  0.0 1027.5 jit_solution(12905447692027817545)
XLA Ops:
  23.5 47.2 %all-gather.6.cloned.1.call-done = bf16[1024,2054]{1,0:T(8,128)(2,1)} async-done(((bf16[64,2054]{1,0:T(8,128)(2,1)}), bf16[1024,2054]{1,0:T(8,128)(2,1)}) %all-gather.6.cloned.1.call-update) | async-done | bytes 4206608 | tf_op jit(solution)/shard_map/all_gather | solution.py:385
  82.3 18.5 %all-to-all-done = bf16[4,512,384]{2,1,0:T(8,128)(2,1)S(1)} async-done(((bf16[4,512,384]{2,1,0:T(8,128)(2,1)}), bf16[4,512,384]{2,1,0:T(8,128)(2,1)S(1)}, u32[]{:S(2)}, u32[]{:S(2)}) %all-to-all-start) | async-done | bytes 1572896 | tf_op jit(solution)/shard_map/all_to_all | solution.py:412
  100.8 22.0 %attention_forward.1 = (bf16[2048,128]{1,0:T(8,128)(2,1)S(1)}, f32[128,2048]{1,0:T(8,128)S(1)}, f32[8,2048]{1,0:T(8,128)S(1)}) custom-call(s32[64]{0:T(128)S(1)} %and_convert_fusion.alive, bf16[2048,384]{1,0:T(8,128)(2,1)S(1)} %bitcast.117, f32[1,2048]{1,0:T(1,128)S(1)} %get-tuple-element.122.segment, f32[2,1024]{1,0:T(2,128)S(1)} %fusion.50.line), custom_call_target="tpu_custom_call" | custom-call | tf_op jit(solution)/shard_map/attention_forward/pallas_call | solution.py:273
  124.9 12.3 %all_to_all.40 = bf16[4,512,128]{1,2,0:T(8,128)(2,1)S(1)} all-to-all(bf16[4,512,128]{1,2,0:T(8,128)(2,1)} %copy.108), channel_id=1, replica_groups=mesh['shard'=4,'ctx'=4,'tensor'=2] {'ctx'}, dimensions={0} | all-to-all | bytes 1048576 | tf_op jit(solution)/shard_map/all_to_all | solution.py:422
  145.8 34.6 %all-reduce.5.cloned.1.call-done = bf16[512,1024]{1,0:T(8,128)(2,1)} async-done(((bf16[512,1024]{1,0:T(8,128)(2,1)}), bf16[512,1024]{1,0:T(8,128)(2,1)}) %all-reduce.5.cloned.1.call-update) | async-done | bytes 1048592 | tf_op jit(solution)/shard_map/psum | solution.py:426
  228.0 47.0 %all-to-all-done.2 = bf16[4,384,1024]{2,1,0:T(8,128)(2,1)} async-done(((bf16[4,384,1024]{2,1,0:T(8,128)(2,1)}), bf16[4,384,1024]{2,1,0:T(8,128)(2,1)}, u32[]{:S(2)}, u32[]{:S(2)}) %all-to-all-start.2) | async-done | bytes 3145760 | tf_op jit(solution)/shard_map/all_to_all | solution.py:455
  282.3 9.5 fusion.18
  291.8 9.5 fusion.22
  309.7 40.2 %all-to-all-done.4 = bf16[4,384,1024]{2,1,0:T(8,128)(2,1)} async-done(((bf16[4,384,1024]{2,1,0:T(8,128)(2,1)}), bf16[4,384,1024]{2,1,0:T(8,128)(2,1)}, u32[]{:S(2)}, u32[]{:S(2)}) %all-to-all-start.4) | async-done | bytes 3145760 | tf_op jit(solution)/shard_map/all_to_all | solution.py:456
  349.9 19.0 %multiply_convert_fusion = (bf16[1536,1408]{1,0:T(8,128)(2,1)S(1)}, bf16[1536,1408]{1,0:T(8,128)(2,1)}, bf16[1536,1408]{1,0:T(8,128)(2,1)}) fusion(f32[1536,1408]{1,0:T(8,128)} %fusion.22, f32[1536,1408]{1,0:T(8,128)} %fusion.18, bf16[1536,1024]{1,0:T(8,128)(2,1)} %bitcast.20, bf16[1,1024,1408]{2,1,0:T(8,128)(2,1)} %all-gather.12.cloned.1.call-done), kind=kOutput, calls=%fused_computation.14 | convolution fusion | flops 4485414912 | bytes 36306944 | tf_op jit(solution)/shard_map/dot_general | solution.py:473
  391.1 151.9 %all-reduce.9.cloned.1.call-done = (bf16[4,384,1024]{2,1,0:T(8,128)(2,1)}, bf16[4,384,1024]{2,1,0:T(8,128)(2,1)}) async-done(((bf16[4,384,1024]{2,1,0:T(8,128)(2,1)}, bf16[4,384,1024]{2,1,0:T(8,128)(2,1)}), (bf16[4,384,1024]{2,1,0:T(8,128)(2,1)}, bf16[4,384,1024]{2,1,0:T(8,128)(2,1)})) %all-reduce.9.cloned.1.call-update) | async-done | bytes 6291472 | tf_op jit(solution)/shard_map/psum | solution.py:491
  543.0 76.3 %all_to_all.41 = bf16[4,384,1024]{2,1,0:T(8,128)(2,1)} all-to-all(bf16[4,384,1024]{2,1,0:T(8,128)(2,1)} %get-tuple-element.112), channel_id=1, replica_groups=mesh['shard'=4,'ctx'=4,'tensor'=2] {'shard'}, dimensions={0} | all-to-all | bytes 6291456 | tf_op jit(solution)/shard_map/all_to_all | solution.py:495
  630.3 20.4 %gather_fusion = f32[1024,1024]{1,0:T(8,128)} fusion(f32[4,384,1024]{2,1,0:T(8,128)} %convert_element_type.213, s32[1024]{0:T(1024)S(1)} %bitcast.122), kind=kCustom, calls=%fused_computation | custom fusion | bytes 8396800 | tf_op jit(solution)/shard_map/gather | solution.py:510
  656.6 10.4 %multiply_reduce_fusion = (f32[512,2]{1,0:T(8,128)S(1)}, f32[512,1024]{1,0:T(8,128)}) fusion(f32[512,2,1024]{2,1,0:T(2,128)} %reshape.408, f32[512,1024]{1,0:T(8,128)} %convert_element_type.215, f32[512,2]{1,0:T(8,128)S(1)} %copy.109), kind=kLoop, calls=%fused_computation.18 | loop fusion | flops 3668992 | bytes 8396800 | tf_op jit(solution)/shard_map/reduce_sum | solution.py:512
  667.2 27.0 %all-to-all-done.5 = bf16[4,384,1024]{2,1,0:T(8,128)(2,1)} async-done(((bf16[4,384,1024]{2,1,0:T(8,128)(2,1)}), bf16[4,384,1024]{2,1,0:T(8,128)(2,1)}, u32[]{:S(2)}, u32[]{:S(2)}) %all-to-all-start.5) | async-done | bytes 3145760 | tf_op jit(solution)/shard_map/all_to_all | solution.py:502
  699.5 20.4 %gather_fusion.1 = f32[1024,1024]{1,0:T(8,128)} fusion(f32[4,384,1024]{2,1,0:T(8,128)} %convert_element_type.221, s32[1024]{0:T(1024)S(1)} %bitcast.123), kind=kCustom, calls=%fused_computation.1 | custom fusion | bytes 8396800 | tf_op jit(solution)/shard_map/gather | solution.py:513
  744.0 11.6 %all_to_all.42 = bf16[4,512,128]{2,1,0:T(8,128)(2,1)S(1)} all-to-all(bf16[4,512,128]{2,1,0:T(8,128)(2,1)S(1)} %bitcast.132), channel_id=1, replica_groups=mesh['shard'=4,'ctx'=4,'tensor'=2] {'ctx'}, dimensions={0} | all-to-all | bytes 1048576 | tf_op jit(solution)/shard_map/all_to_all | solution.py:528
  756.8 26.7 %attention_backward.1 = (bf16[2048,384]{1,0:T(8,128)(2,1)S(1)}, f32[8,1024]{1,0:T(8,128)S(1)}) custom-call(s32[64]{0:T(128)S(1)} %and_convert_fusion.alive, bf16[2048,384]{1,0:T(8,128)(2,1)S(1)} %bitcast.118, f32[1,2048]{1,0:T(1,128)S(1)} %get-tuple-element.122.segment, f32[2,1024]{1,0:T(2,128)S(1)} %fusion.50.line, bf16[2048,128]{1,0:T(8,128)(2,1)S(1)} %bitcast.119, ...), custom_call_target="tpu_custom_call" | custom-call | tf_op jit(solution)/shard_map/attention_backward/pallas_call | solution.py:298
  788.7 9.1 fusion.9
  797.8 9.1 fusion.7
  839.0 13.9 %all-reduce.7.cloned.1.call-done = bf16[512,1024]{1,0:T(8,128)(2,1)} async-done(((bf16[512,1024]{1,0:T(8,128)(2,1)}), bf16[512,1024]{1,0:T(8,128)(2,1)}) %all-reduce.7.cloned.1.call-update) | async-done | bytes 1048592 | tf_op jit(solution)/shard_map/psum | solution.py:547
  855.1 10.1 concatenate.19
  866.7 34.6 %psum.39 = f32[32,8]{0,1:T(8,128)} all-reduce(f32[32,8]{0,1:T(8,128)S(1)} %constant_dynamic-update-slice_fusion), channel_id=1, replica_groups=mesh['shard'=4,'ctx'=4,'tensor'=2] {'shard','ctx'}, use_global_device_ids=true, to_apply=%region_25.26 | all-reduce | flops 256 | bytes 2048 | tf_op jit(solution)/shard_map/psum | solution.py:575
  908.6 102.7 %reduce-scatter.3.cloned.1.call-done = f32[64,2054]{1,0:T(8,128)} async-done(((f32[1024,2054]{1,0:T(8,128)}), f32[64,2054]{1,0:T(8,128)}) %reduce-scatter.3.cloned.1.call-update) | async-done | bytes 525840 | tf_op jit(solution)/shard_map/reduce_scatter | solution.py:560
  (227 shorter events, 226.8 us)
Async XLA Ops:
  8.0 73.8 %copy-start = (f32[32,8]{0,1:T(8,128)S(1)}, f32[32,8]{0,1:T(8,128)}, u32[]{:S(2)}) copy-start(f32[32,8]{0,1:T(8,128)} %param.29) | copy-start | bytes 3076
  8.0 15.1 %copy-start.4 = (bf16[512,1024]{1,0:T(8,128)(2,1)S(1)}, bf16[512,1024]{1,0:T(8,128)(2,1)}, u32[]{:S(2)}) copy-start(bf16[512,1024]{1,0:T(8,128)(2,1)} %param.20) | copy-start | bytes 3145732
  8.1 62.6 %all-gather.6.cloned.1.call-start = ((), (), s32[]{:S(2)}) async-start(), calls=%async_computation.10 | async-start | bytes 4734976 | tf_op jit(solution)/shard_map/all_gather | solution.py:385
  23.4 52.4 %copy-start.23 = (f32[512]{0:T(512)}, f32[512]{0:T(512)S(1)}, u32[]{:S(2)}) copy-start(f32[512]{0:T(512)S(1)} %add_rsqrt_fusion.1) | copy-start | bytes 6148
  77.2 23.6 %all-to-all-start = ((bf16[4,512,384]{2,1,0:T(8,128)(2,1)}), bf16[4,512,384]{2,1,0:T(8,128)(2,1)S(1)}, u32[]{:S(2)}, u32[]{:S(2)}) async-start(bf16[4,512,384]{2,1,0:T(8,128)(2,1)} %bitcast.126), calls=%async_computation | async-start | bytes 3145728 | tf_op jit(solution)/shard_map/all_to_all | solution.py:412
  80.8 99.7 %all-reduce.5.cloned.1.call-start = ((), (), s32[]{:S(2)}) async-start(), calls=%async_computation.11 | async-start | bytes 2097152 | tf_op jit(solution)/shard_map/psum | solution.py:426
  81.8 58.5 %copy-start.25 = (s32[1024]{0:T(1024)}, s32[1024]{0:T(1024)S(1)}, u32[]{:S(2)}) copy-start(s32[1024]{0:T(1024)S(1)} %fusion.73) | copy-start | bytes 12292
  140.3 142.0 %all-gather.10.cloned.1.call-start = ((), (), s32[]{:S(2)}) async-start(), calls=%async_computation.13 | async-start | bytes 3604480 | tf_op jit(solution)/shard_map/all_gather | solution.py:460
  199.3 75.7 %all-to-all-start.2 = ((bf16[4,384,1024]{2,1,0:T(8,128)(2,1)}), bf16[4,384,1024]{2,1,0:T(8,128)(2,1)}, u32[]{:S(2)}, u32[]{:S(2)}) async-start(bf16[4,384,1024]{2,1,0:T(8,128)(2,1)} %bitcast.125), calls=%async_computation.2 | async-start | bytes 6291456 | tf_op jit(solution)/shard_map/all_to_all | solution.py:455
  204.0 87.8 %all-gather.8.cloned.1.call-start = ((), (), s32[]{:S(2)}) async-start(), calls=%async_computation.12 | async-start | bytes 3604480 | tf_op jit(solution)/shard_map/all_gather | solution.py:459
  275.0 74.9 %all-to-all-start.4 = ((bf16[4,384,1024]{2,1,0:T(8,128)(2,1)}), bf16[4,384,1024]{2,1,0:T(8,128)(2,1)}, u32[]{:S(2)}, u32[]{:S(2)}) async-start(bf16[4,384,1024]{2,1,0:T(8,128)(2,1)} %bitcast.124), calls=%async_computation.4 | async-start | bytes 6291456 | tf_op jit(solution)/shard_map/all_to_all | solution.py:456
  279.7 30.0 %all-gather.12.cloned.1.call-start = ((), (), s32[]{:S(2)}) async-start(), calls=%async_computation.14 | async-start | bytes 3604480 | tf_op jit(solution)/shard_map/all_gather | solution.py:461
  282.0 260.9 %all-reduce.9.cloned.1.call-start = ((), (), s32[]{:S(2)}) async-start(), calls=%async_computation.18 | async-start | bytes 12582912 | tf_op jit(solution)/shard_map/psum | solution.py:491
  349.9 19.0 %copy-start.32 = (bf16[1,1024,1408]{2,1,0:T(8,128)(2,1)S(1)}, bf16[1,1024,1408]{2,1,0:T(8,128)(2,1)}, u32[]{:S(2)}) copy-start(bf16[1,1024,1408]{2,1,0:T(8,128)(2,1)} %all-gather.8.cloned.1.call-done) | copy-start | bytes 8650756
  368.9 15.2 %copy-start.34 = (bf16[1536,1408]{1,0:T(8,128)(2,1)}, bf16[1536,1408]{1,0:T(8,128)(2,1)S(1)}, u32[]{:S(2)}) copy-start(bf16[1536,1408]{1,0:T(8,128)(2,1)S(1)} %get-tuple-element.114) | copy-start | bytes 12976132
  368.9 8.5 copy-start.33
  619.2 75.0 %all-to-all-start.5 = ((bf16[4,384,1024]{2,1,0:T(8,128)(2,1)}), bf16[4,384,1024]{2,1,0:T(8,128)(2,1)}, u32[]{:S(2)}, u32[]{:S(2)}) async-start(bf16[4,384,1024]{2,1,0:T(8,128)(2,1)} %get-tuple-element.113), calls=%async_computation.5 | async-start | bytes 6291456 | tf_op jit(solution)/shard_map/all_to_all | solution.py:502
  785.1 23.6 %all-to-all-start.7 = ((bf16[4,512,384]{1,2,0:T(8,128)(2,1)}), bf16[4,512,384]{1,2,0:T(8,128)(2,1)S(1)}, u32[]{:S(2)}, u32[]{:S(2)}) async-start(bf16[4,512,384]{1,2,0:T(8,128)(2,1)} %copy.117), calls=%async_computation.7 | async-start | bytes 3145728 | tf_op jit(solution)/shard_map/all_to_all | solution.py:539
  788.7 64.2 %all-reduce.7.cloned.1.call-start = ((), (), s32[]{:S(2)}) async-start(), calls=%async_computation.15 | async-start | bytes 2097152 | tf_op jit(solution)/shard_map/psum | solution.py:547
  814.0 90.5 %reduce-scatter.5.cloned.1.call-start = ((), (), s32[]{:S(2)}) async-start(), calls=%async_computation.17 | async-start | bytes 10813440 | tf_op jit(solution)/shard_map/reduce_scatter | solution.py:477
  826.6 184.7 %reduce-scatter.3.cloned.1.call-start = ((), (), s32[]{:S(2)}) async-start(), calls=%async_computation.16 | async-start | bytes 9469952 | tf_op jit(solution)/shard_map/reduce_scatter | solution.py:560
  832.8 22.3 %copy-start.17 = (f32[1024,1]{1,0:T(8,128)S(1)}, f32[1024,1]{1,0:T(8,128)}, u32[]{:S(2)}) copy-start(f32[1024,1]{1,0:T(8,128)} %copy.120) | copy-start | bytes 12292
  865.3 36.0 %copy-start.12 = (bf16[512,1024]{1,0:T(8,128)(2,1)S(1)}, bf16[512,1024]{1,0:T(8,128)(2,1)}, u32[]{:S(2)}) copy-start(bf16[512,1024]{1,0:T(8,128)(2,1)} %all-reduce.7.cloned.1.call-done) | copy-start | bytes 3145732
  906.4 113.3 %copy-start.1 = (f32[32,8]{0,1:T(8,128)S(1)}, f32[32,8]{0,1:T(8,128)}, u32[]{:S(2)}) copy-start(f32[32,8]{0,1:T(8,128)} %param.29) | copy-start | bytes 3076
  (26 other events, 120.0 us)
Sparse Core Ops, SparseCore 0:
  15.9 54.6 all-gather.5
  140.5 39.9 all-reduce.4
  391.2 151.6 all-reduce.8
  814.1 38.6 all-reduce.6
Sparse Core Ops, SparseCore 1:
  143.3 26.7 all-gather.9
  206.7 27.3 all-gather.7
  282.4 27.3 all-gather.11
  826.7 72.4 reduce-scatter.4
  903.9 107.4 reduce-scatter.2

commit v2 on v1

--- a/solution.py
+++ b/solution.py
@@ -1,3 +1,4 @@
+import math
 from functools import partial
 
 import jax
@@ -23,6 +24,18 @@
         far = far + (distance >= bound).astype(jnp.int32)
     near = jnp.where(distance < 8, distance, far)
     return near + jnp.where(relative > 0, NBUCK // 2, 0)
+
+
+def contract_rows(left, right):
+    return lax.dot_general(
+        left, right, (((0,), (0,)), ((), ())), preferred_element_type=jnp.float32
+    )
+
+
+def contract_cols(left, right):
+    return lax.dot_general(
+        left, right, (((1,), (1,)), ((), ())), preferred_element_type=jnp.float32
+    )
 
 
 TILE = 256
@@ -340,16 +353,543 @@
     return (meets & (spread == 1)).astype(jnp.int32).reshape(-1)
 
 
-def contract_rows(left, right):
-    return lax.dot_general(
-        left, right, (((0,), (0,)), ((), ())), preferred_element_type=jnp.float32
-    )
-
-
-def contract_cols(left, right):
+MESH = pl.DeviceIdType.MESH
+
+
+def gelu_parts(value):
+    root = math.sqrt(2.0 / math.pi)
+    square = value * value
+    bend = jnp.tanh(root * value * (1.0 + 0.044715 * square))
+    half = 0.5 * (1.0 + bend)
+    slope = half + 0.5 * value * (1.0 - bend * bend) * (root * (1.0 + 0.134145 * square))
+    return value * half, slope
+
+
+def dot_last(left, right):
     return lax.dot_general(
         left, right, (((1,), (1,)), ((), ())), preferred_element_type=jnp.float32
     )
+
+
+def expert_exchange(
+    count,
+    norm,
+    gates,
+    code_rows,
+    code_cols,
+    upstream,
+    gate_hbm,
+    up_hbm,
+    down_hbm,
+    row_grad,
+    dot_rows,
+    rows_hbm,
+    slot_hbm,
+    inner_hbm,
+    gate_grad_hbm,
+    up_grad_hbm,
+    out_hbm,
+    gate_w,
+    up_w,
+    down_w,
+    rows,
+    sent,
+    gates_in,
+    gates_out,
+    slot_grad,
+    inner,
+    gate_grad,
+    up_grad,
+    outs,
+    partial,
+    peer_part,
+    summed,
+    back,
+    dots_out,
+    dots_in,
+    final_out,
+    final_in,
+    final_dots,
+    load_sem,
+    store_sem,
+    rows_send,
+    rows_recv,
+    pass_send,
+    pass_recv,
+    gates_send,
+    gates_recv,
+    part_send,
+    part_recv,
+    back_send,
+    back_recv,
+    dots_send,
+    dots_recv,
+    final_send,
+    final_recv,
+):
+    own = lax.axis_index("shard")
+    ctx = lax.axis_index("ctx")
+    side = lax.axis_index("tensor")
+    tokens, width = norm.shape
+    room = upstream.shape[1]
+    half = room // 2
+    hidden = gate_w.shape[1]
+    peer = (own, ctx, 1 - side)
+
+    def source(step):
+        flip = own // (count // 2)
+        place = flip * (count - 1 - own) + (1 - flip) * own
+        turn = step - 1
+        turn = turn + (turn - place + count) // count
+        other = flip * (count - 1 - turn) + (1 - flip) * turn
+        first = 1 - (step + count - 1) // count
+        return first * own + (1 - first) * other
+
+    barrier = pltpu.get_barrier_semaphore()
+    for step in range(1, count):
+        pl.semaphore_signal(barrier, 1, device_id=(source(step), ctx, side), device_id_type=MESH)
+    pl.semaphore_signal(barrier, 1, device_id=peer, device_id_type=MESH)
+    loads = [
+        pltpu.make_async_copy(source_ref, target, load_sem.at[number])
+        for number, (source_ref, target) in enumerate(
+            ((gate_hbm, gate_w), (up_hbm, up_w), (down_hbm, down_w))
+        )
+    ]
+    for load in loads:
+        load.start()
+    pl.semaphore_wait(barrier, count)
+
+    my_half = pl.ds(pl.multiple_of(side * half, half), half)
+    peer_half = pl.ds(pl.multiple_of((1 - side) * half, half), half)
+
+    def picked(expert, start, amount):
+        slots = lax.broadcasted_iota(jnp.int32, (amount, tokens), 0) + expert * room + start
+        slots = slots.astype(jnp.float32)
+        hit = (code_rows[0:1, :] == slots) | (code_rows[1:2, :] == slots)
+        return jnp.where(hit, 1.0, 0.0).astype(jnp.bfloat16)
+
+    def slot_gates(expert):
+        slots = lax.broadcasted_iota(jnp.int32, (tokens, room), 1) + expert * room
+        slots = slots.astype(jnp.float32)
+        held = jnp.where(code_cols[:, 0:1] == slots, gates[:, 0:1], 0.0)
+        held = held + jnp.where(code_cols[:, 1:2] == slots, gates[:, 1:2], 0.0)
+        return jnp.broadcast_to(jnp.sum(held, axis=0, keepdims=True), (8, room))
+
+    def rows_copy(step):
+        target = source(step)
+        return pltpu.make_async_remote_copy(
+            sent.at[step - 1],
+            rows.at[own, my_half],
+            rows_send.at[step - 1],
+            rows_recv.at[own],
+            device_id=(target, ctx, side),
+            device_id_type=MESH,
+        )
+
+    def gates_copy(step):
+        return pltpu.make_async_remote_copy(
+            gates_out.at[step - 1],
+            gates_in.at[own],
+            gates_send.at[step - 1],
+            gates_recv.at[own],
+            device_id=(source(step), ctx, side),
+            device_id_type=MESH,
+        )
+
+    def send_rows(step, unused):
+        target = source(step)
+        sent[step - 1] = dot32(picked(target, side * half, half), norm[...]).astype(jnp.bfloat16)
+        rows_copy(step).start()
+        gates_out[step - 1] = slot_gates(target)
+        gates_copy(step).start()
+        return unused
+
+    lax.fori_loop(1, count, send_rows, 0)
+    rows[own] = dot32(picked(own, 0, room), norm[...]).astype(jnp.bfloat16)
+    gates_in[own] = slot_gates(own)
+    for load in loads:
+        load.wait()
+
+    def landed(buffer, send, recv, origin):
+        return pltpu.make_async_remote_copy(
+            buffer, buffer, send, recv, device_id=peer, device_id_type=MESH
+        )
+
+    def pass_copy(origin):
+        return pltpu.make_async_remote_copy(
+            rows.at[origin, my_half],
+            rows.at[origin, my_half],
+            pass_send.at[origin],
+            pass_recv.at[origin],
+            device_id=peer,
+            device_id_type=MESH,
+        )
+
+    def part_copy(step):
+        return pltpu.make_async_remote_copy(
+            partial.at[step, peer_half],
+            peer_part.at[step],
+            part_send.at[step],
+            part_recv.at[step],
+            device_id=peer,
+            device_id_type=MESH,
+        )
+
+    def back_copy(step):
+        return pltpu.make_async_remote_copy(
+            summed.at[step],
+            back.at[own],
+            back_send.at[step],
+            back_recv.at[own],
+            device_id=(source(step), ctx, side),
+            device_id_type=MESH,
+        )
+
+    def dots_copy(step):
+        return pltpu.make_async_remote_copy(
+            dots_out.at[step],
+            dots_in.at[own],
+            dots_send.at[step],
+            dots_recv.at[own],
+            device_id=(source(step), ctx, side),
+            device_id_type=MESH,
+        )
+
+    def send_back(step):
+        part_copy(step).wait_recv()
+        summed[step] = (
+            partial[step, my_half].astype(jnp.float32) + peer_part[step].astype(jnp.float32)
+        ).astype(jnp.bfloat16)
+        back_copy(step).start()
+
+    cut = (hidden // 256 + 1) // 2 * 256
+    pieces = (slice(0, cut), slice(cut, hidden))
+
+    def run_chunk(step, unused):
+        origin = source(step)
+
+        @pl.when(step > 0)
+        def _():
+            landed(rows.at[origin, peer_half], pass_send.at[origin], pass_recv.at[origin], 0).wait_recv()
+            landed(gates_in.at[origin], gates_send.at[0], gates_recv.at[origin], 0).wait_recv()
+
+        gate_column = jnp.transpose(gates_in[origin])[:, 0:1]
+        slot_grad[origin] = (upstream[origin].astype(jnp.float32) * gate_column).astype(
+            jnp.bfloat16
+        )
+
+        def inside(piece):
+            block = rows[origin]
+            gate_pre = dot32(block, gate_w[:, piece])
+            up_pre = dot32(block, up_w[:, piece])
+            inner_grad = dot32(slot_grad[origin], down_w[:, piece])
+            active, slope = gelu_parts(gate_pre)
+            held = (active * up_pre).astype(jnp.bfloat16)
+            inner[origin, :, piece] = held
+            gate_grad[origin, :, piece] = (inner_grad * up_pre * slope).astype(jnp.bfloat16)
+            up_grad[origin, :, piece] = (inner_grad * active).astype(jnp.bfloat16)
+            return jnp.sum(active * up_pre * inner_grad, axis=1, keepdims=True)
+
+        dots = inside(pieces[0])
+
+        @pl.when(step < count - 1)
+        def _():
+            following = source(step + 1)
+            landed(
+                rows.at[following, my_half], rows_send.at[0], rows_recv.at[following], 0
+            ).wait_recv()
+            pass_copy(following).start()
+
+        dots = dots + inside(pieces[1])
+        dots_out[step] = jnp.transpose(jnp.broadcast_to(dots, (room, 128)))[0:8, :]
+
+        @pl.when(step > 1)
+        def _():
+            send_back(step - 1)
+
+        partial[step] = (
+            dot_last(gate_grad[origin], gate_w[...]) + dot_last(up_grad[origin], up_w[...])
+        ).astype(jnp.bfloat16)
+
+        @pl.when(step > 0)
+        def _():
+            part_copy(step).start()
+            dots_copy(step).start()
+
+        return unused
+
+    lax.fori_loop(0, count, run_chunk, 0)
+    stores = [
+        pltpu.make_async_copy(source_ref, target, store_sem.at[number])
+        for number, (source_ref, target) in enumerate(
+            (
+                (rows, rows_hbm),
+                (slot_grad, slot_hbm),
+                (inner, inner_hbm),
+                (gate_grad, gate_grad_hbm),
+                (up_grad, up_grad_hbm),
+            )
+        )
+    ]
+    for store in stores:
+        store.start()
+
+    def run_out(step, unused):
+        outs[step] = dot_last(inner[step], down_w[...]).astype(jnp.bfloat16)
+        return unused
+
+    lax.fori_loop(0, 1, run_out, 0)
+    send_back(count - 1)
+    lax.fori_loop(1, count, run_out, 0)
+    out_store = pltpu.make_async_copy(outs, out_hbm, store_sem.at[5])
+    out_store.start()
+
+    def dots_landed(step, unused):
+        origin = source(step)
+        landed(dots_in.at[origin], dots_send.at[0], dots_recv.at[origin], 0).wait_recv()
+        return unused
+
+    def back_landed(step, unused):
+        origin = source(step)
+        landed(back.at[origin], back_send.at[0], back_recv.at[origin], 0).wait_recv()
+        return unused
+
+    lax.fori_loop(1, count, dots_landed, 0)
+    dots_in[own] = dots_out[0]
+    final_dots[0] = jnp.zeros((8, tokens), jnp.float32)
+    for expert in range(count):
+        column = jnp.transpose(dots_in[expert])[:, 0:1]
+        slots = lax.broadcasted_iota(jnp.int32, (room, tokens), 0) + expert * room
+        slots = slots.astype(jnp.float32)
+        for choice in range(2):
+            final_dots[0, choice : choice + 1, :] += jnp.sum(
+                jnp.where(code_rows[choice : choice + 1, :] == slots, column, 0.0),
+                axis=0,
+                keepdims=True,
+            )
+    lax.fori_loop(1, count, back_landed, 0)
+    blocks = final_out.shape[0]
+    span = tokens // blocks
+
+    def final_copy(block):
+        return pltpu.make_async_remote_copy(
+            final_out.at[block],
+            final_in.at[block],
+            final_send.at[block],
+            final_recv.at[block],
+            device_id=peer,
+            device_id_type=MESH,
+        )
+
+    dots_final = pltpu.make_async_remote_copy(
+        final_dots.at[0],
+        final_dots.at[1],
+        final_send.at[blocks],
+        final_recv.at[blocks],
+        device_id=peer,
+        device_id_type=MESH,
+    )
+    dots_final.start()
+
+    def combine(block, unused):
+        spot = pl.ds(pl.multiple_of(block * span, span), span)
+
+        def chosen(start, amount):
+            slots = lax.broadcasted_iota(jnp.int32, (span, amount), 1) + start
+            slots = slots.astype(jnp.float32)
+            hit = (code_cols[spot, 0:1] == slots) | (code_cols[spot, 1:2] == slots)
+            return jnp.where(hit, 1.0, 0.0).astype(jnp.bfloat16)
+
+        total = dot32(chosen(own * room, room), partial[0])
+        for step in range(1, count):
+            origin = source(step)
+            total = total + dot32(chosen(origin * room + side * half, half), back[origin])
+        final_out[block] = total.astype(jnp.bfloat16)
+        final_copy(block).start()
+        return unused
+
+    lax.fori_loop(0, blocks, combine, 0)
+
+    def finish(block, unused):
+        spot = pl.ds(pl.multiple_of(block * span, span), span)
+        final_copy(block).wait_recv()
+        row_grad[spot, :] = final_out[block].astype(jnp.float32) + final_in[block].astype(
+            jnp.float32
+        )
+        return unused
+
+    lax.fori_loop(0, blocks, finish, 0)
+    dots_final.wait_recv()
+    dot_rows[...] = final_dots[0] + final_dots[1]
+
+    def drain(step, unused):
+        rows_copy(step).wait_send()
+        gates_copy(step).wait_send()
+        pass_copy(source(step)).wait_send()
+        part_copy(step).wait_send()
+        back_copy(step).wait_send()
+        dots_copy(step).wait_send()
+        return unused
+
+    lax.fori_loop(1, count, drain, 0)
+
+    def drain_final(block, unused):
+        final_copy(block).wait_send()
+        return unused
+
+    lax.fori_loop(0, blocks, drain_final, 0)
+    dots_final.wait_send()
+    for store in stores:
+        store.wait()
+    out_store.wait()
+
+
+def run_experts(count, norm, gates, code_rows, code_cols, upstream, gate_w, up_w, down_w):
+    tokens, width = norm.shape
+    room = upstream.shape[1]
+    half = room // 2
+    hidden = gate_w.shape[1]
+    blocks = 4
+    low = jnp.bfloat16
+    full = jnp.float32
+    dma = pltpu.SemaphoreType.DMA
+    return pl.pallas_call(
+        partial(expert_exchange, count),
+        out_shape=(
+            jax.ShapeDtypeStruct((tokens, width), full),
+            jax.ShapeDtypeStruct((8, tokens), full),
+            jax.ShapeDtypeStruct((count, room, width), low),
+            jax.ShapeDtypeStruct((count, room, width), low),
+            jax.ShapeDtypeStruct((count, room, hidden), low),
+            jax.ShapeDtypeStruct((count, room, hidden), low),
+            jax.ShapeDtypeStruct((count, room, hidden), low),
+            jax.ShapeDtypeStruct((count, room, width), low),
+        ),
+        in_specs=in_vmem(5) + [pl.BlockSpec(memory_space=pl.ANY)] * 3,
+        out_specs=tuple(in_vmem(2) + [pl.BlockSpec(memory_space=pl.ANY)] * 6),
+        scratch_shapes=[
+            pltpu.VMEM((width, hidden), low),
+            pltpu.VMEM((width, hidden), low),
+            pltpu.VMEM((width, hidden), low),
+            pltpu.VMEM((count, room, width), low),
+            pltpu.VMEM((count - 1, half, width), low),
+            pltpu.VMEM((count, 8, room), full),
+            pltpu.VMEM((count - 1, 8, room), full),
+            pltpu.VMEM((count, room, width), low),
+            pltpu.VMEM((count, room, hidden), low),
+            pltpu.VMEM((count, room, hidden), low),
+            pltpu.VMEM((count, room, hidden), low),
+            pltpu.VMEM((count, room, width), low),
+            pltpu.VMEM((count, room, width), low),
+            pltpu.VMEM((count, half, width), low),
+            pltpu.VMEM((count, half, width), low),
+            pltpu.VMEM((count, half, width), low),
+            pltpu.VMEM((count, 8, room), full),
+            pltpu.VMEM((count, 8, room), full),
+            pltpu.VMEM((blocks, tokens // blocks, width), low),
+            pltpu.VMEM((blocks, tokens // blocks, width), low),
+            pltpu.VMEM((2, 8, tokens), full),
+            dma((3,)),
+            dma((6,)),
+            dma((count,)),
+            dma((count,)),
+            dma((count,)),
+            dma((count,)),
+            dma((count,)),
+            dma((count,)),
+            dma((count,)),
+            dma((count,)),
+            dma((count,)),
+            dma((count,)),
+            dma((count,)),
+            dma((count,)),
+            dma((blocks + 1,)),
+            dma((blocks + 1,)),
+        ],
+        compiler_params=pltpu.CompilerParams(
+            collective_id=3, has_side_effects=True, vmem_limit_bytes=63 * 2**20
+        ),
+        name="expert_exchange",
+    )(norm, gates, code_rows, code_cols, upstream, gate_w, up_w, down_w)
+
+
+def swap_sides(member):
+    return lax.ppermute(member, "tensor", [(0, 1), (1, 0)])
+
+
+def exchange(member, axis):
+    return lax.all_to_all(member, axis, split_axis=0, concat_axis=0, tiled=True)
+
+
+def slot_codes(routes, experts, room):
+    tokens = routes.shape[0]
+    picks = routes[:, :, None] == jnp.arange(experts, dtype=jnp.int32)[None, None, :]
+    named = jnp.sum(picks, axis=1).astype(jnp.bfloat16)
+    index = jnp.arange(tokens, dtype=jnp.int32)
+    before = (index[:, None] > index[None, :]).astype(jnp.bfloat16)
+    rank = jnp.dot(before, named, preferred_element_type=jnp.float32)
+    slots = rank + room * jnp.arange(experts, dtype=jnp.float32)[None, :]
+    return picks, jnp.sum(jnp.where(picks, slots[:, None, :], 0.0), axis=2)
+
+
+def experts_apart(norm_two, upstream, gates, codes, room, count, weights):
+    tokens, width = norm_two.shape
+    codes = codes.astype(jnp.int32).reshape(-1)
+    shaped = (count, room, width)
+
+    def sent(member):
+        slots = jnp.zeros((count * room, width), jnp.bfloat16).at[codes].set(member)
+        return exchange(slots.reshape(shaped), "shard").reshape(-1, width)
+
+    slot_rows = sent(jnp.repeat(norm_two, TOP, axis=0))
+    slot_grads = sent(
+        (gates[:, :, None] * upstream[:, None, :]).reshape(-1, width).astype(jnp.bfloat16)
+    )
+    gate_mat, up_mat, down_mat = weights
+    gate_pre = dot32(slot_rows, gate_mat)
+    up_pre = dot32(slot_rows, up_mat)
+    activated, slope = gelu_parts(gate_pre)
+    inner = (activated * up_pre).astype(jnp.bfloat16)
+    expert_out = contract_cols(inner, down_mat)
+    inner_grad = dot32(slot_grads, down_mat)
+    gate_grad = (inner_grad * up_pre * slope).astype(jnp.bfloat16)
+    up_grad = (inner_grad * activated).astype(jnp.bfloat16)
+    rows_grad = contract_cols(gate_grad, gate_mat) + contract_cols(up_grad, up_mat)
+
+    def returned(member):
+        member = lax.psum(member.astype(jnp.bfloat16), "tensor").reshape(shaped)
+        member = exchange(member, "shard").reshape(-1, width)[codes]
+        return member.astype(jnp.float32).reshape(tokens, TOP, width)
+
+    per_choice = returned(expert_out)
+    mixture = jnp.sum(gates[:, :, None] * per_choice, axis=1)
+    dots = gates * jnp.sum(per_choice * upstream[:, None, :], axis=2)
+    norm_grad = jnp.sum(returned(rows_grad), axis=1)
+    return mixture, dots, norm_grad, slot_rows, slot_grads, inner, gate_grad, up_grad
+
+
+def experts_fused(norm_two, up_slots, gates, codes, code_rows, room, count, weights):
+    width = norm_two.shape[1]
+    half = room // 2
+    side = lax.axis_index("tensor")
+    norm_grad, dots, rows, grads, inner, gate_grad, up_grad, outs = run_experts(
+        count, norm_two, gates, code_rows, codes, up_slots, *weights
+    )
+    theirs = lax.dynamic_slice_in_dim(outs, (1 - side) * half, half, 1)
+    ours = lax.dynamic_slice_in_dim(outs, side * half, half, 1)
+    ours = (ours.astype(jnp.float32) + swap_sides(theirs).astype(jnp.float32)).astype(jnp.bfloat16)
+    ours = exchange(ours, "shard").reshape(-1, width)
+    slots = jnp.arange(count * half, dtype=jnp.int32)
+    slots = (slots // half * room + slots % half + side * half).astype(jnp.float32)
+    mixing = sum(
+        jnp.where(codes[:, k : k + 1] == slots[None, :], gates[:, k : k + 1], 0.0)
+        for k in range(TOP)
+    )
+    mixture = dot32(mixing.astype(jnp.bfloat16), ours).astype(jnp.bfloat16)
+    mixture = mixture.astype(jnp.float32) + swap_sides(mixture).astype(jnp.float32)
+    flat = [member.reshape(-1, member.shape[2]) for member in (rows, grads, inner)]
+    flat += [gate_grad.reshape(-1, inner.shape[2]), up_grad.reshape(-1, inner.shape[2])]
+    return (mixture, jnp.transpose(dots[:TOP]), norm_grad, *flat)
 
 
 def local(
@@ -370,23 +910,35 @@
     w_up,
     w_down,
 ):
-    width = tokens_in.shape[1]
-    rows_here = tokens_in.shape[0]
+    rows_here, width = tokens_in.shape
+    shard_size = lax.axis_size("shard")
     ctx_size = lax.axis_size("ctx")
+    side_count = lax.axis_size("tensor")
     ctx_index = lax.axis_index("ctx")
-    heads_here = w_query.shape[1] // HEAD
-    share = w_query.shape[1] // ctx_size
+    side = lax.axis_index("tensor")
+    head_cols = w_query.shape[1]
+    share = head_cols // ctx_size
+    experts = router.shape[1]
+    room = max(2, 3 * rows_here // experts)
+    fused = shard_size == 4 and experts == shard_size and side_count == 2
+
+    picks, codes = slot_codes(routes, experts, room)
+    code_rows = jnp.pad(jnp.transpose(codes), ((0, 8 - TOP), (0, 0)), constant_values=-1.0)
+    up_slots = None
+    if fused:
+        slots = jnp.arange(experts * room, dtype=jnp.int32).astype(jnp.float32)[:, None]
+        chosen = (code_rows[0:1] == slots) | (code_rows[1:2] == slots)
+        up_slots = dot32(chosen.astype(jnp.bfloat16), cotangent).astype(jnp.bfloat16)
+        up_slots = exchange(up_slots.reshape(experts, room, width), "shard")
 
     def by_owner(member):
         return member.reshape(member.shape[0], ctx_size, share)
 
     packed_rows = jnp.stack([by_owner(w_query), by_owner(w_key), by_owner(w_value)], axis=2)
-    experts = router.shape[1]
     gathered = lax.all_gather(
         jnp.concatenate(
             [
                 packed_rows.reshape(w_query.shape[0], -1),
-                w_out,
                 attn_gain[:, None],
                 ffn_gain[:, None],
                 router,
@@ -397,20 +949,25 @@
         axis=0,
         tiled=True,
     )
-    head_cols = w_query.shape[1]
     packed_w = gathered[:, : 3 * head_cols]
-    out_w = gathered[:, 3 * head_cols : 4 * head_cols]
-    gain_one = gathered[:, 4 * head_cols]
-    gain_two = gathered[:, 4 * head_cols + 1]
-    router_w = gathered[:, 4 * head_cols + 2 :]
+    gain_one = gathered[:, 3 * head_cols]
+    gain_two = gathered[:, 3 * head_cols + 1]
+    router_w = gathered[:, 3 * head_cols + 2 :]
+    out_w = lax.all_gather(w_out.astype(jnp.bfloat16), ("shard", "ctx", "tensor"), axis=0)
+    out_w = out_w.reshape(-1, side_count, w_out.shape[0], head_cols)
+    out_w = jnp.transpose(out_w, (0, 2, 1, 3)).reshape(width, side_count * head_cols)
+    expert_weights = tuple(
+        lax.all_gather(member.astype(jnp.bfloat16), "ctx", axis=1, tiled=True)[0]
+        for member in (w_gate, w_up, w_down)
+    )
+
     inputs = tokens_in.astype(jnp.float32)
     scale_one = lax.rsqrt(jnp.mean(inputs * inputs, axis=1, keepdims=True) + 1e-06)
     normal_one = inputs * scale_one
     norm_one = (normal_one * gain_one.astype(jnp.float32)).astype(jnp.bfloat16)
-    packed = jnp.dot(norm_one, packed_w, preferred_element_type=jnp.float32).astype(jnp.bfloat16)
+    packed = dot32(norm_one, packed_w).astype(jnp.bfloat16)
     packed = jnp.transpose(packed.reshape(rows_here, ctx_size, 3 * share), (1, 0, 2))
-    packed = lax.all_to_all(packed, "ctx", split_axis=0, concat_axis=0, tiled=True)
-    packed = packed.reshape(ctx_size * rows_here, 3 * share)
+    packed = exchange(packed, "ctx").reshape(ctx_size * rows_here, 3 * share)
     segments = lax.all_gather(segment_ids.reshape(-1), "ctx", axis=0, tiled=True)
     alive = live_tiles(segments, live_blocks[0])
     segment_row = segments.astype(jnp.float32)[None]
@@ -419,61 +976,28 @@
     buckets = span_buckets()
     line = jnp.dot(own_bias.T, buckets.T, precision=lax.Precision.HIGHEST)
     attended, attended_t, log_sum = run_forward(alive, packed, segment_row, line)
-    attended_low = lax.all_to_all(
-        attended.reshape(ctx_size, rows_here, share), "ctx", split_axis=0, concat_axis=0, tiled=True
-    )
-    attended_low = jnp.transpose(attended_low, (1, 0, 2)).reshape(rows_here, head_cols)
-    branch = lax.psum(contract_cols(attended_low, out_w).astype(jnp.bfloat16), "tensor").astype(
-        jnp.float32
-    )
-    hidden_one = inputs + branch
+    attended = attended.reshape(ctx_size, 1, rows_here, share)
+    attended = jnp.broadcast_to(attended, (ctx_size, side_count, rows_here, share))
+    attended = exchange(attended.reshape(-1, rows_here, share), ("ctx", "tensor"))
+    attended = attended.reshape(ctx_size, side_count, rows_here, share)
+    attended = jnp.transpose(attended, (2, 1, 0, 3))
+    attended_low = lax.dynamic_index_in_dim(attended, side, 1, False).reshape(rows_here, head_cols)
+    attended = attended.reshape(rows_here, side_count * head_cols)
+    hidden_one = inputs + contract_cols(attended, out_w)
     scale_two = lax.rsqrt(jnp.mean(hidden_one * hidden_one, axis=1, keepdims=True) + 1e-06)
     normal_two = hidden_one * scale_two
     norm_two = (normal_two * gain_two.astype(jnp.float32)).astype(jnp.bfloat16)
-    logits = jnp.dot(norm_two, router_w, preferred_element_type=jnp.float32)
-    picks = routes[:, :, None] == jnp.arange(experts, dtype=jnp.int32)[None, None, :]
+    logits = dot32(norm_two, router_w)
     chosen = jnp.sum(jnp.where(picks, logits[:, None, :], 0.0), axis=2)
     gates = jax.nn.softmax(chosen, axis=1)
     upstream = cotangent.astype(jnp.float32)
-    flat_picks = picks.reshape(rows_here * TOP, experts).astype(jnp.int32)
-    slot_of = jnp.sum(flat_picks * (jnp.cumsum(flat_picks, axis=0) - 1), axis=1)
-    expert_of = routes.reshape(-1)
-    capacity = max(2, 3 * rows_here // experts)
-    shaped = (experts, capacity, width)
-    send_rows = (
-        jnp.zeros(shaped, jnp.bfloat16)
-        .at[expert_of, slot_of]
-        .set(jnp.repeat(norm_two, TOP, axis=0))
-    )
-    grad_rows = (
-        (gates[:, :, None] * upstream[:, None, :])
-        .reshape(rows_here * TOP, width)
-        .astype(jnp.bfloat16)
-    )
-    send_grads = jnp.zeros(shaped, jnp.bfloat16).at[expert_of, slot_of].set(grad_rows)
-    got_rows, got_grads = (
-        lax.all_to_all(send_rows, "shard", split_axis=0, concat_axis=0, tiled=True),
-        lax.all_to_all(send_grads, "shard", split_axis=0, concat_axis=0, tiled=True),
-    )
-    expert_gate, expert_up, expert_down = (
-        lax.all_gather(w_gate.astype(jnp.bfloat16), "ctx", axis=1, tiled=True),
-        lax.all_gather(w_up.astype(jnp.bfloat16), "ctx", axis=1, tiled=True),
-        lax.all_gather(w_down.astype(jnp.bfloat16), "ctx", axis=1, tiled=True),
-    )
-    gate_mat = expert_gate[0]
-    up_mat = expert_up[0]
-    down_mat = expert_down[0]
-    slot_rows = got_rows.reshape(-1, width)
-    slot_grads = got_grads.reshape(-1, width)
-    gate_pre = jnp.dot(slot_rows, gate_mat, preferred_element_type=jnp.float32)
-    up_pre = jnp.dot(slot_rows, up_mat, preferred_element_type=jnp.float32)
-    activated, gelu_back = jax.vjp(partial(jax.nn.gelu, approximate=True), gate_pre)
-    inner = (activated * up_pre).astype(jnp.bfloat16)
-    expert_out = contract_cols(inner, down_mat)
-    inner_grad = jnp.dot(slot_grads, down_mat, preferred_element_type=jnp.float32)
-    gate_grad = gelu_back(inner_grad * up_pre)[0].astype(jnp.bfloat16)
-    up_grad = (inner_grad * activated).astype(jnp.bfloat16)
-    rows_grad = contract_cols(gate_grad, gate_mat) + contract_cols(up_grad, up_mat)
+    if fused:
+        results = experts_fused(
+            norm_two, up_slots, gates, codes, code_rows, room, experts, expert_weights
+        )
+    else:
+        results = experts_apart(norm_two, upstream, gates, codes, room, experts, expert_weights)
+    mixture, gate_dots, norm_grad, slot_rows, slot_grads, inner, gate_grad, up_grad = results
     weight_grads = lax.psum_scatter(
         jnp.stack(
             [
@@ -487,32 +1011,8 @@
         scatter_dimension=0,
         tiled=True,
     ).astype(jnp.float32)
-    expert_out, rows_grad = (
-        lax.psum(expert_out.astype(jnp.bfloat16), "tensor").astype(jnp.float32),
-        lax.psum(rows_grad.astype(jnp.bfloat16), "tensor").astype(jnp.float32),
-    )
-    back_out, back_grad = (
-        lax.all_to_all(
-            expert_out.reshape(shaped).astype(jnp.bfloat16),
-            "shard",
-            split_axis=0,
-            concat_axis=0,
-            tiled=True,
-        ).astype(jnp.float32),
-        lax.all_to_all(
-            rows_grad.reshape(shaped).astype(jnp.bfloat16),
-            "shard",
-            split_axis=0,
-            concat_axis=0,
-            tiled=True,
-        ).astype(jnp.float32),
-    )
-    per_choice = back_out[expert_of, slot_of].reshape(rows_here, TOP, width)
-    mixture = jnp.sum(gates[:, :, None] * per_choice, axis=1)
-    gate_dots = jnp.sum(per_choice * upstream[:, None, :], axis=2)
-    norm_grad = jnp.sum(back_grad[expert_of, slot_of].reshape(rows_here, TOP, width), axis=1)
     mixed = (hidden_one + mixture).astype(jnp.bfloat16)
-    gate_shift = gates * (gate_dots - jnp.sum(gates * gate_dots, axis=1, keepdims=True))
+    gate_shift = gate_dots - gates * jnp.sum(gate_dots, axis=1, keepdims=True)
     logit_grad = jnp.sum(jnp.where(picks, gate_shift[:, :, None], 0.0), axis=1)
     router_f = router_w.astype(jnp.float32)
     norm_grad = norm_grad + jnp.dot(logit_grad, router_f.T, precision=lax.Precision.HIGHEST)
@@ -521,13 +1021,12 @@
         spread_two - normal_two * jnp.mean(spread_two * normal_two, axis=1, keepdims=True)
     )
     branch_grad = hidden_grad.astype(jnp.bfloat16)
-    attended_grad = jnp.dot(branch_grad, out_w, preferred_element_type=jnp.float32).astype(
-        jnp.bfloat16
-    )
-    grad_heads = jnp.transpose(attended_grad.reshape(rows_here, ctx_size, share), (1, 0, 2))
-    grad_heads = lax.all_to_all(grad_heads, "ctx", split_axis=0, concat_axis=0, tiled=True)
+    own_out_w = lax.dynamic_slice_in_dim(out_w, side * head_cols, head_cols, 1)
+    grad_heads = dot32(branch_grad, own_out_w).astype(jnp.bfloat16)
+    grad_heads = jnp.transpose(grad_heads.reshape(rows_here, ctx_size, share), (1, 0, 2))
+    grad_heads = exchange(grad_heads, "ctx").reshape(-1, share)
     packed_grad, bias_line = run_backward(
-        alive, packed, segment_row, line, grad_heads.reshape(-1, share), attended_t, log_sum
+        alive, packed, segment_row, line, grad_heads, attended_t, log_sum
     )
     own_grad = jnp.dot(buckets.T, bias_line[:pair_heads].T, precision=lax.Precision.HIGHEST)
     far = jnp.sum(bias_line[pair_heads : 3 * pair_heads], axis=1)
@@ -536,27 +1035,21 @@
     bias_acc = lax.dynamic_update_slice_in_dim(
         jnp.zeros(rel_bias.shape, jnp.float32), own_grad, ctx_index * pair_heads, 1
     )
-    packed_grad = lax.all_to_all(
-        packed_grad.reshape(ctx_size, rows_here, 3 * share),
-        "ctx",
-        split_axis=0,
-        concat_axis=0,
-        tiled=True,
-    )
+    packed_grad = exchange(packed_grad.reshape(ctx_size, rows_here, 3 * share), "ctx")
     packed_grad = jnp.transpose(packed_grad, (1, 0, 2)).reshape(rows_here, 3 * head_cols)
-    norm_one_grad = lax.psum(
-        contract_cols(packed_grad, packed_w).astype(jnp.bfloat16), "tensor"
-    ).astype(jnp.float32)
+    norm_one_grad = contract_cols(packed_grad, packed_w).astype(jnp.bfloat16)
+    norm_one_grad = norm_one_grad.astype(jnp.float32) + swap_sides(norm_one_grad).astype(
+        jnp.float32
+    )
     spread_one = norm_one_grad * gain_one.astype(jnp.float32)
     input_grad = hidden_grad + scale_one * (
         spread_one - normal_one * jnp.mean(spread_one * normal_one, axis=1, keepdims=True)
     )
-    gain_one_terms = norm_one_grad * normal_one
-    gain_two_terms = norm_grad * normal_two
-    cols_two = norm_two.astype(jnp.float32)
-    first_gain = jnp.sum(gain_one_terms, axis=0)[:, None]
-    second_gain = jnp.sum(gain_two_terms, axis=0)[:, None]
-    router_part = jnp.dot(cols_two.T, logit_grad, precision=lax.Precision.HIGHEST)
+    first_gain = jnp.sum(norm_one_grad * normal_one, axis=0)[:, None]
+    second_gain = jnp.sum(norm_grad * normal_two, axis=0)[:, None]
+    router_part = jnp.dot(
+        norm_two.astype(jnp.float32).T, logit_grad, precision=lax.Precision.HIGHEST
+    )
     reduced = lax.psum_scatter(
         jnp.concatenate(
             [

time: 1030 us -> 706 us (0.69)
  waiting for transfers between devices: 493 us -> 309 us
  Pallas kernels: 48.7 us -> 162 us
  blocking collectives: 141 us -> 50 us
  matrix products: 119 us -> 54.6 us
  local copies, waits for them, and re-layouts: 112 us -> 49.9 us
  other arithmetic: 74.1 us -> 31.4 us
    psum x3 -> x0, waiting for transfers between devices: 200 us -> none  [the longest x1 152 us: local(): lax.psum(expert_out.astype(jnp.bfloat16), 'tensor').astype(jnp.float32)]
    pallas_call x0 -> x1, Pallas kernels: none -> 115 us  [run_experts(): pl.pallas_call(partial(expert_exchange, count), out_shape=(jax.ShapeDtype...]
    all_to_all x3 -> x1, blocking collectives: 100 us -> 13.8 us  [exchange(): return lax.all_to_all(member, axis, split_axis=0, concat_axis=0, tiled=True)]
    ppermute x0 -> x3, waiting for transfers between devices: none -> 58.1 us  [swap_sides(): return lax.ppermute(member, 'tensor', [(0, 1), (1, 0)])]
    gather x2 -> x0, local copies, waits for them, and re-layouts: 40.8 us -> none  [the longest x1 20.4 us: local(): per_choice = back_out[expert_of, slot_of].reshape(rows_here, TOP, width)]
    all_gather x3 -> x4, waiting for transfers between devices: 8.38 us -> 46.9 us  [the longest x3 46.7 us: local(): lax.all_gather(member.astype(jnp.bfloat16), 'ctx', axis=1, tiled=True)[0]]
    all_to_all x5, waiting for transfers between devices: 134 us -> 96.3 us  [exchange(): return lax.all_to_all(member, axis, split_axis=0, concat_axis=0, tiled=True)]
    reduce_scatter x1, waiting for transfers between devices: 103 us -> 70.2 us  [local(): lax.psum_scatter(jnp.concatenate([contract_rows(norm_one, packed_grad), c...]
  transfers between devices with their start and end apart: 14 -> 15, of which waited for: 11 -> 13; matrix products, arithmetic and copies ran while one was open for 17% -> 13% of each run, Pallas kernels for 0% -> 7%
where the time goes in v2:
time: 706 us; the launch traced here: 703 us
  waiting for transfers between devices  309 us (44%)
  Pallas kernels  162 us (23%)
  matrix products  54.6 us (8%)
  blocking collectives  50 us (7%)
  local copies, waits for them, and re-layouts  49.9 us (7%)
  other arithmetic  31.4 us (4%)
  starting transfers between devices  31.3 us (4%)
  between operations  15.1 us (2%)
    pallas_call x1, Pallas kernels, run_experts(): pl.pallas_call(partial(expert_exchange, count), out_shape=(jax.ShapeDtype...  115 us
    all_to_all x5, waiting for transfers between devices, exchange(): return lax.all_to_all(member, axis, split_axis=0, concat_axis=0, tiled=True)  96.3 us
    reduce_scatter x1, waiting for transfers between devices, local(): lax.psum_scatter(jnp.concatenate([contract_rows(norm_one, packed_grad), c...  70.2 us
    ppermute x3, waiting for transfers between devices, swap_sides(): return lax.ppermute(member, 'tensor', [(0, 1), (1, 0)])  58.1 us
    all_gather x3, waiting for transfers between devices, local(): lax.all_gather(member.astype(jnp.bfloat16), 'ctx', axis=1, tiled=True)[0]  46.7 us
    all_gather x1, waiting for transfers between devices, local(): lax.all_gather(jnp.concatenate([packed_rows.reshape(w_query.shape[0], -1)...  37.5 us
    psum x1, blocking collectives, local(): grad_bias = lax.psum(bias_acc, ('shard', 'ctx'))  30.1 us
    all_to_all x5, starting transfers between devices, exchange(): return lax.all_to_all(member, axis, split_axis=0, concat_axis=0, tiled=True)  28 us
  transfers between devices with their start and end apart: 15, of which 13 were waited for; matrix products, arithmetic and copies ran while one was open for 13% of the time, Pallas kernels for 7%

profile of v2, /device:TPU:0, one launch (start us, length us, event | category | flops | bytes accessed | tf_op | source)
XLA Modules:
  0.0 703.2 jit_solution(5503503955773071891)
XLA Ops:
  18.6 6.1 all-gather
  25.9 37.5 %all-gather.8.cloned.1.call-done = bf16[1024,1542]{1,0:T(8,128)(2,1)} async-done(((bf16[64,1542]{1,0:T(8,128)(2,1)}), bf16[1024,1542]{1,0:T(8,128)(2,1)}) %all-gather.8.cloned.1.call-update) | async-done | bytes 3158032 | tf_op jit(solution)/shard_map/all_gather | solution.py:938
  75.1 20.1 %all-to-all-done = bf16[4,512,384]{2,1,0:T(8,128)(2,1)S(1)} async-done(((bf16[4,512,384]{2,1,0:T(8,128)(2,1)}), bf16[4,512,384]{2,1,0:T(8,128)(2,1)S(1)}, u32[]{:S(2)}, u32[]{:S(2)}) %all-to-all-start) | async-done | bytes 1572896 | tf_op jit(solution)/shard_map/all_to_all | solution.py:821
  95.1 21.3 %attention_forward.1 = (bf16[2048,128]{1,0:T(8,128)(2,1)S(1)}, f32[128,2048]{1,0:T(8,128)S(1)}, f32[8,2048]{1,0:T(8,128)S(1)}) custom-call(s32[64]{0:T(128)S(1)} %and_convert_fusion.alive, bf16[2048,384]{1,0:T(8,128)(2,1)S(1)} %bitcast.108, f32[1,2048]{1,0:T(1,128)S(1)} %get-tuple-element.150.segment, f32[2,1024]{1,0:T(2,128)S(1)} %fusion.39.line), custom_call_target="tpu_custom_call" | custom-call | tf_op jit(solution)/shard_map/attention_forward/pallas_call | solution.py:286
  128.5 11.5 %all-to-all-done.1 = bf16[8,512,128]{2,1,0:T(8,128)(2,1)S(1)} async-done(((bf16[8,512,128]{2,1,0:T(8,128)(2,1)}), bf16[8,512,128]{2,1,0:T(8,128)(2,1)S(1)}, u32[]{:S(2)}, u32[]{:S(2)}) %all-to-all-start.1) | async-done | bytes 1048608 | tf_op jit(solution)/shard_map/all_to_all | solution.py:821
  151.0 12.8 %all-to-all-start.2 = ((bf16[4,384,1024]{2,1,0:T(8,128)(2,1)}), bf16[4,384,1024]{2,1,0:T(8,128)(2,1)}, u32[]{:S(2)}, u32[]{:S(2)}) async-start(bf16[4,384,1024]{2,1,0:T(8,128)(2,1)} %bitcast.19), calls=%async_computation.2 | async-start | bytes 6291456 | tf_op jit(solution)/shard_map/all_to_all | solution.py:821
  167.8 18.2 %all-gather.12.cloned.1.call-done = bf16[1,1024,1408]{2,1,0:T(8,128)(2,1)} async-done(((bf16[1,256,1408]{2,1,0:T(8,128)(2,1)}), bf16[1,1024,1408]{2,1,0:T(8,128)(2,1)}) %all-gather.12.cloned.1.call-update) | async-done | bytes 2883600 | tf_op jit(solution)/shard_map/all_gather | solution.py:960
  186.0 28.5 %all-gather.14.cloned.1.call-done = bf16[1,1024,1408]{2,1,0:T(8,128)(2,1)} async-done(((bf16[1,256,1408]{2,1,0:T(8,128)(2,1)}), bf16[1,1024,1408]{2,1,0:T(8,128)(2,1)}) %all-gather.14.cloned.1.call-update) | async-done | bytes 2883600 | tf_op jit(solution)/shard_map/all_gather | solution.py:960
  214.4 19.0 %all-to-all-done.2.upstream = bf16[4,384,1024]{2,1,0:T(8,128)(2,1)} async-done(((bf16[4,384,1024]{2,1,0:T(8,128)(2,1)}), bf16[4,384,1024]{2,1,0:T(8,128)(2,1)}, u32[]{:S(2)}, u32[]{:S(2)}) %all-to-all-start.2) | async-done | bytes 3145760 | tf_op jit(solution)/shard_map/all_to_all | solution.py:821
  233.5 114.7 %expert_exchange.1 = (f32[512,1024]{1,0:T(8,128)}, f32[8,512]{1,0:T(8,128)}, bf16[4,384,1024]{2,1,0:T(8,128)(2,1)}, bf16[4,384,1024]{2,1,0:T(8,128)(2,1)}, bf16[...) custom-call(bf16[512,1024]{1,0:T(8,128)(2,1)} %copy-done.10, ...), custom_call_target="tpu_custom_call" | custom-call | tf_op jit(solution)/shard_map/expert_exchange/pallas_call | solution.py:756
  348.1 8.3 %fusion = bf16[1024,1,1408]{2,0,1:T(8,128)(2,1)S(1)} fusion(bf16[4,384,1024]{2,1,0:T(8,128)(2,1)} %get-tuple-element.58, bf16[4,384,1408]{2,1,0:T(8,128)(2,1)} %get-tuple-element.59), kind=kOutput, calls=%fused_computation.5 | convolution fusion | flops 4430626816 | bytes 10354688 | tf_op jit(solution)/shard_map/dot_general | solution.py:30
  356.5 5.5 fusion.1
  362.1 5.5 fusion.2
  375.3 28.2 %collective-permute-done = bf16[4,192,1024]{2,1,0:T(8,128)(2,1)} collective-permute-done((bf16[4,192,1024]{2,1,0:T(8,128)(2,1)}, bf16[4,192,1024]{2,1,0:T(8,128)(2,1)}, u32[]{:S(2)}, u32[]{:S(2)}) %collective-permute-start) | collective-permute-done | bytes 1572896 | tf_op jit(solution)/shard_map/ppermute | solution.py:817
  411.2 28.1 %all-to-all-done.3 = bf16[4,192,1024]{2,1,0:T(8,128)(2,1)S(1)} async-done(((bf16[4,192,1024]{2,1,0:T(8,128)(2,1)}), bf16[4,192,1024]{2,1,0:T(8,128)(2,1)S(1)}, u32[]{:S(2)}, u32[]{:S(2)}) %all-to-all-start.3) | async-done | bytes 1572896 | tf_op jit(solution)/shard_map/all_to_all | solution.py:821
  448.3 15.8 %collective-permute-done.1 = bf16[512,1024]{1,0:T(8,128)(2,1)} collective-permute-done((bf16[512,1024]{1,0:T(8,128)(2,1)}, bf16[512,1024]{1,0:T(8,128)(2,1)}, u32[]{:S(2)}, u32[]{:S(2)}) %collective-permute-start.1) | collective-permute-done | bytes 1048608 | tf_op jit(solution)/shard_map/ppermute | solution.py:817
  470.1 13.8 %all_to_all.30 = bf16[4,512,128]{2,1,0:T(8,128)(2,1)S(1)} all-to-all(bf16[4,512,128]{2,1,0:T(8,128)(2,1)S(1)} %bitcast.125), channel_id=1, replica_groups=mesh['shard'=4,'ctx'=4,'tensor'=2] {'ctx'}, dimensions={0} | all-to-all | bytes 1048576 | tf_op jit(solution)/shard_map/all_to_all | solution.py:821
  485.1 25.8 %attention_backward.1 = (bf16[2048,384]{1,0:T(8,128)(2,1)S(1)}, f32[8,1024]{1,0:T(8,128)S(1)}) custom-call(s32[64]{0:T(128)S(1)} %and_convert_fusion.alive, bf16[2048,384]{1,0:T(8,128)(2,1)S(1)} %bitcast.109, f32[1,2048]{1,0:T(1,128)S(1)} %get-tuple-element.150.segment, f32[2,1024]{1,0:T(2,128)S(1)} %fusion.39.line, bf16[2048,128]{1,0:T(8,128)(2,1)S(1)} %bitcast.110, ...), custom_call_target="tpu_custom_call" | custom-call | tf_op jit(solution)/shard_map/attention_backward/pallas_call | solution.py:311
  518.7 17.6 %all-to-all-done.5 = bf16[4,512,384]{1,2,0:T(8,128)(2,1)S(1)} async-done(((bf16[4,512,384]{1,2,0:T(8,128)(2,1)}), bf16[4,512,384]{1,2,0:T(8,128)(2,1)S(1)}, u32[]{:S(2)}, u32[]{:S(2)}) %all-to-all-start.5) | async-done | bytes 1572896 | tf_op jit(solution)/shard_map/all_to_all | solution.py:821
  547.8 4.7 fusion.40
  552.5 14.2 %collective-permute-done.2 = bf16[512,1024]{1,0:T(8,128)(2,1)S(1)} collective-permute-done((bf16[512,1024]{1,0:T(8,128)(2,1)S(1)}, bf16[512,1024]{1,0:T(8,128)(2,1)S(1)}, u32[]{:S(2)}, u32[]{:S(2)}) %collective-permute-start.2) | collective-permute-done | bytes 1048608 | tf_op jit(solution)/shard_map/ppermute | solution.py:817
  568.7 10.2 %concatenate.12 = f32[1024,2054]{1,0:T(8,128)} concatenate(f32[1024,1536]{1,0:T(8,128)} %fusion.40, f32[1024,512]{1,0:T(8,128)} %fusion.35, f32[1024,1]{1,0:T(8,128)} %copy.163, f32[1024,1]{1,0:T(8,128)} %copy.164, f32[1024,4]{1,0:T(8,128)} %fusion.79), dimensions={1} | concatenate | bytes 16826368 | tf_op jit(solution)/shard_map/concatenate | solution.py:1054
  580.0 30.1 %psum.7 = f32[32,8]{0,1:T(8,128)} all-reduce(f32[32,8]{0,1:T(8,128)S(1)} %constant_dynamic-update-slice_fusion), channel_id=1, replica_groups=mesh['shard'=4,'ctx'=4,'tensor'=2] {'shard','ctx'}, use_global_device_ids=true, to_apply=%region_15.16 | all-reduce | flops 256 | bytes 2048 | tf_op jit(solution)/shard_map/psum | solution.py:1068
  617.4 70.2 %reduce-scatter.3.cloned.1.call-done = f32[64,2054]{1,0:T(8,128)} async-done(((f32[1024,2054]{1,0:T(8,128)}), f32[64,2054]{1,0:T(8,128)}) %reduce-scatter.3.cloned.1.call-update) | async-done | bytes 525840 | tf_op jit(solution)/shard_map/reduce_scatter | solution.py:1053
  (218 shorter events, 120.5 us)
Async XLA Ops:
  7.2 67.4 %copy-start = (f32[32,8]{0,1:T(8,128)S(1)}, f32[32,8]{0,1:T(8,128)}, u32[]{:S(2)}) copy-start(f32[32,8]{0,1:T(8,128)} %param.29) | copy-start | bytes 3076
  7.2 56.2 %all-gather.8.cloned.1.call-start = ((), (), s32[]{:S(2)}) async-start(), calls=%async_computation.8 | async-start | bytes 3620864 | tf_op jit(solution)/shard_map/all_gather | solution.py:938
  14.1 108.8 %all-gather.16.cloned.1.call-start = ((), (), s32[]{:S(2)}) async-start(), calls=%async_computation.14 | async-start | bytes 2162688 | tf_op jit(solution)/shard_map/all_gather | solution.py:956
  14.8 153.0 %all-gather.10.cloned.1.call-start = ((), (), s32[]{:S(2)}) async-start(), calls=%async_computation.9 | async-start | bytes 3604480 | tf_op jit(solution)/shard_map/all_gather | solution.py:960
  15.8 170.1 %all-gather.12.cloned.1.call-start = ((), (), s32[]{:S(2)}) async-start(), calls=%async_computation.10 | async-start | bytes 3604480 | tf_op jit(solution)/shard_map/all_gather | solution.py:960
  69.8 25.3 %all-to-all-start = ((bf16[4,512,384]{2,1,0:T(8,128)(2,1)}), bf16[4,512,384]{2,1,0:T(8,128)(2,1)S(1)}, u32[]{:S(2)}, u32[]{:S(2)}) async-start(bf16[4,512,384]{2,1,0:T(8,128)(2,1)} %bitcast.116), calls=%async_computation | async-start | bytes 3145728 | tf_op jit(solution)/shard_map/all_to_all | solution.py:821
  95.1 23.4 %copy-start.2 = (bf16[4,512,384]{2,1,0:T(8,128)(2,1)}, bf16[4,512,384]{2,1,0:T(8,128)(2,1)S(1)}, u32[]{:S(2)}) copy-start(bf16[4,512,384]{2,1,0:T(8,128)(2,1)S(1)} %all-to-all-done) | copy-start | bytes 4718596
  118.5 21.5 %all-to-all-start.1 = ((bf16[8,512,128]{2,1,0:T(8,128)(2,1)}), bf16[8,512,128]{2,1,0:T(8,128)(2,1)S(1)}, u32[]{:S(2)}, u32[]{:S(2)}) async-start(bf16[8,512,128]{2,1,0:T(8,128)(2,1)} %bitcast.119), calls=%async_computation.1 | async-start | bytes 2097152 | tf_op jit(solution)/shard_map/all_to_all | solution.py:821
  128.5 12.8 %copy-start.13 = (bf16[512,1024]{1,0:T(8,128)(2,1)S(1)}, bf16[512,1024]{1,0:T(8,128)(2,1)}, u32[]{:S(2)}) copy-start(bf16[512,1024]{1,0:T(8,128)(2,1)} %param.20) | copy-start | bytes 3145732
  151.0 12.8 %copy-start.27 = (f32[1,256,1408]{2,1,0:T(8,128)S(1)}, f32[1,256,1408]{2,1,0:T(8,128)}, u32[]{:S(2)}) copy-start(f32[1,256,1408]{2,1,0:T(8,128)} %param.35) | copy-start | bytes 4325380
  151.0 82.5 %all-to-all-start.2 = ((bf16[4,384,1024]{2,1,0:T(8,128)(2,1)}), bf16[4,384,1024]{2,1,0:T(8,128)(2,1)}, u32[]{:S(2)}, u32[]{:S(2)}) async-start(bf16[4,384,1024]{2,1,0:T(8,128)(2,1)} %bitcast.19), calls=%async_computation.2 | async-start | bytes 6291456 | tf_op jit(solution)/shard_map/all_to_all | solution.py:821
  163.7 50.7 %all-gather.14.cloned.1.call-start = ((), (), s32[]{:S(2)}) async-start(), calls=%async_computation.11 | async-start | bytes 3604480 | tf_op jit(solution)/shard_map/all_gather | solution.py:960
  164.7 448.7 %reduce-scatter.5.cloned.1.call-start = ((), (), s32[]{:S(2)}) async-start(), calls=%async_computation.13 | async-start | bytes 10813440 | tf_op jit(solution)/shard_map/reduce_scatter | solution.py:1001
  348.1 13.9 %slice-start = ((s8[4325376]{0:T(1024)(128)(4,1)}), s8[4194304]{0:T(1024)(128)(4,1)S(1)}, s32[]{:S(2)}) async-start(s8[4325376]{0:T(1024)(128)(4,1)} %bitcast.146), calls=%async_computation.15 | async-start | bytes 8388608
  374.8 28.6 %collective-permute-start = (bf16[4,192,1024]{2,1,0:T(8,128)(2,1)}, bf16[4,192,1024]{2,1,0:T(8,128)(2,1)}, u32[]{:S(2)}, u32[]{:S(2)}) collective-permute-start(bf16[4,192,1024]{2,1,0:T(8,128)(2,1)} %constant_dynamic-slice_fusion), channel_id=1, source_target_pairs={{0,1},{1,0},{2,3},{3,2},{4,5},{5,4},{6,7},{7,6},{8,9},{9,8},{10,11... | collective-permute-start | bytes 4718600 | tf_op jit(solution)/shard_map/ppermute | solution.py:817
  406.8 32.6 %all-to-all-start.3 = ((bf16[4,192,1024]{2,1,0:T(8,128)(2,1)}), bf16[4,192,1024]{2,1,0:T(8,128)(2,1)S(1)}, u32[]{:S(2)}, u32[]{:S(2)}) async-start(bf16[4,192,1024]{2,1,0:T(8,128)(2,1)} %add_convert_fusion), calls=%async_computation.3 | async-start | bytes 3145728 | tf_op jit(solution)/shard_map/all_to_all | solution.py:821
  444.3 19.9 %collective-permute-start.1 = (bf16[512,1024]{1,0:T(8,128)(2,1)}, bf16[512,1024]{1,0:T(8,128)(2,1)}, u32[]{:S(2)}, u32[]{:S(2)}) collective-permute-start(bf16[512,1024]{1,0:T(8,128)(2,1)} %convolution_convert_fusion.2), channel_id=1, source_target_pairs={{0,1},{1,0},{2,3},{3,2},{4,5},{5,4},{6,7},{7,6},{8,9},{9,8},{10,11... | collective-permute-start | bytes 3145736 | tf_op jit(solution)/shard_map/ppermute | solution.py:817
  444.8 19.4 %copy-start.29 = (bf16[512,1024]{1,0:T(8,128)(2,1)S(1)}, bf16[512,1024]{1,0:T(8,128)(2,1)}, u32[]{:S(2)}) copy-start(bf16[512,1024]{1,0:T(8,128)(2,1)} %param.21) | copy-start | bytes 3145732
  469.0 14.8 %copy-start.3 = (bf16[4,512,384]{2,1,0:T(8,128)(2,1)S(1)}, bf16[4,512,384]{2,1,0:T(8,128)(2,1)}, u32[]{:S(2)}) copy-start(bf16[4,512,384]{2,1,0:T(8,128)(2,1)} %copy-done.2) | copy-start | bytes 4718596
  512.6 23.7 %all-to-all-start.5 = ((bf16[4,512,384]{1,2,0:T(8,128)(2,1)}), bf16[4,512,384]{1,2,0:T(8,128)(2,1)S(1)}, u32[]{:S(2)}, u32[]{:S(2)}) async-start(bf16[4,512,384]{1,2,0:T(8,128)(2,1)} %copy.160), calls=%async_computation.5 | async-start | bytes 3145728 | tf_op jit(solution)/shard_map/all_to_all | solution.py:821
  516.3 171.4 %reduce-scatter.3.cloned.1.call-start = ((), (), s32[]{:S(2)}) async-start(), calls=%async_computation.12 | async-start | bytes 9469952 | tf_op jit(solution)/shard_map/reduce_scatter | solution.py:1053
  541.9 24.8 %copy-start.19 = (bf16[512,1024]{1,0:T(8,128)(2,1)}, bf16[512,1024]{1,0:T(8,128)(2,1)S(1)}, u32[]{:S(2)}) copy-start(bf16[512,1024]{1,0:T(8,128)(2,1)S(1)} %fusion.25) | copy-start | bytes 3145732
  541.9 24.8 %collective-permute-start.2 = (bf16[512,1024]{1,0:T(8,128)(2,1)S(1)}, bf16[512,1024]{1,0:T(8,128)(2,1)S(1)}, u32[]{:S(2)}, u32[]{:S(2)}) collective-permute-start(bf16[512,1024]{1,0:T(8,128)(2,1)S(1)} %fusion.25), channel_id=1, source_target_pairs={{0,1},{1,0},{2,3},{3,2},{4,5},{5,4},{6,7},{7,6},{8,9},{9,8},{10,11... | collective-permute-start | bytes 3145736 | tf_op jit(solution)/shard_map/ppermute | solution.py:817
  615.3 80.8 %copy-start.1 = (f32[32,8]{0,1:T(8,128)S(1)}, f32[32,8]{0,1:T(8,128)}, u32[]{:S(2)}) copy-start(f32[32,8]{0,1:T(8,128)} %param.29) | copy-start | bytes 3076
  (31 other events, 126.0 us)
Sparse Core Ops, SparseCore 0:
  14.2 49.1 all-gather.7
  67.1 55.7 all-gather.15
  125.0 28.7 all-gather.9
  155.8 30.1 all-gather.11
  187.4 27.0 all-gather.13
  371.7 72.4 reduce-scatter.4
  579.0 108.6 reduce-scatter.2

commit v3 on v2

--- a/solution.py
+++ b/solution.py
@@ -277,6 +277,10 @@
         bias_grad[4 + head : 5 + head, :TILE] = jnp.sum(bias_acc[head, 4], axis=0, keepdims=True)
 
 
+def estimate(micros):
+    return pl.CostEstimate(flops=int(micros * 1e9), bytes_accessed=0, transcendentals=0)
+
+
 def in_vmem(count):
     return [pl.BlockSpec(memory_space=pltpu.VMEM)] * count
 
@@ -301,6 +305,7 @@
             pltpu.VMEM((2, HEAD + 16, TILE), jnp.float32),
         ],
         compiler_params=pltpu.CompilerParams(vmem_limit_bytes=40 * 2**20),
+        cost_estimate=estimate(20),
         name="attention_forward",
     )(alive, packed, segment, line)
 
@@ -331,6 +336,7 @@
             pltpu.VMEM((TILE, 128), jnp.float32),
         ],
         compiler_params=pltpu.CompilerParams(vmem_limit_bytes=48 * 2**20),
+        cost_estimate=estimate(26),
         name="attention_backward",
     )(alive, packed, segment, line, grads, out_t, log_sum)
 
@@ -809,16 +815,537 @@
         compiler_params=pltpu.CompilerParams(
             collective_id=3, has_side_effects=True, vmem_limit_bytes=63 * 2**20
         ),
+        cost_estimate=estimate(110),
         name="expert_exchange",
     )(norm, gates, code_rows, code_cols, upstream, gate_w, up_w, down_w)
 
 
+LANES = 128
+
+
+def places():
+    own, ctx, side = lax.axis_index("shard"), lax.axis_index("ctx"), lax.axis_index("tensor")
+    return own, ctx, side, ctx // 2, ctx % 2
+
+
+def nearest(own, count, step):
+    flip = own // (count // 2)
+    place = flip * (count - 1 - own) + (1 - flip) * own
+    turn = step - 1
+    turn = turn + (turn - place + count) // count
+    other = flip * (count - 1 - turn) + (1 - flip) * turn
+    first = 1 - (step + count - 1) // count
+    return first * own + (1 - first) * other
+
+
+def across(chip, core, step):
+    return (chip + 1 - step // 2) % 2 * 2 + (core + step + step // 2) % 2
+
+
+def remote(source, target, send, recv, device):
+    return pltpu.make_async_remote_copy(
+        source, target, send, recv, device_id=device, device_id_type=MESH
+    )
+
+
+def greet(devices):
+    barrier = pltpu.get_barrier_semaphore()
+    for device in devices:
+        pl.semaphore_signal(barrier, 1, device_id=device, device_id_type=MESH)
+    pl.semaphore_wait(barrier, len(devices))
+
+
+def gather_project(
+    count,
+    weight,
+    tokens,
+    segment,
+    full,
+    packed,
+    norm,
+    segments,
+    outgoing,
+    line_send,
+    line_recv,
+    chip_send,
+    chip_recv,
+    core_send,
+    core_recv,
+    packed_send,
+    packed_recv,
+    segment_send,
+    segment_recv,
+):
+    own, ctx, side, chip, core = places()
+    rows = weight.shape[0]
+    share = packed.shape[2]
+    ctx_size = packed.shape[0]
+    chip_peer = (own, (1 - chip) * 2 + core, side)
+    core_peer = (own, chip * 2 + 1 - core, side)
+    greet(
+        [(nearest(own, count, step), ctx, side) for step in range(1, count)]
+        + [(own, across(chip, core, step), side) for step in range(3)]
+    )
+
+    def block(shard, place):
+        return pl.ds(pl.multiple_of((shard * ctx_size + place) * rows, rows), rows)
+
+    def to_line(step):
+        device = (nearest(own, count, step), ctx, side)
+        return remote(
+            weight, full.at[block(own, ctx)], line_send.at[step], line_recv.at[own], device
+        )
+
+    def to_chip(shard, source):
+        target = full.at[block(shard, ctx)]
+        return remote(source, target, chip_send.at[shard], chip_recv.at[shard], chip_peer)
+
+    def to_core(shard, place, source):
+        index = shard * 2 + place // 2
+        target = full.at[block(shard, place)]
+        return remote(source, target, core_send.at[index], core_recv.at[index], core_peer)
+
+    def to_segment(step):
+        device = (own, across(chip, core, step), side)
+        return remote(segment, segments.at[ctx], segment_send.at[step], segment_recv.at[ctx], device)
+
+    for step in range(1, count):
+        to_line(step).start()
+    to_chip(own, weight).start()
+    to_core(own, ctx, weight).start()
+    for step in range(3):
+        to_segment(step).start()
+    full[block(own, ctx), :] = weight[...]
+    segments[ctx] = segment[...]
+
+    other_place = (1 - chip) * 2 + core
+
+    def pass_line(step):
+        shard = nearest(own, count, step)
+        source = full.at[block(shard, ctx)]
+        remote(source, source, line_send.at[0], line_recv.at[shard], core_peer).wait_recv()
+        to_chip(shard, source).start()
+        to_core(shard, ctx, source).start()
+
+    def pass_chip(step):
+        shard = nearest(own, count, step)
+        source = full.at[block(shard, other_place)]
+        remote(source, source, chip_send.at[0], chip_recv.at[shard], core_peer).wait_recv()
+        to_core(shard, other_place, source).start()
+
+    pass_chip(0)
+    for step in range(1, count):
+        pass_line(step)
+        pass_chip(step)
+
+    values = tokens[...].astype(jnp.float32)
+    scale = lax.rsqrt(jnp.mean(values * values, axis=1, keepdims=True) + 1e-06)
+    for shard in range(count):
+        for place in range(2):
+            spot = full.at[block(shard, place * 2 + 1 - core)]
+            index = shard * 2 + place
+            remote(spot, spot, core_send.at[0], core_recv.at[index], core_peer).wait_recv()
+    gain = jnp.transpose(full[:, ctx_size * share :].astype(jnp.float32))[0:1, :]
+    norm[...] = (values * scale * gain).astype(jnp.bfloat16)
+
+    def project(place):
+        spot = pl.ds(pl.multiple_of(place * share, LANES), share)
+        return dot32(norm[...], full[:, spot]).astype(jnp.bfloat16)
+
+    def to_packed(step):
+        device = (own, across(chip, core, step), side)
+        return remote(
+            outgoing.at[step], packed.at[ctx], packed_send.at[step], packed_recv.at[ctx], device
+        )
+
+    for step in range(3):
+        outgoing[step] = project(across(chip, core, step))
+        to_packed(step).start()
+    packed[ctx] = project(ctx)
+    for step in range(3):
+        place = across(chip, core, step)
+        spot = packed.at[place]
+        remote(spot, spot, packed_send.at[step], packed_recv.at[place], core_peer).wait_recv()
+        spot = segments.at[place]
+        remote(spot, spot, segment_send.at[step], segment_recv.at[place], core_peer).wait_recv()
+    for step in range(3):
+        to_packed(step).wait_send()
+        to_segment(step).wait_send()
+    for step in range(count):
+        shard = nearest(own, count, step)
+        if step:
+            to_line(step).wait_send()
+        to_chip(shard, weight).wait_send()
+        to_core(shard, ctx, weight).wait_send()
+        to_core(shard, other_place, weight).wait_send()
+
+
+def run_gather(count, ctx_size, weight, tokens, segment):
+    rows, columns = weight.shape
+    here, width = tokens.shape
+    share = (columns - LANES) // ctx_size
+    dma = pltpu.SemaphoreType.DMA
+    return pl.pallas_call(
+        partial(gather_project, count),
+        out_shape=(
+            jax.ShapeDtypeStruct((rows * count * ctx_size, columns), jnp.bfloat16),
+            jax.ShapeDtypeStruct((ctx_size, here, share), jnp.bfloat16),
+            jax.ShapeDtypeStruct((here, width), jnp.bfloat16),
+            jax.ShapeDtypeStruct((ctx_size, 8, here), jnp.float32),
+        ),
+        in_specs=in_vmem(3),
+        out_specs=tuple(in_vmem(4)),
+        scratch_shapes=[
+            pltpu.VMEM((3, here, share), jnp.bfloat16),
+            dma((count,)),
+            dma((count,)),
+            dma((count,)),
+            dma((count,)),
+            dma((2 * count,)),
+            dma((2 * count,)),
+            dma((3,)),
+            dma((ctx_size,)),
+            dma((3,)),
+            dma((ctx_size,)),
+        ],
+        compiler_params=pltpu.CompilerParams(
+            collective_id=1, has_side_effects=True, vmem_limit_bytes=48 * 2**20
+        ),
+        cost_estimate=estimate(45),
+        name="gather_project",
+    )(weight, tokens, segment)
+
+
+def gradient_return(
+    count,
+    packed_grad,
+    full,
+    norm,
+    tokens,
+    bias_line,
+    mixture,
+    norm_grad,
+    weight_grad,
+    bias_grad,
+    gain_grad,
+    mixture_in,
+    incoming,
+    norm_t,
+    outgoing,
+    side_out,
+    side_in,
+    spread,
+    core_in,
+    chip_out,
+    chip_in,
+    line_out,
+    line_in,
+    bias_out,
+    bias_in,
+    spread_gain,
+    grad_send,
+    grad_recv,
+    side_send,
+    side_recv,
+    core_send,
+    core_recv,
+    chip_send,
+    chip_recv,
+    line_send,
+    line_recv,
+    bias_send,
+    bias_recv,
+    mixture_sem,
+):
+    own, ctx, side, chip, core = places()
+    ctx_size, here, share = packed_grad.shape
+    width = norm.shape[1]
+    halves = 2
+    part = here // halves
+    groups = ctx_size
+    pair = (own, ctx, 1 - side)
+    chip_peer = (own, (1 - chip) * 2 + core, side)
+    core_peer = (own, chip * 2 + 1 - core, side)
+    others = [
+        (nearest(own, count, step), across(chip, core, turn), side)
+        for step in range(count)
+        for turn in range(4)
+        if (step, turn) != (0, 3)
+    ]
+    greet(others + [pair])
+
+    def to_owner(step, piece):
+        place = across(chip, core, step)
+        spot = pl.ds(piece * part, part)
+        return remote(
+            packed_grad.at[place, spot],
+            incoming.at[ctx, spot],
+            grad_send.at[step, piece],
+            grad_recv.at[ctx, piece],
+            (own, place, side),
+        )
+
+    for piece in range(halves):
+        for step in range(3):
+            to_owner(step, piece).start()
+    incoming[ctx] = packed_grad[ctx]
+    mixture_copy = remote(mixture, mixture_in, mixture_sem.at[0], mixture_sem.at[1], pair)
+    mixture_copy.start()
+
+    span = bias_line.shape[1]
+    index = lax.broadcasted_iota(jnp.int32, (span, LANES), 0)
+    relative = jnp.where(index < span // 2, -index, span - index)
+    bucket = lax.broadcasted_iota(jnp.int32, (span, LANES), 1)
+    onehot = jnp.where(bucket_ids(relative) == bucket, 1.0, 0.0)
+    sums = jnp.dot(
+        bias_line[...], onehot, precision=lax.Precision.HIGHEST, preferred_element_type=jnp.float32
+    )
+    far = jnp.sum(bias_line[...], axis=1, keepdims=True)
+    lane = lax.broadcasted_iota(jnp.int32, (2, LANES), 1)
+    total = sums[0:2] + jnp.where(lane == NBUCK // 2 - 1, far[2:4], 0.0)
+    total = total + jnp.where(lane == NBUCK - 1, far[4:6], 0.0)
+    bias_sum = jnp.concatenate([total, jnp.zeros((6, LANES), jnp.float32)], axis=0)
+
+    def to_bias(number):
+        return remote(
+            bias_out.at[number],
+            bias_in.at[own, ctx],
+            bias_send.at[number],
+            bias_recv.at[own, ctx],
+            others[number],
+        )
+
+    norm_t[...] = jnp.transpose(norm[...].astype(jnp.float32)).astype(jnp.bfloat16)
+
+    def to_side(piece):
+        return remote(
+            side_out.at[piece],
+            side_in.at[piece],
+            side_send.at[piece],
+            side_recv.at[piece],
+            pair,
+        )
+
+    values = tokens[...].astype(jnp.float32)
+    normal = values * lax.rsqrt(jnp.mean(values * values, axis=1, keepdims=True) + 1e-06)
+    for piece in range(halves):
+        spot = pl.ds(piece * part, part)
+        total = jnp.zeros((part, width), jnp.float32)
+        for step in (3, 2, 0, 1):
+            place = across(chip, core, step)
+            if step != 3:
+                target = incoming.at[place, spot]
+                remote(
+                    target, target, grad_send.at[0, 0], grad_recv.at[place, piece], pair
+                ).wait_recv()
+            columns = pl.ds(pl.multiple_of(place * share, LANES), share)
+            total = total + dot_last(incoming[place, spot, :], full[:, columns])
+        side_out[piece] = total.astype(jnp.bfloat16)
+        to_side(piece).start()
+
+    def to_core(group):
+        return remote(
+            outgoing.at[group, :, 1 - core],
+            core_in.at[group],
+            core_send.at[group],
+            core_recv.at[group],
+            core_peer,
+        )
+
+    def to_chip(group):
+        return remote(
+            chip_out.at[group],
+            chip_in.at[group],
+            chip_send.at[group],
+            chip_recv.at[group],
+            chip_peer,
+        )
+
+    def to_line(group, step):
+        shard = nearest(own, count, step)
+        return remote(
+            line_out.at[group, shard],
+            line_in.at[group, own],
+            line_send.at[group, step],
+            line_recv.at[group, own],
+            (shard, ctx, side),
+        )
+
+    rows = norm_t.shape[0] // (count * ctx_size)
+
+    def contract(group):
+        found = dot32(norm_t[...], incoming[group])
+        found = found.reshape(count * 2, 2, rows, share)
+        outgoing[group] = found.astype(jnp.bfloat16)
+        to_core(group).start()
+
+    def over_chip(group):
+        to_core(group).wait_recv()
+        found = outgoing[group, :, core].astype(jnp.float32) + core_in[group].astype(jnp.float32)
+        spread[group] = found.reshape(count, 2, rows, share)
+        chip_out[group] = spread[group, :, 1 - chip].astype(jnp.bfloat16)
+        to_chip(group).start()
+
+    def over_line(group):
+        to_chip(group).wait_recv()
+        found = spread[group, :, chip] + chip_in[group].astype(jnp.float32)
+        line_out[group] = found.astype(jnp.bfloat16)
+        for step in range(1, count):
+            to_line(group, step).start()
+
+    def collect(group):
+        total = line_out[group, own].astype(jnp.float32)
+        for step in range(1, count):
+            shard = nearest(own, count, step)
+            spot = line_in.at[group, shard]
+            remote(
+                spot, spot, line_send.at[group, 0], line_recv.at[group, shard], pair
+            ).wait_recv()
+            total = total + spot[...].astype(jnp.float32)
+        weight_grad[group] = total
+
+    def finish_sides():
+        gain = jnp.zeros((1, width), jnp.float32)
+        for piece in range(halves):
+            to_side(piece).wait_recv()
+            total = side_out[piece].astype(jnp.float32) + side_in[piece].astype(jnp.float32)
+            norm_grad[pl.ds(piece * part, part), :] = total
+            gain = gain + jnp.sum(
+                total * normal[piece * part : (piece + 1) * part], axis=0, keepdims=True
+            )
+        spread_gain[...] = jnp.broadcast_to(gain, (8, width))
+
+        def message(shard, place):
+            lanes = pl.ds(pl.multiple_of((shard * 2 + place // 2) * LANES, LANES), LANES)
+            return jnp.concatenate([bias_sum, spread_gain[:, lanes]], axis=0)
+
+        for number, (shard, place, _) in enumerate(others):
+            bias_out[number] = message(shard, place)
+            to_bias(number).start()
+        bias_in[own, ctx] = message(own, ctx)
+
+    for moment in range(groups + 3):
+        if moment < groups:
+            contract(moment)
+        if 0 <= moment - 1 < groups:
+            over_chip(moment - 1)
+        if 0 <= moment - 2 < groups:
+            over_line(moment - 2)
+        if moment == groups:
+            finish_sides()
+        if 0 <= moment - 3 < groups:
+            collect(moment - 3)
+
+    for number, (shard, place, _) in enumerate(others):
+        spot = bias_in.at[shard, place]
+        remote(spot, spot, bias_send.at[0], bias_recv.at[shard, place], pair).wait_recv()
+    for place in range(ctx_size):
+        total = bias_in[0, place]
+        for shard in range(1, count):
+            total = total + bias_in[shard, place]
+        bias_grad[place] = total[:8]
+        gain_total = total[8:] if place == 0 else gain_total + total[8:]
+    gain_grad[...] = gain_total
+
+    mixture_copy.wait()
+    for number in range(len(others)):
+        to_bias(number).wait_send()
+    for piece in range(halves):
+        to_side(piece).wait_send()
+        for step in range(3):
+            to_owner(step, piece).wait_send()
+    for group in range(groups):
+        to_core(group).wait_send()
+        to_chip(group).wait_send()
+        for step in range(1, count):
+            to_line(group, step).wait_send()
+
+
+def run_return(count, packed_grad, full, norm, tokens, bias_line, mixture):
+    ctx_size, here, share = packed_grad.shape
+    width = norm.shape[1]
+    rows = width // (count * ctx_size)
+    low, wide = jnp.bfloat16, jnp.float32
+    dma = pltpu.SemaphoreType.DMA
+    columns = share
+    return pl.pallas_call(
+        partial(gradient_return, count),
+        out_shape=(
+            jax.ShapeDtypeStruct((here, width), wide),
+            jax.ShapeDtypeStruct((ctx_size, rows, columns), wide),
+            jax.ShapeDtypeStruct((ctx_size, 8, LANES), wide),
+            jax.ShapeDtypeStruct((8, LANES), wide),
+            jax.ShapeDtypeStruct((here, width), low),
+        ),
+        in_specs=in_vmem(6),
+        out_specs=tuple(in_vmem(5)),
+        scratch_shapes=[
+            pltpu.VMEM((ctx_size, here, share), low),
+            pltpu.VMEM((width, here), low),
+            pltpu.VMEM((ctx_size, count * 2, 2, rows, columns), low),
+            pltpu.VMEM((2, here // 2, width), low),
+            pltpu.VMEM((2, here // 2, width), low),
+            pltpu.VMEM((ctx_size, count, 2, rows, columns), wide),
+            pltpu.VMEM((ctx_size, count * 2, rows, columns), low),
+            pltpu.VMEM((ctx_size, count, rows, columns), low),
+            pltpu.VMEM((ctx_size, count, rows, columns), low),
+            pltpu.VMEM((ctx_size, count, rows, columns), low),
+            pltpu.VMEM((ctx_size, count, rows, columns), low),
+            pltpu.VMEM((15, 16, LANES), wide),
+            pltpu.VMEM((count, ctx_size, 16, LANES), wide),
+            pltpu.VMEM((8, width), wide),
+            dma((3, 2)),
+            dma((ctx_size, 2)),
+            dma((2,)),
+            dma((2,)),
+            dma((ctx_size,)),
+            dma((ctx_size,)),
+            dma((ctx_size,)),
+            dma((ctx_size,)),
+            dma((ctx_size, count)),
+            dma((ctx_size, count)),
+            dma((15,)),
+            dma((count, ctx_size)),
+            dma((2,)),
+        ],
+        compiler_params=pltpu.CompilerParams(
+            collective_id=2, has_side_effects=True, vmem_limit_bytes=60 * 2**20
+        ),
+        cost_estimate=estimate(45),
+        name="gradient_return",
+    )(packed_grad, full, norm, tokens, bias_line, mixture)
+
+
 def swap_sides(member):
     return lax.ppermute(member, "tensor", [(0, 1), (1, 0)])
 
 
 def exchange(member, axis):
     return lax.all_to_all(member, axis, split_axis=0, concat_axis=0, tiled=True)
+
+
+def shifted(member, axis):
+    size = lax.axis_size(axis)
+    index = lax.axis_index(axis)
+
+    def block(place):
+        return lax.dynamic_index_in_dim(member, place, 0, False)
+
+    parts = [block(index)]
+    for shift in range(1, size):
+        pairs = [(place, (place + shift) % size) for place in range(size)]
+        parts.append(lax.ppermute(block((index + shift) % size), axis, pairs))
+    return parts
+
+
+def joined(parts, axis):
+    size = len(parts)
+    index = lax.axis_index(axis)
+    result = jnp.zeros((size,) + parts[0].shape, parts[0].dtype)
+    for shift in range(size):
+        place = (index - shift + size) % size
+        result = lax.dynamic_update_index_in_dim(result, parts[shift], place, 0)
+    return result
 
 
 def slot_codes(routes, experts, room):
@@ -868,31 +1395,7 @@
     return mixture, dots, norm_grad, slot_rows, slot_grads, inner, gate_grad, up_grad
 
 
-def experts_fused(norm_two, up_slots, gates, codes, code_rows, room, count, weights):
-    width = norm_two.shape[1]
-    half = room // 2
-    side = lax.axis_index("tensor")
-    norm_grad, dots, rows, grads, inner, gate_grad, up_grad, outs = run_experts(
-        count, norm_two, gates, code_rows, codes, up_slots, *weights
-    )
-    theirs = lax.dynamic_slice_in_dim(outs, (1 - side) * half, half, 1)
-    ours = lax.dynamic_slice_in_dim(outs, side * half, half, 1)
-    ours = (ours.astype(jnp.float32) + swap_sides(theirs).astype(jnp.float32)).astype(jnp.bfloat16)
-    ours = exchange(ours, "shard").reshape(-1, width)
-    slots = jnp.arange(count * half, dtype=jnp.int32)
-    slots = (slots // half * room + slots % half + side * half).astype(jnp.float32)
-    mixing = sum(
-        jnp.where(codes[:, k : k + 1] == slots[None, :], gates[:, k : k + 1], 0.0)
-        for k in range(TOP)
-    )
-    mixture = dot32(mixing.astype(jnp.bfloat16), ours).astype(jnp.bfloat16)
-    mixture = mixture.astype(jnp.float32) + swap_sides(mixture).astype(jnp.float32)
-    flat = [member.reshape(-1, member.shape[2]) for member in (rows, grads, inner)]
-    flat += [gate_grad.reshape(-1, inner.shape[2]), up_grad.reshape(-1, inner.shape[2])]
-    return (mixture, jnp.transpose(dots[:TOP]), norm_grad, *flat)
-
-
-def local(
+def local_general(
     tokens_in,
     cotangent,
     segment_ids,
@@ -911,7 +1414,6 @@
     w_down,
 ):
     rows_here, width = tokens_in.shape
-    shard_size = lax.axis_size("shard")
     ctx_size = lax.axis_size("ctx")
     side_count = lax.axis_size("tensor")
     ctx_index = lax.axis_index("ctx")
@@ -920,16 +1422,8 @@
     share = head_cols // ctx_size
     experts = router.shape[1]
     room = max(2, 3 * rows_here // experts)
-    fused = shard_size == 4 and experts == shard_size and side_count == 2
 
     picks, codes = slot_codes(routes, experts, room)
-    code_rows = jnp.pad(jnp.transpose(codes), ((0, 8 - TOP), (0, 0)), constant_values=-1.0)
-    up_slots = None
-    if fused:
-        slots = jnp.arange(experts * room, dtype=jnp.int32).astype(jnp.float32)[:, None]
-        chosen = (code_rows[0:1] == slots) | (code_rows[1:2] == slots)
-        up_slots = dot32(chosen.astype(jnp.bfloat16), cotangent).astype(jnp.bfloat16)
-        up_slots = exchange(up_slots.reshape(experts, room, width), "shard")
 
     def by_owner(member):
         return member.reshape(member.shape[0], ctx_size, share)
@@ -991,12 +1485,7 @@
     chosen = jnp.sum(jnp.where(picks, logits[:, None, :], 0.0), axis=2)
     gates = jax.nn.softmax(chosen, axis=1)
     upstream = cotangent.astype(jnp.float32)
-    if fused:
-        results = experts_fused(
-            norm_two, up_slots, gates, codes, code_rows, room, experts, expert_weights
-        )
-    else:
-        results = experts_apart(norm_two, upstream, gates, codes, room, experts, expert_weights)
+    results = experts_apart(norm_two, upstream, gates, codes, room, experts, expert_weights)
     mixture, gate_dots, norm_grad, slot_rows, slot_grads, inner, gate_grad, up_grad = results
     weight_grads = lax.psum_scatter(
         jnp.stack(
@@ -1084,6 +1573,199 @@
     )
 
 
+def local_fused(
+    tokens_in,
+    cotangent,
+    segment_ids,
+    live_blocks,
+    routes,
+    w_query,
+    w_key,
+    w_value,
+    w_out,
+    rel_bias,
+    attn_gain,
+    ffn_gain,
+    router,
+    w_gate,
+    w_up,
+    w_down,
+):
+    rows_here, width = tokens_in.shape
+    count = lax.axis_size("shard")
+    ctx_size = lax.axis_size("ctx")
+    side_count = lax.axis_size("tensor")
+    ctx_index = lax.axis_index("ctx")
+    side = lax.axis_index("tensor")
+    head_cols = w_query.shape[1]
+    share = head_cols // ctx_size
+    experts = router.shape[1]
+    room = max(2, 3 * rows_here // experts)
+
+    picks, codes = slot_codes(routes, experts, room)
+    code_rows = jnp.pad(jnp.transpose(codes), ((0, 8 - TOP), (0, 0)), constant_values=-1.0)
+    slots = jnp.arange(experts * room, dtype=jnp.int32).astype(jnp.float32)[:, None]
+    chosen = (code_rows[0:1] == slots) | (code_rows[1:2] == slots)
+    up_slots = dot32(chosen.astype(jnp.bfloat16), cotangent).astype(jnp.bfloat16)
+    up_parts = shifted(up_slots.reshape(experts, room, width), "shard")
+
+    def by_owner(member):
+        return member.reshape(member.shape[0], ctx_size, share)
+
+    packed_rows = jnp.stack([by_owner(w_query), by_owner(w_key), by_owner(w_value)], axis=2)
+    rows = w_query.shape[0]
+    weight = jnp.concatenate(
+        [
+            packed_rows.reshape(rows, -1),
+            attn_gain[:, None],
+            ffn_gain[:, None],
+            router,
+            jnp.zeros((rows, LANES - 2 - experts), jnp.float32),
+        ],
+        axis=1,
+    ).astype(jnp.bfloat16)
+    segment = jnp.broadcast_to(segment_ids.astype(jnp.float32), (8, rows_here))
+    full, packed, norm_one, segments = run_gather(count, ctx_size, weight, tokens_in, segment)
+    packed = packed.reshape(ctx_size * rows_here, 3 * share)
+    gains = full[:, 3 * head_cols :].astype(jnp.float32)
+    gain_one = gains[:, 0]
+    gain_two = gains[:, 1]
+    router_w = full[:, 3 * head_cols + 2 : 3 * head_cols + 2 + experts]
+    out_w = lax.all_gather(w_out.astype(jnp.bfloat16), ("shard", "ctx", "tensor"), axis=0)
+    out_w = out_w.reshape(-1, side_count, w_out.shape[0], head_cols)
+    out_w = jnp.transpose(out_w, (0, 2, 1, 3)).reshape(width, side_count * head_cols)
+    expert_weights = tuple(
+        lax.all_gather(member.astype(jnp.bfloat16), "ctx", axis=1, tiled=True)[0]
+        for member in (w_gate, w_up, w_down)
+    )
+
+    inputs = tokens_in.astype(jnp.float32)
+    scale_one = lax.rsqrt(jnp.mean(inputs * inputs, axis=1, keepdims=True) + 1e-06)
+    normal_one = inputs * scale_one
+    segment_row = segments[:, 0].reshape(1, -1)
+    alive = live_tiles(segment_row[0], live_blocks[0])
+    pair_heads = share // HEAD
+    own_bias = lax.dynamic_slice_in_dim(rel_bias, ctx_index * pair_heads, pair_heads, 1)
+    line = jnp.dot(own_bias.T, span_buckets().T, precision=lax.Precision.HIGHEST)
+    packed, up_parts[1], up_parts[2] = lax.optimization_barrier((packed, up_parts[1], up_parts[2]))
+    attended, attended_t, log_sum = run_forward(alive, packed, segment_row, line)
+    attended, up_parts[3] = lax.optimization_barrier((attended, up_parts[3]))
+    attended = attended.reshape(ctx_size, 1, rows_here, share)
+    attended = jnp.broadcast_to(attended, (ctx_size, side_count, rows_here, share))
+    attended = exchange(attended.reshape(-1, rows_here, share), ("ctx", "tensor"))
+    attended = attended.reshape(ctx_size, side_count, rows_here, share)
+    attended = jnp.transpose(attended, (2, 1, 0, 3))
+    attended_low = lax.dynamic_index_in_dim(attended, side, 1, False).reshape(rows_here, head_cols)
+    attended = attended.reshape(rows_here, side_count * head_cols)
+    hidden_one = inputs + contract_cols(attended, out_w)
+    scale_two = lax.rsqrt(jnp.mean(hidden_one * hidden_one, axis=1, keepdims=True) + 1e-06)
+    normal_two = hidden_one * scale_two
+    norm_two = (normal_two * gain_two).astype(jnp.bfloat16)
+    logits = dot32(norm_two, router_w)
+    chosen = jnp.sum(jnp.where(picks, logits[:, None, :], 0.0), axis=2)
+    gates = jax.nn.softmax(chosen, axis=1)
+    upstream = cotangent.astype(jnp.float32)
+    norm_grad, dots, slot_rows, slot_grads, inner, gate_grad, up_grad, outs = run_experts(
+        count, norm_two, gates, code_rows, codes, joined(up_parts, "shard"), *expert_weights
+    )
+    half = room // 2
+    theirs = swap_sides(lax.dynamic_slice_in_dim(outs, (1 - side) * half, half, 1))
+    ours = lax.dynamic_slice_in_dim(outs, side * half, half, 1)
+
+    def flat(member):
+        return member.reshape(-1, member.shape[2])
+
+    weight_grads = lax.psum_scatter(
+        jnp.stack(
+            [
+                contract_rows(flat(slot_rows), flat(gate_grad)),
+                contract_rows(flat(slot_rows), flat(up_grad)),
+                contract_rows(flat(slot_grads), flat(inner)),
+            ],
+            axis=1,
+        ).astype(jnp.bfloat16),
+        "ctx",
+        scatter_dimension=0,
+        tiled=True,
+    ).astype(jnp.float32)
+    gate_dots = jnp.transpose(dots[:TOP])
+    gate_shift = gate_dots - gates * jnp.sum(gate_dots, axis=1, keepdims=True)
+    logit_grad = jnp.sum(jnp.where(picks, gate_shift[:, :, None], 0.0), axis=1)
+    router_f = router_w.astype(jnp.float32)
+    norm_grad = norm_grad + jnp.dot(logit_grad, router_f.T, precision=lax.Precision.HIGHEST)
+    spread_two = norm_grad * gain_two
+    hidden_grad = upstream + scale_two * (
+        spread_two - normal_two * jnp.mean(spread_two * normal_two, axis=1, keepdims=True)
+    )
+    branch_grad = hidden_grad.astype(jnp.bfloat16)
+    own_out_w = lax.dynamic_slice_in_dim(out_w, side * head_cols, head_cols, 1)
+    grad_heads = dot32(branch_grad, own_out_w).astype(jnp.bfloat16)
+    grad_heads = jnp.transpose(grad_heads.reshape(rows_here, ctx_size, share), (1, 0, 2))
+    grad_heads = exchange(grad_heads, "ctx").reshape(-1, share)
+    second_gain = jnp.sum(norm_grad * normal_two, axis=0)[:, None]
+    router_part = jnp.dot(
+        norm_two.astype(jnp.float32).T, logit_grad, precision=lax.Precision.HIGHEST
+    )
+    reduced = lax.psum_scatter(
+        jnp.concatenate(
+            [contract_rows(branch_grad, attended_low), second_gain, router_part], axis=1
+        ),
+        ("shard", "ctx"),
+        scatter_dimension=0,
+        tiled=True,
+    )
+    grad_heads, theirs = lax.optimization_barrier((grad_heads, theirs))
+    ours = (ours.astype(jnp.float32) + theirs.astype(jnp.float32)).astype(jnp.bfloat16)
+    ours = joined(shifted(ours, "shard"), "shard").reshape(-1, width)
+    slots = jnp.arange(count * half, dtype=jnp.int32)
+    slots = (slots // half * room + slots % half + side * half).astype(jnp.float32)
+    mixing = sum(
+        jnp.where(codes[:, k : k + 1] == slots[None, :], gates[:, k : k + 1], 0.0)
+        for k in range(TOP)
+    )
+    mixture = dot32(mixing.astype(jnp.bfloat16), ours).astype(jnp.bfloat16)
+    packed_grad, bias_line = run_backward(
+        alive, packed, segment_row, line, grad_heads, attended_t, log_sum
+    )
+    packed_grad, mixture = lax.optimization_barrier((packed_grad, mixture))
+    norm_one_grad, attention_grad, bias_grad, first_gain, peer_mixture = run_return(
+        count,
+        packed_grad.reshape(ctx_size, rows_here, 3 * share),
+        full,
+        norm_one,
+        tokens_in,
+        bias_line,
+        mixture,
+    )
+    mixture = mixture.astype(jnp.float32) + peer_mixture.astype(jnp.float32)
+    mixed = (hidden_one + mixture).astype(jnp.bfloat16)
+    spread_one = norm_one_grad * gain_one
+    input_grad = hidden_grad + scale_one * (
+        spread_one - normal_one * jnp.mean(spread_one * normal_one, axis=1, keepdims=True)
+    )
+    attention_grad = attention_grad.reshape(ctx_size, rows, 3, share)
+
+    def owned(number):
+        return jnp.transpose(attention_grad[:, :, number], (1, 0, 2)).reshape(rows, head_cols)
+
+    bias_grad = jnp.transpose(bias_grad[:, :pair_heads, :NBUCK], (2, 0, 1))
+    return (
+        mixed,
+        input_grad.astype(jnp.bfloat16),
+        owned(0),
+        owned(1),
+        owned(2),
+        reduced[:, :head_cols],
+        bias_grad.reshape(rel_bias.shape),
+        lax.dynamic_slice_in_dim(first_gain[0], ctx_index % 2 * rows, rows, 0),
+        reduced[:, head_cols],
+        reduced[:, head_cols + 1 :],
+        weight_grads[:, 0][None],
+        weight_grads[:, 1][None],
+        weight_grads[:, 2][None],
+    )
+
+
 def solution(mesh):
     placed = (
         P(("shard", "ctx"), None),
@@ -1103,8 +1785,10 @@
         P("shard", "ctx", "tensor"),
         P("shard", "ctx", "tensor"),
     )
+    sizes = (mesh.shape["shard"], mesh.shape["ctx"], mesh.shape["tensor"])
+    fused = sizes == (4, 4, 2)
     return jax.shard_map(
-        local,
+        local_fused if fused else local_general,
         mesh=mesh,
         in_specs=placed,
         out_specs=(

time: 706 us -> 587 us (0.83)
  waiting for transfers between devices: 309 us -> 40.4 us
  Pallas kernels: 162 us -> 394 us
  blocking collectives: 50 us -> 0 us
  matrix products: 54.6 us -> 35.8 us
  starting transfers between devices: 31.3 us -> 20 us
    pallas_call x0 -> x2, Pallas kernels: none -> 233 us  [the longest x1 137 us: run_gather(): pl.pallas_call(partial(gather_project, count), out_shape=(jax.ShapeDtypeS...]
    all_gather x5 -> x4, waiting for transfers between devices: 84.4 us -> 0.03 us  [the longest x1 0.02 us: local_fused(): lax.all_gather(w_out.astype(jnp.bfloat16), ('shard', 'ctx', 'tensor'), ax...]
    reduce_scatter x2 -> x1, waiting for transfers between devices: 70.2 us -> 0.01 us  [local_fused(): lax.psum_scatter(jnp.stack([contract_rows(flat(slot_rows), flat(gate_grad...]
    all_to_all x5 -> x2, waiting for transfers between devices: 96.3 us -> 26.7 us  [exchange(): return lax.all_to_all(member, axis, split_axis=0, concat_axis=0, tiled=True)]
    ppermute x3 -> x1, waiting for transfers between devices: 58.1 us -> 12.7 us  [swap_sides(): return lax.ppermute(member, 'tensor', [(0, 1), (1, 0)])]
    psum x1 -> x0, blocking collectives: 30.1 us -> none  [local(): grad_bias = lax.psum(bias_acc, ('shard', 'ctx'))]
    all_to_all x5 -> x2, starting transfers between devices: 28 us -> 7.05 us  [exchange(): return lax.all_to_all(member, axis, split_axis=0, concat_axis=0, tiled=True)]
    all_to_all x1 -> x0, blocking collectives: 13.8 us -> none  [exchange(): return lax.all_to_all(member, axis, split_axis=0, concat_axis=0, tiled=True)]
  transfers between devices with their start and end apart: 15 -> 15, of which waited for: 13 -> 4; matrix products, arithmetic and copies ran while one was open for 13% -> 15% of each run, Pallas kernels for 7% -> 48%
where the time goes in v3:
time: 587 us; the launch traced here: 579 us
  Pallas kernels  394 us (67%)
  local copies, waits for them, and re-layouts  47.2 us (8%)
  waiting for transfers between devices  40.4 us (7%)
  matrix products  35.8 us (6%)
  other arithmetic  25.9 us (4%)
  starting transfers between devices  20 us (3%)
  between operations  15.4 us (3%)
    pallas_call x1, Pallas kernels, run_gather(): pl.pallas_call(partial(gather_project, count), out_shape=(jax.ShapeDtypeS...  137 us
    pallas_call x1, Pallas kernels, run_experts(): pl.pallas_call(partial(expert_exchange, count), out_shape=(jax.ShapeDtype...  119 us
    pallas_call x1, Pallas kernels, run_return(): pl.pallas_call(partial(gradient_return, count), out_shape=(jax.ShapeDtype...  96.1 us
    all_to_all x2, waiting for transfers between devices, exchange(): return lax.all_to_all(member, axis, split_axis=0, concat_axis=0, tiled=True)  26.7 us
    pallas_call x1, Pallas kernels, run_backward(): pl.pallas_call(attention_backward, out_shape=(jax.ShapeDtypeStruct((lengt...  23.1 us
    dot_general x4, matrix products, contract_rows(): lax.dot_general(left, right, (((0,), (0,)), ((), ())), preferred_element_...  20.3 us
    pallas_call x1, Pallas kernels, run_forward(): pl.pallas_call(attention_forward, out_shape=(jax.ShapeDtypeStruct((length...  18.5 us
    ppermute x1, waiting for transfers between devices, swap_sides(): return lax.ppermute(member, 'tensor', [(0, 1), (1, 0)])  12.7 us
  transfers between devices with their start and end apart: 15, of which 4 were waited for; matrix products, arithmetic and copies ran while one was open for 15% of the time, Pallas kernels for 48%

profile of v3, /device:TPU:0, one launch (start us, length us, event | category | flops | bytes accessed | tf_op | source)
XLA Modules:
  0.0 578.6 jit_solution(15308696998642908556)
XLA Ops:
  9.0 2.3 convert_element_type.166
  16.6 3.1 collective-permute-start
  19.6 2.6 collective-permute-start.1
  26.9 137.3 %gather_project.1 = (bf16[1024,1664]{1,0:T(8,128)(2,1)}, bf16[4,512,384]{2,1,0:T(8,128)(2,1)S(1)}, bf16[512,1024]{1,0:T(8,128)(2,1)S(1)}, f32[4,8,512]{2,1,0:T(8,128)S(1)}) custom-call(bf16[64,1664]{1,0:T(8,128)(2,1)S(1)} %concatenate.7.weight, bf16[512,1024]{1,0:T(8,128)(2,1)S(1)} %copy-done.2, f32[8,512]{1,0:T(8,128)S(1)} %broadcast_in_dim.140.segment), custom_call_target="tpu_custom_call" | custom-call | flops 44999999488 | tf_op jit(solution)/shard_map/gather_project/pallas_call | solution.py:988
  170.0 18.5 %attention_forward.1 = (bf16[2048,128]{1,0:T(8,128)(2,1)S(1)}, f32[128,2048]{1,0:T(8,128)S(1)}, f32[8,2048]{1,0:T(8,128)S(1)}) custom-call(s32[64]{0:T(128)S(1)} %and_convert_fusion.alive, bf16[2048,384]{1,0:T(8,128)(2,1)S(1)} %bitcast.148, f32[1,2048]{1,0:T(1,128)S(1)} %bitcast.146, f32[2,1024]{1,0:T(2,128)S(1)} %fusion.27.line), custom_call_target="tpu_custom_call" | custom-call | flops 20000000000 | tf_op jit(solution)/shard_map/attention_forward/pallas_call | solution.py:290
  189.9 3.6 all-to-all-start
  201.1 18.3 %all-to-all-done = bf16[8,512,128]{2,1,0:T(8,128)(2,1)S(1)} async-done(((bf16[8,512,128]{2,1,0:T(8,128)(2,1)}), bf16[8,512,128]{2,1,0:T(8,128)(2,1)S(1)}, u32[]{:S(2)}, u32[]{:S(2)}) %all-to-all-start) | async-done | bytes 1048608 | tf_op jit(solution)/shard_map/all_to_all | solution.py:1324
  222.8 3.8 copy.162
  233.2 118.8 %expert_exchange.1 = (f32[512,1024]{1,0:T(8,128)}, f32[8,512]{1,0:T(8,128)}, bf16[4,384,1024]{2,1,0:T(8,128)(2,1)}, bf16[4,384,1024]{2,1,0:T(8,128)(2,1)}, bf16[...) custom-call(bf16[512,1024]{1,0:T(8,128)(2,1)} %copy-done.24, ...), custom_call_target="tpu_custom_call" | custom-call | flops 109999996928 | tf_op jit(solution)/shard_map/expert_exchange/pallas_call | solution.py:762
  356.9 3.6 multiply_reduce_fusion
  364.9 8.6 %fusion = bf16[1024,1,1408]{2,0,1:T(8,128)(2,1)S(1)} fusion(bf16[4,384,1024]{2,1,0:T(8,128)(2,1)} %get-tuple-element.70, bf16[4,384,1408]{2,1,0:T(8,128)(2,1)} %get-tuple-element.71), kind=kOutput, calls=%fused_computation.5 | convolution fusion | flops 4430626816 | bytes 10354688 | tf_op jit(solution)/shard_map/dot_general | solution.py:30
  373.6 5.5 fusion.1
  379.1 5.5 fusion.2
  384.6 4.1 pad_maximum_fusion
  388.8 2.8 constant_dynamic-slice_fusion
  393.2 2.7 convolution_convert_fusion.2
  396.9 3.5 all-to-all-start.1
  400.7 8.4 %all-to-all-done.1 = bf16[4,512,128]{2,1,0:T(8,128)(2,1)S(1)} async-done(((bf16[4,512,128]{2,1,0:T(8,128)(2,1)}), bf16[4,512,128]{2,1,0:T(8,128)(2,1)S(1)}, u32[]{:S(2)}, u32[]{:S(2)}) %all-to-all-start.1) | async-done | bytes 524320 | tf_op jit(solution)/shard_map/all_to_all | solution.py:1324
  409.2 12.7 %collective-permute-done.3 = bf16[4,192,1024]{2,1,0:T(8,128)(2,1)} collective-permute-done((bf16[4,192,1024]{2,1,0:T(8,128)(2,1)}, bf16[4,192,1024]{2,1,0:T(8,128)(2,1)}, u32[]{:S(2)}, u32[]{:S(2)}) %collective-permute-start.3) | collective-permute-done | bytes 1572896 | tf_op jit(solution)/shard_map/ppermute | solution.py:1320
  421.9 2.6 add_convert_fusion
  425.0 3.9 collective-permute-start.5
  428.9 23.1 %attention_backward.1 = (bf16[2048,384]{1,0:T(8,128)(2,1)S(1)}, f32[8,1024]{1,0:T(8,128)S(1)}) custom-call(s32[64]{0:T(128)S(1)} %copy-done.12, bf16[2048,384]{1,0:T(8,128)(2,1)S(1)} %bitcast.149, f32[1,2048]{1,0:T(1,128)S(1)} %bitcast.147, f32[2,1024]{1,0:T(2,128)S(1)} %copy-done.14, bf16[2048,128]{1,0:T(8,128)(2,1)S(1)} %bitcast.145, ...), custom_call_target="tpu_custom_call" | custom-call | flops 25999998976 | tf_op jit(solution)/shard_map/attention_backward/pallas_call | solution.py:316
  455.2 96.1 %gradient_return.1 = (f32[512,1024]{1,0:T(8,128)}, f32[4,64,384]{2,1,0:T(8,128)}, f32[4,8,128]{2,1,0:T(8,128)}, f32[8,128]{1,0:T(8,128)}, bf16[512,1024]{1,0:T(8,128)(2,1)}) custom-call(bf16[4,512,384]{2,1,0:T(8,128)(2,1)} %bitcast.150, bf16[1024,1664]{1,0:T(8,128)(2,1)} %get-tuple-element.49.full, bf16[512,1024]{1,0:T(8,128)(2,1)} %copy-done.17, ...), custom_call_target="tpu_custom_call" | custom-call | flops 44999999488 | tf_op jit(solution)/shard_map/gradient_return/pallas_call | solution.py:1271
  559.0 4.0 fusion.12
  (241 shorter events, 67.9 us)
Async XLA Ops:
  7.2 159.9 %copy-start = (f32[32,8]{0,1:T(8,128)S(1)}, f32[32,8]{0,1:T(8,128)}, u32[]{:S(2)}) copy-start(f32[32,8]{0,1:T(8,128)} %param.25) | copy-start | bytes 3076
  7.2 215.6 %all-gather.12.cloned.1.call-start = ((), (), s32[]{:S(2)}) async-start(), calls=%async_computation.8 | async-start | bytes 2162688 | tf_op jit(solution)/shard_map/all_gather | solution.py:1634
  8.9 224.3 %all-gather.6.cloned.1.call-start = ((), (), s32[]{:S(2)}) async-start(), calls=%async_computation.4 | async-start | bytes 3604480 | tf_op jit(solution)/shard_map/all_gather | solution.py:1638
  11.3 221.9 %all-gather.8.cloned.1.call-start = ((), (), s32[]{:S(2)}) async-start(), calls=%async_computation.5 | async-start | bytes 3604480 | tf_op jit(solution)/shard_map/all_gather | solution.py:1638
  12.3 220.8 %all-gather.10.cloned.1.call-start = ((), (), s32[]{:S(2)}) async-start(), calls=%async_computation.6 | async-start | bytes 3604480 | tf_op jit(solution)/shard_map/all_gather | solution.py:1638
  12.8 153.6 %copy-start.37 = (f32[512,2]{0,1:T(2,128)}, f32[512,2]{0,1:T(2,128)S(1)}, u32[]{:S(2)}) copy-start(f32[512,2]{0,1:T(2,128)S(1)} %select_reduce_fusion.2) | copy-start | bytes 12292
  16.6 152.0 %collective-permute-start = (bf16[384,1024]{1,0:T(8,128)(2,1)}, bf16[384,1024]{1,0:T(8,128)(2,1)}, u32[]{:S(2)}, u32[]{:S(2)}) collective-permute-start(bf16[384,1024]{1,0:T(8,128)(2,1)} %get-tuple-element.167), channel_id=1, source_target_pairs={{0,8},{8,16},{16,24},{24,0},{1,9},{9,17},{17,25},{25,1},{2,10},{10... | collective-permute-start | bytes 2359304 | tf_op jit(solution)/shard_map/ppermute | solution.py:1337
  19.6 148.9 %collective-permute-start.1 = (bf16[384,1024]{1,0:T(8,128)(2,1)}, bf16[384,1024]{1,0:T(8,128)(2,1)}, u32[]{:S(2)}, u32[]{:S(2)}) collective-permute-start(bf16[384,1024]{1,0:T(8,128)(2,1)} %get-tuple-element.166), channel_id=1, source_target_pairs={{0,16},{8,24},{16,0},{24,8},{1,17},{9,25},{17,1},{25,9},{2,18},{10... | collective-permute-start | bytes 2359304 | tf_op jit(solution)/shard_map/ppermute | solution.py:1337
  22.2 166.3 %collective-permute-start.2 = (bf16[384,1024]{1,0:T(8,128)(2,1)}, bf16[384,1024]{1,0:T(8,128)(2,1)}, u32[]{:S(2)}, u32[]{:S(2)}) collective-permute-start(bf16[384,1024]{1,0:T(8,128)(2,1)} %get-tuple-element.165), channel_id=1, source_target_pairs={{0,24},{8,0},{16,8},{24,16},{1,25},{9,1},{17,9},{25,17},{2,26},{10... | collective-permute-start | bytes 2359304 | tf_op jit(solution)/shard_map/ppermute | solution.py:1337
  26.9 139.0 %copy-start.41 = (s32[1,4,4]{2,1,0:T(4,128)S(1)}, s32[1,4,4]{2,1,0:T(4,128)}, u32[]{:S(2)}) copy-start(s32[1,4,4]{2,1,0:T(4,128)} %param.19) | copy-start | bytes 196
  165.4 23.1 %copy-start.17 = (bf16[512,1024]{1,0:T(8,128)(2,1)}, bf16[512,1024]{1,0:T(8,128)(2,1)S(1)}, u32[]{:S(2)}) copy-start(bf16[512,1024]{1,0:T(8,128)(2,1)S(1)} %get-tuple-element.63.norm) | copy-start | bytes 3145732
  165.4 23.1 %copy-start.5 = (f32[4,1,512]{2,1,0:T(1,128)}, f32[4,1,512]{2,1,0:T(1,128)S(1)}, u32[]{:S(2)}) copy-start(f32[4,1,512]{2,1,0:T(1,128)S(1)} %get-tuple-element.175) | copy-start | bytes 24580
  167.1 21.4 %copy-start.11 = (s32[64]{0:T(128)}, s32[64]{0:T(128)S(1)}, u32[]{:S(2)}) copy-start(s32[64]{0:T(128)S(1)} %and_convert_fusion.alive) | copy-start | bytes 772
  189.9 29.5 %all-to-all-start = ((bf16[8,512,128]{2,1,0:T(8,128)(2,1)}), bf16[8,512,128]{2,1,0:T(8,128)(2,1)S(1)}, u32[]{:S(2)}, u32[]{:S(2)}) async-start(bf16[8,512,128]{2,1,0:T(8,128)(2,1)} %bitcast.156), calls=%async_computation | async-start | bytes 2097152 | tf_op jit(solution)/shard_map/all_to_all | solution.py:1324
  193.4 369.6 %reduce-scatter.7.cloned.1.call-start = ((), (), s32[]{:S(2)}) async-start(), calls=%async_computation.9 | async-start | bytes 2785280
  364.8 202.7 %reduce-scatter.5.cloned.1.call-start = ((), (), s32[]{:S(2)}) async-start(), calls=%async_computation.7 | async-start | bytes 10813440 | tf_op jit(solution)/shard_map/reduce_scatter | solution.py:1678
  391.6 30.3 %collective-permute-start.3 = (bf16[4,192,1024]{2,1,0:T(8,128)(2,1)}, bf16[4,192,1024]{2,1,0:T(8,128)(2,1)}, u32[]{:S(2)}, u32[]{:S(2)}) collective-permute-start(bf16[4,192,1024]{2,1,0:T(8,128)(2,1)} %constant_dynamic-slice_fusion), channel_id=1, source_target_pairs={{0,1},{1,0},{2,3},{3,2},{4,5},{5,4},{6,7},{7,6},{8,9},{9,8},{10,11... | collective-permute-start | bytes 4718600 | tf_op jit(solution)/shard_map/ppermute | solution.py:1320
  396.9 12.3 %all-to-all-start.1 = ((bf16[4,512,128]{2,1,0:T(8,128)(2,1)}), bf16[4,512,128]{2,1,0:T(8,128)(2,1)S(1)}, u32[]{:S(2)}, u32[]{:S(2)}) async-start(bf16[4,512,128]{2,1,0:T(8,128)(2,1)} %bitcast.30), calls=%async_computation.1 | async-start | bytes 1048576 | tf_op jit(solution)/shard_map/all_to_all | solution.py:1324
  424.9 27.1 %collective-permute-start.4 = (bf16[192,1024]{1,0:T(8,128)(2,1)S(1)}, bf16[192,1024]{1,0:T(8,128)(2,1)S(1)}, u32[]{:S(2)}, u32[]{:S(2)}) collective-permute-start(bf16[192,1024]{1,0:T(8,128)(2,1)S(1)} %get-tuple-element.170), channel_id=1, source_target_pairs={{0,8},{8,16},{16,24},{24,0},{1,9},{9,17},{17,25},{25,1},{2,10},{10... | collective-permute-start | bytes 1179656 | tf_op jit(solution)/shard_map/ppermute | solution.py:1337
  425.0 28.0 %collective-permute-start.5 = (bf16[192,1024]{1,0:T(8,128)(2,1)S(1)}, bf16[192,1024]{1,0:T(8,128)(2,1)S(1)}, u32[]{:S(2)}, u32[]{:S(2)}) collective-permute-start(bf16[192,1024]{1,0:T(8,128)(2,1)S(1)} %get-tuple-element.169), channel_id=1, source_target_pairs={{0,16},{8,24},{16,0},{24,8},{1,17},{9,25},{17,1},{25,9},{2,18},{10... | collective-permute-start | bytes 1179656 | tf_op jit(solution)/shard_map/ppermute | solution.py:1337
  428.8 24.1 %collective-permute-start.6 = (bf16[192,1024]{1,0:T(8,128)(2,1)S(1)}, bf16[192,1024]{1,0:T(8,128)(2,1)S(1)}, u32[]{:S(2)}, u32[]{:S(2)}) collective-permute-start(bf16[192,1024]{1,0:T(8,128)(2,1)S(1)} %get-tuple-element.168), channel_id=1, source_target_pairs={{0,24},{8,0},{16,8},{24,16},{1,25},{9,1},{17,9},{25,17},{2,26},{10... | collective-permute-start | bytes 1179656 | tf_op jit(solution)/shard_map/ppermute | solution.py:1337
  455.2 99.9 %copy-start.4 = (bf16[512,1024]{1,0:T(8,128)(2,1)S(1)}, bf16[512,1024]{1,0:T(8,128)(2,1)}, u32[]{:S(2)}) copy-start(bf16[512,1024]{1,0:T(8,128)(2,1)} %tokens.3) | copy-start | bytes 3145732
  455.2 99.9 %copy-start.40 = (f32[1024]{0:T(1024)S(1)}, f32[1024]{0:T(1024)}, u32[]{:S(2)}) copy-start(f32[1024]{0:T(1024)} %get-tuple-element.155) | copy-start | bytes 12292
  455.2 103.8 %copy-start.30 = (bf16[512,1024]{1,0:T(8,128)(2,1)S(1)}, bf16[512,1024]{1,0:T(8,128)(2,1)}, u32[]{:S(2)}) copy-start(bf16[512,1024]{1,0:T(8,128)(2,1)} %convolution_convert_fusion.1.mixture) | copy-start | bytes 3145732
  (43 other events, 209.9 us)
Sparse Core Ops, SparseCore 0:
  11.7 100.3 all-gather.11
  114.2 35.4 all-gather.5
  151.2 30.5 all-gather.7
  183.2 38.3 all-gather.9
  364.9 78.6 reduce-scatter.6
  446.0 106.0 reduce-scatter.4

commit v4 on v3

--- a/solution.py
+++ b/solution.py
@@ -384,17 +384,23 @@
     code_rows,
     code_cols,
     upstream,
-    gate_hbm,
-    up_hbm,
-    down_hbm,
+    gate_own,
+    gate_chip,
+    gate_core,
+    gate_far,
+    up_own,
+    up_chip,
+    up_core,
+    up_far,
+    down_own,
+    down_chip,
+    down_core,
+    down_far,
     row_grad,
     dot_rows,
-    rows_hbm,
-    slot_hbm,
-    inner_hbm,
-    gate_grad_hbm,
-    up_grad_hbm,
     out_hbm,
+    kept_hbm,
+    given_hbm,
     gate_w,
     up_w,
     down_w,
@@ -416,6 +422,7 @@
     final_out,
     final_in,
     final_dots,
+    core_in,
     load_sem,
     store_sem,
     rows_send,
@@ -432,6 +439,8 @@
     dots_recv,
     final_send,
     final_recv,
+    core_send,
+    core_recv,
 ):
     own = lax.axis_index("shard")
     ctx = lax.axis_index("ctx")
@@ -454,16 +463,26 @@
     barrier = pltpu.get_barrier_semaphore()
     for step in range(1, count):
         pl.semaphore_signal(barrier, 1, device_id=(source(step), ctx, side), device_id_type=MESH)
-    pl.semaphore_signal(barrier, 1, device_id=peer, device_id_type=MESH)
-    loads = [
-        pltpu.make_async_copy(source_ref, target, load_sem.at[number])
-        for number, (source_ref, target) in enumerate(
-            ((gate_hbm, gate_w), (up_hbm, up_w), (down_hbm, down_w))
-        )
-    ]
+    chip, core = ctx // 2, ctx % 2
+    core_peer = (own, chip * 2 + 1 - core, side)
+    for device in (peer, core_peer):
+        pl.semaphore_signal(barrier, 1, device_id=device, device_id_type=MESH)
+    deep = gate_own.shape[0]
+    origins = (ctx, (1 - chip) * 2 + core, chip * 2 + 1 - core, (1 - chip) * 2 + 1 - core)
+    pieces_of = (
+        (gate_w, (gate_own, gate_chip, gate_core, gate_far)),
+        (up_w, (up_own, up_chip, up_core, up_far)),
+        (down_w, (down_own, down_chip, down_core, down_far)),
+    )
+    loads = []
+    for number, (target, sources) in enumerate(pieces_of):
+        for turn, source_ref in enumerate(sources):
+            spot = pl.ds(pl.multiple_of(origins[turn] * deep, deep), deep)
+            sem = load_sem.at[4 * number + turn]
+            loads.append(pltpu.make_async_copy(source_ref, target.at[spot], sem))
     for load in loads:
         load.start()
-    pl.semaphore_wait(barrier, count)
+    pl.semaphore_wait(barrier, count + 1)
 
     my_half = pl.ds(pl.multiple_of(side * half, half), half)
     peer_half = pl.ds(pl.multiple_of((1 - side) * half, half), half)
@@ -625,30 +644,53 @@
         return unused
 
     lax.fori_loop(0, count, run_chunk, 0)
-    stores = [
-        pltpu.make_async_copy(source_ref, target, store_sem.at[number])
-        for number, (source_ref, target) in enumerate(
-            (
-                (rows, rows_hbm),
-                (slot_grad, slot_hbm),
-                (inner, inner_hbm),
-                (gate_grad, gate_grad_hbm),
-                (up_grad, up_grad_hbm),
-            )
-        )
-    ]
-    for store in stores:
-        store.start()
+    products = ((gate_w, rows, gate_grad), (up_w, rows, up_grad), (down_w, slot_grad, inner))
+
+    def owner(turn):
+        return turn % 2 * 2 + (core + 1 + turn // 2) % 2
+
+    def to_core(number, turn):
+        spot = pl.ds(pl.multiple_of(owner(turn) * deep, deep), deep)
+        return pltpu.make_async_remote_copy(
+            products[number][0].at[spot],
+            core_in.at[number, turn],
+            core_send.at[number, turn],
+            core_recv.at[number, turn],
+            device_id=core_peer,
+            device_id_type=MESH,
+        )
+
+    def weigh(number):
+        target, left, right = products[number]
+
+        def block(turn, unused):
+            spot = pl.ds(pl.multiple_of(owner(turn) * deep, deep), deep)
+            lines = left[:, :, spot].reshape(count * room, deep)
+            target[spot, :] = lax.dot_general(
+                lines,
+                right[...].reshape(count * room, hidden),
+                (((0,), (0,)), ((), ())),
+                preferred_element_type=jnp.float32,
+            ).astype(jnp.bfloat16)
+
+            @pl.when(turn < 2)
+            def _():
+                to_core(number, turn).start()
+
+            return unused
+
+        lax.fori_loop(0, 4, block, 0)
 
     def run_out(step, unused):
         outs[step] = dot_last(inner[step], down_w[...]).astype(jnp.bfloat16)
         return unused
 
-    lax.fori_loop(0, 1, run_out, 0)
+    weigh(0)
     send_back(count - 1)
-    lax.fori_loop(1, count, run_out, 0)
-    out_store = pltpu.make_async_copy(outs, out_hbm, store_sem.at[5])
+    lax.fori_loop(0, count, run_out, 0)
+    out_store = pltpu.make_async_copy(outs, out_hbm, store_sem.at[0])
     out_store.start()
+    weigh(1)
 
     def dots_landed(step, unused):
         origin = source(step)
@@ -716,6 +758,8 @@
 
     lax.fori_loop(0, blocks, combine, 0)
 
+    weigh(2)
+
     def finish(block, unused):
         spot = pl.ds(pl.multiple_of(block * span, span), span)
         final_copy(block).wait_recv()
@@ -727,6 +771,21 @@
     lax.fori_loop(0, blocks, finish, 0)
     dots_final.wait_recv()
     dot_rows[...] = final_dots[0] + final_dots[1]
+    stores = []
+    for number in range(3):
+        for turn in range(2):
+            spot = pl.ds(pl.multiple_of(owner(turn + 2) * deep, deep), deep)
+            to_core(number, turn).wait_recv()
+            core_in[number, turn] = (
+                products[number][0][spot, :].astype(jnp.float32)
+                + core_in[number, turn].astype(jnp.float32)
+            ).astype(jnp.bfloat16)
+        for place, target in enumerate((kept_hbm, given_hbm)):
+            source_ref = core_in.at[number, chip * (1 - place) + (1 - chip) * place]
+            sem = store_sem.at[1 + 2 * number + place]
+            store = pltpu.make_async_copy(source_ref, target.at[number], sem)
+            store.start()
+            stores.append(store)
 
     def drain(step, unused):
         rows_copy(step).wait_send()
@@ -745,16 +804,19 @@
 
     lax.fori_loop(0, blocks, drain_final, 0)
     dots_final.wait_send()
+    for number in range(3):
+        for turn in range(2):
+            to_core(number, turn).wait_send()
     for store in stores:
         store.wait()
     out_store.wait()
 
 
-def run_experts(count, norm, gates, code_rows, code_cols, upstream, gate_w, up_w, down_w):
+def run_experts(count, ctx_size, norm, gates, code_rows, code_cols, upstream, weights):
     tokens, width = norm.shape
     room = upstream.shape[1]
     half = room // 2
-    hidden = gate_w.shape[1]
+    hidden = weights[0].shape[1]
     blocks = 4
     low = jnp.bfloat16
     full = jnp.float32
@@ -765,14 +827,11 @@
             jax.ShapeDtypeStruct((tokens, width), full),
             jax.ShapeDtypeStruct((8, tokens), full),
             jax.ShapeDtypeStruct((count, room, width), low),
-            jax.ShapeDtypeStruct((count, room, width), low),
-            jax.ShapeDtypeStruct((count, room, hidden), low),
-            jax.ShapeDtypeStruct((count, room, hidden), low),
-            jax.ShapeDtypeStruct((count, room, hidden), low),
-            jax.ShapeDtypeStruct((count, room, width), low),
+            jax.ShapeDtypeStruct((3, width // ctx_size, hidden), low),
+            jax.ShapeDtypeStruct((3, width // ctx_size, hidden), low),
         ),
-        in_specs=in_vmem(5) + [pl.BlockSpec(memory_space=pl.ANY)] * 3,
-        out_specs=tuple(in_vmem(2) + [pl.BlockSpec(memory_space=pl.ANY)] * 6),
+        in_specs=in_vmem(5) + [pl.BlockSpec(memory_space=pl.ANY)] * 12,
+        out_specs=tuple(in_vmem(2) + [pl.BlockSpec(memory_space=pl.ANY)] * 3),
         scratch_shapes=[
             pltpu.VMEM((width, hidden), low),
             pltpu.VMEM((width, hidden), low),
@@ -795,8 +854,9 @@
             pltpu.VMEM((blocks, tokens // blocks, width), low),
             pltpu.VMEM((blocks, tokens // blocks, width), low),
             pltpu.VMEM((2, 8, tokens), full),
-            dma((3,)),
-            dma((6,)),
+            pltpu.VMEM((3, 2, width // ctx_size, hidden), low),
+            dma((12,)),
+            dma((7,)),
             dma((count,)),
             dma((count,)),
             dma((count,)),
@@ -811,13 +871,15 @@
             dma((count,)),
             dma((blocks + 1,)),
             dma((blocks + 1,)),
+            dma((3, 2)),
+            dma((3, 2)),
         ],
+        cost_estimate=estimate(110),
         compiler_params=pltpu.CompilerParams(
             collective_id=3, has_side_effects=True, vmem_limit_bytes=63 * 2**20
         ),
-        cost_estimate=estimate(110),
         name="expert_exchange",
-    )(norm, gates, code_rows, code_cols, upstream, gate_w, up_w, down_w)
+    )(norm, gates, code_rows, code_cols, upstream, *weights)
 
 
 LANES = 128
@@ -858,13 +920,31 @@
 def gather_project(
     count,
     weight,
+    out_weight,
     tokens,
     segment,
+    cotangent,
+    code_rows,
+    gate_hbm,
+    up_hbm,
+    down_hbm,
     full,
     packed,
     norm,
     segments,
+    out_full,
+    upstream,
+    gate_low,
+    up_low,
+    down_low,
+    gate_core,
+    up_core,
+    down_core,
+    gate_chip,
+    gate_far,
     outgoing,
+    sent,
+    experts_wide,
     line_send,
     line_recv,
     chip_send,
@@ -875,26 +955,67 @@
     packed_recv,
     segment_send,
     segment_recv,
+    out_line_send,
+    out_line_recv,
+    out_chip_send,
+    out_chip_recv,
+    out_core_send,
+    out_core_recv,
+    out_pair_send,
+    out_pair_recv,
+    rows_send,
+    rows_recv,
+    pass_send,
+    pass_recv,
+    expert_send,
+    expert_recv,
+    load_sem,
 ):
     own, ctx, side, chip, core = places()
     rows = weight.shape[0]
-    share = packed.shape[2]
-    ctx_size = packed.shape[0]
+    ctx_size, here, share = packed.shape
+    room = upstream.shape[1]
+    half = room // 2
     chip_peer = (own, (1 - chip) * 2 + core, side)
     core_peer = (own, chip * 2 + 1 - core, side)
+    pair = (own, ctx, 1 - side)
+    loads = [
+        pltpu.make_async_copy(source, experts_wide.at[number], load_sem.at[number])
+        for number, source in enumerate((gate_hbm, up_hbm, down_hbm))
+    ]
+    for load in loads:
+        load.start()
     greet(
         [(nearest(own, count, step), ctx, side) for step in range(1, count)]
         + [(own, across(chip, core, step), side) for step in range(3)]
+        + [pair]
     )
 
     def block(shard, place):
         return pl.ds(pl.multiple_of((shard * ctx_size + place) * rows, rows), rows)
 
-    def to_line(step):
-        device = (nearest(own, count, step), ctx, side)
+    def along(origin, forward):
+        turn = 2 * forward - 1
+        target = own + turn
+        there = (target + count) // count * (1 - target // count)
+        return (target + count) % count, there
+
+    def onward(origin):
+        return 1 - (origin - own + count) // count
+
+    def to_line(origin, forward, source, number):
+        target, _ = along(origin, forward)
+        spot = full.at[block(origin, ctx)]
         return remote(
-            weight, full.at[block(own, ctx)], line_send.at[step], line_recv.at[own], device
-        )
+            source, spot, line_send.at[number], line_recv.at[origin], (target, ctx, side)
+        )
+
+    def in_line(copy_of, origin, forward, source, number, act):
+        _, there = along(origin, forward)
+
+        @pl.when(there == 1)
+        def _():
+            act(copy_of(origin, forward, source, number))
 
     def to_chip(shard, source):
         target = full.at[block(shard, ctx)]
@@ -909,14 +1030,88 @@
         device = (own, across(chip, core, step), side)
         return remote(segment, segments.at[ctx], segment_send.at[step], segment_recv.at[ctx], device)
 
-    for step in range(1, count):
-        to_line(step).start()
+    def out_to_line(origin, forward, source, number):
+        target, _ = along(origin, forward)
+        spot = out_full.at[side, block(origin, ctx)]
+        return remote(
+            source, spot, out_line_send.at[number], out_line_recv.at[origin], (target, ctx, side)
+        )
+
+    def start(copy):
+        copy.start()
+
+    def sent_off(copy):
+        copy.wait_send()
+
+    def out_to_chip(shard, source):
+        target = out_full.at[side, block(shard, ctx)]
+        return remote(source, target, out_chip_send.at[shard], out_chip_recv.at[shard], chip_peer)
+
+    def out_to_core(which, shard, place, source):
+        index = shard * 2 + place // 2
+        target = out_full.at[which, block(shard, place)]
+        return remote(
+            source, target, out_core_send.at[which, index], out_core_recv.at[which, index], core_peer
+        )
+
+    def out_to_pair(shard, place, source):
+        index = shard * 2 + place // 2
+        target = out_full.at[side, block(shard, place)]
+        return remote(source, target, out_pair_send.at[index], out_pair_recv.at[index], pair)
+
+    for forward in range(2):
+        in_line(to_line, own, forward, weight, forward, start)
     to_chip(own, weight).start()
     to_core(own, ctx, weight).start()
     for step in range(3):
         to_segment(step).start()
+    for forward in range(2):
+        in_line(out_to_line, own, forward, out_weight, forward, start)
+    out_to_core(side, own, ctx, out_weight).start()
+    out_to_pair(own, ctx, out_weight).start()
     full[block(own, ctx), :] = weight[...]
+    out_full[side, block(own, ctx), :] = out_weight[...]
     segments[ctx] = segment[...]
+
+    my_half = pl.ds(pl.multiple_of(side * half, half), half)
+    peer_half = pl.ds(pl.multiple_of((1 - side) * half, half), half)
+
+    def picked(expert, start, amount):
+        slots = lax.broadcasted_iota(jnp.int32, (amount, here), 0) + expert * room + start
+        slots = slots.astype(jnp.float32)
+        hit = (code_rows[0:1, :] == slots) | (code_rows[1:2, :] == slots)
+        rows_found = jnp.where(hit, 1.0, 0.0).astype(jnp.bfloat16)
+        return dot32(rows_found, cotangent[...]).astype(jnp.bfloat16)
+
+    def to_expert(step):
+        return remote(
+            sent.at[step - 1],
+            upstream.at[own, my_half],
+            rows_send.at[step - 1],
+            rows_recv.at[own],
+            (nearest(own, count, step), ctx, side),
+        )
+
+    def pass_rows(shard):
+        spot = upstream.at[shard, my_half]
+        return remote(spot, spot, pass_send.at[shard], pass_recv.at[shard], pair)
+
+    lows = (gate_low, up_low, down_low)
+    near = (gate_core, up_core, down_core)
+    for number, load in enumerate(loads):
+        load.wait()
+        lows[number][...] = experts_wide[number].astype(jnp.bfloat16)
+    for step in range(1, count):
+        sent[step - 1] = picked(nearest(own, count, step), side * half, half)
+    upstream[own] = picked(own, 0, room)
+
+    def to_near(number):
+        return remote(
+            lows[number], near[number], expert_send.at[number], expert_recv.at[number], core_peer
+        )
+
+    gate_over = remote(gate_low, gate_chip, expert_send.at[3], expert_recv.at[3], chip_peer)
+    gate_far_copy = remote(gate_chip, gate_far, expert_send.at[4], expert_recv.at[4], core_peer)
 
     other_place = (1 - chip) * 2 + core
 
@@ -924,6 +1119,7 @@
         shard = nearest(own, count, step)
         source = full.at[block(shard, ctx)]
         remote(source, source, line_send.at[0], line_recv.at[shard], core_peer).wait_recv()
+        in_line(to_line, shard, onward(shard), source, 1 + step, start)
         to_chip(shard, source).start()
         to_core(shard, ctx, source).start()
 
@@ -937,7 +1133,19 @@
     for step in range(1, count):
         pass_line(step)
         pass_chip(step)
-
+    out_to_chip(own, out_weight).start()
+    for step in range(1, count):
+        shard = nearest(own, count, step)
+        source = out_full.at[side, block(shard, ctx)]
+        remote(source, source, line_send.at[0], out_line_recv.at[shard], core_peer).wait_recv()
+        in_line(out_to_line, shard, onward(shard), source, 1 + step, start)
+        out_to_chip(shard, source).start()
+        out_to_core(side, shard, ctx, source).start()
+        out_to_pair(shard, ctx, source).start()
+
+    for step in range(1, count):
+        to_expert(step).start()
+    gate_over.start()
     values = tokens[...].astype(jnp.float32)
     scale = lax.rsqrt(jnp.mean(values * values, axis=1, keepdims=True) + 1e-06)
     for shard in range(count):
@@ -962,42 +1170,97 @@
         outgoing[step] = project(across(chip, core, step))
         to_packed(step).start()
     packed[ctx] = project(ctx)
+    for number in range(3):
+        to_near(number).start()
+    for step in range(count):
+        shard = nearest(own, count, step)
+        source = out_full.at[side, block(shard, other_place)]
+        remote(source, source, line_send.at[0], out_chip_recv.at[shard], core_peer).wait_recv()
+        out_to_core(side, shard, other_place, source).start()
+        out_to_pair(shard, other_place, source).start()
+    for step in range(1, count):
+        shard = nearest(own, count, step)
+        spot = upstream.at[shard, my_half]
+        remote(spot, spot, rows_send.at[0], rows_recv.at[shard], pair).wait_recv()
+        pass_rows(shard).start()
+    gate_over.wait_recv()
+    gate_far_copy.start()
+    for step in range(count):
+        shard = nearest(own, count, step)
+        for place in (core, 2 + core):
+            index = shard * 2 + place // 2
+            source = out_full.at[1 - side, block(shard, place)]
+            remote(source, source, line_send.at[0], out_pair_recv.at[index], pair).wait_recv()
+            out_to_core(1 - side, shard, place, source).start()
     for step in range(3):
         place = across(chip, core, step)
         spot = packed.at[place]
         remote(spot, spot, packed_send.at[step], packed_recv.at[place], core_peer).wait_recv()
         spot = segments.at[place]
         remote(spot, spot, segment_send.at[step], segment_recv.at[place], core_peer).wait_recv()
+    for which in (side, 1 - side):
+        for shard in range(count):
+            for place in range(2):
+                spot = out_full.at[which, block(shard, place * 2 + 1 - core)]
+                index = shard * 2 + place
+                remote(
+                    spot, spot, line_send.at[0], out_core_recv.at[which, index], core_peer
+                ).wait_recv()
+    for step in range(1, count):
+        shard = nearest(own, count, step)
+        spot = upstream.at[shard, peer_half]
+        remote(spot, spot, pass_send.at[0], pass_recv.at[shard], pair).wait_recv()
+
     for step in range(3):
         to_packed(step).wait_send()
         to_segment(step).wait_send()
+        to_near(step).wait()
+    gate_over.wait_send()
+    gate_far_copy.wait()
+    for forward in range(2):
+        in_line(to_line, own, forward, weight, forward, sent_off)
+        in_line(out_to_line, own, forward, out_weight, forward, sent_off)
     for step in range(count):
         shard = nearest(own, count, step)
         if step:
-            to_line(step).wait_send()
+            in_line(to_line, shard, onward(shard), weight, 1 + step, sent_off)
+            in_line(out_to_line, shard, onward(shard), out_weight, 1 + step, sent_off)
+            to_expert(step).wait_send()
+            pass_rows(shard).wait_send()
         to_chip(shard, weight).wait_send()
-        to_core(shard, ctx, weight).wait_send()
-        to_core(shard, other_place, weight).wait_send()
-
-
-def run_gather(count, ctx_size, weight, tokens, segment):
+        out_to_chip(shard, out_weight).wait_send()
+        for place in (ctx, other_place):
+            to_core(shard, place, weight).wait_send()
+            out_to_pair(shard, place, out_weight).wait_send()
+            out_to_core(side, shard, place, out_weight).wait_send()
+            out_to_core(1 - side, shard, place, out_weight).wait_send()
+
+
+def run_gather(count, ctx_size, room, weight, out_weight, tokens, segment, cotangent, code_rows, experts):
     rows, columns = weight.shape
     here, width = tokens.shape
     share = (columns - LANES) // ctx_size
     dma = pltpu.SemaphoreType.DMA
+    low = jnp.bfloat16
+    deep, hidden = experts[0].shape
     return pl.pallas_call(
         partial(gather_project, count),
         out_shape=(
-            jax.ShapeDtypeStruct((rows * count * ctx_size, columns), jnp.bfloat16),
-            jax.ShapeDtypeStruct((ctx_size, here, share), jnp.bfloat16),
-            jax.ShapeDtypeStruct((here, width), jnp.bfloat16),
+            jax.ShapeDtypeStruct((rows * count * ctx_size, columns), low),
+            jax.ShapeDtypeStruct((ctx_size, here, share), low),
+            jax.ShapeDtypeStruct((here, width), low),
             jax.ShapeDtypeStruct((ctx_size, 8, here), jnp.float32),
+            jax.ShapeDtypeStruct((2, rows * count * ctx_size, out_weight.shape[1]), low),
+            jax.ShapeDtypeStruct((count, room, width), low),
+            *[jax.ShapeDtypeStruct((deep, hidden), low)] * 8,
         ),
-        in_specs=in_vmem(3),
-        out_specs=tuple(in_vmem(4)),
+        in_specs=in_vmem(6) + [pl.BlockSpec(memory_space=pl.ANY)] * 3,
+        out_specs=tuple(in_vmem(14)),
         scratch_shapes=[
-            pltpu.VMEM((3, here, share), jnp.bfloat16),
-            dma((count,)),
+            pltpu.VMEM((3, here, share), low),
+            pltpu.VMEM((count - 1, room // 2, width), low),
+            pltpu.VMEM((3, deep, hidden), jnp.float32),
+            dma((count + 1,)),
             dma((count,)),
             dma((count,)),
             dma((count,)),
@@ -1007,13 +1270,28 @@
             dma((ctx_size,)),
             dma((3,)),
             dma((ctx_size,)),
+            dma((count + 1,)),
+            dma((count,)),
+            dma((count,)),
+            dma((count,)),
+            dma((2, 2 * count)),
+            dma((2, 2 * count)),
+            dma((2 * count,)),
+            dma((2 * count,)),
+            dma((count,)),
+            dma((count,)),
+            dma((count,)),
+            dma((count,)),
+            dma((5,)),
+            dma((5,)),
+            dma((3,)),
         ],
         compiler_params=pltpu.CompilerParams(
-            collective_id=1, has_side_effects=True, vmem_limit_bytes=48 * 2**20
+            collective_id=1, has_side_effects=True, vmem_limit_bytes=60 * 2**20
         ),
-        cost_estimate=estimate(45),
+        cost_estimate=estimate(60),
         name="gather_project",
-    )(weight, tokens, segment)
+    )(weight, out_weight, tokens, segment, cotangent, code_rows, *experts)
 
 
 def gradient_return(
@@ -1023,12 +1301,20 @@
     norm,
     tokens,
     bias_line,
-    mixture,
+    ours,
+    theirs,
+    gates,
+    codes,
+    branch_grad,
+    attended,
+    small,
     norm_grad,
     weight_grad,
     bias_grad,
     gain_grad,
+    mixture,
     mixture_in,
+    out_grad,
     incoming,
     norm_t,
     outgoing,
@@ -1040,9 +1326,18 @@
     chip_in,
     line_out,
     line_in,
+    out_going,
+    out_core_in,
+    out_spread,
+    out_chip_out,
+    out_chip_in,
+    out_line_out,
+    out_line_in,
     bias_out,
     bias_in,
     spread_gain,
+    mix_out,
+    mix_in,
     grad_send,
     grad_recv,
     side_send,
@@ -1056,6 +1351,8 @@
     bias_send,
     bias_recv,
     mixture_sem,
+    mix_send,
+    mix_recv,
 ):
     own, ctx, side, chip, core = places()
     ctx_size, here, share = packed_grad.shape
@@ -1089,8 +1386,42 @@
         for step in range(3):
             to_owner(step, piece).start()
     incoming[ctx] = packed_grad[ctx]
+
+    def to_tokens(step):
+        return remote(
+            mix_out.at[step],
+            mix_in.at[own],
+            mix_send.at[step],
+            mix_recv.at[own],
+            (nearest(own, count, step), ctx, side),
+        )
+
+    for step in range(count):
+        origin = nearest(own, count, step)
+        found = ours[origin].astype(jnp.float32) + theirs[origin].astype(jnp.float32)
+        if step:
+            mix_out[step] = found.astype(jnp.bfloat16)
+            to_tokens(step).start()
+        else:
+            mix_in[own] = found.astype(jnp.bfloat16)
     mixture_copy = remote(mixture, mixture_in, mixture_sem.at[0], mixture_sem.at[1], pair)
-    mixture_copy.start()
+
+    def mix():
+        half = mix_in.shape[1]
+        total = jnp.zeros((here, width), jnp.float32)
+        for step in range(count):
+            origin = nearest(own, count, step)
+            spot = mix_in.at[origin]
+            if step:
+                remote(spot, spot, mix_send.at[0], mix_recv.at[origin], pair).wait_recv()
+            slots = lax.broadcasted_iota(jnp.int32, (here, half), 1)
+            slots = (slots + (2 * origin + side) * half).astype(jnp.float32)
+            mixing = jnp.where(codes[:, 0:1] == slots, gates[:, 0:1], 0.0)
+            mixing = mixing + jnp.where(codes[:, 1:2] == slots, gates[:, 1:2], 0.0)
+            total = total + dot32(mixing.astype(jnp.bfloat16), spot[...])
+        mixture[...] = total.astype(jnp.bfloat16)
+        mixture_copy.start()
+
 
     span = bias_line.shape[1]
     index = lax.broadcasted_iota(jnp.int32, (span, LANES), 0)
@@ -1115,6 +1446,81 @@
             others[number],
         )
 
+    stages = [
+        (
+            outgoing.at[group],
+            core_in.at[group],
+            spread.at[group],
+            chip_out.at[group],
+            chip_in.at[group],
+            line_out.at[group],
+            line_in.at[group],
+            weight_grad.at[group],
+        )
+        for group in range(groups)
+    ]
+    stages.append(
+        (
+            out_going,
+            out_core_in,
+            out_spread,
+            out_chip_out,
+            out_chip_in,
+            out_line_out,
+            out_line_in,
+            out_grad,
+        )
+    )
+    rows = norm_t.shape[0] // (count * ctx_size)
+
+    def to_core(group):
+        source, target = stages[group][0].at[:, 1 - core], stages[group][1]
+        return remote(source, target, core_send.at[group], core_recv.at[group], core_peer)
+
+    def to_chip(group):
+        source, target = stages[group][3], stages[group][4]
+        return remote(source, target, chip_send.at[group], chip_recv.at[group], chip_peer)
+
+    def to_line(group, step):
+        shard = nearest(own, count, step)
+        source, target = stages[group][5].at[shard], stages[group][6].at[own]
+        send, recv = line_send.at[group, step], line_recv.at[group, own]
+        return remote(source, target, send, recv, (shard, ctx, side))
+
+    def contract(group):
+        found = dot32(norm_t[...], incoming[group] if group < groups else attended[...])
+        found = found.reshape(count * 2, 2, rows, found.shape[1])
+        stages[group][0][...] = found.astype(jnp.bfloat16)
+        to_core(group).start()
+
+    def over_chip(group):
+        to_core(group).wait_recv()
+        source, arrived, summed, target = stages[group][:4]
+        found = source[:, core].astype(jnp.float32) + arrived[...].astype(jnp.float32)
+        summed[...] = found.reshape(count, 2, rows, found.shape[2])
+        target[...] = summed[:, 1 - chip].astype(jnp.bfloat16)
+        to_chip(group).start()
+
+    def over_line(group):
+        to_chip(group).wait_recv()
+        found = stages[group][2][:, chip] + stages[group][4][...].astype(jnp.float32)
+        stages[group][5][...] = found.astype(jnp.bfloat16)
+        for step in range(1, count):
+            to_line(group, step).start()
+
+    def collect(group):
+        total = stages[group][5][own].astype(jnp.float32)
+        for step in range(1, count):
+            shard = nearest(own, count, step)
+            spot = stages[group][6].at[shard]
+            remote(
+                spot, spot, line_send.at[group, 0], line_recv.at[group, shard], pair
+            ).wait_recv()
+            total = total + spot[...].astype(jnp.float32)
+        stages[group][7][...] = total
+
+    norm_t[...] = jnp.transpose(branch_grad[...].astype(jnp.float32)).astype(jnp.bfloat16)
+    contract(groups)
     norm_t[...] = jnp.transpose(norm[...].astype(jnp.float32)).astype(jnp.bfloat16)
 
     def to_side(piece):
@@ -1143,67 +1549,6 @@
         side_out[piece] = total.astype(jnp.bfloat16)
         to_side(piece).start()
 
-    def to_core(group):
-        return remote(
-            outgoing.at[group, :, 1 - core],
-            core_in.at[group],
-            core_send.at[group],
-            core_recv.at[group],
-            core_peer,
-        )
-
-    def to_chip(group):
-        return remote(
-            chip_out.at[group],
-            chip_in.at[group],
-            chip_send.at[group],
-            chip_recv.at[group],
-            chip_peer,
-        )
-
-    def to_line(group, step):
-        shard = nearest(own, count, step)
-        return remote(
-            line_out.at[group, shard],
-            line_in.at[group, own],
-            line_send.at[group, step],
-            line_recv.at[group, own],
-            (shard, ctx, side),
-        )
-
-    rows = norm_t.shape[0] // (count * ctx_size)
-
-    def contract(group):
-        found = dot32(norm_t[...], incoming[group])
-        found = found.reshape(count * 2, 2, rows, share)
-        outgoing[group] = found.astype(jnp.bfloat16)
-        to_core(group).start()
-
-    def over_chip(group):
-        to_core(group).wait_recv()
-        found = outgoing[group, :, core].astype(jnp.float32) + core_in[group].astype(jnp.float32)
-        spread[group] = found.reshape(count, 2, rows, share)
-        chip_out[group] = spread[group, :, 1 - chip].astype(jnp.bfloat16)
-        to_chip(group).start()
-
-    def over_line(group):
-        to_chip(group).wait_recv()
-        found = spread[group, :, chip] + chip_in[group].astype(jnp.float32)
-        line_out[group] = found.astype(jnp.bfloat16)
-        for step in range(1, count):
-            to_line(group, step).start()
-
-    def collect(group):
-        total = line_out[group, own].astype(jnp.float32)
-        for step in range(1, count):
-            shard = nearest(own, count, step)
-            spot = line_in.at[group, shard]
-            remote(
-                spot, spot, line_send.at[group, 0], line_recv.at[group, shard], pair
-            ).wait_recv()
-            total = total + spot[...].astype(jnp.float32)
-        weight_grad[group] = total
-
     def finish_sides():
         gain = jnp.zeros((1, width), jnp.float32)
         for piece in range(halves):
@@ -1213,7 +1558,8 @@
             gain = gain + jnp.sum(
                 total * normal[piece * part : (piece + 1) * part], axis=0, keepdims=True
             )
-        spread_gain[...] = jnp.broadcast_to(gain, (8, width))
+        spread_gain[...] = small[...]
+        spread_gain[0:1, :] = gain
 
         def message(shard, place):
             lanes = pl.ds(pl.multiple_of((shard * 2 + place // 2) * LANES, LANES), LANES)
@@ -1224,15 +1570,21 @@
             to_bias(number).start()
         bias_in[own, ctx] = message(own, ctx)
 
+    over_chip(groups)
     for moment in range(groups + 3):
         if moment < groups:
             contract(moment)
+        if moment == 0:
+            over_line(groups)
         if 0 <= moment - 1 < groups:
             over_chip(moment - 1)
         if 0 <= moment - 2 < groups:
             over_line(moment - 2)
+        if moment == 1:
+            mix()
         if moment == groups:
             finish_sides()
+            collect(groups)
         if 0 <= moment - 3 < groups:
             collect(moment - 3)
 
@@ -1248,26 +1600,43 @@
     gain_grad[...] = gain_total
 
     mixture_copy.wait()
+    for step in range(1, count):
+        to_tokens(step).wait_send()
     for number in range(len(others)):
         to_bias(number).wait_send()
     for piece in range(halves):
         to_side(piece).wait_send()
         for step in range(3):
             to_owner(step, piece).wait_send()
-    for group in range(groups):
+    for group in range(groups + 1):
         to_core(group).wait_send()
         to_chip(group).wait_send()
         for step in range(1, count):
             to_line(group, step).wait_send()
 
 
-def run_return(count, packed_grad, full, norm, tokens, bias_line, mixture):
+def run_return(
+    count,
+    packed_grad,
+    full,
+    norm,
+    tokens,
+    bias_line,
+    ours,
+    theirs,
+    gates,
+    codes,
+    branch_grad,
+    attended,
+    small,
+):
     ctx_size, here, share = packed_grad.shape
     width = norm.shape[1]
     rows = width // (count * ctx_size)
     low, wide = jnp.bfloat16, jnp.float32
     dma = pltpu.SemaphoreType.DMA
     columns = share
+    out_columns = attended.shape[1]
     return pl.pallas_call(
         partial(gradient_return, count),
         out_shape=(
@@ -1276,9 +1645,11 @@
             jax.ShapeDtypeStruct((ctx_size, 8, LANES), wide),
             jax.ShapeDtypeStruct((8, LANES), wide),
             jax.ShapeDtypeStruct((here, width), low),
+            jax.ShapeDtypeStruct((here, width), low),
+            jax.ShapeDtypeStruct((rows, out_columns), wide),
         ),
-        in_specs=in_vmem(6),
-        out_specs=tuple(in_vmem(5)),
+        in_specs=in_vmem(12),
+        out_specs=tuple(in_vmem(7)),
         scratch_shapes=[
             pltpu.VMEM((ctx_size, here, share), low),
             pltpu.VMEM((width, here), low),
@@ -1291,29 +1662,53 @@
             pltpu.VMEM((ctx_size, count, rows, columns), low),
             pltpu.VMEM((ctx_size, count, rows, columns), low),
             pltpu.VMEM((ctx_size, count, rows, columns), low),
+            pltpu.VMEM((count * 2, 2, rows, out_columns), low),
+            pltpu.VMEM((count * 2, rows, out_columns), low),
+            pltpu.VMEM((count, 2, rows, out_columns), wide),
+            pltpu.VMEM((count, rows, out_columns), low),
+            pltpu.VMEM((count, rows, out_columns), low),
+            pltpu.VMEM((count, rows, out_columns), low),
+            pltpu.VMEM((count, rows, out_columns), low),
             pltpu.VMEM((15, 16, LANES), wide),
             pltpu.VMEM((count, ctx_size, 16, LANES), wide),
             pltpu.VMEM((8, width), wide),
+            pltpu.VMEM(ours.shape, low),
+            pltpu.VMEM(ours.shape, low),
             dma((3, 2)),
             dma((ctx_size, 2)),
             dma((2,)),
             dma((2,)),
-            dma((ctx_size,)),
-            dma((ctx_size,)),
-            dma((ctx_size,)),
-            dma((ctx_size,)),
-            dma((ctx_size, count)),
-            dma((ctx_size, count)),
+            dma((ctx_size + 1,)),
+            dma((ctx_size + 1,)),
+            dma((ctx_size + 1,)),
+            dma((ctx_size + 1,)),
+            dma((ctx_size + 1, count)),
+            dma((ctx_size + 1, count)),
             dma((15,)),
             dma((count, ctx_size)),
             dma((2,)),
+            dma((count,)),
+            dma((count,)),
         ],
         compiler_params=pltpu.CompilerParams(
             collective_id=2, has_side_effects=True, vmem_limit_bytes=60 * 2**20
         ),
         cost_estimate=estimate(45),
         name="gradient_return",
-    )(packed_grad, full, norm, tokens, bias_line, mixture)
+    )(
+        packed_grad,
+        full,
+        norm,
+        tokens,
+        bias_line,
+        ours,
+        theirs,
+        gates,
+        codes,
+        branch_grad,
+        attended,
+        small,
+    )
 
 
 def swap_sides(member):
@@ -1322,30 +1717,6 @@
 
 def exchange(member, axis):
     return lax.all_to_all(member, axis, split_axis=0, concat_axis=0, tiled=True)
-
-
-def shifted(member, axis):
-    size = lax.axis_size(axis)
-    index = lax.axis_index(axis)
-
-    def block(place):
-        return lax.dynamic_index_in_dim(member, place, 0, False)
-
-    parts = [block(index)]
-    for shift in range(1, size):
-        pairs = [(place, (place + shift) % size) for place in range(size)]
-        parts.append(lax.ppermute(block((index + shift) % size), axis, pairs))
-    return parts
-
-
-def joined(parts, axis):
-    size = len(parts)
-    index = lax.axis_index(axis)
-    result = jnp.zeros((size,) + parts[0].shape, parts[0].dtype)
-    for shift in range(size):
-        place = (index - shift + size) % size
-        result = lax.dynamic_update_index_in_dim(result, parts[shift], place, 0)
-    return result
 
 
 def slot_codes(routes, experts, room):
@@ -1573,6 +1944,10 @@
     )
 
 
+def ppermute_ctx(member, flip):
+    return lax.ppermute(member, "ctx", [(place, place ^ flip) for place in range(4)])
+
+
 def local_fused(
     tokens_in,
     cotangent,
@@ -1604,11 +1979,6 @@
 
     picks, codes = slot_codes(routes, experts, room)
     code_rows = jnp.pad(jnp.transpose(codes), ((0, 8 - TOP), (0, 0)), constant_values=-1.0)
-    slots = jnp.arange(experts * room, dtype=jnp.int32).astype(jnp.float32)[:, None]
-    chosen = (code_rows[0:1] == slots) | (code_rows[1:2] == slots)
-    up_slots = dot32(chosen.astype(jnp.bfloat16), cotangent).astype(jnp.bfloat16)
-    up_parts = shifted(up_slots.reshape(experts, room, width), "shard")
-
     def by_owner(member):
         return member.reshape(member.shape[0], ctx_size, share)
 
@@ -1625,19 +1995,25 @@
         axis=1,
     ).astype(jnp.bfloat16)
     segment = jnp.broadcast_to(segment_ids.astype(jnp.float32), (8, rows_here))
-    full, packed, norm_one, segments = run_gather(count, ctx_size, weight, tokens_in, segment)
+    full, packed, norm_one, segments, out_w, up_slots, *lows = run_gather(
+        count,
+        ctx_size,
+        room,
+        weight,
+        w_out.astype(jnp.bfloat16),
+        tokens_in,
+        segment,
+        cotangent,
+        code_rows,
+        (w_gate[0], w_up[0], w_down[0]),
+    )
     packed = packed.reshape(ctx_size * rows_here, 3 * share)
     gains = full[:, 3 * head_cols :].astype(jnp.float32)
     gain_one = gains[:, 0]
     gain_two = gains[:, 1]
     router_w = full[:, 3 * head_cols + 2 : 3 * head_cols + 2 + experts]
-    out_w = lax.all_gather(w_out.astype(jnp.bfloat16), ("shard", "ctx", "tensor"), axis=0)
-    out_w = out_w.reshape(-1, side_count, w_out.shape[0], head_cols)
-    out_w = jnp.transpose(out_w, (0, 2, 1, 3)).reshape(width, side_count * head_cols)
-    expert_weights = tuple(
-        lax.all_gather(member.astype(jnp.bfloat16), "ctx", axis=1, tiled=True)[0]
-        for member in (w_gate, w_up, w_down)
-    )
+    gate_low, up_low, down_low, gate_core, up_core, down_core, gate_chip, gate_far = lows
+    up_chip, down_chip = ppermute_ctx(up_low, 2), ppermute_ctx(down_low, 2)
 
     inputs = tokens_in.astype(jnp.float32)
     scale_one = lax.rsqrt(jnp.mean(inputs * inputs, axis=1, keepdims=True) + 1e-06)
@@ -1647,17 +2023,22 @@
     pair_heads = share // HEAD
     own_bias = lax.dynamic_slice_in_dim(rel_bias, ctx_index * pair_heads, pair_heads, 1)
     line = jnp.dot(own_bias.T, span_buckets().T, precision=lax.Precision.HIGHEST)
-    packed, up_parts[1], up_parts[2] = lax.optimization_barrier((packed, up_parts[1], up_parts[2]))
     attended, attended_t, log_sum = run_forward(alive, packed, segment_row, line)
-    attended, up_parts[3] = lax.optimization_barrier((attended, up_parts[3]))
+    attended, up_chip = lax.optimization_barrier((attended, up_chip))
+    expert_weights = [gate_low, gate_chip, gate_core, gate_far]
+    expert_weights += [up_low, up_chip, up_core, ppermute_ctx(up_chip, 1)]
+    expert_weights += [down_low, down_chip, down_core, ppermute_ctx(down_chip, 1)]
     attended = attended.reshape(ctx_size, 1, rows_here, share)
     attended = jnp.broadcast_to(attended, (ctx_size, side_count, rows_here, share))
     attended = exchange(attended.reshape(-1, rows_here, share), ("ctx", "tensor"))
     attended = attended.reshape(ctx_size, side_count, rows_here, share)
     attended = jnp.transpose(attended, (2, 1, 0, 3))
     attended_low = lax.dynamic_index_in_dim(attended, side, 1, False).reshape(rows_here, head_cols)
-    attended = attended.reshape(rows_here, side_count * head_cols)
-    hidden_one = inputs + contract_cols(attended, out_w)
+    branch = [
+        contract_cols(attended[:, place].reshape(rows_here, head_cols), out_w[place])
+        for place in range(side_count)
+    ]
+    hidden_one = inputs + (branch[0] + branch[1])
     scale_two = lax.rsqrt(jnp.mean(hidden_one * hidden_one, axis=1, keepdims=True) + 1e-06)
     normal_two = hidden_one * scale_two
     norm_two = (normal_two * gain_two).astype(jnp.bfloat16)
@@ -1665,29 +2046,14 @@
     chosen = jnp.sum(jnp.where(picks, logits[:, None, :], 0.0), axis=2)
     gates = jax.nn.softmax(chosen, axis=1)
     upstream = cotangent.astype(jnp.float32)
-    norm_grad, dots, slot_rows, slot_grads, inner, gate_grad, up_grad, outs = run_experts(
-        count, norm_two, gates, code_rows, codes, joined(up_parts, "shard"), *expert_weights
+    norm_grad, dots, outs, kept, given = run_experts(
+        count, ctx_size, norm_two, gates, code_rows, codes, up_slots, expert_weights
     )
     half = room // 2
     theirs = swap_sides(lax.dynamic_slice_in_dim(outs, (1 - side) * half, half, 1))
     ours = lax.dynamic_slice_in_dim(outs, side * half, half, 1)
 
-    def flat(member):
-        return member.reshape(-1, member.shape[2])
-
-    weight_grads = lax.psum_scatter(
-        jnp.stack(
-            [
-                contract_rows(flat(slot_rows), flat(gate_grad)),
-                contract_rows(flat(slot_rows), flat(up_grad)),
-                contract_rows(flat(slot_grads), flat(inner)),
-            ],
-            axis=1,
-        ).astype(jnp.bfloat16),
-        "ctx",
-        scatter_dimension=0,
-        tiled=True,
-    ).astype(jnp.float32)
+    weight_grads = kept.astype(jnp.float32) + ppermute_ctx(given, 2).astype(jnp.float32)
     gate_dots = jnp.transpose(dots[:TOP])
     gate_shift = gate_dots - gates * jnp.sum(gate_dots, axis=1, keepdims=True)
     logit_grad = jnp.sum(jnp.where(picks, gate_shift[:, :, None], 0.0), axis=1)
@@ -1698,45 +2064,36 @@
         spread_two - normal_two * jnp.mean(spread_two * normal_two, axis=1, keepdims=True)
     )
     branch_grad = hidden_grad.astype(jnp.bfloat16)
-    own_out_w = lax.dynamic_slice_in_dim(out_w, side * head_cols, head_cols, 1)
+    own_out_w = lax.dynamic_index_in_dim(out_w, side, 0, False)
     grad_heads = dot32(branch_grad, own_out_w).astype(jnp.bfloat16)
     grad_heads = jnp.transpose(grad_heads.reshape(rows_here, ctx_size, share), (1, 0, 2))
     grad_heads = exchange(grad_heads, "ctx").reshape(-1, share)
-    second_gain = jnp.sum(norm_grad * normal_two, axis=0)[:, None]
+    second_gain = jnp.sum(norm_grad * normal_two, axis=0)[None]
     router_part = jnp.dot(
-        norm_two.astype(jnp.float32).T, logit_grad, precision=lax.Precision.HIGHEST
-    )
-    reduced = lax.psum_scatter(
-        jnp.concatenate(
-            [contract_rows(branch_grad, attended_low), second_gain, router_part], axis=1
-        ),
-        ("shard", "ctx"),
-        scatter_dimension=0,
-        tiled=True,
-    )
-    grad_heads, theirs = lax.optimization_barrier((grad_heads, theirs))
-    ours = (ours.astype(jnp.float32) + theirs.astype(jnp.float32)).astype(jnp.bfloat16)
-    ours = joined(shifted(ours, "shard"), "shard").reshape(-1, width)
-    slots = jnp.arange(count * half, dtype=jnp.int32)
-    slots = (slots // half * room + slots % half + side * half).astype(jnp.float32)
-    mixing = sum(
-        jnp.where(codes[:, k : k + 1] == slots[None, :], gates[:, k : k + 1], 0.0)
-        for k in range(TOP)
-    )
-    mixture = dot32(mixing.astype(jnp.bfloat16), ours).astype(jnp.bfloat16)
+        logit_grad.T, norm_two.astype(jnp.float32), precision=lax.Precision.HIGHEST
+    )
+    small = jnp.concatenate(
+        [jnp.zeros_like(second_gain), second_gain, router_part, jnp.zeros((6 - experts, width))]
+    )
     packed_grad, bias_line = run_backward(
         alive, packed, segment_row, line, grad_heads, attended_t, log_sum
     )
-    packed_grad, mixture = lax.optimization_barrier((packed_grad, mixture))
-    norm_one_grad, attention_grad, bias_grad, first_gain, peer_mixture = run_return(
+    returned = run_return(
         count,
         packed_grad.reshape(ctx_size, rows_here, 3 * share),
         full,
         norm_one,
         tokens_in,
         bias_line,
-        mixture,
-    )
+        ours,
+        theirs,
+        gates,
+        codes,
+        branch_grad,
+        attended_low,
+        small,
+    )
+    norm_one_grad, attention_grad, bias_grad, gains_grad, mixture, peer_mixture, out_grad = returned
     mixture = mixture.astype(jnp.float32) + peer_mixture.astype(jnp.float32)
     mixed = (hidden_one + mixture).astype(jnp.bfloat16)
     spread_one = norm_one_grad * gain_one
@@ -1748,6 +2105,7 @@
     def owned(number):
         return jnp.transpose(attention_grad[:, :, number], (1, 0, 2)).reshape(rows, head_cols)
 
+    gains_grad = lax.dynamic_slice_in_dim(gains_grad, ctx_index % 2 * rows, rows, 1)
     bias_grad = jnp.transpose(bias_grad[:, :pair_heads, :NBUCK], (2, 0, 1))
     return (
         mixed,
@@ -1755,14 +2113,14 @@
         owned(0),
         owned(1),
         owned(2),
-        reduced[:, :head_cols],
+        out_grad,
         bias_grad.reshape(rel_bias.shape),
-        lax.dynamic_slice_in_dim(first_gain[0], ctx_index % 2 * rows, rows, 0),
-        reduced[:, head_cols],
-        reduced[:, head_cols + 1 :],
-        weight_grads[:, 0][None],
-        weight_grads[:, 1][None],
-        weight_grads[:, 2][None],
+        gains_grad[0],
+        gains_grad[1],
+        jnp.transpose(gains_grad[2 : 2 + experts]),
+        weight_grads[0][None],
+        weight_grads[1][None],
+        weight_grads[2][None],
     )
 
 

time: 587 us -> 458 us (0.78); the launches traced: 579 us -> 457 us
  Pallas kernels: 394 us -> 341 us
  matrix products: 35.8 us -> 10.7 us
  local copies, waits for them, and re-layouts: 47.2 us -> 33.1 us
  between operations: 15.4 us -> 1.35 us
  waiting for transfers between devices: 40.4 us -> 32.9 us
    pallas_call x1, Pallas kernels: 137 us -> 84.4 us  [run_gather(): pl.pallas_call(partial(gather_project, count), out_shape=(jax.ShapeDtypeS...]
    all_to_all x2, waiting for transfers between devices: 26.7 us -> 1.57 us  [exchange(): return lax.all_to_all(member, axis, split_axis=0, concat_axis=0, tiled=True)]
    ppermute x6 -> x5, waiting for transfers between devices: 0.9 us -> 24.2 us  [ppermute_ctx(): lax.ppermute(member, 'ctx', [(place, place ^ flip) for place in range(4)])]
    dot_general x5 -> x1, matrix products: 22.1 us -> 0.51 us  [local_fused(): jnp.dot(logit_grad.T, norm_two.astype(jnp.float32), precision=lax.Precisi...]
    pallas_call x1, Pallas kernels: 119 us -> 138 us  [run_experts(): pl.pallas_call(partial(expert_exchange, count), out_shape=(jax.ShapeDtype...]
    pallas_call x1, Pallas kernels: 96.1 us -> 77.3 us  [run_return(): pl.pallas_call(partial(gradient_return, count), out_shape=(jax.ShapeDtype...]
    dynamic_update_slice x7 -> x0, local copies, waits for them, and re-layouts: 7.77 us -> none  [joined(): result = lax.dynamic_update_index_in_dim(result, parts[shift], place, 0)]
    convert_element_type x7 -> x1, other arithmetic: 8.74 us -> 1.96 us  [local_fused(): branch_grad = hidden_grad.astype(jnp.bfloat16)]
  transfers between devices with their start and end apart: 15 -> 8, of which waited for: 4 -> 3; matrix products, arithmetic and copies ran while one was open for 15% -> 7% of each run, Pallas kernels for 48% -> 26%
where the time goes in v4:
time: 458 us; the launch traced here: 457 us
  Pallas kernels  341 us (74%)
  local copies, waits for them, and re-layouts  33.1 us (7%)
  waiting for transfers between devices  32.9 us (7%)
  other arithmetic  22.3 us (5%)
  starting transfers between devices  15 us (3%)
  matrix products  10.7 us (2%)
    pallas_call x1, Pallas kernels, run_experts(): pl.pallas_call(partial(expert_exchange, count), out_shape=(jax.ShapeDtype...  138 us
    pallas_call x1, Pallas kernels, run_gather(): pl.pallas_call(partial(gather_project, count), out_shape=(jax.ShapeDtypeS...  84.4 us
    pallas_call x1, Pallas kernels, run_return(): pl.pallas_call(partial(gradient_return, count), out_shape=(jax.ShapeDtype...  77.3 us
    ppermute x5, waiting for transfers between devices, ppermute_ctx(): lax.ppermute(member, 'ctx', [(place, place ^ flip) for place in range(4)])  24.2 us
    pallas_call x1, Pallas kernels, run_backward(): pl.pallas_call(attention_backward, out_shape=(jax.ShapeDtypeStruct((lengt...  23.1 us
    pallas_call x1, Pallas kernels, run_forward(): pl.pallas_call(attention_forward, out_shape=(jax.ShapeDtypeStruct((length...  18.6 us
  transfers between devices with their start and end apart: 8, of which 3 were waited for; matrix products, arithmetic and copies ran while one was open for 7% of the time, Pallas kernels for 26%

profile of v4, /device:TPU:0, one launch (start us, length us, event | category | flops | bytes accessed | tf_op | source)
XLA Modules:
  0.0 456.7 jit_solution(1589776909099937494)
XLA Ops:
  11.6 84.4 %gather_project.1 = (bf16[1024,1664]{1,0:T(8,128)(2,1)}, bf16[4,512,384]{2,1,0:T(8,128)(2,1)}, bf16[512,1024]{1,0:T(8,128)(2,1)}, f32[4,8,512]{2,1,0:T(8,128)}, ...) custom-call(bf16[64,1664]{1,0:T(8,128)(2,1)} %concatenate.7.weight, ...), custom_call_target="tpu_custom_call" | custom-call | flops 60000002048 | tf_op jit(solution)/shard_map/gather_project/pallas_call | solution.py:1246
  96.0 3.0 collective-permute-start
  101.4 1.4 copy-done.2
  102.9 18.6 %attention_forward.1 = (bf16[2048,128]{1,0:T(8,128)(2,1)S(1)}, f32[128,2048]{1,0:T(8,128)S(1)}, f32[8,2048]{1,0:T(8,128)S(1)}) custom-call(s32[64]{0:T(128)S(1)} %and_convert_fusion.alive, bf16[2048,384]{1,0:T(8,128)(2,1)S(1)} %bitcast.101, f32[1,2048]{1,0:T(1,128)S(1)} %bitcast.99, f32[2,1024]{1,0:T(2,128)S(1)} %fusion.15.line), custom_call_target="tpu_custom_call" | custom-call | flops 20000000000 | tf_op jit(solution)/shard_map/attention_forward/pallas_call | solution.py:290
  123.0 3.9 all-to-all-start
  126.9 2.0 collective-permute-start.2
  132.7 24.2 %collective-permute-done.2.down_chip = bf16[256,1408]{1,0:T(8,128)(2,1)} collective-permute-done((bf16[256,1408]{1,0:T(8,128)(2,1)}, bf16[256,1408]{1,0:T(8,128)(2,1)}, u32[]{:S(2)}, u32[]{:S(2)}) %collective-permute-start.2) | collective-permute-done | bytes 720928 | tf_op jit(solution)/shard_map/ppermute | solution.py:1948
  160.6 2.1 fusion.10
  165.2 1.4 fusion.19
  167.7 138.0 %expert_exchange.1 = (f32[512,1024]{1,0:T(8,128)}, f32[8,512]{1,0:T(8,128)}, bf16[4,384,1024]{2,1,0:T(8,128)(2,1)}, bf16[3,256,1408]{2,1,0:T(8,128)(2,1)}, bf16[3,256,1408]{2,1,0:T(8,128)(2,1)}) custom-call(bf16[512,1024]{1,0:T(8,128)(2,1)} %copy-done.13, f32[512,2]{1,0:T(8,128)} %broadcast_divide_fusion.gates, f32[8,512]{1,0:T(8,128)} %pad.4.code_rows, ...), custom_call_target="tpu_custom_call" | custom-call | flops 109999996928 | tf_op jit(solution)/shard_map/expert_exchange/pallas_call | solution.py:824
  307.2 4.2 multiply_reduce_fusion
  311.4 2.0 fusion.34
  315.3 3.5 all-to-all-start.1
  318.8 2.0 collective-permute-start.5
  320.8 4.0 constant_dynamic-slice_fusion.1
  326.5 1.6 all-to-all-done.1
  329.3 23.1 %attention_backward.1 = (bf16[2048,384]{1,0:T(8,128)(2,1)S(1)}, f32[8,1024]{1,0:T(8,128)S(1)}) custom-call(s32[64]{0:T(128)S(1)} %and_convert_fusion.alive, bf16[2048,384]{1,0:T(8,128)(2,1)S(1)} %bitcast.102, f32[1,2048]{1,0:T(1,128)S(1)} %bitcast.100, f32[2,1024]{1,0:T(2,128)S(1)} %fusion.15.line, bf16[2048,128]{1,0:T(8,128)(2,1)S(1)} %bitcast.98, ...), custom_call_target="tpu_custom_call" | custom-call | flops 25999998976 | tf_op jit(solution)/shard_map/attention_backward/pallas_call | solution.py:316
  354.2 7.1 %collective-permute-done.4.theirs = bf16[4,192,1024]{2,1,0:T(8,128)(2,1)} collective-permute-done((bf16[4,192,1024]{2,1,0:T(8,128)(2,1)}, bf16[4,192,1024]{2,1,0:T(8,128)(2,1)}, u32[]{:S(2)}, u32[]{:S(2)}) %collective-permute-start.4) | collective-permute-done | bytes 1572896 | tf_op jit(solution)/shard_map/ppermute | solution.py:1715
  361.3 77.3 %gradient_return.1 = (f32[512,1024]{1,0:T(8,128)}, f32[4,64,384]{2,1,0:T(8,128)}, f32[4,8,128]{2,1,0:T(8,128)}, f32[8,128]{1,0:T(8,128)}, bf16[512,1024]{1,0:T(8...) custom-call(bf16[4,512,384]{2,1,0:T(8,128)(2,1)} %bitcast.103, bf16[1024,1664]{1,0:T(8,128)(2,1)} %get-tuple-element.52.full, ...), custom_call_target="tpu_custom_call" | custom-call | flops 44999999488 | tf_op jit(solution)/shard_map/gradient_return/pallas_call | solution.py:1640
  440.0 1.9 reshape.170
  442.7 2.3 fusion.2
  447.8 3.8 fusion.6
  451.6 2.0 convert_add_fusion
  453.7 2.1 fusion.36
  (152 shorter events, 39.4 us)
Async XLA Ops:
  0.6 100.3 %copy-start = (f32[32,8]{0,1:T(8,128)S(1)}, f32[32,8]{0,1:T(8,128)}, u32[]{:S(2)}) copy-start(f32[32,8]{0,1:T(8,128)} %param.25) | copy-start | bytes 3076
  0.7 8.3 %copy-start.24 = (f32[64,512]{1,0:T(8,128)S(1)}, f32[64,512]{1,0:T(8,128)}, u32[]{:S(2)}) copy-start(f32[64,512]{1,0:T(8,128)} %param.24) | copy-start | bytes 393220
  11.6 87.5 %copy-start.29 = (s32[1,4,4]{2,1,0:T(4,128)S(1)}, s32[1,4,4]{2,1,0:T(4,128)}, u32[]{:S(2)}) copy-start(s32[1,4,4]{2,1,0:T(4,128)} %param.19) | copy-start | bytes 196
  96.0 25.4 %collective-permute-start = (bf16[256,1408]{1,0:T(8,128)(2,1)}, bf16[256,1408]{1,0:T(8,128)(2,1)S(1)}, u32[]{:S(2)}, u32[]{:S(2)}) collective-permute-start(bf16[256,1408]{1,0:T(8,128)(2,1)} %get-tuple-element.49.up_own), channel_id=1, source_target_pairs={{0,4},{2,6},{4,0},{6,2},{1,5},{3,7},{5,1},{7,3},{8,12},{10,14},{12... | collective-permute-start | bytes 2162696 | tf_op jit(solution)/shard_map/ppermute | solution.py:1948
  123.0 8.9 %copy-start.11 = (bf16[512,1024]{1,0:T(8,128)(2,1)S(1)}, bf16[512,1024]{1,0:T(8,128)(2,1)}, u32[]{:S(2)}) copy-start(bf16[512,1024]{1,0:T(8,128)(2,1)} %tokens.3) | copy-start | bytes 3145732
  123.0 33.9 %all-to-all-start = ((bf16[8,512,128]{2,1,0:T(8,128)(2,1)}), bf16[8,512,128]{2,1,0:T(8,128)(2,1)S(1)}, u32[]{:S(2)}, u32[]{:S(2)}) async-start(bf16[8,512,128]{2,1,0:T(8,128)(2,1)} %bitcast.106), calls=%async_computation | async-start | bytes 2097152 | tf_op jit(solution)/shard_map/all_to_all | solution.py:1719
  126.9 30.0 %collective-permute-start.2 = (bf16[256,1408]{1,0:T(8,128)(2,1)}, bf16[256,1408]{1,0:T(8,128)(2,1)}, u32[]{:S(2)}, u32[]{:S(2)}) collective-permute-start(bf16[256,1408]{1,0:T(8,128)(2,1)} %get-tuple-element.60.down_own), channel_id=1, source_target_pairs={{0,4},{2,6},{4,0},{6,2},{1,5},{3,7},{5,1},{7,3},{8,12},{10,14},{12... | collective-permute-start | bytes 2162696 | tf_op jit(solution)/shard_map/ppermute | solution.py:1948
  132.7 35.0 %collective-permute-start.1 = (bf16[256,1408]{1,0:T(8,128)(2,1)}, bf16[256,1408]{1,0:T(8,128)(2,1)}, u32[]{:S(2)}, u32[]{:S(2)}) collective-permute-start(bf16[256,1408]{1,0:T(8,128)(2,1)} %copy-done.30), channel_id=1, source_target_pairs={{0,2},{2,0},{4,6},{6,4},{1,3},{3,1},{5,7},{7,5},{8,10},{10,8},{12,... | collective-permute-start | bytes 2162696 | tf_op jit(solution)/shard_map/ppermute | solution.py:1948
  156.9 10.8 %collective-permute-start.3 = (bf16[256,1408]{1,0:T(8,128)(2,1)}, bf16[256,1408]{1,0:T(8,128)(2,1)}, u32[]{:S(2)}, u32[]{:S(2)}) collective-permute-start(bf16[256,1408]{1,0:T(8,128)(2,1)} %collective-permute-done.2.down_chip), channel_id=1, source_target_pairs={{0,2},{2,0},{4,6},{6,4},{1,3},{3,1},{5,7},{7,5},{8,10},{10,8},{12,... | collective-permute-start | bytes 2162696 | tf_op jit(solution)/shard_map/ppermute | solution.py:1948
  307.1 4.3 copy-start.9
  307.1 4.3 copy-start.17
  307.1 4.3 copy-start.22
  315.3 12.8 %all-to-all-start.1 = ((bf16[4,512,128]{2,1,0:T(8,128)(2,1)}), bf16[4,512,128]{2,1,0:T(8,128)(2,1)S(1)}, u32[]{:S(2)}, u32[]{:S(2)}) async-start(bf16[4,512,128]{2,1,0:T(8,128)(2,1)} %bitcast.24), calls=%async_computation.1 | async-start | bytes 1048576 | tf_op jit(solution)/shard_map/all_to_all | solution.py:1719
  318.8 132.8 %collective-permute-start.5 = (bf16[3,256,1408]{2,1,0:T(8,128)(2,1)}, bf16[3,256,1408]{2,1,0:T(8,128)(2,1)}, u32[]{:S(2)}, u32[]{:S(2)}) collective-permute-start(bf16[3,256,1408]{2,1,0:T(8,128)(2,1)} %get-tuple-element.78), channel_id=1, source_target_pairs={{0,4},{2,6},{4,0},{6,2},{1,5},{3,7},{5,1},{7,3},{8,12},{10,14},{12... | collective-permute-start | bytes 6488072 | tf_op jit(solution)/shard_map/ppermute | solution.py:1948
  320.8 4.5 copy-start.14
  320.8 7.3 %copy-start.3 = (bf16[4,512,384]{2,1,0:T(8,128)(2,1)S(1)}, bf16[4,512,384]{2,1,0:T(8,128)(2,1)}, u32[]{:S(2)}) copy-start(bf16[4,512,384]{2,1,0:T(8,128)(2,1)} %get-tuple-element.47) | copy-start | bytes 4718596
  324.8 36.5 %collective-permute-start.4 = (bf16[4,192,1024]{2,1,0:T(8,128)(2,1)}, bf16[4,192,1024]{2,1,0:T(8,128)(2,1)}, u32[]{:S(2)}, u32[]{:S(2)}) collective-permute-start(bf16[4,192,1024]{2,1,0:T(8,128)(2,1)} %get-tuple-element.90), channel_id=1, source_target_pairs={{0,1},{1,0},{2,3},{3,2},{4,5},{5,4},{6,7},{7,6},{8,9},{9,8},{10,11... | collective-permute-start | bytes 4718600 | tf_op jit(solution)/shard_map/ppermute | solution.py:1715
  361.3 81.4 %copy-start.12 = (bf16[512,1024]{1,0:T(8,128)(2,1)S(1)}, bf16[512,1024]{1,0:T(8,128)(2,1)}, u32[]{:S(2)}) copy-start(bf16[512,1024]{1,0:T(8,128)(2,1)} %tokens.3) | copy-start | bytes 3145732
  361.3 81.4 %copy-start.27 = (f32[1024]{0:T(1024)S(1)}, f32[1024]{0:T(1024)}, u32[]{:S(2)}) copy-start(f32[1024]{0:T(1024)} %get-tuple-element.81) | copy-start | bytes 12292
  361.3 81.4 %copy-start.28 = (f32[512]{0:T(512)S(1)}, f32[512]{0:T(512)}, u32[]{:S(2)}) copy-start(f32[512]{0:T(512)} %add_rsqrt_fusion) | copy-start | bytes 6148
  361.3 86.5 %copy-start.16 = (f32[512,1024]{1,0:T(8,128)S(1)}, f32[512,1024]{1,0:T(8,128)}, u32[]{:S(2)}) copy-start(f32[512,1024]{1,0:T(8,128)} %get-tuple-element.84) | copy-start | bytes 6291460
  441.9 4.2 copy-start.21
  442.7 5.1 %copy-start.10 = (f32[512,1024]{1,0:T(8,128)S(1)}, f32[512,1024]{1,0:T(8,128)}, u32[]{:S(2)}) copy-start(f32[512,1024]{1,0:T(8,128)} %copy-done.8) | copy-start | bytes 6291460
  442.7 5.1 %copy-start.15 = (f32[512,1024]{1,0:T(8,128)S(1)}, f32[512,1024]{1,0:T(8,128)}, u32[]{:S(2)}) copy-start(f32[512,1024]{1,0:T(8,128)} %get-tuple-element.72) | copy-start | bytes 6291460
  (15 other events, 28.1 us)

commit v5 on v4

--- a/solution.py
+++ b/solution.py
@@ -360,6 +360,43 @@
 
 
 MESH = pl.DeviceIdType.MESH
+LANES = 128
+
+
+def places():
+    own, ctx, side = lax.axis_index("shard"), lax.axis_index("ctx"), lax.axis_index("tensor")
+    return own, ctx, side, ctx // 2, ctx % 2
+
+
+def nearest(own, count, step):
+    flip = own // (count // 2)
+    place = flip * (count - 1 - own) + (1 - flip) * own
+    turn = step - 1
+    turn = turn + (turn - place + count) // count
+    other = flip * (count - 1 - turn) + (1 - flip) * turn
+    first = 1 - (step + count - 1) // count
+    return first * own + (1 - first) * other
+
+
+def partner(own, turn):
+    return (own // 2 + turn // 2) % 2 * 2 + (own + turn) % 2
+
+
+def across(chip, core, step):
+    return (chip + 1 - step // 2) % 2 * 2 + (core + step + step // 2) % 2
+
+
+def remote(source, target, send, recv, device):
+    return pltpu.make_async_remote_copy(
+        source, target, send, recv, device_id=device, device_id_type=MESH
+    )
+
+
+def greet(devices):
+    barrier = pltpu.get_barrier_semaphore()
+    for device in devices:
+        pl.semaphore_signal(barrier, 1, device_id=device, device_id_type=MESH)
+    pl.semaphore_wait(barrier, len(devices))
 
 
 def gelu_parts(value):
@@ -398,9 +435,13 @@
     down_far,
     row_grad,
     dot_rows,
-    out_hbm,
+    own_hbm,
+    mine_hbm,
+    other_hbm,
     kept_hbm,
-    given_hbm,
+    gate_given,
+    up_given,
+    down_given,
     gate_w,
     up_w,
     down_w,
@@ -423,6 +464,7 @@
     final_in,
     final_dots,
     core_in,
+    chip_in,
     load_sem,
     store_sem,
     rows_send,
@@ -441,6 +483,8 @@
     final_recv,
     core_send,
     core_recv,
+    chip_send,
+    chip_recv,
 ):
     own = lax.axis_index("shard")
     ctx = lax.axis_index("ctx")
@@ -452,20 +496,15 @@
     peer = (own, ctx, 1 - side)
 
     def source(step):
-        flip = own // (count // 2)
-        place = flip * (count - 1 - own) + (1 - flip) * own
-        turn = step - 1
-        turn = turn + (turn - place + count) // count
-        other = flip * (count - 1 - turn) + (1 - flip) * turn
-        first = 1 - (step + count - 1) // count
-        return first * own + (1 - first) * other
+        return partner(own, step)
 
     barrier = pltpu.get_barrier_semaphore()
     for step in range(1, count):
         pl.semaphore_signal(barrier, 1, device_id=(source(step), ctx, side), device_id_type=MESH)
     chip, core = ctx // 2, ctx % 2
     core_peer = (own, chip * 2 + 1 - core, side)
-    for device in (peer, core_peer):
+    chip_peer = (own, (1 - chip) * 2 + core, side)
+    for device in (peer, core_peer, chip_peer):
         pl.semaphore_signal(barrier, 1, device_id=device, device_id_type=MESH)
     deep = gate_own.shape[0]
     origins = (ctx, (1 - chip) * 2 + core, chip * 2 + 1 - core, (1 - chip) * 2 + 1 - core)
@@ -482,7 +521,7 @@
             loads.append(pltpu.make_async_copy(source_ref, target.at[spot], sem))
     for load in loads:
         load.start()
-    pl.semaphore_wait(barrier, count + 1)
+    pl.semaphore_wait(barrier, count + 2)
 
     my_half = pl.ds(pl.multiple_of(side * half, half), half)
     peer_half = pl.ds(pl.multiple_of((1 - side) * half, half), half)
@@ -685,12 +724,40 @@
         outs[step] = dot_last(inner[step], down_w[...]).astype(jnp.bfloat16)
         return unused
 
+    def to_chip(number):
+        return remote(
+            core_in.at[number, 1 - chip],
+            chip_in.at[0],
+            chip_send.at[number],
+            chip_recv.at[number],
+            chip_peer,
+        )
+
+    def over_chip(number):
+        for turn in range(2):
+            spot = pl.ds(pl.multiple_of(owner(turn + 2) * deep, deep), deep)
+            to_core(number, turn).wait_recv()
+            core_in[number, turn] = (
+                products[number][0][spot, :].astype(jnp.float32)
+                + core_in[number, turn].astype(jnp.float32)
+            ).astype(jnp.bfloat16)
+        if number == 0:
+            to_chip(number).start()
+
     weigh(0)
     send_back(count - 1)
     lax.fori_loop(0, count, run_out, 0)
-    out_store = pltpu.make_async_copy(outs, out_hbm, store_sem.at[0])
-    out_store.start()
+    stores = [pltpu.make_async_copy(outs.at[own], own_hbm, store_sem.at[0])]
+    for turn in range(1, count):
+        origin = partner(own, turn)
+        for place, (spot, target) in enumerate(((my_half, mine_hbm), (peer_half, other_hbm))):
+            sem = store_sem.at[8 + 2 * turn + place]
+            source_ref = outs.at[origin, spot]
+            stores.append(pltpu.make_async_copy(source_ref, target.at[turn - 1], sem))
+    for store in stores:
+        store.start()
     weigh(1)
+    over_chip(0)
 
     def dots_landed(step, unused):
         origin = source(step)
@@ -771,19 +838,15 @@
     lax.fori_loop(0, blocks, finish, 0)
     dots_final.wait_recv()
     dot_rows[...] = final_dots[0] + final_dots[1]
-    stores = []
+    to_chip(0).wait_recv()
     for number in range(3):
-        for turn in range(2):
-            spot = pl.ds(pl.multiple_of(owner(turn + 2) * deep, deep), deep)
-            to_core(number, turn).wait_recv()
-            core_in[number, turn] = (
-                products[number][0][spot, :].astype(jnp.float32)
-                + core_in[number, turn].astype(jnp.float32)
-            ).astype(jnp.bfloat16)
-        for place, target in enumerate((kept_hbm, given_hbm)):
-            source_ref = core_in.at[number, chip * (1 - place) + (1 - chip) * place]
-            sem = store_sem.at[1 + 2 * number + place]
-            store = pltpu.make_async_copy(source_ref, target.at[number], sem)
+        if number:
+            over_chip(number)
+        given = core_in.at[number, 1 - chip] if number else chip_in.at[0]
+        for place, source_ref in enumerate((core_in.at[number, chip], given)):
+            target = (kept_hbm.at[number], (gate_given, up_given, down_given)[number])[place]
+            sem = store_sem.at[4 + 2 * number + place]
+            store = pltpu.make_async_copy(source_ref, target, sem)
             store.start()
             stores.append(store)
 
@@ -807,9 +870,10 @@
     for number in range(3):
         for turn in range(2):
             to_core(number, turn).wait_send()
+        if number == 0:
+            to_chip(number).wait_send()
     for store in stores:
         store.wait()
-    out_store.wait()
 
 
 def run_experts(count, ctx_size, norm, gates, code_rows, code_cols, upstream, weights):
@@ -826,12 +890,14 @@
         out_shape=(
             jax.ShapeDtypeStruct((tokens, width), full),
             jax.ShapeDtypeStruct((8, tokens), full),
-            jax.ShapeDtypeStruct((count, room, width), low),
+            jax.ShapeDtypeStruct((room, width), low),
+            jax.ShapeDtypeStruct((count - 1, half, width), low),
+            jax.ShapeDtypeStruct((count - 1, half, width), low),
             jax.ShapeDtypeStruct((3, width // ctx_size, hidden), low),
-            jax.ShapeDtypeStruct((3, width // ctx_size, hidden), low),
+            *[jax.ShapeDtypeStruct((width // ctx_size, hidden), low)] * 3,
         ),
         in_specs=in_vmem(5) + [pl.BlockSpec(memory_space=pl.ANY)] * 12,
-        out_specs=tuple(in_vmem(2) + [pl.BlockSpec(memory_space=pl.ANY)] * 3),
+        out_specs=tuple(in_vmem(2) + [pl.BlockSpec(memory_space=pl.ANY)] * 7),
         scratch_shapes=[
             pltpu.VMEM((width, hidden), low),
             pltpu.VMEM((width, hidden), low),
@@ -855,8 +921,9 @@
             pltpu.VMEM((blocks, tokens // blocks, width), low),
             pltpu.VMEM((2, 8, tokens), full),
             pltpu.VMEM((3, 2, width // ctx_size, hidden), low),
+            pltpu.VMEM((1, width // ctx_size, hidden), low),
             dma((12,)),
-            dma((7,)),
+            dma((16,)),
             dma((count,)),
             dma((count,)),
             dma((count,)),
@@ -873,75 +940,59 @@
             dma((blocks + 1,)),
             dma((3, 2)),
             dma((3, 2)),
+            dma((3,)),
+            dma((3,)),
         ],
         cost_estimate=estimate(110),
         compiler_params=pltpu.CompilerParams(
-            collective_id=3, has_side_effects=True, vmem_limit_bytes=63 * 2**20
+            collective_id=3, has_side_effects=True, vmem_limit_bytes=67043328
         ),
         name="expert_exchange",
     )(norm, gates, code_rows, code_cols, upstream, *weights)
 
 
-LANES = 128
-
-
-def places():
-    own, ctx, side = lax.axis_index("shard"), lax.axis_index("ctx"), lax.axis_index("tensor")
-    return own, ctx, side, ctx // 2, ctx % 2
-
-
-def nearest(own, count, step):
-    flip = own // (count // 2)
-    place = flip * (count - 1 - own) + (1 - flip) * own
-    turn = step - 1
-    turn = turn + (turn - place + count) // count
-    other = flip * (count - 1 - turn) + (1 - flip) * turn
-    first = 1 - (step + count - 1) // count
-    return first * own + (1 - first) * other
-
-
-def across(chip, core, step):
-    return (chip + 1 - step // 2) % 2 * 2 + (core + step + step // 2) % 2
-
-
-def remote(source, target, send, recv, device):
-    return pltpu.make_async_remote_copy(
-        source, target, send, recv, device_id=device, device_id_type=MESH
-    )
-
-
-def greet(devices):
-    barrier = pltpu.get_barrier_semaphore()
-    for device in devices:
-        pl.semaphore_signal(barrier, 1, device_id=device, device_id_type=MESH)
-    pl.semaphore_wait(barrier, len(devices))
-
-
 def gather_project(
     count,
-    weight,
-    out_weight,
+    w_query,
+    w_key,
+    w_value,
+    w_out,
+    gains,
+    router,
     tokens,
-    segment,
+    segment_ids,
     cotangent,
-    code_rows,
+    routes,
     gate_hbm,
     up_hbm,
     down_hbm,
+    full_hbm,
+    packed,
+    norm_hbm,
+    segments,
+    out_hbm,
+    upstream_hbm,
+    gate_hbm_low,
+    up_hbm_low,
+    down_hbm_low,
+    gate_core,
+    up_core,
+    down_core,
+    gate_chip,
+    gate_far,
+    codes,
+    code_rows,
+    extras,
     full,
-    packed,
     norm,
-    segments,
     out_full,
     upstream,
     gate_low,
     up_low,
     down_low,
-    gate_core,
-    up_core,
-    down_core,
-    gate_chip,
-    gate_far,
+    weight,
+    out_weight,
+    segment,
     outgoing,
     sent,
     experts_wide,
@@ -970,6 +1021,7 @@
     expert_send,
     expert_recv,
     load_sem,
+    store_sem,
 ):
     own, ctx, side, chip, core = places()
     rows = weight.shape[0]
@@ -985,6 +1037,27 @@
     ]
     for load in loads:
         load.start()
+    stores = []
+
+    def store(source, target):
+        copy = pltpu.make_async_copy(source, target, store_sem.at[len(stores)])
+        copy.start()
+        stores.append(copy)
+
+    lane = lax.broadcasted_iota(jnp.int32, (rows, LANES), 1)
+    column = jnp.transpose(jnp.concatenate([gains[...], jnp.zeros((6, rows))], axis=0))
+    extra = jnp.where(lane == 0, column[:, 0:1], 0.0)
+    extra = jnp.where(lane == 1, column[:, 1:2], extra)
+    for expert in range(router.shape[1]):
+        extra = jnp.where(lane == 2 + expert, router[:, expert : expert + 1], extra)
+    for place in range(ctx_size):
+        for number, member in enumerate((w_query, w_key, w_value)):
+            target = slice(place * share + number * LANES, place * share + (number + 1) * LANES)
+            found = member[:, place * LANES : (place + 1) * LANES]
+            weight[:, target] = found.astype(jnp.bfloat16)
+    weight[:, ctx_size * share :] = extra.astype(jnp.bfloat16)
+    out_weight[...] = w_out[...].astype(jnp.bfloat16)
+    segment[...] = jnp.broadcast_to(segment_ids[...].astype(jnp.float32), segment.shape)
     greet(
         [(nearest(own, count, step), ctx, side) for step in range(1, count)]
         + [(own, across(chip, core, step), side) for step in range(3)]
@@ -1073,6 +1146,19 @@
     out_full[side, block(own, ctx), :] = out_weight[...]
     segments[ctx] = segment[...]
 
+    lane = lax.broadcasted_iota(jnp.int32, (here, LANES), 1).astype(jnp.float32)
+    first = routes[:, 0:1].astype(jnp.float32)
+    second = routes[:, 1:2].astype(jnp.float32)
+    named = jnp.where((first == lane) | (second == lane), 1.0, 0.0).astype(jnp.bfloat16)
+    later = lax.broadcasted_iota(jnp.int32, (here, here), 0)
+    before = later > lax.broadcasted_iota(jnp.int32, (here, here), 1)
+    slots = dot32(jnp.where(before, 1.0, 0.0).astype(jnp.bfloat16), named) + room * lane
+    first = jnp.sum(jnp.where(first == lane, slots, 0.0), axis=1, keepdims=True)
+    second = jnp.sum(jnp.where(second == lane, slots, 0.0), axis=1, keepdims=True)
+    codes[:, 0:1] = first
+    codes[:, 1:2] = second
+    both = jnp.where(lane == 0.0, first, jnp.where(lane == 1.0, second, -1.0))
+    code_rows[...] = jnp.transpose(both)[0:8]
     my_half = pl.ds(pl.multiple_of(side * half, half), half)
     peer_half = pl.ds(pl.multiple_of((1 - side) * half, half), half)
 
@@ -1093,17 +1179,19 @@
         )
 
     def pass_rows(shard):
-        spot = upstream.at[shard, my_half]
-        return remote(spot, spot, pass_send.at[shard], pass_recv.at[shard], pair)
+        spot, target = upstream.at[shard, my_half], upstream_hbm.at[shard, my_half]
+        return remote(spot, target, pass_send.at[shard], pass_recv.at[shard], pair)
 
     lows = (gate_low, up_low, down_low)
     near = (gate_core, up_core, down_core)
     for number, load in enumerate(loads):
         load.wait()
         lows[number][...] = experts_wide[number].astype(jnp.bfloat16)
+        store(lows[number], (gate_hbm_low, up_hbm_low, down_hbm_low)[number])
     for step in range(1, count):
         sent[step - 1] = picked(nearest(own, count, step), side * half, half)
     upstream[own] = picked(own, 0, room)
+    store(upstream.at[own], upstream_hbm.at[own])
 
     def to_near(number):
         return remote(
@@ -1153,8 +1241,11 @@
             spot = full.at[block(shard, place * 2 + 1 - core)]
             index = shard * 2 + place
             remote(spot, spot, core_send.at[0], core_recv.at[index], core_peer).wait_recv()
-    gain = jnp.transpose(full[:, ctx_size * share :].astype(jnp.float32))[0:1, :]
+    store(full, full_hbm)
+    extras[...] = full[:, ctx_size * share :]
+    gain = jnp.transpose(extras[...].astype(jnp.float32))[0:1, :]
     norm[...] = (values * scale * gain).astype(jnp.bfloat16)
+    store(norm, norm_hbm)
 
     def project(place):
         spot = pl.ds(pl.multiple_of(place * share, LANES), share)
@@ -1183,6 +1274,7 @@
         spot = upstream.at[shard, my_half]
         remote(spot, spot, rows_send.at[0], rows_recv.at[shard], pair).wait_recv()
         pass_rows(shard).start()
+        store(spot, upstream_hbm.at[shard, my_half])
     gate_over.wait_recv()
     gate_far_copy.start()
     for step in range(count):
@@ -1206,11 +1298,14 @@
                 remote(
                     spot, spot, line_send.at[0], out_core_recv.at[which, index], core_peer
                 ).wait_recv()
+        store(out_full.at[which], out_hbm.at[which])
     for step in range(1, count):
         shard = nearest(own, count, step)
-        spot = upstream.at[shard, peer_half]
+        spot = upstream_hbm.at[shard, peer_half]
         remote(spot, spot, pass_send.at[0], pass_recv.at[shard], pair).wait_recv()
 
+    for copy in stores:
+        copy.wait()
     for step in range(3):
         to_packed(step).wait_send()
         to_segment(step).wait_send()
@@ -1236,10 +1331,11 @@
             out_to_core(1 - side, shard, place, out_weight).wait_send()
 
 
-def run_gather(count, ctx_size, room, weight, out_weight, tokens, segment, cotangent, code_rows, experts):
-    rows, columns = weight.shape
-    here, width = tokens.shape
-    share = (columns - LANES) // ctx_size
+def run_gather(count, ctx_size, room, members, experts):
+    rows, head_columns = members[0].shape
+    here, width = members[6].shape
+    share = 3 * head_columns // ctx_size
+    columns = ctx_size * share + LANES
     dma = pltpu.SemaphoreType.DMA
     low = jnp.bfloat16
     deep, hidden = experts[0].shape
@@ -1250,13 +1346,29 @@
             jax.ShapeDtypeStruct((ctx_size, here, share), low),
             jax.ShapeDtypeStruct((here, width), low),
             jax.ShapeDtypeStruct((ctx_size, 8, here), jnp.float32),
-            jax.ShapeDtypeStruct((2, rows * count * ctx_size, out_weight.shape[1]), low),
+            jax.ShapeDtypeStruct((2, rows * count * ctx_size, head_columns), low),
             jax.ShapeDtypeStruct((count, room, width), low),
             *[jax.ShapeDtypeStruct((deep, hidden), low)] * 8,
+            jax.ShapeDtypeStruct((here, 2), jnp.float32),
+            jax.ShapeDtypeStruct((8, here), jnp.float32),
+            jax.ShapeDtypeStruct((rows * count * ctx_size, LANES), low),
         ),
-        in_specs=in_vmem(6) + [pl.BlockSpec(memory_space=pl.ANY)] * 3,
-        out_specs=tuple(in_vmem(14)),
+        in_specs=in_vmem(10) + [pl.BlockSpec(memory_space=pl.ANY)] * 3,
+        out_specs=tuple(
+            pl.BlockSpec(memory_space=pltpu.VMEM if number in (1, 3, 14, 15, 16) else pl.ANY)
+            for number in range(17)
+        ),
         scratch_shapes=[
+            pltpu.VMEM((rows * count * ctx_size, columns), low),
+            pltpu.VMEM((here, width), low),
+            pltpu.VMEM((2, rows * count * ctx_size, head_columns), low),
+            pltpu.VMEM((count, room, width), low),
+            pltpu.VMEM((deep, hidden), low),
+            pltpu.VMEM((deep, hidden), low),
+            pltpu.VMEM((deep, hidden), low),
+            pltpu.VMEM((rows, columns), low),
+            pltpu.VMEM((rows, head_columns), low),
+            pltpu.VMEM((8, here), jnp.float32),
             pltpu.VMEM((3, here, share), low),
             pltpu.VMEM((count - 1, room // 2, width), low),
             pltpu.VMEM((3, deep, hidden), jnp.float32),
@@ -1285,36 +1397,250 @@
             dma((5,)),
             dma((5,)),
             dma((3,)),
+            dma((12,)),
         ],
         compiler_params=pltpu.CompilerParams(
             collective_id=1, has_side_effects=True, vmem_limit_bytes=60 * 2**20
         ),
         cost_estimate=estimate(60),
         name="gather_project",
-    )(weight, out_weight, tokens, segment, cotangent, code_rows, *experts)
+    )(*members, *experts)
+
+
+def attend_out(
+    attended,
+    tokens,
+    out_w,
+    extras,
+    routes,
+    hidden_one,
+    norm_two,
+    gates,
+    attended_low,
+    gathered,
+    send,
+    recv,
+):
+    own, ctx, side, chip, core = places()
+    here, width = tokens.shape
+    heads = attended.shape[2]
+    peers = [
+        (across(chip, core, step), (side + other) % 2)
+        for other in range(2)
+        for step in range(4)
+        if (other, step) != (0, 3)
+    ]
+    peers = peers[:2] + peers[3:5] + peers[2:3] + peers[5:]
+    greet([(own, place, which) for place, which in peers])
+    columns = pl.ds(pl.multiple_of(ctx * heads, heads), heads)
+
+    def copy(number):
+        place, which = peers[number]
+        return remote(
+            attended.at[place],
+            gathered.at[side, :, columns],
+            send.at[number],
+            recv.at[side, ctx],
+            (own, place, which),
+        )
+
+    for number in range(len(peers)):
+        copy(number).start()
+    gathered[side, :, columns] = attended[ctx]
+    for place, which in peers:
+        spot = gathered.at[which, :, pl.ds(pl.multiple_of(place * heads, heads), heads)]
+        remote(
+            spot, spot, send.at[0], recv.at[which, place], (own, place, which)
+        ).wait_recv()
+    attended_low[...] = gathered[side]
+    hidden = tokens[...].astype(jnp.float32) + (
+        dot_last(gathered[0], out_w[0]) + dot_last(gathered[1], out_w[1])
+    )
+    hidden_one[...] = hidden
+    scale = lax.rsqrt(jnp.mean(hidden * hidden, axis=1, keepdims=True) + 1e-06)
+    gain = jnp.transpose(extras[...].astype(jnp.float32))[1:2, :]
+    norm = (hidden * scale * gain).astype(jnp.bfloat16)
+    norm_two[...] = norm
+    logits = dot32(norm, extras[...])
+    lane = lax.broadcasted_iota(jnp.int32, (here, LANES), 1)
+    first = jnp.sum(jnp.where(lane == routes[:, 0:1] + 2, logits, 0.0), axis=1, keepdims=True)
+    second = jnp.sum(jnp.where(lane == routes[:, 1:2] + 2, logits, 0.0), axis=1, keepdims=True)
+    highest = jnp.maximum(first, second)
+    first, second = jnp.exp(first - highest), jnp.exp(second - highest)
+    gates[:, 0:1] = first / (first + second)
+    gates[:, 1:2] = second / (first + second)
+    for number in range(len(peers)):
+        copy(number).wait_send()
+
+
+def run_attend_out(attended, tokens, out_w, extras, routes):
+    here, width = tokens.shape
+    heads = out_w.shape[2]
+    low, wide = jnp.bfloat16, jnp.float32
+    return pl.pallas_call(
+        attend_out,
+        out_shape=(
+            jax.ShapeDtypeStruct((here, width), wide),
+            jax.ShapeDtypeStruct((here, width), low),
+            jax.ShapeDtypeStruct((here, 2), wide),
+            jax.ShapeDtypeStruct((here, heads), low),
+        ),
+        in_specs=in_vmem(5),
+        out_specs=tuple(in_vmem(4)),
+        scratch_shapes=[
+            pltpu.VMEM((2, here, heads), low),
+            pltpu.SemaphoreType.DMA((7,)),
+            pltpu.SemaphoreType.DMA((2, 4)),
+        ],
+        compiler_params=pltpu.CompilerParams(
+            collective_id=4, has_side_effects=True, vmem_limit_bytes=40 * 2**20
+        ),
+        cost_estimate=estimate(25),
+        name="attend_out",
+    )(attended, tokens, out_w, extras, routes)
+
+
+def attend_back(
+    rows_grad,
+    dot_rows,
+    gates,
+    routes,
+    extras,
+    hidden_one,
+    cotangent,
+    norm_two,
+    out_w,
+    hidden_grad,
+    branch_grad,
+    heads_grad,
+    small,
+    outgoing,
+    send,
+    recv,
+):
+    own, ctx, side, chip, core = places()
+    here, width = hidden_one.shape
+    heads = heads_grad.shape[2]
+    greet([(own, across(chip, core, step), side) for step in range(3)])
+    lane = lax.broadcasted_iota(jnp.int32, (here, LANES), 1)
+    dots = jnp.transpose(dot_rows[...])
+    total = dots[:, 0:1] + dots[:, 1:2]
+    logit_grad = jnp.zeros((here, LANES), jnp.float32)
+    for choice in range(TOP):
+        shift = dots[:, choice : choice + 1] - gates[:, choice : choice + 1] * total
+        logit_grad = jnp.where(lane == routes[:, choice : choice + 1] + 2, shift, logit_grad)
+    extra = extras[...].astype(jnp.float32)
+    norm_grad = rows_grad[...] + lax.dot_general(
+        logit_grad,
+        extra,
+        (((1,), (1,)), ((), ())),
+        precision=lax.Precision.HIGHEST,
+        preferred_element_type=jnp.float32,
+    )
+    hidden = hidden_one[...]
+    scale = lax.rsqrt(jnp.mean(hidden * hidden, axis=1, keepdims=True) + 1e-06)
+    normal = hidden * scale
+    spread = norm_grad * jnp.transpose(extra)[1:2, :]
+    found = cotangent[...].astype(jnp.float32) + scale * (
+        spread - normal * jnp.mean(spread * normal, axis=1, keepdims=True)
+    )
+    hidden_grad[...] = found
+    branch_grad[...] = found.astype(jnp.bfloat16)
+
+    def project(place):
+        columns = pl.ds(pl.multiple_of(place * heads, heads), heads)
+        return dot32(branch_grad[...], out_w[side, :, columns]).astype(jnp.bfloat16)
+
+    def copy(step):
+        place = across(chip, core, step)
+        return remote(
+            outgoing.at[step], heads_grad.at[ctx], send.at[step], recv.at[ctx], (own, place, side)
+        )
+
+    for step in range(3):
+        outgoing[step] = project(across(chip, core, step))
+        copy(step).start()
+    heads_grad[ctx] = project(ctx)
+    gain_row = jnp.sum(norm_grad * normal, axis=0, keepdims=True)
+    routed = jnp.dot(
+        jnp.transpose(logit_grad),
+        norm_two[...].astype(jnp.float32),
+        precision=lax.Precision.HIGHEST,
+        preferred_element_type=jnp.float32,
+    )
+    line = lax.broadcasted_iota(jnp.int32, (8, width), 0)
+    small[...] = jnp.where(line == 1, gain_row, routed[0:8])
+    for step in range(3):
+        place = across(chip, core, step)
+        spot = heads_grad.at[place]
+        remote(spot, spot, send.at[0], recv.at[place], (own, place, side)).wait_recv()
+    for step in range(3):
+        copy(step).wait_send()
+
+
+def run_attend_back(
+    rows_grad, dot_rows, gates, routes, extras, hidden_one, cotangent, norm_two, out_w
+):
+    here, width = hidden_one.shape
+    low, wide = jnp.bfloat16, jnp.float32
+    heads = out_w.shape[2] // 4
+    return pl.pallas_call(
+        attend_back,
+        out_shape=(
+            jax.ShapeDtypeStruct((here, width), wide),
+            jax.ShapeDtypeStruct((here, width), low),
+            jax.ShapeDtypeStruct((4, here, heads), low),
+            jax.ShapeDtypeStruct((8, width), wide),
+        ),
+        in_specs=in_vmem(9),
+        out_specs=tuple(in_vmem(4)),
+        scratch_shapes=[
+            pltpu.VMEM((3, here, heads), low),
+            pltpu.SemaphoreType.DMA((3,)),
+            pltpu.SemaphoreType.DMA((4,)),
+        ],
+        compiler_params=pltpu.CompilerParams(
+            collective_id=5, has_side_effects=True, vmem_limit_bytes=48 * 2**20
+        ),
+        cost_estimate=estimate(20),
+        name="attend_back",
+    )(rows_grad, dot_rows, gates, routes, extras, hidden_one, cotangent, norm_two, out_w)
 
 
 def gradient_return(
     count,
     packed_grad,
-    full,
+    full_hbm,
     norm,
     tokens,
     bias_line,
-    ours,
+    own_hbm,
+    mine,
     theirs,
     gates,
     codes,
     branch_grad,
     attended,
     small,
-    norm_grad,
-    weight_grad,
+    one_hbm,
+    grad_hbm,
+    extras,
+    mixed,
+    input_grad,
+    query_grad,
+    key_grad,
+    value_grad,
     bias_grad,
     gain_grad,
+    out_grad,
     mixture,
     mixture_in,
-    out_grad,
+    full,
+    own_out,
+    hidden_one,
+    hidden_grad,
+    mix_out,
+    mix_in,
     incoming,
     norm_t,
     outgoing,
@@ -1336,8 +1662,6 @@
     bias_out,
     bias_in,
     spread_gain,
-    mix_out,
-    mix_in,
     grad_send,
     grad_recv,
     side_send,
@@ -1353,6 +1677,7 @@
     mixture_sem,
     mix_send,
     mix_recv,
+    load_sem,
 ):
     own, ctx, side, chip, core = places()
     ctx_size, here, share = packed_grad.shape
@@ -1369,6 +1694,13 @@
         for turn in range(4)
         if (step, turn) != (0, 3)
     ]
+    pairs = ((full_hbm, full), (own_hbm, own_out), (grad_hbm, hidden_grad), (one_hbm, hidden_one))
+    loads = [
+        pltpu.make_async_copy(source, target, load_sem.at[number])
+        for number, (source, target) in enumerate(pairs)
+    ]
+    for load in loads:
+        load.start()
     greet(others + [pair])
 
     def to_owner(step, piece):
@@ -1387,41 +1719,41 @@
             to_owner(step, piece).start()
     incoming[ctx] = packed_grad[ctx]
 
-    def to_tokens(step):
+    mixture_copy = remote(mixture, mixture_in, mixture_sem.at[0], mixture_sem.at[1], pair)
+
+    def mixing(start, amount):
+        slots = lax.broadcasted_iota(jnp.int32, (here, amount), 1) + start
+        slots = slots.astype(jnp.float32)
+        held = jnp.where(codes[:, 0:1] == slots, gates[:, 0:1], 0.0)
+        held = held + jnp.where(codes[:, 1:2] == slots, gates[:, 1:2], 0.0)
+        return held.astype(jnp.bfloat16)
+
+    room, half = own_out.shape[0], mine.shape[1]
+
+    def to_tokens(turn):
         return remote(
-            mix_out.at[step],
-            mix_in.at[own],
-            mix_send.at[step],
-            mix_recv.at[own],
-            (nearest(own, count, step), ctx, side),
-        )
-
-    for step in range(count):
-        origin = nearest(own, count, step)
-        found = ours[origin].astype(jnp.float32) + theirs[origin].astype(jnp.float32)
-        if step:
-            mix_out[step] = found.astype(jnp.bfloat16)
-            to_tokens(step).start()
-        else:
-            mix_in[own] = found.astype(jnp.bfloat16)
-    mixture_copy = remote(mixture, mixture_in, mixture_sem.at[0], mixture_sem.at[1], pair)
+            mix_out.at[turn],
+            mix_in.at[turn],
+            mix_send.at[turn],
+            mix_recv.at[turn],
+            (partner(own, turn + 1), ctx, side),
+        )
+
+    for turn in range(count - 1):
+        mix_out[turn] = (
+            mine[turn].astype(jnp.float32) + theirs[turn].astype(jnp.float32)
+        ).astype(jnp.bfloat16)
+        to_tokens(turn).start()
 
     def mix():
-        half = mix_in.shape[1]
-        total = jnp.zeros((here, width), jnp.float32)
-        for step in range(count):
-            origin = nearest(own, count, step)
-            spot = mix_in.at[origin]
-            if step:
-                remote(spot, spot, mix_send.at[0], mix_recv.at[origin], pair).wait_recv()
-            slots = lax.broadcasted_iota(jnp.int32, (here, half), 1)
-            slots = (slots + (2 * origin + side) * half).astype(jnp.float32)
-            mixing = jnp.where(codes[:, 0:1] == slots, gates[:, 0:1], 0.0)
-            mixing = mixing + jnp.where(codes[:, 1:2] == slots, gates[:, 1:2], 0.0)
-            total = total + dot32(mixing.astype(jnp.bfloat16), spot[...])
+        loads[1].wait()
+        total = dot32(mixing(own * room, room), own_out[...])
+        for turn in range(count - 1):
+            to_tokens(turn).wait_recv()
+            start = partner(own, turn + 1) * room + side * half
+            total = total + dot32(mixing(start, half), mix_in[turn])
         mixture[...] = total.astype(jnp.bfloat16)
         mixture_copy.start()
-
 
     span = bias_line.shape[1]
     index = lax.broadcasted_iota(jnp.int32, (span, LANES), 0)
@@ -1455,7 +1787,7 @@
             chip_in.at[group],
             line_out.at[group],
             line_in.at[group],
-            weight_grad.at[group],
+            None,
         )
         for group in range(groups)
     ]
@@ -1468,7 +1800,7 @@
             out_chip_in,
             out_line_out,
             out_line_in,
-            out_grad,
+            None,
         )
     )
     rows = norm_t.shape[0] // (count * ctx_size)
@@ -1517,7 +1849,12 @@
                 spot, spot, line_send.at[group, 0], line_recv.at[group, shard], pair
             ).wait_recv()
             total = total + spot[...].astype(jnp.float32)
-        stages[group][7][...] = total
+        if group == groups:
+            out_grad[...] = total
+        else:
+            columns = slice(group * LANES, (group + 1) * LANES)
+            for number, target in enumerate((query_grad, key_grad, value_grad)):
+                target[:, columns] = total[:, number * LANES : (number + 1) * LANES]
 
     norm_t[...] = jnp.transpose(branch_grad[...].astype(jnp.float32)).astype(jnp.bfloat16)
     contract(groups)
@@ -1533,7 +1870,10 @@
         )
 
     values = tokens[...].astype(jnp.float32)
-    normal = values * lax.rsqrt(jnp.mean(values * values, axis=1, keepdims=True) + 1e-06)
+    scale = lax.rsqrt(jnp.mean(values * values, axis=1, keepdims=True) + 1e-06)
+    normal = values * scale
+    first_gain = jnp.transpose(extras[...].astype(jnp.float32))[0:1, :]
+    loads[0].wait()
     for piece in range(halves):
         spot = pl.ds(piece * part, part)
         total = jnp.zeros((part, width), jnp.float32)
@@ -1550,13 +1890,18 @@
         to_side(piece).start()
 
     def finish_sides():
+        loads[2].wait()
         gain = jnp.zeros((1, width), jnp.float32)
         for piece in range(halves):
             to_side(piece).wait_recv()
             total = side_out[piece].astype(jnp.float32) + side_in[piece].astype(jnp.float32)
-            norm_grad[pl.ds(piece * part, part), :] = total
-            gain = gain + jnp.sum(
-                total * normal[piece * part : (piece + 1) * part], axis=0, keepdims=True
+            lines = slice(piece * part, (piece + 1) * part)
+            upright = normal[lines]
+            gain = gain + jnp.sum(total * upright, axis=0, keepdims=True)
+            total = total * first_gain
+            total = total - upright * jnp.mean(total * upright, axis=1, keepdims=True)
+            input_grad[lines, :] = (hidden_grad[lines, :] + scale[lines] * total).astype(
+                jnp.bfloat16
             )
         spread_gain[...] = small[...]
         spread_gain[0:1, :] = gain
@@ -1580,7 +1925,7 @@
             over_chip(moment - 1)
         if 0 <= moment - 2 < groups:
             over_line(moment - 2)
-        if moment == 1:
+        if moment == 2:
             mix()
         if moment == groups:
             finish_sides()
@@ -1600,8 +1945,12 @@
     gain_grad[...] = gain_total
 
     mixture_copy.wait()
-    for step in range(1, count):
-        to_tokens(step).wait_send()
+    loads[3].wait()
+    for turn in range(count - 1):
+        to_tokens(turn).wait_send()
+    mixed[...] = (
+        hidden_one[...] + (mixture[...].astype(jnp.float32) + mixture_in[...].astype(jnp.float32))
+    ).astype(jnp.bfloat16)
     for number in range(len(others)):
         to_bias(number).wait_send()
     for piece in range(halves):
@@ -1622,13 +1971,15 @@
     norm,
     tokens,
     bias_line,
-    ours,
-    theirs,
+    outs,
     gates,
     codes,
     branch_grad,
     attended,
     small,
+    hidden_one,
+    hidden_grad,
+    extras,
 ):
     ctx_size, here, share = packed_grad.shape
     width = norm.shape[1]
@@ -1640,17 +1991,27 @@
     return pl.pallas_call(
         partial(gradient_return, count),
         out_shape=(
-            jax.ShapeDtypeStruct((here, width), wide),
-            jax.ShapeDtypeStruct((ctx_size, rows, columns), wide),
+            jax.ShapeDtypeStruct((here, width), low),
+            jax.ShapeDtypeStruct((here, width), low),
+            *[jax.ShapeDtypeStruct((rows, ctx_size * LANES), wide)] * 3,
             jax.ShapeDtypeStruct((ctx_size, 8, LANES), wide),
             jax.ShapeDtypeStruct((8, LANES), wide),
-            jax.ShapeDtypeStruct((here, width), low),
-            jax.ShapeDtypeStruct((here, width), low),
             jax.ShapeDtypeStruct((rows, out_columns), wide),
         ),
-        in_specs=in_vmem(12),
-        out_specs=tuple(in_vmem(7)),
+        in_specs=[
+            pl.BlockSpec(memory_space=pl.ANY if number in (1, 5, 13, 14) else pltpu.VMEM)
+            for number in range(16)
+        ],
+        out_specs=tuple(in_vmem(8)),
         scratch_shapes=[
+            pltpu.VMEM((here, width), low),
+            pltpu.VMEM((here, width), low),
+            pltpu.VMEM(full.shape, low),
+            pltpu.VMEM(outs[0].shape, low),
+            pltpu.VMEM((here, width), wide),
+            pltpu.VMEM((here, width), wide),
+            pltpu.VMEM(outs[1].shape, low),
+            pltpu.VMEM(outs[1].shape, low),
             pltpu.VMEM((ctx_size, here, share), low),
             pltpu.VMEM((width, here), low),
             pltpu.VMEM((ctx_size, count * 2, 2, rows, columns), low),
@@ -1672,8 +2033,6 @@
             pltpu.VMEM((15, 16, LANES), wide),
             pltpu.VMEM((count, ctx_size, 16, LANES), wide),
             pltpu.VMEM((8, width), wide),
-            pltpu.VMEM(ours.shape, low),
-            pltpu.VMEM(ours.shape, low),
             dma((3, 2)),
             dma((ctx_size, 2)),
             dma((2,)),
@@ -1687,8 +2046,9 @@
             dma((15,)),
             dma((count, ctx_size)),
             dma((2,)),
-            dma((count,)),
-            dma((count,)),
+            dma((3,)),
+            dma((3,)),
+            dma((4,)),
         ],
         compiler_params=pltpu.CompilerParams(
             collective_id=2, has_side_effects=True, vmem_limit_bytes=60 * 2**20
@@ -1701,13 +2061,15 @@
         norm,
         tokens,
         bias_line,
-        ours,
-        theirs,
+        *outs,
         gates,
         codes,
         branch_grad,
         attended,
         small,
+        hidden_one,
+        hidden_grad,
+        extras,
     )
 
 
@@ -1969,114 +2331,58 @@
     rows_here, width = tokens_in.shape
     count = lax.axis_size("shard")
     ctx_size = lax.axis_size("ctx")
-    side_count = lax.axis_size("tensor")
     ctx_index = lax.axis_index("ctx")
-    side = lax.axis_index("tensor")
-    head_cols = w_query.shape[1]
-    share = head_cols // ctx_size
+    share = w_query.shape[1] // ctx_size
+    rows = w_query.shape[0]
     experts = router.shape[1]
     room = max(2, 3 * rows_here // experts)
-
-    picks, codes = slot_codes(routes, experts, room)
-    code_rows = jnp.pad(jnp.transpose(codes), ((0, 8 - TOP), (0, 0)), constant_values=-1.0)
-    def by_owner(member):
-        return member.reshape(member.shape[0], ctx_size, share)
-
-    packed_rows = jnp.stack([by_owner(w_query), by_owner(w_key), by_owner(w_value)], axis=2)
-    rows = w_query.shape[0]
-    weight = jnp.concatenate(
-        [
-            packed_rows.reshape(rows, -1),
-            attn_gain[:, None],
-            ffn_gain[:, None],
-            router,
-            jnp.zeros((rows, LANES - 2 - experts), jnp.float32),
-        ],
-        axis=1,
-    ).astype(jnp.bfloat16)
-    segment = jnp.broadcast_to(segment_ids.astype(jnp.float32), (8, rows_here))
+    members = (
+        w_query,
+        w_key,
+        w_value,
+        w_out,
+        jnp.stack([attn_gain, ffn_gain]),
+        router,
+        tokens_in,
+        segment_ids,
+        cotangent,
+        routes,
+    )
     full, packed, norm_one, segments, out_w, up_slots, *lows = run_gather(
-        count,
-        ctx_size,
-        room,
-        weight,
-        w_out.astype(jnp.bfloat16),
-        tokens_in,
-        segment,
-        cotangent,
-        code_rows,
-        (w_gate[0], w_up[0], w_down[0]),
-    )
+        count, ctx_size, room, members, (w_gate[0], w_up[0], w_down[0])
+    )
+    gate_low, up_low, down_low, gate_core, up_core, down_core, gate_chip, gate_far = lows[:8]
+    codes, code_rows, extras = lows[8:]
+    up_chip, down_chip = ppermute_ctx(up_low, 2), ppermute_ctx(down_low, 2)
+
     packed = packed.reshape(ctx_size * rows_here, 3 * share)
-    gains = full[:, 3 * head_cols :].astype(jnp.float32)
-    gain_one = gains[:, 0]
-    gain_two = gains[:, 1]
-    router_w = full[:, 3 * head_cols + 2 : 3 * head_cols + 2 + experts]
-    gate_low, up_low, down_low, gate_core, up_core, down_core, gate_chip, gate_far = lows
-    up_chip, down_chip = ppermute_ctx(up_low, 2), ppermute_ctx(down_low, 2)
-
-    inputs = tokens_in.astype(jnp.float32)
-    scale_one = lax.rsqrt(jnp.mean(inputs * inputs, axis=1, keepdims=True) + 1e-06)
-    normal_one = inputs * scale_one
     segment_row = segments[:, 0].reshape(1, -1)
     alive = live_tiles(segment_row[0], live_blocks[0])
     pair_heads = share // HEAD
     own_bias = lax.dynamic_slice_in_dim(rel_bias, ctx_index * pair_heads, pair_heads, 1)
     line = jnp.dot(own_bias.T, span_buckets().T, precision=lax.Precision.HIGHEST)
     attended, attended_t, log_sum = run_forward(alive, packed, segment_row, line)
-    attended, up_chip = lax.optimization_barrier((attended, up_chip))
+    attended, up_chip, down_chip = lax.optimization_barrier((attended, up_chip, down_chip))
     expert_weights = [gate_low, gate_chip, gate_core, gate_far]
     expert_weights += [up_low, up_chip, up_core, ppermute_ctx(up_chip, 1)]
     expert_weights += [down_low, down_chip, down_core, ppermute_ctx(down_chip, 1)]
-    attended = attended.reshape(ctx_size, 1, rows_here, share)
-    attended = jnp.broadcast_to(attended, (ctx_size, side_count, rows_here, share))
-    attended = exchange(attended.reshape(-1, rows_here, share), ("ctx", "tensor"))
-    attended = attended.reshape(ctx_size, side_count, rows_here, share)
-    attended = jnp.transpose(attended, (2, 1, 0, 3))
-    attended_low = lax.dynamic_index_in_dim(attended, side, 1, False).reshape(rows_here, head_cols)
-    branch = [
-        contract_cols(attended[:, place].reshape(rows_here, head_cols), out_w[place])
-        for place in range(side_count)
+    hidden_one, norm_two, gates, attended_low = run_attend_out(
+        attended.reshape(ctx_size, rows_here, share), tokens_in, out_w, extras, routes
+    )
+    rows_grad, dots, own_out, mine, other, kept, *given = run_experts(
+        count, ctx_size, norm_two, gates, code_rows, codes, up_slots, expert_weights
+    )
+    outs = [own_out, mine, swap_sides(other)]
+    hidden_grad, branch_grad, heads_grad, small = run_attend_back(
+        rows_grad, dots, gates, routes, extras, hidden_one, cotangent, norm_two, out_w
+    )
+    heads_grad, given[1], given[2] = lax.optimization_barrier((heads_grad, given[1], given[2]))
+    given = [given[0], ppermute_ctx(given[1], 2), ppermute_ctx(given[2], 2)]
+    weight_grads = [
+        kept[number].astype(jnp.float32) + given[number].astype(jnp.float32) for number in range(3)
     ]
-    hidden_one = inputs + (branch[0] + branch[1])
-    scale_two = lax.rsqrt(jnp.mean(hidden_one * hidden_one, axis=1, keepdims=True) + 1e-06)
-    normal_two = hidden_one * scale_two
-    norm_two = (normal_two * gain_two).astype(jnp.bfloat16)
-    logits = dot32(norm_two, router_w)
-    chosen = jnp.sum(jnp.where(picks, logits[:, None, :], 0.0), axis=2)
-    gates = jax.nn.softmax(chosen, axis=1)
-    upstream = cotangent.astype(jnp.float32)
-    norm_grad, dots, outs, kept, given = run_experts(
-        count, ctx_size, norm_two, gates, code_rows, codes, up_slots, expert_weights
-    )
-    half = room // 2
-    theirs = swap_sides(lax.dynamic_slice_in_dim(outs, (1 - side) * half, half, 1))
-    ours = lax.dynamic_slice_in_dim(outs, side * half, half, 1)
-
-    weight_grads = kept.astype(jnp.float32) + ppermute_ctx(given, 2).astype(jnp.float32)
-    gate_dots = jnp.transpose(dots[:TOP])
-    gate_shift = gate_dots - gates * jnp.sum(gate_dots, axis=1, keepdims=True)
-    logit_grad = jnp.sum(jnp.where(picks, gate_shift[:, :, None], 0.0), axis=1)
-    router_f = router_w.astype(jnp.float32)
-    norm_grad = norm_grad + jnp.dot(logit_grad, router_f.T, precision=lax.Precision.HIGHEST)
-    spread_two = norm_grad * gain_two
-    hidden_grad = upstream + scale_two * (
-        spread_two - normal_two * jnp.mean(spread_two * normal_two, axis=1, keepdims=True)
-    )
-    branch_grad = hidden_grad.astype(jnp.bfloat16)
-    own_out_w = lax.dynamic_index_in_dim(out_w, side, 0, False)
-    grad_heads = dot32(branch_grad, own_out_w).astype(jnp.bfloat16)
-    grad_heads = jnp.transpose(grad_heads.reshape(rows_here, ctx_size, share), (1, 0, 2))
-    grad_heads = exchange(grad_heads, "ctx").reshape(-1, share)
-    second_gain = jnp.sum(norm_grad * normal_two, axis=0)[None]
-    router_part = jnp.dot(
-        logit_grad.T, norm_two.astype(jnp.float32), precision=lax.Precision.HIGHEST
-    )
-    small = jnp.concatenate(
-        [jnp.zeros_like(second_gain), second_gain, router_part, jnp.zeros((6 - experts, width))]
-    )
     packed_grad, bias_line = run_backward(
-        alive, packed, segment_row, line, grad_heads, attended_t, log_sum
+        alive, packed, segment_row, line, heads_grad.reshape(-1, share), attended_t, log_sum
     )
     returned = run_return(
         count,
@@ -2085,34 +2391,25 @@
         norm_one,
         tokens_in,
         bias_line,
-        ours,
-        theirs,
+        outs,
         gates,
         codes,
         branch_grad,
         attended_low,
         small,
-    )
-    norm_one_grad, attention_grad, bias_grad, gains_grad, mixture, peer_mixture, out_grad = returned
-    mixture = mixture.astype(jnp.float32) + peer_mixture.astype(jnp.float32)
-    mixed = (hidden_one + mixture).astype(jnp.bfloat16)
-    spread_one = norm_one_grad * gain_one
-    input_grad = hidden_grad + scale_one * (
-        spread_one - normal_one * jnp.mean(spread_one * normal_one, axis=1, keepdims=True)
-    )
-    attention_grad = attention_grad.reshape(ctx_size, rows, 3, share)
-
-    def owned(number):
-        return jnp.transpose(attention_grad[:, :, number], (1, 0, 2)).reshape(rows, head_cols)
-
+        hidden_one,
+        hidden_grad,
+        extras,
+    )
+    mixed, input_grad, query_grad, key_grad, value_grad, bias_grad, gains_grad, out_grad = returned
     gains_grad = lax.dynamic_slice_in_dim(gains_grad, ctx_index % 2 * rows, rows, 1)
     bias_grad = jnp.transpose(bias_grad[:, :pair_heads, :NBUCK], (2, 0, 1))
     return (
         mixed,
-        input_grad.astype(jnp.bfloat16),
-        owned(0),
-        owned(1),
-        owned(2),
+        input_grad,
+        query_grad,
+        key_grad,
+        value_grad,
         out_grad,
         bias_grad.reshape(rel_bias.shape),
         gains_grad[0],

time: 458 us -> 416 us (0.908); the launches traced: 457 us -> 408 us
  waiting for transfers between devices: 32.9 us -> 6.43 us
  other arithmetic: 22.3 us -> 3.54 us
  Pallas kernels: 341 us -> 358 us
  matrix products: 10.7 us -> 1.14 us
  starting transfers between devices: 15 us -> 6.2 us
    pallas_call x0 -> x2, Pallas kernels: none -> 33.7 us  [the longest x1 17.4 us: run_attend_out(): pl.pallas_call(attend_out, out_shape=(jax.ShapeDtypeStruct((here, width),...]
    unnamed x66 -> x102, local copies, waits for them, and re-layouts: 7.94 us -> 26.8 us
    ppermute x5 -> x6, waiting for transfers between devices: 24.2 us -> 6.43 us  [ppermute_ctx(): lax.ppermute(member, 'ctx', [(place, place ^ flip) for place in range(4)])]
    pallas_call x1, Pallas kernels: 138 us -> 121 us  [run_experts(): pl.pallas_call(partial(expert_exchange, count), out_shape=(jax.ShapeDtype...]
    dot_general x7 -> x0, matrix products: 10.2 us -> none  [the longest x1 4.21 us: local_fused(): jnp.dot(logit_grad, router_f.T, precision=lax.Precision.HIGHEST)]
    convert_element_type x6 -> x0, other arithmetic: 8.28 us -> none  [the longest x1 3.77 us: local_fused(): input_grad.astype(jnp.bfloat16)]
    all_to_all x2 -> x0, starting transfers between devices: 7.38 us -> none  [exchange(): return lax.all_to_all(member, axis, split_axis=0, concat_axis=0, tiled=True)]
    ppermute x1, waiting for transfers between devices: 7.08 us -> 0.01 us  [swap_sides(): return lax.ppermute(member, 'tensor', [(0, 1), (1, 0)])]
  transfers between devices with their start and end apart: 8 -> 7, of which waited for: 3 -> 2; matrix products, arithmetic and copies ran while one was open for 7% -> 1% of each run, Pallas kernels for 26% -> 16%
where the time goes in v5:
time: 416 us; the launch traced here: 408 us
  Pallas kernels  358 us (86%)
  local copies, waits for them, and re-layouts  31.7 us (8%)
  waiting for transfers between devices  6.43 us (2%)
  starting transfers between devices  6.2 us (1%)
    pallas_call x1, Pallas kernels, run_experts(): pl.pallas_call(partial(expert_exchange, count), out_shape=(jax.ShapeDtype...  121 us
    pallas_call x1, Pallas kernels, run_gather(): pl.pallas_call(partial(gather_project, count), out_shape=(jax.ShapeDtypeS...  80.6 us
    pallas_call x1, Pallas kernels, run_return(): pl.pallas_call(partial(gradient_return, count), out_shape=(jax.ShapeDtype...  74 us
    unnamed x102, local copies, waits for them, and re-layouts  26.8 us
    pallas_call x1, Pallas kernels, run_backward(): pl.pallas_call(attention_backward, out_shape=(jax.ShapeDtypeStruct((lengt...  26.7 us
    pallas_call x1, Pallas kernels, run_forward(): pl.pallas_call(attention_forward, out_shape=(jax.ShapeDtypeStruct((length...  22.1 us
    pallas_call x1, Pallas kernels, run_attend_out(): pl.pallas_call(attend_out, out_shape=(jax.ShapeDtypeStruct((here, width),...  17.4 us
    pallas_call x1, Pallas kernels, run_attend_back(): pl.pallas_call(attend_back, out_shape=(jax.ShapeDtypeStruct((here, width)...  16.3 us
  transfers between devices with their start and end apart: 7, of which 2 were waited for; matrix products, arithmetic and copies ran while one was open for 1% of the time, Pallas kernels for 16%

profile of v5, /device:TPU:0, one launch (start us, length us, event | category | flops | bytes accessed | tf_op | source)
XLA Modules:
  0.0 408.1 jit_solution(12584792614935876226)
XLA Ops:
  0.6 1.4 copy.37.router
  2.0 1.6 copy.38.routes
  3.6 1.2 pad_maximum_fusion.gains
  4.8 80.6 %gather_project.1 = (bf16[1024,1664]{1,0:T(8,128)(2,1)}, bf16[4,512,384]{2,1,0:T(8,128)(2,1)}, bf16[512,1024]{1,0:T(8,128)(2,1)}, f32[4,8,512]{2,1,0:T(8,128)}, ...) custom-call(f32[64,512]{1,0:T(8,128)} %w_query.1, ...), custom_call_target="tpu_custom_call" | custom-call | flops 60000002048 | tf_op jit(solution)/shard_map/gather_project/pallas_call | solution.py:1342
  85.5 3.0 collective-permute-start
  90.5 1.1 fusion.3.line
  91.6 1.4 copy-done.6
  93.0 22.1 %attention_forward.1 = (bf16[2048,128]{1,0:T(8,128)(2,1)S(1)}, f32[128,2048]{1,0:T(8,128)S(1)}, f32[8,2048]{1,0:T(8,128)S(1)}) custom-call(s32[64]{0:T(128)S(1)} %and_convert_fusion.alive, bf16[2048,384]{1,0:T(8,128)(2,1)S(1)} %bitcast.42, f32[1,2048]{1,0:T(1,128)S(1)} %bitcast.40, f32[2,1024]{1,0:T(2,128)S(1)} %fusion.3.line), custom_call_target="tpu_custom_call" | custom-call | flops 20000000000 | tf_op jit(solution)/shard_map/attention_forward/pallas_call | solution.py:290
  117.4 2.0 collective-permute-done.1.down_chip
  119.9 1.6 copy-done.13
  121.5 17.4 %attend_out.1 = (f32[512,1024]{1,0:T(8,128)S(1)}, bf16[512,1024]{1,0:T(8,128)(2,1)S(1)}, f32[512,2]{1,0:T(8,128)S(1)}, bf16[512,512]{1,0:T(8,128)(2,1)S(1)}) custom-call(bf16[4,512,128]{2,1,0:T(8,128)(2,1)S(1)} %bitcast.45, bf16[512,1024]{1,0:T(8,128)(2,1)S(1)} %copy-done.5, bf16[2,1024,512]{2,1,0:T(8,128)(2,1)S(1)} %copy-done.13, ...), custom_call_target="tpu_custom_call" | custom-call | flops 24999999488 | tf_op jit(solution)/shard_map/attend_out/pallas_call | solution.py:1480
  138.9 1.3 copy-done.14
  144.5 120.7 %expert_exchange.1 = (f32[512,1024]{1,0:T(8,128)}, f32[8,512]{1,0:T(8,128)}, bf16[384,1024]{1,0:T(8,128)(2,1)}, bf16[3,192,1024]{2,1,0:T(8,128)(2,1)}, bf16[3,19...) custom-call(bf16[512,1024]{1,0:T(8,128)(2,1)} %copy-done.16, ...), custom_call_target="tpu_custom_call" | custom-call | flops 109999996928 | tf_op jit(solution)/shard_map/expert_exchange/pallas_call | solution.py:888
  266.1 1.2 copy-done.4
  267.3 1.2 copy-done.17
  271.3 16.3 %attend_back.1 = (f32[512,1024]{1,0:T(8,128)}, bf16[512,1024]{1,0:T(8,128)(2,1)S(1)}, bf16[4,512,128]{2,1,0:T(8,128)(2,1)S(1)}, f32[8,1024]{1,0:T(8,128)S(1)}) custom-call(f32[512,1024]{1,0:T(8,128)} %get-tuple-element.87.rows_grad, f32[8,512]{1,0:T(8,128)S(1)} %copy-done.28, f32[512,2]{1,0:T(8,128)S(1)} %copy-done.24, s32[512,2]{1,0:T(8,128)S(1)} %copy-done.1, ...), custom_call_target="tpu_custom_call" | custom-call | flops 20000000000 | tf_op jit(solution)/shard_map/attend_back/pallas_call | solution.py:1587
  287.6 1.0 collective-permute-start.5
  288.7 1.1 collective-permute-start.6
  290.3 26.7 %attention_backward.1 = (bf16[2048,384]{1,0:T(8,128)(2,1)S(1)}, f32[8,1024]{1,0:T(8,128)S(1)}) custom-call(s32[64]{0:T(128)S(1)} %copy-done.10, bf16[2048,384]{1,0:T(8,128)(2,1)S(1)} %bitcast.43, f32[1,2048]{1,0:T(1,128)S(1)} %bitcast.41, f32[2,1024]{1,0:T(2,128)S(1)} %copy-done.12, bf16[2048,128]{1,0:T(8,128)(2,1)S(1)} %bitcast.46, ...), custom_call_target="tpu_custom_call" | custom-call | flops 25999998976 | tf_op jit(solution)/shard_map/attention_backward/pallas_call | solution.py:316
  317.1 4.4 %collective-permute-done.6 = bf16[256,1408]{1,0:T(8,128)(2,1)S(1)} collective-permute-done((bf16[256,1408]{1,0:T(8,128)(2,1)S(1)}, bf16[256,1408]{1,0:T(8,128)(2,1)S(1)}, u32[]{:S(2)}, u32[]{:S(2)}) %collective-permute-start.6) | collective-permute-done | bytes 720928 | tf_op jit(solution)/shard_map/ppermute | solution.py:2310
  321.5 2.2 fusion
  324.7 74.0 %gradient_return.1 = (bf16[512,1024]{1,0:T(8,128)(2,1)}, bf16[512,1024]{1,0:T(8,128)(2,1)}, f32[64,512]{1,0:T(8,128)}, f32[64,512]{1,0:T(8,128)}, f32[64,512]{1,...) custom-call(bf16[4,512,384]{2,1,0:T(8,128)(2,1)} %bitcast.44, ...), custom_call_target="tpu_custom_call" | custom-call | flops 44999999488 | tf_op jit(solution)/shard_map/gradient_return/pallas_call | solution.py:1991
  400.7 1.3 slice.33
  402.0 2.3 copy.53
  (120 shorter events, 19.7 us)
Async XLA Ops:
  4.8 83.7 %copy-start.37 = (s32[1,4,4]{2,1,0:T(4,128)S(1)}, s32[1,4,4]{2,1,0:T(4,128)}, u32[]{:S(2)}) copy-start(s32[1,4,4]{2,1,0:T(4,128)} %param.19) | copy-start | bytes 196
  85.5 31.9 %collective-permute-start = (bf16[256,1408]{1,0:T(8,128)(2,1)}, bf16[256,1408]{1,0:T(8,128)(2,1)S(1)}, u32[]{:S(2)}, u32[]{:S(2)}) collective-permute-start(bf16[256,1408]{1,0:T(8,128)(2,1)} %get-tuple-element.69.up_own), channel_id=1, source_target_pairs={{0,4},{2,6},{4,0},{6,2},{1,5},{3,7},{5,1},{7,3},{8,12},{10,14},{12... | collective-permute-start | bytes 2162696 | tf_op jit(solution)/shard_map/ppermute | solution.py:2310
  88.4 31.0 %collective-permute-start.1 = (bf16[256,1408]{1,0:T(8,128)(2,1)}, bf16[256,1408]{1,0:T(8,128)(2,1)S(1)}, u32[]{:S(2)}, u32[]{:S(2)}) collective-permute-start(bf16[256,1408]{1,0:T(8,128)(2,1)} %get-tuple-element.70.down_own), channel_id=1, source_target_pairs={{0,4},{2,6},{4,0},{6,2},{1,5},{3,7},{5,1},{7,3},{8,12},{10,14},{12... | collective-permute-start | bytes 2162696 | tf_op jit(solution)/shard_map/ppermute | solution.py:2310
  90.0 25.1 %copy-start.2 = (f32[4,1,512]{2,1,0:T(1,128)}, f32[4,1,512]{2,1,0:T(1,128)S(1)}, u32[]{:S(2)}) copy-start(f32[4,1,512]{2,1,0:T(1,128)S(1)} %get-tuple-element.122) | copy-start | bytes 24580
  93.0 26.9 %copy-start = (s32[512,2]{1,0:T(8,128)S(1)}, s32[512,2]{1,0:T(8,128)}, u32[]{:S(2)}) copy-start(s32[512,2]{1,0:T(8,128)} %copy.38.routes) | copy-start | bytes 12292
  93.0 26.9 %copy-start.5 = (bf16[512,1024]{1,0:T(8,128)(2,1)S(1)}, bf16[512,1024]{1,0:T(8,128)(2,1)}, u32[]{:S(2)}) copy-start(bf16[512,1024]{1,0:T(8,128)(2,1)} %tokens.5) | copy-start | bytes 3145732
  93.0 26.9 %copy-start.21 = (bf16[1024,128]{1,0:T(8,128)(2,1)S(1)}, bf16[1024,128]{1,0:T(8,128)(2,1)}, u32[]{:S(2)}) copy-start(bf16[1024,128]{1,0:T(8,128)(2,1)} %get-tuple-element.73.extras) | copy-start | bytes 786436
  117.4 21.5 %copy-start.40 = (bf16[256,1408]{1,0:T(8,128)(2,1)}, bf16[256,1408]{1,0:T(8,128)(2,1)S(1)}, u32[]{:S(2)}) copy-start(bf16[256,1408]{1,0:T(8,128)(2,1)S(1)} %collective-permute-done.up_chip) | copy-start | bytes 2162692
  119.4 19.5 %copy-start.41 = (bf16[256,1408]{1,0:T(8,128)(2,1)}, bf16[256,1408]{1,0:T(8,128)(2,1)S(1)}, u32[]{:S(2)}) copy-start(bf16[256,1408]{1,0:T(8,128)(2,1)S(1)} %collective-permute-done.1.down_chip) | copy-start | bytes 2162692
  119.4 23.3 %collective-permute-start.2 = (bf16[256,1408]{1,0:T(8,128)(2,1)S(1)}, bf16[256,1408]{1,0:T(8,128)(2,1)S(1)}, u32[]{:S(2)}, u32[]{:S(2)}) collective-permute-start(bf16[256,1408]{1,0:T(8,128)(2,1)S(1)} %collective-permute-done.up_chip), channel_id=1, source_target_pairs={{0,2},{2,0},{4,6},{6,4},{1,3},{3,1},{5,7},{7,5},{8,10},{10,8},{12,... | collective-permute-start | bytes 2162696 | tf_op jit(solution)/shard_map/ppermute | solution.py:2310
  119.4 23.3 %collective-permute-start.3 = (bf16[256,1408]{1,0:T(8,128)(2,1)S(1)}, bf16[256,1408]{1,0:T(8,128)(2,1)S(1)}, u32[]{:S(2)}, u32[]{:S(2)}) collective-permute-start(bf16[256,1408]{1,0:T(8,128)(2,1)S(1)} %collective-permute-done.1.down_chip), channel_id=1, source_target_pairs={{0,2},{2,0},{4,6},{6,4},{1,3},{3,1},{5,7},{7,5},{8,10},{10,8},{12,... | collective-permute-start | bytes 2162696 | tf_op jit(solution)/shard_map/ppermute | solution.py:2310
  271.2 19.1 %copy-start.3 = (f32[4,1,512]{2,1,0:T(1,128)S(1)}, f32[4,1,512]{2,1,0:T(1,128)}, u32[]{:S(2)}) copy-start(f32[4,1,512]{2,1,0:T(1,128)} %copy-done.2) | copy-start | bytes 24580
  271.2 19.1 %copy-start.7 = (bf16[4,512,384]{2,1,0:T(8,128)(2,1)S(1)}, bf16[4,512,384]{2,1,0:T(8,128)(2,1)}, u32[]{:S(2)}) copy-start(bf16[4,512,384]{2,1,0:T(8,128)(2,1)} %get-tuple-element.67) | copy-start | bytes 4718596
  271.2 19.1 %copy-start.10 = (s32[64]{0:T(128)S(1)}, s32[64]{0:T(128)}, u32[]{:S(2)}) copy-start(s32[64]{0:T(128)} %copy-done.9) | copy-start | bytes 772
  271.2 19.1 %copy-start.12 = (f32[2,1024]{1,0:T(2,128)S(1)}, f32[2,1024]{1,0:T(2,128)}, u32[]{:S(2)}) copy-start(f32[2,1024]{1,0:T(2,128)} %copy-done.11) | copy-start | bytes 24580
  271.2 19.1 %copy-start.19 = (f32[128,2048]{1,0:T(8,128)S(1)}, f32[128,2048]{1,0:T(8,128)}, u32[]{:S(2)}) copy-start(f32[128,2048]{1,0:T(8,128)} %copy-done.18) | copy-start | bytes 3145732
  271.2 19.1 %copy-start.26 = (f32[8,2048]{1,0:T(8,128)S(1)}, f32[8,2048]{1,0:T(8,128)}, u32[]{:S(2)}) copy-start(f32[8,2048]{1,0:T(8,128)} %copy-done.25) | copy-start | bytes 196612
  287.6 29.5 %copy-start.15 = (bf16[512,1024]{1,0:T(8,128)(2,1)}, bf16[512,1024]{1,0:T(8,128)(2,1)S(1)}, u32[]{:S(2)}) copy-start(bf16[512,1024]{1,0:T(8,128)(2,1)S(1)} %get-tuple-element.103.branch_grad) | copy-start | bytes 3145732
  287.6 29.5 %copy-start.27 = (f32[8,1024]{1,0:T(8,128)}, f32[8,1024]{1,0:T(8,128)S(1)}, u32[]{:S(2)}) copy-start(f32[8,1024]{1,0:T(8,128)S(1)} %get-tuple-element.105.small) | copy-start | bytes 98308
  287.6 29.5 %collective-permute-start.5 = (bf16[256,1408]{1,0:T(8,128)(2,1)S(1)}, bf16[256,1408]{1,0:T(8,128)(2,1)S(1)}, u32[]{:S(2)}, u32[]{:S(2)}) collective-permute-start(bf16[256,1408]{1,0:T(8,128)(2,1)S(1)} %copy-done.43), channel_id=1, source_target_pairs={{0,4},{2,6},{4,0},{6,2},{1,5},{3,7},{5,1},{7,3},{8,12},{10,14},{12... | collective-permute-start | bytes 2162696 | tf_op jit(solution)/shard_map/ppermute | solution.py:2310
  288.7 32.8 %collective-permute-start.6 = (bf16[256,1408]{1,0:T(8,128)(2,1)S(1)}, bf16[256,1408]{1,0:T(8,128)(2,1)S(1)}, u32[]{:S(2)}, u32[]{:S(2)}) collective-permute-start(bf16[256,1408]{1,0:T(8,128)(2,1)S(1)} %copy-done.42), channel_id=1, source_target_pairs={{0,4},{2,6},{4,0},{6,2},{1,5},{3,7},{5,1},{7,3},{8,12},{10,14},{12... | collective-permute-start | bytes 2162696 | tf_op jit(solution)/shard_map/ppermute | solution.py:2310
  289.7 34.0 %collective-permute-start.4 = (bf16[3,192,1024]{2,1,0:T(8,128)(2,1)S(1)}, bf16[3,192,1024]{2,1,0:T(8,128)(2,1)S(1)}, u32[]{:S(2)}, u32[]{:S(2)}) collective-permute-start(bf16[3,192,1024]{2,1,0:T(8,128)(2,1)S(1)} %copy-done.38), channel_id=1, source_target_pairs={{0,1},{1,0},{2,3},{3,2},{4,5},{5,4},{6,7},{7,6},{8,9},{9,8},{10,11... | collective-permute-start | bytes 3538952 | tf_op jit(solution)/shard_map/ppermute | solution.py:2077
  290.3 31.2 %copy-start.30 = (bf16[3,256,1408]{2,1,0:T(8,128)(2,1)S(1)}, bf16[3,256,1408]{2,1,0:T(8,128)(2,1)}, u32[]{:S(2)}) copy-start(bf16[3,256,1408]{2,1,0:T(8,128)(2,1)} %get-tuple-element.115) | copy-start | bytes 6488068
  290.3 31.2 %copy-start.32 = (bf16[256,1408]{1,0:T(8,128)(2,1)S(1)}, bf16[256,1408]{1,0:T(8,128)(2,1)}, u32[]{:S(2)}) copy-start(bf16[256,1408]{1,0:T(8,128)(2,1)} %get-tuple-element.116) | copy-start | bytes 2162692
  (29 other events, 98.1 us)

commit v6 on v5

--- a/solution.py
+++ b/solution.py
@@ -277,6 +277,10 @@
         bias_grad[4 + head : 5 + head, :TILE] = jnp.sum(bias_acc[head, 4], axis=0, keepdims=True)
 
 
+def in_hbm(count):
+    return [pl.BlockSpec(memory_space=pl.ANY)] * count
+
+
 def estimate(micros):
     return pl.CostEstimate(flops=int(micros * 1e9), bytes_accessed=0, transcendentals=0)
 
@@ -304,7 +308,7 @@
             pltpu.VMEM((8, TILE), jnp.float32),
             pltpu.VMEM((2, HEAD + 16, TILE), jnp.float32),
         ],
-        compiler_params=pltpu.CompilerParams(vmem_limit_bytes=40 * 2**20),
+        compiler_params=pltpu.CompilerParams(vmem_limit_bytes=67043328),
         cost_estimate=estimate(20),
         name="attention_forward",
     )(alive, packed, segment, line)
@@ -335,8 +339,8 @@
             pltpu.VMEM((TILE, 128), jnp.float32),
             pltpu.VMEM((TILE, 128), jnp.float32),
         ],
-        compiler_params=pltpu.CompilerParams(vmem_limit_bytes=48 * 2**20),
-        cost_estimate=estimate(26),
+        compiler_params=pltpu.CompilerParams(vmem_limit_bytes=67043328),
+        cost_estimate=estimate(4),
         name="attention_backward",
     )(alive, packed, segment, line, grads, out_t, log_sum)
 
@@ -420,7 +424,7 @@
     gates,
     code_rows,
     code_cols,
-    upstream,
+    upstream_hbm,
     gate_own,
     gate_chip,
     gate_core,
@@ -436,12 +440,16 @@
     row_grad,
     dot_rows,
     own_hbm,
-    mine_hbm,
-    other_hbm,
+    out_first,
+    out_one,
+    out_near,
+    out_two,
+    out_three,
+    out_last,
     kept_hbm,
     gate_given,
-    up_given,
-    down_given,
+    pair_given,
+    upstream,
     gate_w,
     up_w,
     down_w,
@@ -519,6 +527,7 @@
             spot = pl.ds(pl.multiple_of(origins[turn] * deep, deep), deep)
             sem = load_sem.at[4 * number + turn]
             loads.append(pltpu.make_async_copy(source_ref, target.at[spot], sem))
+    loads.append(pltpu.make_async_copy(upstream_hbm, upstream, load_sem.at[12]))
     for load in loads:
         load.start()
     pl.semaphore_wait(barrier, count + 2)
@@ -747,13 +756,19 @@
     weigh(0)
     send_back(count - 1)
     lax.fori_loop(0, count, run_out, 0)
-    stores = [pltpu.make_async_copy(outs.at[own], own_hbm, store_sem.at[0])]
-    for turn in range(1, count):
-        origin = partner(own, turn)
-        for place, (spot, target) in enumerate(((my_half, mine_hbm), (peer_half, other_hbm))):
-            sem = store_sem.at[8 + 2 * turn + place]
-            source_ref = outs.at[origin, spot]
-            stores.append(pltpu.make_async_copy(source_ref, target.at[turn - 1], sem))
+    moves = (
+        (outs.at[own], own_hbm),
+        (outs.at[partner(own, 1), pl.ds(0, half)], out_first),
+        (outs.at[partner(own, 1), pl.ds(half, half)], out_one),
+        (outs.at[partner(own, 2), pl.ds(0, half)], out_near),
+        (outs.at[partner(own, 2), pl.ds(half, half)], out_two),
+        (outs.at[partner(own, 3), pl.ds(0, half)], out_three),
+        (outs.at[partner(own, 3), pl.ds(half, half)], out_last),
+    )
+    stores = []
+    for number, (source_ref, target) in enumerate(moves):
+        sem = store_sem.at[number if number == 0 else 10 + number]
+        stores.append(pltpu.make_async_copy(source_ref, target, sem))
     for store in stores:
         store.start()
     weigh(1)
@@ -844,7 +859,7 @@
             over_chip(number)
         given = core_in.at[number, 1 - chip] if number else chip_in.at[0]
         for place, source_ref in enumerate((core_in.at[number, chip], given)):
-            target = (kept_hbm.at[number], (gate_given, up_given, down_given)[number])[place]
+            target = (kept_hbm.at[number], pair_given.at[number - 1] if number else gate_given)[place]
             sem = store_sem.at[4 + 2 * number + place]
             store = pltpu.make_async_copy(source_ref, target, sem)
             store.start()
@@ -891,14 +906,15 @@
             jax.ShapeDtypeStruct((tokens, width), full),
             jax.ShapeDtypeStruct((8, tokens), full),
             jax.ShapeDtypeStruct((room, width), low),
-            jax.ShapeDtypeStruct((count - 1, half, width), low),
-            jax.ShapeDtypeStruct((count - 1, half, width), low),
+            *[jax.ShapeDtypeStruct((half, width), low)] * 6,
             jax.ShapeDtypeStruct((3, width // ctx_size, hidden), low),
-            *[jax.ShapeDtypeStruct((width // ctx_size, hidden), low)] * 3,
+            jax.ShapeDtypeStruct((width // ctx_size, hidden), low),
+            jax.ShapeDtypeStruct((2, width // ctx_size, hidden), low),
         ),
-        in_specs=in_vmem(5) + [pl.BlockSpec(memory_space=pl.ANY)] * 12,
-        out_specs=tuple(in_vmem(2) + [pl.BlockSpec(memory_space=pl.ANY)] * 7),
+        in_specs=in_vmem(4) + [pl.BlockSpec(memory_space=pl.ANY)] * 13,
+        out_specs=tuple(in_vmem(2) + [pl.BlockSpec(memory_space=pl.ANY)] * 10),
         scratch_shapes=[
+            pltpu.VMEM(upstream.shape, low),
             pltpu.VMEM((width, hidden), low),
             pltpu.VMEM((width, hidden), low),
             pltpu.VMEM((width, hidden), low),
@@ -922,8 +938,8 @@
             pltpu.VMEM((2, 8, tokens), full),
             pltpu.VMEM((3, 2, width // ctx_size, hidden), low),
             pltpu.VMEM((1, width // ctx_size, hidden), low),
-            dma((12,)),
-            dma((16,)),
+            dma((13,)),
+            dma((18,)),
             dma((count,)),
             dma((count,)),
             dma((count,)),
@@ -951,13 +967,24 @@
     )(norm, gates, code_rows, code_cols, upstream, *weights)
 
 
+def begin(pairs, sems):
+    copies = [
+        pltpu.make_async_copy(source, target, sems.at[number])
+        for number, (source, target) in enumerate(pairs)
+    ]
+    for copy in copies:
+        copy.start()
+    return copies
+
+
 def gather_project(
     count,
     w_query,
     w_key,
     w_value,
     w_out,
-    gains,
+    first_gain,
+    second_gain,
     router,
     tokens,
     segment_ids,
@@ -1044,18 +1071,18 @@
         copy.start()
         stores.append(copy)
 
-    lane = lax.broadcasted_iota(jnp.int32, (rows, LANES), 1)
-    column = jnp.transpose(jnp.concatenate([gains[...], jnp.zeros((6, rows))], axis=0))
-    extra = jnp.where(lane == 0, column[:, 0:1], 0.0)
-    extra = jnp.where(lane == 1, column[:, 1:2], extra)
-    for expert in range(router.shape[1]):
-        extra = jnp.where(lane == 2 + expert, router[:, expert : expert + 1], extra)
+    experts = router.shape[0]
+    extra = jnp.concatenate(
+        [first_gain[...], second_gain[...], router[...], jnp.zeros((6 - experts, rows))], axis=0
+    )
+    weight[:, ctx_size * share :] = jnp.zeros((rows, LANES), jnp.bfloat16)
+    extra_columns = slice(ctx_size * share, ctx_size * share + 8)
+    weight[:, extra_columns] = jnp.transpose(extra).astype(jnp.bfloat16)
     for place in range(ctx_size):
         for number, member in enumerate((w_query, w_key, w_value)):
             target = slice(place * share + number * LANES, place * share + (number + 1) * LANES)
             found = member[:, place * LANES : (place + 1) * LANES]
             weight[:, target] = found.astype(jnp.bfloat16)
-    weight[:, ctx_size * share :] = extra.astype(jnp.bfloat16)
     out_weight[...] = w_out[...].astype(jnp.bfloat16)
     segment[...] = jnp.broadcast_to(segment_ids[...].astype(jnp.float32), segment.shape)
     greet(
@@ -1147,8 +1174,11 @@
     segments[ctx] = segment[...]
 
     lane = lax.broadcasted_iota(jnp.int32, (here, LANES), 1).astype(jnp.float32)
-    first = routes[:, 0:1].astype(jnp.float32)
-    second = routes[:, 1:2].astype(jnp.float32)
+    named = jnp.concatenate([routes[...].astype(jnp.float32), jnp.zeros((6, here))], axis=0)
+    columns = jnp.transpose(named)
+    first, second = columns[:, 0:1], columns[:, 1:2]
+    codes[:, 2:3] = first
+    codes[:, 3:4] = second
     named = jnp.where((first == lane) | (second == lane), 1.0, 0.0).astype(jnp.bfloat16)
     later = lax.broadcasted_iota(jnp.int32, (here, here), 0)
     before = later > lax.broadcasted_iota(jnp.int32, (here, here), 1)
@@ -1333,7 +1363,7 @@
 
 def run_gather(count, ctx_size, room, members, experts):
     rows, head_columns = members[0].shape
-    here, width = members[6].shape
+    here, width = members[7].shape
     share = 3 * head_columns // ctx_size
     columns = ctx_size * share + LANES
     dma = pltpu.SemaphoreType.DMA
@@ -1349,11 +1379,11 @@
             jax.ShapeDtypeStruct((2, rows * count * ctx_size, head_columns), low),
             jax.ShapeDtypeStruct((count, room, width), low),
             *[jax.ShapeDtypeStruct((deep, hidden), low)] * 8,
-            jax.ShapeDtypeStruct((here, 2), jnp.float32),
+            jax.ShapeDtypeStruct((here, 4), jnp.float32),
             jax.ShapeDtypeStruct((8, here), jnp.float32),
             jax.ShapeDtypeStruct((rows * count * ctx_size, LANES), low),
         ),
-        in_specs=in_vmem(10) + [pl.BlockSpec(memory_space=pl.ANY)] * 3,
+        in_specs=in_vmem(11) + [pl.BlockSpec(memory_space=pl.ANY)] * 3,
         out_specs=tuple(
             pl.BlockSpec(memory_space=pltpu.VMEM if number in (1, 3, 14, 15, 16) else pl.ANY)
             for number in range(17)
@@ -1400,7 +1430,7 @@
             dma((12,)),
         ],
         compiler_params=pltpu.CompilerParams(
-            collective_id=1, has_side_effects=True, vmem_limit_bytes=60 * 2**20
+            collective_id=1, has_side_effects=True, vmem_limit_bytes=67043328
         ),
         cost_estimate=estimate(60),
         name="gather_project",
@@ -1409,17 +1439,24 @@
 
 def attend_out(
     attended,
+    tokens_hbm,
+    out_hbm,
+    extras_hbm,
+    codes,
+    hidden_hbm,
+    norm_hbm,
+    gates,
+    low_hbm,
+    gathered,
     tokens,
     out_w,
     extras,
-    routes,
     hidden_one,
     norm_two,
-    gates,
-    attended_low,
-    gathered,
     send,
     recv,
+    load_sem,
+    store_sem,
 ):
     own, ctx, side, chip, core = places()
     here, width = tokens.shape
@@ -1431,8 +1468,17 @@
         if (other, step) != (0, 3)
     ]
     peers = peers[:2] + peers[3:5] + peers[2:3] + peers[5:]
+    columns = pl.ds(pl.multiple_of(ctx * heads, heads), heads)
+    loads = begin(
+        (
+            (attended.at[ctx], gathered.at[side, :, columns]),
+            (tokens_hbm, tokens),
+            (out_hbm, out_w),
+            (extras_hbm, extras),
+        ),
+        load_sem,
+    )
     greet([(own, place, which) for place, which in peers])
-    columns = pl.ds(pl.multiple_of(ctx * heads, heads), heads)
 
     def copy(number):
         place, which = peers[number]
@@ -1446,34 +1492,39 @@
 
     for number in range(len(peers)):
         copy(number).start()
-    gathered[side, :, columns] = attended[ctx]
+    for load in loads:
+        load.wait()
     for place, which in peers:
         spot = gathered.at[which, :, pl.ds(pl.multiple_of(place * heads, heads), heads)]
         remote(
             spot, spot, send.at[0], recv.at[which, place], (own, place, which)
         ).wait_recv()
-    attended_low[...] = gathered[side]
+    stores = begin(((gathered.at[side], low_hbm),), store_sem)
     hidden = tokens[...].astype(jnp.float32) + (
         dot_last(gathered[0], out_w[0]) + dot_last(gathered[1], out_w[1])
     )
     hidden_one[...] = hidden
+    stores += begin(((hidden_one, hidden_hbm),), store_sem.at[pl.ds(1, 1)])
     scale = lax.rsqrt(jnp.mean(hidden * hidden, axis=1, keepdims=True) + 1e-06)
     gain = jnp.transpose(extras[...].astype(jnp.float32))[1:2, :]
     norm = (hidden * scale * gain).astype(jnp.bfloat16)
     norm_two[...] = norm
+    stores += begin(((norm_two, norm_hbm),), store_sem.at[pl.ds(2, 1)])
     logits = dot32(norm, extras[...])
-    lane = lax.broadcasted_iota(jnp.int32, (here, LANES), 1)
-    first = jnp.sum(jnp.where(lane == routes[:, 0:1] + 2, logits, 0.0), axis=1, keepdims=True)
-    second = jnp.sum(jnp.where(lane == routes[:, 1:2] + 2, logits, 0.0), axis=1, keepdims=True)
+    lane = lax.broadcasted_iota(jnp.int32, (here, LANES), 1).astype(jnp.float32)
+    first = jnp.sum(jnp.where(lane == codes[:, 2:3] + 2.0, logits, 0.0), axis=1, keepdims=True)
+    second = jnp.sum(jnp.where(lane == codes[:, 3:4] + 2.0, logits, 0.0), axis=1, keepdims=True)
     highest = jnp.maximum(first, second)
     first, second = jnp.exp(first - highest), jnp.exp(second - highest)
     gates[:, 0:1] = first / (first + second)
     gates[:, 1:2] = second / (first + second)
     for number in range(len(peers)):
         copy(number).wait_send()
-
-
-def run_attend_out(attended, tokens, out_w, extras, routes):
+    for store in stores:
+        store.wait()
+
+
+def run_attend_out(attended, tokens, out_w, extras, codes):
     here, width = tokens.shape
     heads = out_w.shape[2]
     low, wide = jnp.bfloat16, jnp.float32
@@ -1485,26 +1536,43 @@
             jax.ShapeDtypeStruct((here, 2), wide),
             jax.ShapeDtypeStruct((here, heads), low),
         ),
-        in_specs=in_vmem(5),
-        out_specs=tuple(in_vmem(4)),
+        in_specs=in_hbm(4) + in_vmem(1),
+        out_specs=tuple(in_hbm(2) + in_vmem(1) + in_hbm(1)),
         scratch_shapes=[
             pltpu.VMEM((2, here, heads), low),
+            pltpu.VMEM(tokens.shape, low),
+            pltpu.VMEM(out_w.shape, low),
+            pltpu.VMEM(extras.shape, low),
+            pltpu.VMEM((here, width), wide),
+            pltpu.VMEM((here, width), low),
             pltpu.SemaphoreType.DMA((7,)),
             pltpu.SemaphoreType.DMA((2, 4)),
+            pltpu.SemaphoreType.DMA((4,)),
+            pltpu.SemaphoreType.DMA((3,)),
         ],
         compiler_params=pltpu.CompilerParams(
-            collective_id=4, has_side_effects=True, vmem_limit_bytes=40 * 2**20
+            collective_id=4, has_side_effects=True, vmem_limit_bytes=67043328
         ),
         cost_estimate=estimate(25),
         name="attend_out",
-    )(attended, tokens, out_w, extras, routes)
+    )(attended, tokens, out_w, extras, codes)
 
 
 def attend_back(
-    rows_grad,
+    rows_hbm,
     dot_rows,
     gates,
-    routes,
+    codes,
+    extras_hbm,
+    one_hbm,
+    cotangent_hbm,
+    norm_hbm,
+    out_hbm,
+    hidden_hbm,
+    branch_hbm,
+    heads_grad,
+    small,
+    rows_grad,
     extras,
     hidden_one,
     cotangent,
@@ -1512,23 +1580,36 @@
     out_w,
     hidden_grad,
     branch_grad,
-    heads_grad,
-    small,
     outgoing,
     send,
     recv,
+    load_sem,
+    store_sem,
 ):
     own, ctx, side, chip, core = places()
     here, width = hidden_one.shape
     heads = heads_grad.shape[2]
+    loads = begin(
+        (
+            (rows_hbm, rows_grad),
+            (extras_hbm, extras),
+            (one_hbm, hidden_one),
+            (cotangent_hbm, cotangent),
+            (out_hbm.at[side], out_w),
+            (norm_hbm, norm_two),
+        ),
+        load_sem,
+    )
     greet([(own, across(chip, core, step), side) for step in range(3)])
-    lane = lax.broadcasted_iota(jnp.int32, (here, LANES), 1)
+    lane = lax.broadcasted_iota(jnp.int32, (here, LANES), 1).astype(jnp.float32)
     dots = jnp.transpose(dot_rows[...])
     total = dots[:, 0:1] + dots[:, 1:2]
     logit_grad = jnp.zeros((here, LANES), jnp.float32)
     for choice in range(TOP):
         shift = dots[:, choice : choice + 1] - gates[:, choice : choice + 1] * total
-        logit_grad = jnp.where(lane == routes[:, choice : choice + 1] + 2, shift, logit_grad)
+        logit_grad = jnp.where(lane == codes[:, 2 + choice : 3 + choice] + 2.0, shift, logit_grad)
+    for load in loads:
+        load.wait()
     extra = extras[...].astype(jnp.float32)
     norm_grad = rows_grad[...] + lax.dot_general(
         logit_grad,
@@ -1546,10 +1627,11 @@
     )
     hidden_grad[...] = found
     branch_grad[...] = found.astype(jnp.bfloat16)
+    stores = begin(((hidden_grad, hidden_hbm), (branch_grad, branch_hbm)), store_sem)
 
     def project(place):
         columns = pl.ds(pl.multiple_of(place * heads, heads), heads)
-        return dot32(branch_grad[...], out_w[side, :, columns]).astype(jnp.bfloat16)
+        return dot32(branch_grad[...], out_w[:, columns]).astype(jnp.bfloat16)
 
     def copy(step):
         place = across(chip, core, step)
@@ -1560,7 +1642,8 @@
     for step in range(3):
         outgoing[step] = project(across(chip, core, step))
         copy(step).start()
-    heads_grad[ctx] = project(ctx)
+    outgoing[3] = project(ctx)
+    stores += begin(((outgoing.at[3], heads_grad.at[ctx]),), store_sem.at[pl.ds(2, 1)])
     gain_row = jnp.sum(norm_grad * normal, axis=0, keepdims=True)
     routed = jnp.dot(
         jnp.transpose(logit_grad),
@@ -1576,10 +1659,12 @@
         remote(spot, spot, send.at[0], recv.at[place], (own, place, side)).wait_recv()
     for step in range(3):
         copy(step).wait_send()
+    for store in stores:
+        store.wait()
 
 
 def run_attend_back(
-    rows_grad, dot_rows, gates, routes, extras, hidden_one, cotangent, norm_two, out_w
+    rows_grad, dot_rows, gates, codes, extras, hidden_one, cotangent, norm_two, out_w
 ):
     here, width = hidden_one.shape
     low, wide = jnp.bfloat16, jnp.float32
@@ -1592,19 +1677,29 @@
             jax.ShapeDtypeStruct((4, here, heads), low),
             jax.ShapeDtypeStruct((8, width), wide),
         ),
-        in_specs=in_vmem(9),
-        out_specs=tuple(in_vmem(4)),
+        in_specs=in_hbm(1) + in_vmem(3) + in_hbm(5),
+        out_specs=tuple(in_hbm(3) + in_vmem(1)),
         scratch_shapes=[
-            pltpu.VMEM((3, here, heads), low),
+            pltpu.VMEM((here, width), wide),
+            pltpu.VMEM(extras.shape, low),
+            pltpu.VMEM((here, width), wide),
+            pltpu.VMEM((here, width), low),
+            pltpu.VMEM((here, width), low),
+            pltpu.VMEM(out_w.shape[1:], low),
+            pltpu.VMEM((here, width), wide),
+            pltpu.VMEM((here, width), low),
+            pltpu.VMEM((4, here, heads), low),
             pltpu.SemaphoreType.DMA((3,)),
             pltpu.SemaphoreType.DMA((4,)),
+            pltpu.SemaphoreType.DMA((6,)),
+            pltpu.SemaphoreType.DMA((3,)),
         ],
         compiler_params=pltpu.CompilerParams(
-            collective_id=5, has_side_effects=True, vmem_limit_bytes=48 * 2**20
+            collective_id=5, has_side_effects=True, vmem_limit_bytes=67043328
         ),
-        cost_estimate=estimate(20),
+        cost_estimate=estimate(4),
         name="attend_back",
-    )(rows_grad, dot_rows, gates, routes, extras, hidden_one, cotangent, norm_two, out_w)
+    )(rows_grad, dot_rows, gates, codes, extras, hidden_one, cotangent, norm_two, out_w)
 
 
 def gradient_return(
@@ -1615,8 +1710,12 @@
     tokens,
     bias_line,
     own_hbm,
-    mine,
-    theirs,
+    first_hbm,
+    one_out_hbm,
+    near_out_hbm,
+    two_out_hbm,
+    three_out_hbm,
+    last_hbm,
     gates,
     codes,
     branch_grad,
@@ -1636,11 +1735,9 @@
     mixture,
     mixture_in,
     full,
-    own_out,
+    outs,
     hidden_one,
     hidden_grad,
-    mix_out,
-    mix_in,
     incoming,
     norm_t,
     outgoing,
@@ -1675,8 +1772,7 @@
     bias_send,
     bias_recv,
     mixture_sem,
-    mix_send,
-    mix_recv,
+    mix_sem,
     load_sem,
 ):
     own, ctx, side, chip, core = places()
@@ -1694,7 +1790,18 @@
         for turn in range(4)
         if (step, turn) != (0, 3)
     ]
-    pairs = ((full_hbm, full), (own_hbm, own_out), (grad_hbm, hidden_grad), (one_hbm, hidden_one))
+    room, half = outs.shape[1], last_hbm.shape[0]
+    pairs = (
+        (full_hbm, full),
+        (own_hbm, outs.at[0]),
+        (grad_hbm, hidden_grad),
+        (one_hbm, hidden_one),
+        (first_hbm, outs.at[1, pl.ds(0, half)]),
+        (one_out_hbm, outs.at[1, pl.ds(half, half)]),
+        (near_out_hbm, outs.at[2, pl.ds(0, half)]),
+        (two_out_hbm, outs.at[2, pl.ds(half, half)]),
+        (three_out_hbm, outs.at[3, pl.ds(0, half)]),
+    )
     loads = [
         pltpu.make_async_copy(source, target, load_sem.at[number])
         for number, (source, target) in enumerate(pairs)
@@ -1728,30 +1835,22 @@
         held = held + jnp.where(codes[:, 1:2] == slots, gates[:, 1:2], 0.0)
         return held.astype(jnp.bfloat16)
 
-    room, half = own_out.shape[0], mine.shape[1]
-
-    def to_tokens(turn):
-        return remote(
-            mix_out.at[turn],
-            mix_in.at[turn],
-            mix_send.at[turn],
-            mix_recv.at[turn],
-            (partner(own, turn + 1), ctx, side),
-        )
-
-    for turn in range(count - 1):
-        mix_out[turn] = (
-            mine[turn].astype(jnp.float32) + theirs[turn].astype(jnp.float32)
-        ).astype(jnp.bfloat16)
-        to_tokens(turn).start()
+    last_copy = remote(
+        last_hbm,
+        outs.at[3, pl.ds(half, half)],
+        mix_sem.at[0],
+        mix_sem.at[1],
+        (partner(own, 3), ctx, side),
+    )
+    last_copy.start()
 
     def mix():
-        loads[1].wait()
-        total = dot32(mixing(own * room, room), own_out[...])
-        for turn in range(count - 1):
-            to_tokens(turn).wait_recv()
-            start = partner(own, turn + 1) * room + side * half
-            total = total + dot32(mixing(start, half), mix_in[turn])
+        for number in (1, 4, 5, 6, 7, 8):
+            loads[number].wait()
+        last_copy.wait_recv()
+        total = jnp.zeros((here, width), jnp.float32)
+        for turn in range(count):
+            total = total + dot32(mixing(partner(own, turn) * room, room), outs[turn])
         mixture[...] = total.astype(jnp.bfloat16)
         mixture_copy.start()
 
@@ -1859,6 +1958,7 @@
     norm_t[...] = jnp.transpose(branch_grad[...].astype(jnp.float32)).astype(jnp.bfloat16)
     contract(groups)
     norm_t[...] = jnp.transpose(norm[...].astype(jnp.float32)).astype(jnp.bfloat16)
+    over_chip(groups)
 
     def to_side(piece):
         return remote(
@@ -1874,17 +1974,20 @@
     normal = values * scale
     first_gain = jnp.transpose(extras[...].astype(jnp.float32))[0:1, :]
     loads[0].wait()
-    for piece in range(halves):
+
+    def landed(piece):
+        for step in range(3):
+            place = across(chip, core, step)
+            target = incoming.at[place, pl.ds(piece * part, part)]
+            remote(
+                target, target, grad_send.at[0, 0], grad_recv.at[place, piece], pair
+            ).wait_recv()
+
+    def send_side(piece):
         spot = pl.ds(piece * part, part)
         total = jnp.zeros((part, width), jnp.float32)
-        for step in (3, 2, 0, 1):
-            place = across(chip, core, step)
-            if step != 3:
-                target = incoming.at[place, spot]
-                remote(
-                    target, target, grad_send.at[0, 0], grad_recv.at[place, piece], pair
-                ).wait_recv()
-            columns = pl.ds(pl.multiple_of(place * share, LANES), share)
+        for place in range(ctx_size):
+            columns = slice(place * share, (place + 1) * share)
             total = total + dot_last(incoming[place, spot, :], full[:, columns])
         side_out[piece] = total.astype(jnp.bfloat16)
         to_side(piece).start()
@@ -1915,23 +2018,27 @@
             to_bias(number).start()
         bias_in[own, ctx] = message(own, ctx)
 
-    over_chip(groups)
-    for moment in range(groups + 3):
-        if moment < groups:
-            contract(moment)
-        if moment == 0:
-            over_line(groups)
-        if 0 <= moment - 1 < groups:
-            over_chip(moment - 1)
-        if 0 <= moment - 2 < groups:
-            over_line(moment - 2)
-        if moment == 2:
-            mix()
-        if moment == groups:
-            finish_sides()
-            collect(groups)
-        if 0 <= moment - 3 < groups:
-            collect(moment - 3)
+    landed(0)
+    send_side(0)
+    landed(1)
+    contract(0)
+    send_side(1)
+    over_chip(0)
+    contract(1)
+    contract(2)
+    over_chip(1)
+    mix()
+    contract(3)
+    over_chip(2)
+    over_line(groups)
+    over_chip(3)
+    over_line(0)
+    over_line(1)
+    over_line(2)
+    over_line(3)
+    finish_sides()
+    for group in (groups, 0, 1, 2, 3):
+        collect(group)
 
     for number, (shard, place, _) in enumerate(others):
         spot = bias_in.at[shard, place]
@@ -1946,8 +2053,7 @@
 
     mixture_copy.wait()
     loads[3].wait()
-    for turn in range(count - 1):
-        to_tokens(turn).wait_send()
+    last_copy.wait_send()
     mixed[...] = (
         hidden_one[...] + (mixture[...].astype(jnp.float32) + mixture_in[...].astype(jnp.float32))
     ).astype(jnp.bfloat16)
@@ -1999,19 +2105,17 @@
             jax.ShapeDtypeStruct((rows, out_columns), wide),
         ),
         in_specs=[
-            pl.BlockSpec(memory_space=pl.ANY if number in (1, 5, 13, 14) else pltpu.VMEM)
-            for number in range(16)
+            pl.BlockSpec(memory_space=pl.ANY if number in (1, 5, 6, 7, 8, 9, 10, 11, 17, 18) else pltpu.VMEM)
+            for number in range(20)
         ],
         out_specs=tuple(in_vmem(8)),
         scratch_shapes=[
             pltpu.VMEM((here, width), low),
             pltpu.VMEM((here, width), low),
             pltpu.VMEM(full.shape, low),
-            pltpu.VMEM(outs[0].shape, low),
+            pltpu.VMEM((count,) + outs[0].shape, low),
             pltpu.VMEM((here, width), wide),
             pltpu.VMEM((here, width), wide),
-            pltpu.VMEM(outs[1].shape, low),
-            pltpu.VMEM(outs[1].shape, low),
             pltpu.VMEM((ctx_size, here, share), low),
             pltpu.VMEM((width, here), low),
             pltpu.VMEM((ctx_size, count * 2, 2, rows, columns), low),
@@ -2046,12 +2150,11 @@
             dma((15,)),
             dma((count, ctx_size)),
             dma((2,)),
-            dma((3,)),
-            dma((3,)),
-            dma((4,)),
+            dma((2,)),
+            dma((9,)),
         ],
         compiler_params=pltpu.CompilerParams(
-            collective_id=2, has_side_effects=True, vmem_limit_bytes=60 * 2**20
+            collective_id=2, has_side_effects=True, vmem_limit_bytes=67043328
         ),
         cost_estimate=estimate(45),
         name="gradient_return",
@@ -2341,12 +2444,13 @@
         w_key,
         w_value,
         w_out,
-        jnp.stack([attn_gain, ffn_gain]),
-        router,
+        attn_gain[None],
+        ffn_gain[None],
+        router.T,
         tokens_in,
         segment_ids,
         cotangent,
-        routes,
+        routes.T,
     )
     full, packed, norm_one, segments, out_w, up_slots, *lows = run_gather(
         count, ctx_size, room, members, (w_gate[0], w_up[0], w_down[0])
@@ -2367,17 +2471,21 @@
     expert_weights += [up_low, up_chip, up_core, ppermute_ctx(up_chip, 1)]
     expert_weights += [down_low, down_chip, down_core, ppermute_ctx(down_chip, 1)]
     hidden_one, norm_two, gates, attended_low = run_attend_out(
-        attended.reshape(ctx_size, rows_here, share), tokens_in, out_w, extras, routes
-    )
-    rows_grad, dots, own_out, mine, other, kept, *given = run_experts(
+        attended.reshape(ctx_size, rows_here, share), tokens_in, out_w, extras, codes
+    )
+    rows_grad, dots, own_out, *outs, last_out, kept, gate_given, pair_given = run_experts(
         count, ctx_size, norm_two, gates, code_rows, codes, up_slots, expert_weights
     )
-    outs = [own_out, mine, swap_sides(other)]
+    for number, turn in enumerate((1, 1, 2, 2, 3)):
+        pairs = [(place, place ^ turn) for place in range(count)]
+        outs[number] = lax.ppermute(outs[number], "shard", pairs)
     hidden_grad, branch_grad, heads_grad, small = run_attend_back(
-        rows_grad, dots, gates, routes, extras, hidden_one, cotangent, norm_two, out_w
-    )
-    heads_grad, given[1], given[2] = lax.optimization_barrier((heads_grad, given[1], given[2]))
-    given = [given[0], ppermute_ctx(given[1], 2), ppermute_ctx(given[2], 2)]
+        rows_grad, dots, gates, codes, extras, hidden_one, cotangent, norm_two, out_w
+    )
+    heads_grad, pair_given, outs[0] = lax.optimization_barrier((heads_grad, pair_given, outs[0]))
+    pair_given = ppermute_ctx(pair_given, 2)
+    outs = [own_out, *outs, last_out]
+    given = [gate_given, pair_given[0], pair_given[1]]
     weight_grads = [
         kept[number].astype(jnp.float32) + given[number].astype(jnp.float32) for number in range(3)
     ]

time: 416 us -> 402 us (0.966)
  local copies, waits for them, and re-layouts: 31.7 us -> 10.7 us
  starting transfers between devices: 6.2 us -> 14.4 us
    unnamed x102 -> x20, local copies, waits for them, and re-layouts: 26.8 us -> 5.38 us
    ppermute x1 -> x5, starting transfers between devices: 0.53 us -> 9.93 us  [local_fused(): outs[number] = lax.ppermute(outs[number], 'shard', pairs)]
    pallas_call x1, Pallas kernels: 74 us -> 67 us  [run_return(): pl.pallas_call(partial(gradient_return, count), out_shape=(jax.ShapeDtype...]
    ppermute x1 -> x5, waiting for transfers between devices: 0.01 us -> 5.62 us  [local_fused(): outs[number] = lax.ppermute(outs[number], 'shard', pairs)]
    ppermute x6 -> x5, waiting for transfers between devices: 6.43 us -> 1.44 us  [ppermute_ctx(): lax.ppermute(member, 'ctx', [(place, place ^ flip) for place in range(4)])]
  transfers between devices with their start and end apart: 7 -> 10, of which waited for: 2 -> 2; matrix products, arithmetic and copies ran while one was open for 1% -> 3% of each run, Pallas kernels for 16% -> 38%
where the time goes in v6:
time: 402 us; the launch traced here: 398 us
  Pallas kernels  356 us (89%)
  starting transfers between devices  14.4 us (4%)
  local copies, waits for them, and re-layouts  10.7 us (3%)
  other arithmetic  7.57 us (2%)
  waiting for transfers between devices  7.06 us (2%)
    pallas_call x1, Pallas kernels, run_experts(): pl.pallas_call(partial(expert_exchange, count), out_shape=(jax.ShapeDtype...  122 us
    pallas_call x1, Pallas kernels, run_gather(): pl.pallas_call(partial(gather_project, count), out_shape=(jax.ShapeDtypeS...  80.5 us
    pallas_call x1, Pallas kernels, run_return(): pl.pallas_call(partial(gradient_return, count), out_shape=(jax.ShapeDtype...  67 us
    pallas_call x1, Pallas kernels, run_backward(): pl.pallas_call(attention_backward, out_shape=(jax.ShapeDtypeStruct((lengt...  28.7 us
    pallas_call x1, Pallas kernels, run_forward(): pl.pallas_call(attention_forward, out_shape=(jax.ShapeDtypeStruct((length...  24.1 us
    pallas_call x1, Pallas kernels, run_attend_out(): pl.pallas_call(attend_out, out_shape=(jax.ShapeDtypeStruct((here, width),...  20 us
    pallas_call x1, Pallas kernels, run_attend_back(): pl.pallas_call(attend_back, out_shape=(jax.ShapeDtypeStruct((here, width)...  13 us
    ppermute x5, starting transfers between devices, local_fused(): outs[number] = lax.ppermute(outs[number], 'shard', pairs)  9.93 us
  transfers between devices with their start and end apart: 10, of which 2 were waited for; matrix products, arithmetic and copies ran while one was open for 3% of the time, Pallas kernels for 38%

profile of v6, /device:TPU:0, one launch (start us, length us, event | category | flops | bytes accessed | tf_op | source)
XLA Modules:
  0.0 397.9 jit_solution(16370344141554164484)
XLA Ops:
  0.7 80.5 %gather_project.1 = (bf16[1024,1664]{1,0:T(8,128)(2,1)}, bf16[4,512,384]{2,1,0:T(8,128)(2,1)}, bf16[512,1024]{1,0:T(8,128)(2,1)}, f32[4,8,512]{2,1,0:T(8,128)}, ...) custom-call(f32[64,512]{1,0:T(8,128)} %w_query.1, ...), custom_call_target="tpu_custom_call" | custom-call | flops 60000002048 | tf_op jit(solution)/shard_map/gather_project/pallas_call | solution.py:1372
  81.2 3.0 collective-permute-start
  84.2 0.7 compare_bitcast_fusion
  85.5 1.5 fusion.16
  87.9 1.7 fusion.1.line
  89.6 24.1 %attention_forward.1 = (bf16[2048,128]{1,0:T(8,128)(2,1)}, f32[128,2048]{1,0:T(8,128)}, f32[8,2048]{1,0:T(8,128)}) custom-call(s32[64]{0:T(128)} %and_convert_fusion.alive, bf16[2048,384]{1,0:T(8,128)(2,1)} %bitcast.44, f32[1,2048]{1,0:T(1,128)} %bitcast.32, f32[2,1024]{1,0:T(2,128)} %fusion.1.line), custom_call_target="tpu_custom_call" | custom-call | flops 20000000000 | tf_op jit(solution)/shard_map/attention_forward/pallas_call | solution.py:294
  113.7 1.4 collective-permute-done.1.down_chip
  115.6 20.0 %attend_out.1 = (f32[512,1024]{1,0:T(8,128)}, bf16[512,1024]{1,0:T(8,128)(2,1)}, f32[512,2]{1,0:T(8,128)}, bf16[512,512]{1,0:T(8,128)(2,1)}) custom-call(bf16[4,512,128]{2,1,0:T(8,128)(2,1)} %bitcast.47, bf16[512,1024]{1,0:T(8,128)(2,1)} %tokens.3, bf16[2,1024,512]{2,1,0:T(8,128)(2,1)} %get-tuple-element.75.out_hbm, ...), custom_call_target="tpu_custom_call" | custom-call | flops 24999999488 | tf_op jit(solution)/shard_map/attend_out/pallas_call | solution.py:1531
  135.6 122.3 %expert_exchange.1 = (f32[512,1024]{1,0:T(8,128)}, f32[8,512]{1,0:T(8,128)}, bf16[384,1024]{1,0:T(8,128)(2,1)}, bf16[192,1024]{1,0:T(8,128)(2,1)}, bf16[192,1024...) custom-call(bf16[512,1024]{1,0:T(8,128)(2,1)} %get-tuple-element.78., ...), custom_call_target="tpu_custom_call" | custom-call | flops 109999996928 | tf_op jit(solution)/shard_map/expert_exchange/pallas_call | solution.py:903
  258.0 5.2 %collective-permute-start.4 = (bf16[192,1024]{1,0:T(8,128)(2,1)}, bf16[192,1024]{1,0:T(8,128)(2,1)}, u32[]{:S(2)}, u32[]{:S(2)}) collective-permute-start(bf16[192,1024]{1,0:T(8,128)(2,1)} %get-tuple-element.95), channel_id=1, source_target_pairs={{0,8},{8,0},{16,24},{24,16},{1,9},{9,1},{17,25},{25,17},{2,10},{10... | collective-permute-start | bytes 1179656 | tf_op jit(solution)/shard_map/ppermute | solution.py:2481
  263.3 2.2 collective-permute-start.6
  265.5 0.7 collective-permute-start.7
  266.2 1.7 collective-permute-start.8
  267.9 2.6 fusion
  270.5 13.0 %attend_back.1 = (f32[512,1024]{1,0:T(8,128)}, bf16[512,1024]{1,0:T(8,128)(2,1)}, bf16[4,512,128]{2,1,0:T(8,128)(2,1)}, f32[8,1024]{1,0:T(8,128)}) custom-call(f32[512,1024]{1,0:T(8,128)} %get-tuple-element.90.rows_hbm, f32[8,512]{1,0:T(8,128)} %get-tuple-element.91.dot_rows, f32[512,2]{1,0:T(8,128)} %get-tuple-element.79.gates, ...), custom_call_target="tpu_custom_call" | custom-call | flops 4000000000 | tf_op jit(solution)/shard_map/attend_back/pallas_call | solution.py:1672
  283.4 5.6 %collective-permute-done.4.first_hbm = bf16[192,1024]{1,0:T(8,128)(2,1)} collective-permute-done((bf16[192,1024]{1,0:T(8,128)(2,1)}, bf16[192,1024]{1,0:T(8,128)(2,1)}, u32[]{:S(2)}, u32[]{:S(2)}) %collective-permute-start.4) | collective-permute-done | bytes 393248 | tf_op jit(solution)/shard_map/ppermute | solution.py:2481
  289.1 0.9 collective-permute-start.9
  289.9 28.7 %attention_backward.1 = (bf16[2048,384]{1,0:T(8,128)(2,1)}, f32[8,1024]{1,0:T(8,128)}) custom-call(s32[64]{0:T(128)} %and_convert_fusion.alive, bf16[2048,384]{1,0:T(8,128)(2,1)} %bitcast.45, f32[1,2048]{1,0:T(1,128)} %bitcast.33, f32[2,1024]{1,0:T(2,128)} %fusion.1.line, bf16[2048,128]{1,0:T(8,128)(2,1)} %bitcast.48, f32[128,2048]{1,0:T(8,128)} %get-tuple-element.97.out_t, ...), custom_call_target="tpu_custom_call" | custom-call | flops 4000000000 | tf_op jit(solution)/shard_map/attention_backward/pallas_call | solution.py:320
  318.7 67.0 %gradient_return.1 = (bf16[512,1024]{1,0:T(8,128)(2,1)}, bf16[512,1024]{1,0:T(8,128)(2,1)}, f32[64,512]{1,0:T(8,128)}, f32[64,512]{1,0:T(8,128)}, f32[64,512]{1,...) custom-call(bf16[4,512,384]{2,1,0:T(8,128)(2,1)} %bitcast.46, ...), custom_call_target="tpu_custom_call" | custom-call | flops 44999999488 | tf_op jit(solution)/shard_map/gradient_return/pallas_call | solution.py:2097
  385.6 1.3 slice.39
  387.0 0.8 constant_dynamic-slice_fusion
  388.8 3.7 convert_add_fusion.1
  392.5 1.0 copy.45
  394.1 1.0 copy.46
  (44 shorter events, 6.6 us)
Async XLA Ops:
  81.2 32.5 %collective-permute-start = (bf16[256,1408]{1,0:T(8,128)(2,1)}, bf16[256,1408]{1,0:T(8,128)(2,1)}, u32[]{:S(2)}, u32[]{:S(2)}) collective-permute-start(bf16[256,1408]{1,0:T(8,128)(2,1)} %get-tuple-element.72.up_own), channel_id=1, source_target_pairs={{0,4},{2,6},{4,0},{6,2},{1,5},{3,7},{5,1},{7,3},{8,12},{10,14},{12... | collective-permute-start | bytes 2162696 | tf_op jit(solution)/shard_map/ppermute | solution.py:2413
  84.1 31.0 %collective-permute-start.1 = (bf16[256,1408]{1,0:T(8,128)(2,1)}, bf16[256,1408]{1,0:T(8,128)(2,1)}, u32[]{:S(2)}, u32[]{:S(2)}) collective-permute-start(bf16[256,1408]{1,0:T(8,128)(2,1)} %get-tuple-element.73.down_own), channel_id=1, source_target_pairs={{0,4},{2,6},{4,0},{6,2},{1,5},{3,7},{5,1},{7,3},{8,12},{10,14},{12... | collective-permute-start | bytes 2162696 | tf_op jit(solution)/shard_map/ppermute | solution.py:2413
  115.1 20.5 %collective-permute-start.2 = (bf16[256,1408]{1,0:T(8,128)(2,1)}, bf16[256,1408]{1,0:T(8,128)(2,1)}, u32[]{:S(2)}, u32[]{:S(2)}) collective-permute-start(bf16[256,1408]{1,0:T(8,128)(2,1)} %collective-permute-done.up_chip), channel_id=1, source_target_pairs={{0,2},{2,0},{4,6},{6,4},{1,3},{3,1},{5,7},{7,5},{8,10},{10,8},{12,... | collective-permute-start | bytes 2162696 | tf_op jit(solution)/shard_map/ppermute | solution.py:2413
  115.1 20.5 %collective-permute-start.3 = (bf16[256,1408]{1,0:T(8,128)(2,1)}, bf16[256,1408]{1,0:T(8,128)(2,1)}, u32[]{:S(2)}, u32[]{:S(2)}) collective-permute-start(bf16[256,1408]{1,0:T(8,128)(2,1)} %collective-permute-done.1.down_chip), channel_id=1, source_target_pairs={{0,2},{2,0},{4,6},{6,4},{1,3},{3,1},{5,7},{7,5},{8,10},{10,8},{12,... | collective-permute-start | bytes 2162696 | tf_op jit(solution)/shard_map/ppermute | solution.py:2413
  258.0 31.1 %collective-permute-start.4 = (bf16[192,1024]{1,0:T(8,128)(2,1)}, bf16[192,1024]{1,0:T(8,128)(2,1)}, u32[]{:S(2)}, u32[]{:S(2)}) collective-permute-start(bf16[192,1024]{1,0:T(8,128)(2,1)} %get-tuple-element.95), channel_id=1, source_target_pairs={{0,8},{8,0},{16,24},{24,16},{1,9},{9,1},{17,25},{25,17},{2,10},{10... | collective-permute-start | bytes 1179656 | tf_op jit(solution)/shard_map/ppermute | solution.py:2481
  263.2 55.5 %collective-permute-start.5 = (bf16[192,1024]{1,0:T(8,128)(2,1)}, bf16[192,1024]{1,0:T(8,128)(2,1)}, u32[]{:S(2)}, u32[]{:S(2)}) collective-permute-start(bf16[192,1024]{1,0:T(8,128)(2,1)} %get-tuple-element.105), channel_id=1, source_target_pairs={{0,8},{8,0},{16,24},{24,16},{1,9},{9,1},{17,25},{25,17},{2,10},{10... | collective-permute-start | bytes 1179656 | tf_op jit(solution)/shard_map/ppermute | solution.py:2481
  263.3 55.4 %collective-permute-start.6 = (bf16[192,1024]{1,0:T(8,128)(2,1)}, bf16[192,1024]{1,0:T(8,128)(2,1)}, u32[]{:S(2)}, u32[]{:S(2)}) collective-permute-start(bf16[192,1024]{1,0:T(8,128)(2,1)} %get-tuple-element.106), channel_id=1, source_target_pairs={{0,16},{8,24},{16,0},{24,8},{1,17},{9,25},{17,1},{25,9},{2,18},{10... | collective-permute-start | bytes 1179656 | tf_op jit(solution)/shard_map/ppermute | solution.py:2481
  265.5 53.2 %collective-permute-start.7 = (bf16[192,1024]{1,0:T(8,128)(2,1)}, bf16[192,1024]{1,0:T(8,128)(2,1)}, u32[]{:S(2)}, u32[]{:S(2)}) collective-permute-start(bf16[192,1024]{1,0:T(8,128)(2,1)} %get-tuple-element.107), channel_id=1, source_target_pairs={{0,16},{8,24},{16,0},{24,8},{1,17},{9,25},{17,1},{25,9},{2,18},{10... | collective-permute-start | bytes 1179656 | tf_op jit(solution)/shard_map/ppermute | solution.py:2481
  266.2 52.5 %collective-permute-start.8 = (bf16[192,1024]{1,0:T(8,128)(2,1)}, bf16[192,1024]{1,0:T(8,128)(2,1)}, u32[]{:S(2)}, u32[]{:S(2)}) collective-permute-start(bf16[192,1024]{1,0:T(8,128)(2,1)} %get-tuple-element.108), channel_id=1, source_target_pairs={{0,24},{8,16},{16,8},{24,0},{1,25},{9,17},{17,9},{25,1},{2,26},{10... | collective-permute-start | bytes 1179656 | tf_op jit(solution)/shard_map/ppermute | solution.py:2481
  289.1 99.8 %collective-permute-start.9 = (bf16[2,256,1408]{2,1,0:T(8,128)(2,1)}, bf16[2,256,1408]{2,1,0:T(8,128)(2,1)}, u32[]{:S(2)}, u32[]{:S(2)}) collective-permute-start(bf16[2,256,1408]{2,1,0:T(8,128)(2,1)} %get-tuple-element.124), channel_id=1, source_target_pairs={{0,4},{2,6},{4,0},{6,2},{1,5},{3,7},{5,1},{7,3},{8,12},{10,14},{12... | collective-permute-start | bytes 4325384 | tf_op jit(solution)/shard_map/ppermute | solution.py:2413
  388.8 3.7 copy-start.1
  392.5 1.6 copy-start
  394.1 1.0 copy-start.5
  394.1 1.6 copy-start.4
  394.1 2.3 copy-start.3
  394.1 3.0 copy-start.2

commit v7 on v6

--- a/solution.py
+++ b/solution.py
@@ -365,6 +365,8 @@
 
 MESH = pl.DeviceIdType.MESH
 LANES = 128
+CUTS = 2
+HALVES = 4
 
 
 def places():
@@ -534,6 +536,11 @@
 
     my_half = pl.ds(pl.multiple_of(side * half, half), half)
     peer_half = pl.ds(pl.multiple_of((1 - side) * half, half), half)
+    cut = half // CUTS
+
+    def lines(which, piece):
+        return pl.ds(pl.multiple_of(which * half + piece * cut, cut), cut)
+
 
     def picked(expert, start, amount):
         slots = lax.broadcasted_iota(jnp.int32, (amount, tokens), 0) + expert * room + start
@@ -548,13 +555,13 @@
         held = held + jnp.where(code_cols[:, 1:2] == slots, gates[:, 1:2], 0.0)
         return jnp.broadcast_to(jnp.sum(held, axis=0, keepdims=True), (8, room))
 
-    def rows_copy(step):
+    def rows_copy(step, piece):
         target = source(step)
         return pltpu.make_async_remote_copy(
-            sent.at[step - 1],
-            rows.at[own, my_half],
-            rows_send.at[step - 1],
-            rows_recv.at[own],
+            sent.at[step - 1, lines(0, piece)],
+            rows.at[own, lines(side, piece)],
+            rows_send.at[step - 1, piece],
+            rows_recv.at[own, piece],
             device_id=(target, ctx, side),
             device_id_type=MESH,
         )
@@ -572,7 +579,8 @@
     def send_rows(step, unused):
         target = source(step)
         sent[step - 1] = dot32(picked(target, side * half, half), norm[...]).astype(jnp.bfloat16)
-        rows_copy(step).start()
+        for piece in range(CUTS):
+            rows_copy(step, piece).start()
         gates_out[step - 1] = slot_gates(target)
         gates_copy(step).start()
         return unused
@@ -588,34 +596,26 @@
             buffer, buffer, send, recv, device_id=peer, device_id_type=MESH
         )
 
-    def pass_copy(origin):
-        return pltpu.make_async_remote_copy(
-            rows.at[origin, my_half],
-            rows.at[origin, my_half],
-            pass_send.at[origin],
-            pass_recv.at[origin],
-            device_id=peer,
-            device_id_type=MESH,
-        )
-
-    def part_copy(step):
-        return pltpu.make_async_remote_copy(
-            partial.at[step, peer_half],
-            peer_part.at[step],
-            part_send.at[step],
-            part_recv.at[step],
-            device_id=peer,
-            device_id_type=MESH,
-        )
-
-    def back_copy(step):
-        return pltpu.make_async_remote_copy(
-            summed.at[step],
-            back.at[own],
-            back_send.at[step],
-            back_recv.at[own],
-            device_id=(source(step), ctx, side),
-            device_id_type=MESH,
+    def pass_copy(origin, piece):
+        spot = rows.at[origin, lines(side, piece)]
+        return remote(spot, spot, pass_send.at[origin, piece], pass_recv.at[origin, piece], peer)
+
+    def part_copy(step, piece):
+        return remote(
+            partial.at[step, lines(1 - side, piece)],
+            peer_part.at[step, lines(0, piece)],
+            part_send.at[step, piece],
+            part_recv.at[step, piece],
+            peer,
+        )
+
+    def back_copy(step, piece):
+        return remote(
+            summed.at[step, lines(0, piece)],
+            back.at[own, lines(0, piece)],
+            back_send.at[step, piece],
+            back_recv.at[own, piece],
+            (source(step), ctx, side),
         )
 
     def dots_copy(step):
@@ -629,21 +629,25 @@
         )
 
     def send_back(step):
-        part_copy(step).wait_recv()
-        summed[step] = (
-            partial[step, my_half].astype(jnp.float32) + peer_part[step].astype(jnp.float32)
-        ).astype(jnp.bfloat16)
-        back_copy(step).start()
-
-    cut = (hidden // 256 + 1) // 2 * 256
-    pieces = (slice(0, cut), slice(cut, hidden))
+        for piece in range(CUTS):
+            part_copy(step, piece).wait_recv()
+            summed[step, lines(0, piece), :] = (
+                partial[step, lines(side, piece), :].astype(jnp.float32)
+                + peer_part[step, lines(0, piece), :].astype(jnp.float32)
+            ).astype(jnp.bfloat16)
+            back_copy(step, piece).start()
+
+    edge = (hidden // 256 + 1) // 2 * 256
+    pieces = (slice(0, edge), slice(edge, hidden))
 
     def run_chunk(step, unused):
         origin = source(step)
 
         @pl.when(step > 0)
         def _():
-            landed(rows.at[origin, peer_half], pass_send.at[origin], pass_recv.at[origin], 0).wait_recv()
+            for piece in range(CUTS):
+                spot = rows.at[origin, lines(1 - side, piece)]
+                landed(spot, pass_send.at[0, 0], pass_recv.at[origin, piece], 0).wait_recv()
             landed(gates_in.at[origin], gates_send.at[0], gates_recv.at[origin], 0).wait_recv()
 
         gate_column = jnp.transpose(gates_in[origin])[:, 0:1]
@@ -668,10 +672,10 @@
         @pl.when(step < count - 1)
         def _():
             following = source(step + 1)
-            landed(
-                rows.at[following, my_half], rows_send.at[0], rows_recv.at[following], 0
-            ).wait_recv()
-            pass_copy(following).start()
+            for piece in range(CUTS):
+                spot = rows.at[following, lines(side, piece)]
+                landed(spot, rows_send.at[0, 0], rows_recv.at[following, piece], 0).wait_recv()
+                pass_copy(following, piece).start()
 
         dots = dots + inside(pieces[1])
         dots_out[step] = jnp.transpose(jnp.broadcast_to(dots, (room, 128)))[0:8, :]
@@ -680,14 +684,17 @@
         def _():
             send_back(step - 1)
 
-        partial[step] = (
-            dot_last(gate_grad[origin], gate_w[...]) + dot_last(up_grad[origin], up_w[...])
-        ).astype(jnp.bfloat16)
-
-        @pl.when(step > 0)
-        def _():
-            part_copy(step).start()
-            dots_copy(step).start()
+        for spot in (peer_half, my_half):
+            found = dot_last(gate_grad[origin, spot, :], gate_w[...])
+            found = found + dot_last(up_grad[origin, spot, :], up_w[...])
+            partial[step, spot, :] = found.astype(jnp.bfloat16)
+            if spot is peer_half:
+
+                @pl.when(step > 0)
+                def _():
+                    for piece in range(CUTS):
+                        part_copy(step, piece).start()
+                    dots_copy(step).start()
 
         return unused
 
@@ -781,7 +788,9 @@
 
     def back_landed(step, unused):
         origin = source(step)
-        landed(back.at[origin], back_send.at[0], back_recv.at[origin], 0).wait_recv()
+        for piece in range(CUTS):
+            spot = back.at[origin, lines(0, piece)]
+            landed(spot, back_send.at[0, 0], back_recv.at[origin, piece], 0).wait_recv()
         return unused
 
     lax.fori_loop(1, count, dots_landed, 0)
@@ -866,11 +875,12 @@
             stores.append(store)
 
     def drain(step, unused):
-        rows_copy(step).wait_send()
+        for piece in range(CUTS):
+            rows_copy(step, piece).wait_send()
+            pass_copy(source(step), piece).wait_send()
+            part_copy(step, piece).wait_send()
+            back_copy(step, piece).wait_send()
         gates_copy(step).wait_send()
-        pass_copy(source(step)).wait_send()
-        part_copy(step).wait_send()
-        back_copy(step).wait_send()
         dots_copy(step).wait_send()
         return unused
 
@@ -940,16 +950,16 @@
             pltpu.VMEM((1, width // ctx_size, hidden), low),
             dma((13,)),
             dma((18,)),
+            dma((count, CUTS)),
+            dma((count, CUTS)),
+            dma((count, CUTS)),
+            dma((count, CUTS)),
             dma((count,)),
             dma((count,)),
-            dma((count,)),
-            dma((count,)),
-            dma((count,)),
-            dma((count,)),
-            dma((count,)),
-            dma((count,)),
-            dma((count,)),
-            dma((count,)),
+            dma((count, CUTS)),
+            dma((count, CUTS)),
+            dma((count, CUTS)),
+            dma((count, CUTS)),
             dma((count,)),
             dma((count,)),
             dma((blocks + 1,)),
@@ -1199,18 +1209,24 @@
         rows_found = jnp.where(hit, 1.0, 0.0).astype(jnp.bfloat16)
         return dot32(rows_found, cotangent[...]).astype(jnp.bfloat16)
 
-    def to_expert(step):
+    cut = half // CUTS
+
+    def lines(which, piece):
+        return pl.ds(pl.multiple_of(which * half + piece * cut, cut), cut)
+
+    def to_expert(step, piece):
         return remote(
-            sent.at[step - 1],
-            upstream.at[own, my_half],
-            rows_send.at[step - 1],
-            rows_recv.at[own],
+            sent.at[step - 1, lines(0, piece)],
+            upstream.at[own, lines(side, piece)],
+            rows_send.at[step - 1, piece],
+            rows_recv.at[own, piece],
             (nearest(own, count, step), ctx, side),
         )
 
-    def pass_rows(shard):
-        spot, target = upstream.at[shard, my_half], upstream_hbm.at[shard, my_half]
-        return remote(spot, target, pass_send.at[shard], pass_recv.at[shard], pair)
+    def pass_rows(shard, piece):
+        spot = lines(side, piece)
+        source, target = upstream.at[shard, spot], upstream_hbm.at[shard, spot]
+        return remote(source, target, pass_send.at[shard, piece], pass_recv.at[shard, piece], pair)
 
     lows = (gate_low, up_low, down_low)
     near = (gate_core, up_core, down_core)
@@ -1262,7 +1278,8 @@
         out_to_pair(shard, ctx, source).start()
 
     for step in range(1, count):
-        to_expert(step).start()
+        for piece in range(CUTS):
+            to_expert(step, piece).start()
     gate_over.start()
     values = tokens[...].astype(jnp.float32)
     scale = lax.rsqrt(jnp.mean(values * values, axis=1, keepdims=True) + 1e-06)
@@ -1301,10 +1318,11 @@
         out_to_pair(shard, other_place, source).start()
     for step in range(1, count):
         shard = nearest(own, count, step)
-        spot = upstream.at[shard, my_half]
-        remote(spot, spot, rows_send.at[0], rows_recv.at[shard], pair).wait_recv()
-        pass_rows(shard).start()
-        store(spot, upstream_hbm.at[shard, my_half])
+        for piece in range(CUTS):
+            spot = upstream.at[shard, lines(side, piece)]
+            remote(spot, spot, line_send.at[0], rows_recv.at[shard, piece], pair).wait_recv()
+            pass_rows(shard, piece).start()
+        store(upstream.at[shard, my_half], upstream_hbm.at[shard, my_half])
     gate_over.wait_recv()
     gate_far_copy.start()
     for step in range(count):
@@ -1331,8 +1349,9 @@
         store(out_full.at[which], out_hbm.at[which])
     for step in range(1, count):
         shard = nearest(own, count, step)
-        spot = upstream_hbm.at[shard, peer_half]
-        remote(spot, spot, pass_send.at[0], pass_recv.at[shard], pair).wait_recv()
+        for piece in range(CUTS):
+            spot = upstream_hbm.at[shard, lines(1 - side, piece)]
+            remote(spot, spot, line_send.at[0], pass_recv.at[shard, piece], pair).wait_recv()
 
     for copy in stores:
         copy.wait()
@@ -1350,8 +1369,9 @@
         if step:
             in_line(to_line, shard, onward(shard), weight, 1 + step, sent_off)
             in_line(out_to_line, shard, onward(shard), out_weight, 1 + step, sent_off)
-            to_expert(step).wait_send()
-            pass_rows(shard).wait_send()
+            for piece in range(CUTS):
+                to_expert(step, piece).wait_send()
+                pass_rows(shard, piece).wait_send()
         to_chip(shard, weight).wait_send()
         out_to_chip(shard, out_weight).wait_send()
         for place in (ctx, other_place):
@@ -1420,10 +1440,10 @@
             dma((2, 2 * count)),
             dma((2 * count,)),
             dma((2 * count,)),
-            dma((count,)),
-            dma((count,)),
-            dma((count,)),
-            dma((count,)),
+            dma((count, CUTS)),
+            dma((count, CUTS)),
+            dma((count, CUTS)),
+            dma((count, CUTS)),
             dma((5,)),
             dma((5,)),
             dma((3,)),
@@ -1778,7 +1798,7 @@
     own, ctx, side, chip, core = places()
     ctx_size, here, share = packed_grad.shape
     width = norm.shape[1]
-    halves = 2
+    halves = HALVES
     part = here // halves
     groups = ctx_size
     pair = (own, ctx, 1 - side)
@@ -2018,11 +2038,12 @@
             to_bias(number).start()
         bias_in[own, ctx] = message(own, ctx)
 
-    landed(0)
-    send_side(0)
-    landed(1)
+    for piece in range(halves - 1):
+        landed(piece)
+        send_side(piece)
+    landed(halves - 1)
     contract(0)
-    send_side(1)
+    send_side(halves - 1)
     over_chip(0)
     contract(1)
     contract(2)
@@ -2119,8 +2140,8 @@
             pltpu.VMEM((ctx_size, here, share), low),
             pltpu.VMEM((width, here), low),
             pltpu.VMEM((ctx_size, count * 2, 2, rows, columns), low),
-            pltpu.VMEM((2, here // 2, width), low),
-            pltpu.VMEM((2, here // 2, width), low),
+            pltpu.VMEM((HALVES, here // HALVES, width), low),
+            pltpu.VMEM((HALVES, here // HALVES, width), low),
             pltpu.VMEM((ctx_size, count, 2, rows, columns), wide),
             pltpu.VMEM((ctx_size, count * 2, rows, columns), low),
             pltpu.VMEM((ctx_size, count, rows, columns), low),
@@ -2137,10 +2158,10 @@
             pltpu.VMEM((15, 16, LANES), wide),
             pltpu.VMEM((count, ctx_size, 16, LANES), wide),
             pltpu.VMEM((8, width), wide),
-            dma((3, 2)),
-            dma((ctx_size, 2)),
-            dma((2,)),
-            dma((2,)),
+            dma((3, HALVES)),
+            dma((ctx_size, HALVES)),
+            dma((HALVES,)),
+            dma((HALVES,)),
             dma((ctx_size + 1,)),
             dma((ctx_size + 1,)),
             dma((ctx_size + 1,)),

time: 402 us -> 393 us (0.978)
  Pallas kernels: 356 us -> 342 us
  waiting for transfers between devices: 7.06 us -> 12.2 us
    ppermute x5, waiting for transfers between devices: 1.44 us -> 6.49 us  [ppermute_ctx(): lax.ppermute(member, 'ctx', [(place, place ^ flip) for place in range(4)])]
    pallas_call x1, Pallas kernels: 122 us -> 118 us  [run_experts(): pl.pallas_call(partial(expert_exchange, count), out_shape=(jax.ShapeDtype...]
    pallas_call x1, Pallas kernels: 28.7 us -> 24.3 us  [run_backward(): pl.pallas_call(attention_backward, out_shape=(jax.ShapeDtypeStruct((lengt...]
    pallas_call x1, Pallas kernels: 24.1 us -> 20 us  [run_forward(): pl.pallas_call(attention_forward, out_shape=(jax.ShapeDtypeStruct((length...]
  transfers between devices with their start and end apart: 10 -> 10, of which waited for: 2 -> 2; matrix products, arithmetic and copies ran while one was open for 3% -> 3% of each run, Pallas kernels for 38% -> 37%
where the time goes in v7:
time: 393 us; the launch traced here: 386 us
  Pallas kernels  342 us (87%)
  waiting for transfers between devices  12.2 us (3%)
  starting transfers between devices  11.6 us (3%)
  local copies, waits for them, and re-layouts  10.7 us (3%)
  other arithmetic  7.57 us (2%)
    pallas_call x1, Pallas kernels, run_experts(): pl.pallas_call(partial(expert_exchange, count), out_shape=(jax.ShapeDtype...  118 us
    pallas_call x1, Pallas kernels, run_gather(): pl.pallas_call(partial(gather_project, count), out_shape=(jax.ShapeDtypeS...  80.6 us
    pallas_call x1, Pallas kernels, run_return(): pl.pallas_call(partial(gradient_return, count), out_shape=(jax.ShapeDtype...  66.1 us
    pallas_call x1, Pallas kernels, run_backward(): pl.pallas_call(attention_backward, out_shape=(jax.ShapeDtypeStruct((lengt...  24.3 us
    pallas_call x1, Pallas kernels, run_forward(): pl.pallas_call(attention_forward, out_shape=(jax.ShapeDtypeStruct((length...  20 us
    pallas_call x1, Pallas kernels, run_attend_out(): pl.pallas_call(attend_out, out_shape=(jax.ShapeDtypeStruct((here, width),...  20 us
    pallas_call x1, Pallas kernels, run_attend_back(): pl.pallas_call(attend_back, out_shape=(jax.ShapeDtypeStruct((here, width)...  12.8 us
    ppermute x5, starting transfers between devices, local_fused(): outs[number] = lax.ppermute(outs[number], 'shard', pairs)  8.31 us
  transfers between devices with their start and end apart: 10, of which 2 were waited for; matrix products, arithmetic and copies ran while one was open for 3% of the time, Pallas kernels for 37%

profile of v7, /device:TPU:0, one launch (start us, length us, event | category | flops | bytes accessed | tf_op | source)
XLA Modules:
  0.0 386.4 jit_solution(9477386463848535365)
XLA Ops:
  0.7 80.6 %gather_project.1 = (bf16[1024,1664]{1,0:T(8,128)(2,1)}, bf16[4,512,384]{2,1,0:T(8,128)(2,1)}, bf16[512,1024]{1,0:T(8,128)(2,1)}, f32[4,8,512]{2,1,0:T(8,128)}, ...) custom-call(f32[64,512]{1,0:T(8,128)} %w_query.1, ...), custom_call_target="tpu_custom_call" | custom-call | flops 60000002048 | tf_op jit(solution)/shard_map/gather_project/pallas_call | solution.py:1392
  81.3 0.9 collective-permute-start
  82.2 1.2 collective-permute-start.1
  83.4 0.7 compare_bitcast_fusion
  84.7 1.5 fusion.16
  87.1 1.7 fusion.1.line
  88.8 20.0 %attention_forward.1 = (bf16[2048,128]{1,0:T(8,128)(2,1)}, f32[128,2048]{1,0:T(8,128)}, f32[8,2048]{1,0:T(8,128)}) custom-call(s32[64]{0:T(128)} %and_convert_fusion.alive, bf16[2048,384]{1,0:T(8,128)(2,1)} %bitcast.44, f32[1,2048]{1,0:T(1,128)} %bitcast.32, f32[2,1024]{1,0:T(2,128)} %fusion.1.line), custom_call_target="tpu_custom_call" | custom-call | flops 20000000000 | tf_op jit(solution)/shard_map/attention_forward/pallas_call | solution.py:294
  108.8 6.5 %collective-permute-done.1.down_chip = bf16[256,1408]{1,0:T(8,128)(2,1)} collective-permute-done((bf16[256,1408]{1,0:T(8,128)(2,1)}, bf16[256,1408]{1,0:T(8,128)(2,1)}, u32[]{:S(2)}, u32[]{:S(2)}) %collective-permute-start.1) | collective-permute-done | bytes 720928 | tf_op jit(solution)/shard_map/ppermute | solution.py:2434
  115.8 20.0 %attend_out.1 = (f32[512,1024]{1,0:T(8,128)}, bf16[512,1024]{1,0:T(8,128)(2,1)}, f32[512,2]{1,0:T(8,128)}, bf16[512,512]{1,0:T(8,128)(2,1)}) custom-call(bf16[4,512,128]{2,1,0:T(8,128)(2,1)} %bitcast.47, bf16[512,1024]{1,0:T(8,128)(2,1)} %tokens.3, bf16[2,1024,512]{2,1,0:T(8,128)(2,1)} %get-tuple-element.75.out_hbm, ...), custom_call_target="tpu_custom_call" | custom-call | flops 24999999488 | tf_op jit(solution)/shard_map/attend_out/pallas_call | solution.py:1551
  135.8 117.8 %expert_exchange.1 = (f32[512,1024]{1,0:T(8,128)}, f32[8,512]{1,0:T(8,128)}, bf16[384,1024]{1,0:T(8,128)(2,1)}, bf16[192,1024]{1,0:T(8,128)(2,1)}, bf16[192,1024...) custom-call(bf16[512,1024]{1,0:T(8,128)(2,1)} %get-tuple-element.78., ...), custom_call_target="tpu_custom_call" | custom-call | flops 109999996928 | tf_op jit(solution)/shard_map/expert_exchange/pallas_call | solution.py:913
  253.6 3.6 collective-permute-start.4
  257.3 2.2 collective-permute-start.6
  259.5 0.7 collective-permute-start.7
  260.2 1.7 collective-permute-start.8
  261.9 2.6 fusion
  264.5 12.8 %attend_back.1 = (f32[512,1024]{1,0:T(8,128)}, bf16[512,1024]{1,0:T(8,128)(2,1)}, bf16[4,512,128]{2,1,0:T(8,128)(2,1)}, f32[8,1024]{1,0:T(8,128)}) custom-call(f32[512,1024]{1,0:T(8,128)} %get-tuple-element.90.rows_hbm, f32[8,512]{1,0:T(8,128)} %get-tuple-element.91.dot_rows, f32[512,2]{1,0:T(8,128)} %get-tuple-element.79.gates, ...), custom_call_target="tpu_custom_call" | custom-call | flops 4000000000 | tf_op jit(solution)/shard_map/attend_back/pallas_call | solution.py:1692
  277.3 5.7 %collective-permute-done.4.first_hbm = bf16[192,1024]{1,0:T(8,128)(2,1)} collective-permute-done((bf16[192,1024]{1,0:T(8,128)(2,1)}, bf16[192,1024]{1,0:T(8,128)(2,1)}, u32[]{:S(2)}, u32[]{:S(2)}) %collective-permute-start.4) | collective-permute-done | bytes 393248 | tf_op jit(solution)/shard_map/ppermute | solution.py:2502
  283.7 24.3 %attention_backward.1 = (bf16[2048,384]{1,0:T(8,128)(2,1)}, f32[8,1024]{1,0:T(8,128)}) custom-call(s32[64]{0:T(128)} %and_convert_fusion.alive, bf16[2048,384]{1,0:T(8,128)(2,1)} %bitcast.45, f32[1,2048]{1,0:T(1,128)} %bitcast.33, f32[2,1024]{1,0:T(2,128)} %fusion.1.line, bf16[2048,128]{1,0:T(8,128)(2,1)} %bitcast.48, f32[128,2048]{1,0:T(8,128)} %get-tuple-element.97.out_t, ...), custom_call_target="tpu_custom_call" | custom-call | flops 4000000000 | tf_op jit(solution)/shard_map/attention_backward/pallas_call | solution.py:320
  308.0 66.1 %gradient_return.1 = (bf16[512,1024]{1,0:T(8,128)(2,1)}, bf16[512,1024]{1,0:T(8,128)(2,1)}, f32[64,512]{1,0:T(8,128)}, f32[64,512]{1,0:T(8,128)}, f32[64,512]{1,...) custom-call(bf16[4,512,384]{2,1,0:T(8,128)(2,1)} %bitcast.46, ...), custom_call_target="tpu_custom_call" | custom-call | flops 44999999488 | tf_op jit(solution)/shard_map/gradient_return/pallas_call | solution.py:2118
  374.1 1.3 slice.39
  375.4 0.8 constant_dynamic-slice_fusion
  377.3 3.7 convert_add_fusion.1
  381.0 1.0 copy.45
  382.6 1.0 copy.46
  (44 shorter events, 7.2 us)
Async XLA Ops:
  81.3 27.5 %collective-permute-start = (bf16[256,1408]{1,0:T(8,128)(2,1)}, bf16[256,1408]{1,0:T(8,128)(2,1)}, u32[]{:S(2)}, u32[]{:S(2)}) collective-permute-start(bf16[256,1408]{1,0:T(8,128)(2,1)} %get-tuple-element.72.up_own), channel_id=1, source_target_pairs={{0,4},{2,6},{4,0},{6,2},{1,5},{3,7},{5,1},{7,3},{8,12},{10,14},{12... | collective-permute-start | bytes 2162696 | tf_op jit(solution)/shard_map/ppermute | solution.py:2434
  82.2 33.1 %collective-permute-start.1 = (bf16[256,1408]{1,0:T(8,128)(2,1)}, bf16[256,1408]{1,0:T(8,128)(2,1)}, u32[]{:S(2)}, u32[]{:S(2)}) collective-permute-start(bf16[256,1408]{1,0:T(8,128)(2,1)} %get-tuple-element.73.down_own), channel_id=1, source_target_pairs={{0,4},{2,6},{4,0},{6,2},{1,5},{3,7},{5,1},{7,3},{8,12},{10,14},{12... | collective-permute-start | bytes 2162696 | tf_op jit(solution)/shard_map/ppermute | solution.py:2434
  115.3 20.5 %collective-permute-start.2 = (bf16[256,1408]{1,0:T(8,128)(2,1)}, bf16[256,1408]{1,0:T(8,128)(2,1)}, u32[]{:S(2)}, u32[]{:S(2)}) collective-permute-start(bf16[256,1408]{1,0:T(8,128)(2,1)} %collective-permute-done.up_chip), channel_id=1, source_target_pairs={{0,2},{2,0},{4,6},{6,4},{1,3},{3,1},{5,7},{7,5},{8,10},{10,8},{12,... | collective-permute-start | bytes 2162696 | tf_op jit(solution)/shard_map/ppermute | solution.py:2434
  115.3 20.5 %collective-permute-start.3 = (bf16[256,1408]{1,0:T(8,128)(2,1)}, bf16[256,1408]{1,0:T(8,128)(2,1)}, u32[]{:S(2)}, u32[]{:S(2)}) collective-permute-start(bf16[256,1408]{1,0:T(8,128)(2,1)} %collective-permute-done.1.down_chip), channel_id=1, source_target_pairs={{0,2},{2,0},{4,6},{6,4},{1,3},{3,1},{5,7},{7,5},{8,10},{10,8},{12,... | collective-permute-start | bytes 2162696 | tf_op jit(solution)/shard_map/ppermute | solution.py:2434
  253.6 29.4 %collective-permute-start.4 = (bf16[192,1024]{1,0:T(8,128)(2,1)}, bf16[192,1024]{1,0:T(8,128)(2,1)}, u32[]{:S(2)}, u32[]{:S(2)}) collective-permute-start(bf16[192,1024]{1,0:T(8,128)(2,1)} %get-tuple-element.95), channel_id=1, source_target_pairs={{0,8},{8,0},{16,24},{24,16},{1,9},{9,1},{17,25},{25,17},{2,10},{10... | collective-permute-start | bytes 1179656 | tf_op jit(solution)/shard_map/ppermute | solution.py:2502
  257.2 50.8 %collective-permute-start.5 = (bf16[192,1024]{1,0:T(8,128)(2,1)}, bf16[192,1024]{1,0:T(8,128)(2,1)}, u32[]{:S(2)}, u32[]{:S(2)}) collective-permute-start(bf16[192,1024]{1,0:T(8,128)(2,1)} %get-tuple-element.105), channel_id=1, source_target_pairs={{0,8},{8,0},{16,24},{24,16},{1,9},{9,1},{17,25},{25,17},{2,10},{10... | collective-permute-start | bytes 1179656 | tf_op jit(solution)/shard_map/ppermute | solution.py:2502
  257.3 50.8 %collective-permute-start.6 = (bf16[192,1024]{1,0:T(8,128)(2,1)}, bf16[192,1024]{1,0:T(8,128)(2,1)}, u32[]{:S(2)}, u32[]{:S(2)}) collective-permute-start(bf16[192,1024]{1,0:T(8,128)(2,1)} %get-tuple-element.106), channel_id=1, source_target_pairs={{0,16},{8,24},{16,0},{24,8},{1,17},{9,25},{17,1},{25,9},{2,18},{10... | collective-permute-start | bytes 1179656 | tf_op jit(solution)/shard_map/ppermute | solution.py:2502
  259.5 48.5 %collective-permute-start.7 = (bf16[192,1024]{1,0:T(8,128)(2,1)}, bf16[192,1024]{1,0:T(8,128)(2,1)}, u32[]{:S(2)}, u32[]{:S(2)}) collective-permute-start(bf16[192,1024]{1,0:T(8,128)(2,1)} %get-tuple-element.107), channel_id=1, source_target_pairs={{0,16},{8,24},{16,0},{24,8},{1,17},{9,25},{17,1},{25,9},{2,18},{10... | collective-permute-start | bytes 1179656 | tf_op jit(solution)/shard_map/ppermute | solution.py:2502
  260.2 47.8 %collective-permute-start.8 = (bf16[192,1024]{1,0:T(8,128)(2,1)}, bf16[192,1024]{1,0:T(8,128)(2,1)}, u32[]{:S(2)}, u32[]{:S(2)}) collective-permute-start(bf16[192,1024]{1,0:T(8,128)(2,1)} %get-tuple-element.108), channel_id=1, source_target_pairs={{0,24},{8,16},{16,8},{24,0},{1,25},{9,17},{17,9},{25,1},{2,26},{10... | collective-permute-start | bytes 1179656 | tf_op jit(solution)/shard_map/ppermute | solution.py:2502
  283.1 94.2 %collective-permute-start.9 = (bf16[2,256,1408]{2,1,0:T(8,128)(2,1)}, bf16[2,256,1408]{2,1,0:T(8,128)(2,1)}, u32[]{:S(2)}, u32[]{:S(2)}) collective-permute-start(bf16[2,256,1408]{2,1,0:T(8,128)(2,1)} %get-tuple-element.124), channel_id=1, source_target_pairs={{0,4},{2,6},{4,0},{6,2},{1,5},{3,7},{5,1},{7,3},{8,12},{10,14},{12... | collective-permute-start | bytes 4325384 | tf_op jit(solution)/shard_map/ppermute | solution.py:2434
  377.3 3.7 copy-start.1
  381.0 1.6 copy-start
  382.6 1.0 copy-start.5
  382.6 1.6 copy-start.4
  382.6 2.3 copy-start.3
  382.6 3.0 copy-start.2

commit v8 on v7

--- a/solution.py
+++ b/solution.py
@@ -1000,6 +1000,8 @@
     segment_ids,
     cotangent,
     routes,
+    live,
+    rel_bias,
     gate_hbm,
     up_hbm,
     down_hbm,
@@ -1020,6 +1022,8 @@
     codes,
     code_rows,
     extras,
+    alive,
+    bias_line,
     full,
     norm,
     out_full,
@@ -1183,6 +1187,17 @@
     out_full[side, block(own, ctx), :] = out_weight[...]
     segments[ctx] = segment[...]
 
+    index = lax.broadcasted_iota(jnp.int32, (NBUCK, SPAN), 1)
+    relative = jnp.where(index < SPAN // 2, -index, SPAN - index)
+    bucket = lax.broadcasted_iota(jnp.int32, (NBUCK, SPAN), 0)
+    onehot = jnp.where(bucket_ids(relative) == bucket, 1.0, 0.0)
+    found = jnp.dot(
+        rel_bias[...], onehot, precision=lax.Precision.HIGHEST, preferred_element_type=jnp.float32
+    )
+    head = lax.broadcasted_iota(jnp.int32, found.shape, 0)
+    for number in range(2):
+        chosen = jnp.where(head == 2 * ctx + number, found, 0.0)
+        bias_line[number : number + 1, :] = jnp.sum(chosen, axis=0, keepdims=True)
     lane = lax.broadcasted_iota(jnp.int32, (here, LANES), 1).astype(jnp.float32)
     named = jnp.concatenate([routes[...].astype(jnp.float32), jnp.zeros((6, here))], axis=0)
     columns = jnp.transpose(named)
@@ -1353,6 +1368,27 @@
             spot = upstream_hbm.at[shard, lines(1 - side, piece)]
             remote(spot, spot, line_send.at[0], pass_recv.at[shard, piece], pair).wait_recv()
 
+    shape = alive.shape
+    query = lax.broadcasted_iota(jnp.int32, shape, 0)
+    keys = lax.broadcasted_iota(jnp.int32, shape, 1)
+    ends = [jnp.zeros(shape, jnp.float32)] * 4
+    for tile in range(shape[0]):
+        place, start = tile * TILE // here, tile * TILE % here
+        first = segments[place, 0:1, start : start + 1]
+        last = segments[place, 0:1, start + TILE - 1 : start + TILE]
+        for number, (which, value) in enumerate(
+            ((query, first), (query, last), (keys, first), (keys, last))
+        ):
+            ends[number] = jnp.where(which == tile, value, ends[number])
+    open_blocks = jnp.zeros(shape, jnp.int32)
+    ratio = ATT_BLK // TILE
+    for row in range(live.shape[0]):
+        for column in range(live.shape[1]):
+            here_now = (query // ratio == row) & (keys // ratio == column)
+            value = live[row : row + 1, column : column + 1]
+            open_blocks = jnp.where(here_now, value, open_blocks)
+    meets = (ends[0] <= ends[3]) & (ends[2] <= ends[1]) & (open_blocks == 1)
+    alive[...] = jnp.where(meets, 1, 0)
     for copy in stores:
         copy.wait()
     for step in range(3):
@@ -1402,11 +1438,13 @@
             jax.ShapeDtypeStruct((here, 4), jnp.float32),
             jax.ShapeDtypeStruct((8, here), jnp.float32),
             jax.ShapeDtypeStruct((rows * count * ctx_size, LANES), low),
+            jax.ShapeDtypeStruct((ctx_size * here // TILE,) * 2, jnp.int32),
+            jax.ShapeDtypeStruct((2, SPAN), jnp.float32),
         ),
-        in_specs=in_vmem(11) + [pl.BlockSpec(memory_space=pl.ANY)] * 3,
+        in_specs=in_vmem(13) + [pl.BlockSpec(memory_space=pl.ANY)] * 3,
         out_specs=tuple(
-            pl.BlockSpec(memory_space=pltpu.VMEM if number in (1, 3, 14, 15, 16) else pl.ANY)
-            for number in range(17)
+            pl.BlockSpec(memory_space=pltpu.VMEM if number in (1, 3, 14, 15, 16, 17, 18) else pl.ANY)
+            for number in range(19)
         ),
         scratch_shapes=[
             pltpu.VMEM((rows * count * ctx_size, columns), low),
@@ -1573,7 +1611,7 @@
         compiler_params=pltpu.CompilerParams(
             collective_id=4, has_side_effects=True, vmem_limit_bytes=67043328
         ),
-        cost_estimate=estimate(25),
+        cost_estimate=estimate(1),
         name="attend_out",
     )(attended, tokens, out_w, extras, codes)
 
@@ -2472,22 +2510,22 @@
         segment_ids,
         cotangent,
         routes.T,
+        live_blocks[0],
+        rel_bias.T,
     )
     full, packed, norm_one, segments, out_w, up_slots, *lows = run_gather(
         count, ctx_size, room, members, (w_gate[0], w_up[0], w_down[0])
     )
     gate_low, up_low, down_low, gate_core, up_core, down_core, gate_chip, gate_far = lows[:8]
-    codes, code_rows, extras = lows[8:]
+    codes, code_rows, extras, alive, line = lows[8:]
+    alive = alive.reshape(-1)
     up_chip, down_chip = ppermute_ctx(up_low, 2), ppermute_ctx(down_low, 2)
 
     packed = packed.reshape(ctx_size * rows_here, 3 * share)
     segment_row = segments[:, 0].reshape(1, -1)
-    alive = live_tiles(segment_row[0], live_blocks[0])
     pair_heads = share // HEAD
-    own_bias = lax.dynamic_slice_in_dim(rel_bias, ctx_index * pair_heads, pair_heads, 1)
-    line = jnp.dot(own_bias.T, span_buckets().T, precision=lax.Precision.HIGHEST)
     attended, attended_t, log_sum = run_forward(alive, packed, segment_row, line)
-    attended, up_chip, down_chip = lax.optimization_barrier((attended, up_chip, down_chip))
+    attended, up_chip = lax.optimization_barrier((attended, up_chip))
     expert_weights = [gate_low, gate_chip, gate_core, gate_far]
     expert_weights += [up_low, up_chip, up_core, ppermute_ctx(up_chip, 1)]
     expert_weights += [down_low, down_chip, down_core, ppermute_ctx(down_chip, 1)]

time: 393 us -> 392 us (level)
  transfers between devices with their start and end apart: 10 -> 10, of which waited for: 2 -> 2; matrix products, arithmetic and copies ran while one was open for 3% -> 2% of each run, Pallas kernels for 37% -> 37%
where the time goes in v8:
time: 392 us; the launch traced here: 385 us
  Pallas kernels  342 us (87%)
  waiting for transfers between devices  14.2 us (4%)
  local copies, waits for them, and re-layouts  11.1 us (3%)
  starting transfers between devices  10.8 us (3%)
  other arithmetic  6.27 us (2%)
    pallas_call x1, Pallas kernels, run_experts(): pl.pallas_call(partial(expert_exchange, count), out_shape=(jax.ShapeDtype...  118 us
    pallas_call x1, Pallas kernels, run_gather(): pl.pallas_call(partial(gather_project, count), out_shape=(jax.ShapeDtypeS...  80.8 us
    pallas_call x1, Pallas kernels, run_return(): pl.pallas_call(partial(gradient_return, count), out_shape=(jax.ShapeDtype...  64.4 us
    pallas_call x1, Pallas kernels, run_backward(): pl.pallas_call(attention_backward, out_shape=(jax.ShapeDtypeStruct((lengt...  25 us
    pallas_call x1, Pallas kernels, run_forward(): pl.pallas_call(attention_forward, out_shape=(jax.ShapeDtypeStruct((length...  20.6 us
    pallas_call x1, Pallas kernels, run_attend_out(): pl.pallas_call(attend_out, out_shape=(jax.ShapeDtypeStruct((here, width),...  20 us
    pallas_call x1, Pallas kernels, run_attend_back(): pl.pallas_call(attend_back, out_shape=(jax.ShapeDtypeStruct((here, width)...  12.8 us
    ppermute x5, waiting for transfers between devices, ppermute_ctx(): lax.ppermute(member, 'ctx', [(place, place ^ flip) for place in range(4)])  8.4 us
  transfers between devices with their start and end apart: 10, of which 2 were waited for; matrix products, arithmetic and copies ran while one was open for 2% of the time, Pallas kernels for 37%

profile of v8, /device:TPU:0, one launch (start us, length us, event | category | flops | bytes accessed | tf_op | source)
XLA Modules:
  0.0 385.0 jit_solution(4807584073011198305)
XLA Ops:
  0.7 80.8 %gather_project.1 = (bf16[1024,1664]{1,0:T(8,128)(2,1)}, bf16[4,512,384]{2,1,0:T(8,128)(2,1)}, bf16[512,1024]{1,0:T(8,128)(2,1)}, f32[4,8,512]{2,1,0:T(8,128)}, ...) custom-call(f32[64,512]{1,0:T(8,128)} %w_query.1, ...), custom_call_target="tpu_custom_call" | custom-call | flops 60000002048 | tf_op jit(solution)/shard_map/gather_project/pallas_call | solution.py:1428
  81.5 0.8 collective-permute-start
  82.3 1.3 collective-permute-start.2
  83.6 1.4 slice.30
  85.0 1.3 reshape.46.alive
  86.3 20.6 %attention_forward.1 = (bf16[2048,128]{1,0:T(8,128)(2,1)}, f32[128,2048]{1,0:T(8,128)}, f32[8,2048]{1,0:T(8,128)}) custom-call(s32[64]{0:T(128)} %reshape.46.alive, bf16[2048,384]{1,0:T(8,128)(2,1)} %bitcast.41, f32[1,2048]{1,0:T(1,128)} %bitcast.29, f32[2,1024]{1,0:T(2,128)} %get-tuple-element.73.line), custom_call_target="tpu_custom_call" | custom-call | flops 20000000000 | tf_op jit(solution)/shard_map/attention_forward/pallas_call | solution.py:294
  106.9 8.4 %collective-permute-done.2.down_chip = bf16[256,1408]{1,0:T(8,128)(2,1)} collective-permute-done((bf16[256,1408]{1,0:T(8,128)(2,1)}, bf16[256,1408]{1,0:T(8,128)(2,1)}, u32[]{:S(2)}, u32[]{:S(2)}) %collective-permute-start.2) | collective-permute-done | bytes 720928 | tf_op jit(solution)/shard_map/ppermute | solution.py:2472
  115.3 20.0 %attend_out.1 = (f32[512,1024]{1,0:T(8,128)}, bf16[512,1024]{1,0:T(8,128)(2,1)}, f32[512,2]{1,0:T(8,128)}, bf16[512,512]{1,0:T(8,128)(2,1)}) custom-call(bf16[4,512,128]{2,1,0:T(8,128)(2,1)} %bitcast.28, bf16[512,1024]{1,0:T(8,128)(2,1)} %tokens.3, bf16[2,1024,512]{2,1,0:T(8,128)(2,1)} %get-tuple-element.77.out_hbm, ...), custom_call_target="tpu_custom_call" | custom-call | flops 1000000000 | tf_op jit(solution)/shard_map/attend_out/pallas_call | solution.py:1589
  135.3 118.2 %expert_exchange.1 = (f32[512,1024]{1,0:T(8,128)}, f32[8,512]{1,0:T(8,128)}, bf16[384,1024]{1,0:T(8,128)(2,1)}, bf16[192,1024]{1,0:T(8,128)(2,1)}, bf16[192,1024...) custom-call(bf16[512,1024]{1,0:T(8,128)(2,1)} %get-tuple-element.80., ...), custom_call_target="tpu_custom_call" | custom-call | flops 109999996928 | tf_op jit(solution)/shard_map/expert_exchange/pallas_call | solution.py:913
  253.5 3.3 collective-permute-start.4
  256.9 2.2 collective-permute-start.6
  259.1 0.7 collective-permute-start.7
  259.8 1.7 collective-permute-start.8
  261.5 2.6 fusion
  264.1 12.8 %attend_back.1 = (f32[512,1024]{1,0:T(8,128)}, bf16[512,1024]{1,0:T(8,128)(2,1)}, bf16[4,512,128]{2,1,0:T(8,128)(2,1)}, f32[8,1024]{1,0:T(8,128)}) custom-call(f32[512,1024]{1,0:T(8,128)} %get-tuple-element.92.rows_hbm, f32[8,512]{1,0:T(8,128)} %get-tuple-element.93.dot_rows, f32[512,2]{1,0:T(8,128)} %get-tuple-element.81.gates, ...), custom_call_target="tpu_custom_call" | custom-call | flops 4000000000 | tf_op jit(solution)/shard_map/attend_back/pallas_call | solution.py:1730
  276.9 5.8 %collective-permute-done.4.first_hbm = bf16[192,1024]{1,0:T(8,128)(2,1)} collective-permute-done((bf16[192,1024]{1,0:T(8,128)(2,1)}, bf16[192,1024]{1,0:T(8,128)(2,1)}, u32[]{:S(2)}, u32[]{:S(2)}) %collective-permute-start.4) | collective-permute-done | bytes 393248 | tf_op jit(solution)/shard_map/ppermute | solution.py:2540
  282.7 0.7 collective-permute-start.9
  283.4 25.0 %attention_backward.1 = (bf16[2048,384]{1,0:T(8,128)(2,1)}, f32[8,1024]{1,0:T(8,128)}) custom-call(s32[64]{0:T(128)} %reshape.46.alive, bf16[2048,384]{1,0:T(8,128)(2,1)} %bitcast.42, f32[1,2048]{1,0:T(1,128)} %bitcast.30, f32[2,1024]{1,0:T(2,128)} %get-tuple-element.73.line, bf16[2048,128]{1,0:T(8,128)(2,1)} %bitcast.44, ...), custom_call_target="tpu_custom_call" | custom-call | flops 4000000000 | tf_op jit(solution)/shard_map/attention_backward/pallas_call | solution.py:320
  308.4 64.4 %gradient_return.1 = (bf16[512,1024]{1,0:T(8,128)(2,1)}, bf16[512,1024]{1,0:T(8,128)(2,1)}, f32[64,512]{1,0:T(8,128)}, f32[64,512]{1,0:T(8,128)}, f32[64,512]{1,...) custom-call(bf16[4,512,384]{2,1,0:T(8,128)(2,1)} %bitcast.43, ...), custom_call_target="tpu_custom_call" | custom-call | flops 44999999488 | tf_op jit(solution)/shard_map/gradient_return/pallas_call | solution.py:2156
  372.8 1.3 slice.31
  374.1 0.8 constant_dynamic-slice_fusion
  375.9 3.7 convert_add_fusion.1
  379.6 1.0 copy.35
  381.3 1.0 copy.36
  (29 shorter events, 4.5 us)
Async XLA Ops:
  81.5 25.4 %collective-permute-start = (bf16[256,1408]{1,0:T(8,128)(2,1)}, bf16[256,1408]{1,0:T(8,128)(2,1)}, u32[]{:S(2)}, u32[]{:S(2)}) collective-permute-start(bf16[256,1408]{1,0:T(8,128)(2,1)} %get-tuple-element.75.up_own), channel_id=1, source_target_pairs={{0,4},{2,6},{4,0},{6,2},{1,5},{3,7},{5,1},{7,3},{8,12},{10,14},{12... | collective-permute-start | bytes 2162696 | tf_op jit(solution)/shard_map/ppermute | solution.py:2472
  82.3 33.0 %collective-permute-start.2 = (bf16[256,1408]{1,0:T(8,128)(2,1)}, bf16[256,1408]{1,0:T(8,128)(2,1)}, u32[]{:S(2)}, u32[]{:S(2)}) collective-permute-start(bf16[256,1408]{1,0:T(8,128)(2,1)} %get-tuple-element.90.down_own), channel_id=1, source_target_pairs={{0,4},{2,6},{4,0},{6,2},{1,5},{3,7},{5,1},{7,3},{8,12},{10,14},{12... | collective-permute-start | bytes 2162696 | tf_op jit(solution)/shard_map/ppermute | solution.py:2472
  106.9 28.4 %collective-permute-start.1 = (bf16[256,1408]{1,0:T(8,128)(2,1)}, bf16[256,1408]{1,0:T(8,128)(2,1)}, u32[]{:S(2)}, u32[]{:S(2)}) collective-permute-start(bf16[256,1408]{1,0:T(8,128)(2,1)} %collective-permute-done.up_chip), channel_id=1, source_target_pairs={{0,2},{2,0},{4,6},{6,4},{1,3},{3,1},{5,7},{7,5},{8,10},{10,8},{12,... | collective-permute-start | bytes 2162696 | tf_op jit(solution)/shard_map/ppermute | solution.py:2472
  115.3 20.0 %collective-permute-start.3 = (bf16[256,1408]{1,0:T(8,128)(2,1)}, bf16[256,1408]{1,0:T(8,128)(2,1)}, u32[]{:S(2)}, u32[]{:S(2)}) collective-permute-start(bf16[256,1408]{1,0:T(8,128)(2,1)} %collective-permute-done.2.down_chip), channel_id=1, source_target_pairs={{0,2},{2,0},{4,6},{6,4},{1,3},{3,1},{5,7},{7,5},{8,10},{10,8},{12,... | collective-permute-start | bytes 2162696 | tf_op jit(solution)/shard_map/ppermute | solution.py:2472
  253.5 29.2 %collective-permute-start.4 = (bf16[192,1024]{1,0:T(8,128)(2,1)}, bf16[192,1024]{1,0:T(8,128)(2,1)}, u32[]{:S(2)}, u32[]{:S(2)}) collective-permute-start(bf16[192,1024]{1,0:T(8,128)(2,1)} %get-tuple-element.97), channel_id=1, source_target_pairs={{0,8},{8,0},{16,24},{24,16},{1,9},{9,1},{17,25},{25,17},{2,10},{10... | collective-permute-start | bytes 1179656 | tf_op jit(solution)/shard_map/ppermute | solution.py:2540
  256.8 51.5 %collective-permute-start.5 = (bf16[192,1024]{1,0:T(8,128)(2,1)}, bf16[192,1024]{1,0:T(8,128)(2,1)}, u32[]{:S(2)}, u32[]{:S(2)}) collective-permute-start(bf16[192,1024]{1,0:T(8,128)(2,1)} %get-tuple-element.107), channel_id=1, source_target_pairs={{0,8},{8,0},{16,24},{24,16},{1,9},{9,1},{17,25},{25,17},{2,10},{10... | collective-permute-start | bytes 1179656 | tf_op jit(solution)/shard_map/ppermute | solution.py:2540
  256.9 51.5 %collective-permute-start.6 = (bf16[192,1024]{1,0:T(8,128)(2,1)}, bf16[192,1024]{1,0:T(8,128)(2,1)}, u32[]{:S(2)}, u32[]{:S(2)}) collective-permute-start(bf16[192,1024]{1,0:T(8,128)(2,1)} %get-tuple-element.108), channel_id=1, source_target_pairs={{0,16},{8,24},{16,0},{24,8},{1,17},{9,25},{17,1},{25,9},{2,18},{10... | collective-permute-start | bytes 1179656 | tf_op jit(solution)/shard_map/ppermute | solution.py:2540
  259.1 49.3 %collective-permute-start.7 = (bf16[192,1024]{1,0:T(8,128)(2,1)}, bf16[192,1024]{1,0:T(8,128)(2,1)}, u32[]{:S(2)}, u32[]{:S(2)}) collective-permute-start(bf16[192,1024]{1,0:T(8,128)(2,1)} %get-tuple-element.109), channel_id=1, source_target_pairs={{0,16},{8,24},{16,0},{24,8},{1,17},{9,25},{17,1},{25,9},{2,18},{10... | collective-permute-start | bytes 1179656 | tf_op jit(solution)/shard_map/ppermute | solution.py:2540
  259.8 48.5 %collective-permute-start.8 = (bf16[192,1024]{1,0:T(8,128)(2,1)}, bf16[192,1024]{1,0:T(8,128)(2,1)}, u32[]{:S(2)}, u32[]{:S(2)}) collective-permute-start(bf16[192,1024]{1,0:T(8,128)(2,1)} %get-tuple-element.110), channel_id=1, source_target_pairs={{0,24},{8,16},{16,8},{24,0},{1,25},{9,17},{17,9},{25,1},{2,26},{10... | collective-permute-start | bytes 1179656 | tf_op jit(solution)/shard_map/ppermute | solution.py:2540
  282.7 93.2 %collective-permute-start.9 = (bf16[2,256,1408]{2,1,0:T(8,128)(2,1)}, bf16[2,256,1408]{2,1,0:T(8,128)(2,1)}, u32[]{:S(2)}, u32[]{:S(2)}) collective-permute-start(bf16[2,256,1408]{2,1,0:T(8,128)(2,1)} %get-tuple-element.126), channel_id=1, source_target_pairs={{0,4},{2,6},{4,0},{6,2},{1,5},{3,7},{5,1},{7,3},{8,12},{10,14},{12... | collective-permute-start | bytes 4325384 | tf_op jit(solution)/shard_map/ppermute | solution.py:2472
  375.9 3.7 copy-start.1
  379.6 1.6 copy-start
  381.2 1.0 copy-start.5
  381.2 1.6 copy-start.4
  381.2 2.3 copy-start.3
  381.2 3.0 copy-start.2
